TPU v7x, 32 devices: a whole 2x2x4 slice. The times are simulated.
32 devices in a mesh: dp: 16 (over z, x, core), tensor: 2 (over y).
Axes of the slice: x: 2, y: 2, z: 4, core: 2. Of those that a mesh axis runs over, the one named last changes fastest.
Arguments:
- tokens: bfloat16 [4096, 2048], P(('dp', 'tensor')), may hold values from -6 to 6
- segment_ids: int32 [16, 256], P('dp'), may hold values from 0 to 3, never falling along the last dimension, each value on 1 to 128 neighbouring positions
- w_query: bfloat16 [2048, 2048], P('dp', 'tensor'), may hold values from -0.125 to 0.125
- w_key: bfloat16 [2048, 2048], P('dp', 'tensor'), may hold values from -0.125 to 0.125
- w_value: bfloat16 [2048, 2048], P('dp', 'tensor'), may hold values from -0.125 to 0.125
- w_output: bfloat16 [2048, 2048], P('dp', 'tensor'), may hold values from -0.125 to 0.125
- w_gate: bfloat16 [2048, 8192], P('dp', 'tensor'), may hold values from -0.125 to 0.125
- w_up: bfloat16 [2048, 8192], P('dp', 'tensor'), may hold values from -0.125 to 0.125
- w_down: bfloat16 [2048, 8192], P('dp', 'tensor'), may hold values from -0.0625 to 0.0625
- query_gain: float32 [2048], P(('dp', 'tensor')), may hold values from 0.5 to 2
- key_gain: float32 [2048], P(('dp', 'tensor')), may hold values from 0.5 to 2
- attn_gain: float32 [2048], P(('dp', 'tensor')), may hold values from 0.1 to 1.9
- ffn_gain: float32 [2048], P(('dp', 'tensor')), may hold values from 0.1 to 1.9
- cotangent: bfloat16 [4096, 2048], P(('dp', 'tensor')), may hold values from -6 to 6
Outputs:
- output: bfloat16 [4096, 2048], P(('dp', 'tensor'))
- grad_tokens: float32 [4096, 2048], P(('dp', 'tensor'))
- grad_query: float32 [2048, 2048], P('dp', 'tensor')
- grad_key: float32 [2048, 2048], P('dp', 'tensor')
- grad_value: float32 [2048, 2048], P('dp', 'tensor')
- grad_output: float32 [2048, 2048], P('dp', 'tensor')
- grad_gate: float32 [2048, 8192], P('dp', 'tensor')
- grad_up: float32 [2048, 8192], P('dp', 'tensor')
- grad_down: float32 [2048, 8192], P('dp', 'tensor')
- grad_query_gain: float32 [2048], P(('dp', 'tensor'))
- grad_key_gain: float32 [2048], P(('dp', 'tensor'))
- grad_attn_gain: float32 [2048], P(('dp', 'tensor'))
- grad_ffn_gain: float32 [2048], P(('dp', 'tensor'))
Inputs may be any that keep to these rules, and one draw needn't show every extreme that they name: `segment_ids`: within each sequence the ids never fall; each document has 1 to 128 tokens, and one has exactly 128.
All inputs are finite; a program needn't handle non-finite values.
Results may differ from a plain program's by a relative error of at most 0.015.
Values may be sent and summed in bfloat16 or wider, within the bound.
No kernel may reach another device: no remote copies, remote signals or barrier semaphores. Data moves between devices by JAX's collectives and lax.ppermute only.
A program may use at most 384 MiB of HBM per device.

v0:
```python
import math

import jax
import jax.numpy as jnp
from jax import lax
from jax.sharding import PartitionSpec as P

HD = 128


EPSILON = 1e-06
NEGATIVE = -1e30


def rms_scale(values):
    return lax.rsqrt(jnp.mean(values * values, axis=1, keepdims=True) + EPSILON)


def whole_rows(halves):
    return lax.all_gather(halves, "tensor", axis=0, tiled=True)


def to_halves(partial_value):
    return lax.psum_scatter(partial_value, "tensor", scatter_dimension=0, tiled=True)


def norm_totals(pair):
    return lax.psum((pair[0], pair[1]), "tensor")


def shards(
    tokens,
    segment_ids,
    w_query,
    w_key,
    w_value,
    w_output,
    w_gate,
    w_up,
    w_down,
    query_gain,
    key_gain,
    attn_gain,
    ffn_gain,
    cotangent,
):
    tensor_index = lax.axis_index("tensor")
    head_width = w_query.shape[1]
    ffn_width = w_gate.shape[1]
    own_rows = w_query.shape[0]
    model_width = own_rows * lax.axis_size("dp")
    seq_length = tokens.shape[0] * lax.axis_size("tensor")
    local_heads = head_width // HD
    score_scale = 1.0 / math.sqrt(HD)
    gains = lax.all_gather(
        jnp.stack([query_gain, key_gain, attn_gain, ffn_gain]), ("dp", "tensor"), axis=1, tiled=True
    )
    query_scale = lax.dynamic_slice_in_dim(gains[0], tensor_index * head_width, head_width)
    key_scale = lax.dynamic_slice_in_dim(gains[1], tensor_index * head_width, head_width)
    attn_scale = gains[2]
    ffn_scale = gains[3]
    positions = jnp.arange(seq_length)
    seq_ids = segment_ids[0]
    visible = (positions[:, None] >= positions[None, :]) & (seq_ids[:, None] == seq_ids[None, :])
    whole_input = whole_rows(tokens)
    pieces = (
        lax.all_gather(w_query, "dp", axis=0, tiled=True),
        lax.all_gather(w_key, "dp", axis=0, tiled=True),
        lax.all_gather(w_value, "dp", axis=0, tiled=True),
        lax.all_gather(w_output, "dp", axis=0, tiled=True),
    )
    columns = whole_input
    query_acc = jnp.dot(columns, pieces[0], preferred_element_type=jnp.float32)
    key_acc = jnp.dot(columns, pieces[1], preferred_element_type=jnp.float32)
    value_acc = jnp.dot(columns, pieces[2], preferred_element_type=jnp.float32)
    stored = pieces[3]
    query, key_proj, value_acc, output_rows = (query_acc, key_acc, value_acc, stored)
    squares = norm_totals((jnp.sum(query * query, axis=1), jnp.sum(key_proj * key_proj, axis=1)))
    q_rms = lax.rsqrt(squares[0] / model_width + EPSILON)[:, None]
    k_rms = lax.rsqrt(squares[1] / model_width + EPSILON)[:, None]
    normed_query = (query * q_rms * query_scale).astype(jnp.bfloat16)
    normed_key = (key_proj * k_rms * key_scale).astype(jnp.bfloat16)
    value_bf = value_acc.astype(jnp.bfloat16)
    query_heads = normed_query.reshape(seq_length, local_heads, HD)
    key_heads = normed_key.reshape(seq_length, local_heads, HD)
    value_heads = value_bf.reshape(seq_length, local_heads, HD)
    scores = (
        jnp.einsum("qhd,khd->hqk", query_heads, key_heads, preferred_element_type=jnp.float32)
        * score_scale
    )
    scores = jnp.where(visible[None], scores, NEGATIVE)
    peak = jnp.max(scores, axis=-1, keepdims=True)
    expo = jnp.exp(scores - peak)
    total = jnp.sum(expo, axis=-1, keepdims=True)
    log_total = peak + jnp.log(total)
    prob_bf = (expo / total).astype(jnp.bfloat16)
    attn_heads = jnp.einsum(
        "hqk,khd->qhd", prob_bf, value_heads, preferred_element_type=jnp.float32
    ).astype(jnp.bfloat16)
    attn = attn_heads.reshape(seq_length, head_width)
    proj = to_halves(jnp.einsum("sc,oc->so", attn, output_rows, preferred_element_type=jnp.float32))
    attn_rms = rms_scale(proj)
    resid = tokens.astype(jnp.float32) + proj * attn_rms * attn_scale
    whole_hidden = whole_rows(resid.astype(jnp.bfloat16))
    pieces = (
        lax.all_gather(w_gate, "dp", axis=0, tiled=True),
        lax.all_gather(w_up, "dp", axis=0, tiled=True),
        lax.all_gather(w_down, "dp", axis=0, tiled=True),
    )
    columns = whole_hidden
    gate_acc = jnp.dot(columns, pieces[0], preferred_element_type=jnp.float32)
    up_acc = jnp.dot(columns, pieces[1], preferred_element_type=jnp.float32)
    stored = pieces[2]
    sigma = jax.nn.sigmoid(gate_acc)
    act = (gate_acc * sigma * up_acc).astype(jnp.bfloat16)
    ffn = to_halves(jnp.einsum("sf,of->so", act, stored, preferred_element_type=jnp.float32))
    ffn_rms = rms_scale(ffn)
    output = (resid + ffn * ffn_rms * ffn_scale).astype(jnp.bfloat16)
    d_out = cotangent.astype(jnp.float32)
    ffn_gain_term = jnp.sum(d_out * ffn * ffn_rms, axis=0)
    scaled_out = d_out * ffn_scale
    d_ffn = (
        ffn_rms
        * (scaled_out - ffn * ffn_rms * ffn_rms * jnp.mean(scaled_out * ffn, axis=1, keepdims=True))
    ).astype(jnp.bfloat16)
    whole_dffn = whole_rows(d_ffn)
    d_act = jnp.dot(whole_dffn, stored, preferred_element_type=jnp.float32)
    d_gate = (d_act * up_acc * sigma * (1.0 + gate_acc * (1.0 - sigma))).astype(jnp.bfloat16)
    d_up = (d_act * gate_acc * sigma).astype(jnp.bfloat16)
    pieces = (
        lax.all_gather(w_gate, "dp", axis=0, tiled=True),
        lax.all_gather(w_up, "dp", axis=0, tiled=True),
    )
    block = jnp.einsum(
        "sf,rf->sr", d_gate, pieces[0], preferred_element_type=jnp.float32
    ) + jnp.einsum("sf,rf->sr", d_up, pieces[1], preferred_element_type=jnp.float32)
    hidden_part = block
    d_resid = d_out + to_halves(hidden_part)
    attn_gain_term = jnp.sum(d_resid * proj * attn_rms, axis=0)
    scaled_resid = d_resid * attn_scale
    d_proj = (
        attn_rms
        * (
            scaled_resid
            - proj * attn_rms * attn_rms * jnp.mean(scaled_resid * proj, axis=1, keepdims=True)
        )
    ).astype(jnp.bfloat16)
    whole_dproj = whole_rows(d_proj)
    d_attn = jnp.dot(whole_dproj, output_rows, preferred_element_type=jnp.float32).astype(
        jnp.bfloat16
    )
    d_attn_heads = d_attn.reshape(seq_length, local_heads, HD)
    back_prob = jnp.where(visible[None], jnp.exp(scores - log_total), 0.0)
    back_bf = back_prob.astype(jnp.bfloat16)
    d_value = (
        jnp.einsum("hqk,qhd->khd", back_bf, d_attn_heads, preferred_element_type=jnp.float32)
        .reshape(seq_length, head_width)
        .astype(jnp.bfloat16)
    )
    d_prob = jnp.einsum(
        "qhd,khd->hqk", d_attn_heads, value_heads, preferred_element_type=jnp.float32
    )
    delta = jnp.einsum("qhd,qhd->hq", d_attn_heads, attn_heads, preferred_element_type=jnp.float32)[
        ..., None
    ]
    d_score = (back_prob * (d_prob - delta)).astype(jnp.bfloat16)
    d_nq = (
        jnp.einsum("hqk,khd->qhd", d_score, key_heads, preferred_element_type=jnp.float32).reshape(
            seq_length, head_width
        )
        * score_scale
    )
    d_nk = (
        jnp.einsum(
            "hqk,qhd->khd", d_score, query_heads, preferred_element_type=jnp.float32
        ).reshape(seq_length, head_width)
        * score_scale
    )
    query_gain_term = jnp.sum(d_nq * query * q_rms, axis=0)
    key_gain_term = jnp.sum(d_nk * key_proj * k_rms, axis=0)
    scaled_q = d_nq * query_scale
    scaled_k = d_nk * key_scale
    inner = norm_totals((jnp.sum(scaled_q * query, axis=1), jnp.sum(scaled_k * key_proj, axis=1)))
    d_query = (
        q_rms * (scaled_q - query * q_rms * q_rms * (inner[0] / model_width)[:, None])
    ).astype(jnp.bfloat16)
    d_key = (
        k_rms * (scaled_k - key_proj * k_rms * k_rms * (inner[1] / model_width)[:, None])
    ).astype(jnp.bfloat16)
    pieces = (
        lax.all_gather(w_query, "dp", axis=0, tiled=True),
        lax.all_gather(w_key, "dp", axis=0, tiled=True),
        lax.all_gather(w_value, "dp", axis=0, tiled=True),
    )
    block = (
        jnp.einsum("sc,rc->sr", d_query, pieces[0], preferred_element_type=jnp.float32)
        + jnp.einsum("sc,rc->sr", d_key, pieces[1], preferred_element_type=jnp.float32)
        + jnp.einsum("sc,rc->sr", d_value, pieces[2], preferred_element_type=jnp.float32)
    )
    grad_tokens = d_resid + to_halves(block)
    gate_term = jnp.einsum("sr,sf->rf", whole_hidden, d_gate, preferred_element_type=jnp.float32)
    up_term = jnp.einsum("sr,sf->rf", whole_hidden, d_up, preferred_element_type=jnp.float32)
    down_term = jnp.einsum("sr,sf->rf", whole_dffn, act, preferred_element_type=jnp.float32)
    query_term = jnp.einsum("sr,sc->rc", whole_input, d_query, preferred_element_type=jnp.float32)
    key_term = jnp.einsum("sr,sc->rc", whole_input, d_key, preferred_element_type=jnp.float32)
    value_term = jnp.einsum("sr,sc->rc", whole_input, d_value, preferred_element_type=jnp.float32)
    output_term = jnp.einsum("sr,sc->rc", whole_dproj, attn, preferred_element_type=jnp.float32)
    combined = lax.psum_scatter(
        jnp.concatenate(
            [
                jnp.concatenate([query_term, key_term, value_term, output_term], axis=1),
                jnp.concatenate([gate_term, up_term, down_term], axis=1),
            ],
            axis=1,
        ),
        "dp",
        scatter_dimension=0,
        tiled=True,
    )
    attn_sums = combined[:, : 4 * head_width]
    mlp_sums = combined[:, 4 * head_width :]
    gain_zero = jnp.zeros((model_width,), jnp.float32)
    query_placed = lax.dynamic_update_slice_in_dim(
        gain_zero, query_gain_term, tensor_index * head_width, 0
    )
    key_placed = lax.dynamic_update_slice_in_dim(
        gain_zero, key_gain_term, tensor_index * head_width, 0
    )
    gain_parts = lax.psum_scatter(
        jnp.stack([query_placed, key_placed, attn_gain_term, ffn_gain_term]),
        ("dp", "tensor"),
        scatter_dimension=1,
        tiled=True,
    )
    grad_query = attn_sums[:, :head_width]
    grad_key = attn_sums[:, head_width : 2 * head_width]
    grad_value = attn_sums[:, 2 * head_width : 3 * head_width]
    grad_output = attn_sums[:, 3 * head_width :]
    grad_gate = mlp_sums[:, :ffn_width]
    grad_up = mlp_sums[:, ffn_width : 2 * ffn_width]
    grad_down = mlp_sums[:, 2 * ffn_width :]
    return (
        output,
        grad_tokens,
        grad_query,
        grad_key,
        grad_value,
        grad_output,
        grad_gate,
        grad_up,
        grad_down,
        gain_parts[0],
        gain_parts[1],
        gain_parts[2],
        gain_parts[3],
    )


def solution(mesh):
    return jax.shard_map(
        shards,
        mesh=mesh,
        in_specs=(
            P(("dp", "tensor"), None),
            P("dp", None),
            P("dp", "tensor"),
            P("dp", "tensor"),
            P("dp", "tensor"),
            P("dp", "tensor"),
            P("dp", "tensor"),
            P("dp", "tensor"),
            P("dp", "tensor"),
            P(("dp", "tensor")),
            P(("dp", "tensor")),
            P(("dp", "tensor")),
            P(("dp", "tensor")),
            P(("dp", "tensor"), None),
        ),
        out_specs=(
            P(("dp", "tensor"), None),
            P(("dp", "tensor"), None),
            P("dp", "tensor"),
            P("dp", "tensor"),
            P("dp", "tensor"),
            P("dp", "tensor"),
            P("dp", "tensor"),
            P("dp", "tensor"),
            P("dp", "tensor"),
            P(("dp", "tensor")),
            P(("dp", "tensor")),
            P(("dp", "tensor")),
            P(("dp", "tensor")),
        ),
        check_vma=False,
    )
```

profile of v0, /device:TPU:0, one launch (start us, length us, event | category | flops | bytes accessed | tf_op | source)
XLA Modules:
  0.0 2322.3 jit_solution(9547360384983591995)
XLA Ops:
  11.3 71.0 %all-gather = f32[32,64,4]{1,2,0:T(4,128)S(1)} all-gather(f32[1,64,4]{1,2,0:T(4,128)S(1)} %maximum_bitcast_fusion), channel_id=1, replica_groups=mesh['dp'=16,'tensor'=2] {'dp','tensor'}, dimensions={0}, use_global_device_ids=true | all-gather | bytes 33792 | tf_op jit(solution)/shard_map/all_gather | solution.py:55
  83.4 3.1 all-gather.17.cloned.1.call-done
  86.5 3.8 multiply_reduce_fusion.10
  90.3 47.3 %all-gather.19.cloned.1.call-done = bf16[2048,1024]{1,0:T(8,128)(2,1)} async-done(((bf16[128,1024]{1,0:T(8,128)(2,1)}), bf16[2048,1024]{1,0:T(8,128)(2,1)}) %all-gather.19.cloned.1.call-update) | async-done | bytes 4194320 | tf_op jit(solution)/shard_map/all_gather | solution.py:68
  137.6 3.5 multiply_reduce_fusion.9
  141.2 4.9 all-reduce.1
  152.3 36.3 %all-gather.15.cloned.1.call-done = bf16[2048,1024]{1,0:T(8,128)(2,1)} async-done(((bf16[128,1024]{1,0:T(8,128)(2,1)}), bf16[2048,1024]{1,0:T(8,128)(2,1)}) %all-gather.15.cloned.1.call-update) | async-done | bytes 4194320 | tf_op jit(solution)/shard_map/all_gather | solution.py:69
  188.6 3.4 fusion.4
  193.4 46.1 %all-gather.21.cloned.1.call-done = bf16[2048,1024]{1,0:T(8,128)(2,1)} async-done(((bf16[128,1024]{1,0:T(8,128)(2,1)}), bf16[2048,1024]{1,0:T(8,128)(2,1)}) %all-gather.21.cloned.1.call-update) | async-done | bytes 4194320 | tf_op jit(solution)/shard_map/all_gather | solution.py:70
  239.5 4.9 fusion.28
  244.5 30.5 %reduce-scatter.9.cloned.1.call-done = f32[128,2048]{1,0:T(8,128)} async-done(((f32[256,2048]{1,0:T(8,128)}), f32[128,2048]{1,0:T(8,128)}) %reduce-scatter.9.cloned.1.call-update) | async-done | bytes 1048592 | tf_op jit(solution)/shard_map/reduce_scatter | solution.py:24
  281.0 19.1 all-gather.23.cloned.1.call-done
  300.1 128.6 %all-gather.25.cloned.1.call-done = bf16[2048,4096]{1,0:T(8,128)(2,1)} async-done(((bf16[128,4096]{1,0:T(8,128)(2,1)}), bf16[2048,4096]{1,0:T(8,128)(2,1)}) %all-gather.25.cloned.1.call-update) | async-done | bytes 16777232 | tf_op jit(solution)/shard_map/all_gather | solution.py:106
  428.8 12.6 fusion.29
  441.3 114.2 %all-gather.27.cloned.1.call-done = bf16[2048,4096]{1,0:T(8,128)(2,1)} async-done(((bf16[128,4096]{1,0:T(8,128)(2,1)}), bf16[2048,4096]{1,0:T(8,128)(2,1)}) %all-gather.27.cloned.1.call-update) | async-done | bytes 16777232 | tf_op jit(solution)/shard_map/all_gather | solution.py:107
  555.6 13.4 multiply_convert_fusion.2
  569.0 113.2 %all-gather.29.cloned.1.call-done = bf16[2048,4096]{1,0:T(8,128)(2,1)} async-done(((bf16[128,4096]{1,0:T(8,128)(2,1)}), bf16[2048,4096]{1,0:T(8,128)(2,1)}) %all-gather.29.cloned.1.call-update) | async-done | bytes 16777232 | tf_op jit(solution)/shard_map/all_gather | solution.py:108
  682.2 12.3 fusion.30
  694.6 30.2 %reduce-scatter.11.cloned.1.call-done = f32[128,2048]{1,0:T(8,128)} async-done(((f32[256,2048]{1,0:T(8,128)}), f32[128,2048]{1,0:T(8,128)}) %reduce-scatter.11.cloned.1.call-update) | async-done | bytes 1048592 | tf_op jit(solution)/shard_map/reduce_scatter | solution.py:24
  730.3 21.2 all-gather.31.cloned.1.call-done
  751.5 15.9 multiply_convert_fusion
  767.4 12.2 fusion.31
  779.7 13.3 convolution_add_fusion.2
  793.0 32.0 %reduce-scatter.13.cloned.1.call-done = f32[128,2048]{1,0:T(8,128)} async-done(((f32[256,2048]{1,0:T(8,128)}), f32[128,2048]{1,0:T(8,128)}) %reduce-scatter.13.cloned.1.call-update) | async-done | bytes 1048592 | tf_op jit(solution)/shard_map/reduce_scatter | solution.py:24
  826.8 3.4 multiply_convert_fusion.6
  830.2 21.4 all-gather.33.cloned.1.call-done
  851.6 3.8 fusion.5
  869.3 2.9 copy.99
  874.3 4.9 all-reduce
  882.5 4.6 convolution_bitcast_fusion.2
  887.1 9.4 copy.82
  898.1 3.5 fusion.33
  901.6 4.5 convolution_bitcast_fusion.1
  907.5 4.5 convolution_bitcast_fusion
  914.7 8.3 constant_dynamic-update-slice_fusion.2
  922.9 9.3 copy.83
  932.3 9.3 copy.84
  941.8 8.5 constant_dynamic-update-slice_fusion.1
  950.3 4.3 constant_dynamic-update-slice_fusion
  954.6 4.5 convolution_dynamic-update-slice_fusion.3
  959.2 13.3 convolution_dynamic-update-slice_fusion.2
  972.5 13.2 convolution_dynamic-update-slice_fusion.1
  985.7 13.2 convolution_dynamic-update-slice_fusion
  999.0 35.6 %reduce-scatter.19.cloned.1.call-done = f32[64,4]{1,0:T(8,128)} async-done(((f32[2048,4]{1,0:T(8,128)}), f32[64,4]{1,0:T(8,128)}) %reduce-scatter.19.cloned.1.call-update) | async-done | bytes 1040
  1037.9 26.7 %reduce-scatter.15.cloned.1.call-done = f32[128,2048]{1,0:T(8,128)} async-done(((f32[256,2048]{1,0:T(8,128)}), f32[128,2048]{1,0:T(8,128)}) %reduce-scatter.15.cloned.1.call-update) | async-done | bytes 1048592 | tf_op jit(solution)/shard_map/reduce_scatter | solution.py:24
  1067.0 1240.0 %reduce-scatter.17.cloned.1.call-done = f32[128,16384]{1,0:T(8,128)} async-done(((f32[2048,16384]{1,0:T(8,128)}), f32[128,16384]{1,0:T(8,128)}) %reduce-scatter.17.cloned.1.call-update) | async-done | bytes 8388624 | tf_op jit(solution)/shard_map/reduce_scatter | solution.py:208
  2306.9 2.9 fusion.24
  2309.8 5.8 fusion.23
  (157 shorter events, 56.8 us)
Async XLA Ops:
  7.2 76.2 %all-gather.13.cloned.1.call-start = ((), (), s32[]{:S(2)}) async-start(), calls=%async_computation.6 | async-start | bytes 1572864 | tf_op jit(solution)/shard_map/all_gather | solution.py:20
  7.9 78.5 %all-gather.17.cloned.1.call-start = ((), (), s32[]{:S(2)}) async-start(), calls=%async_computation.8 | async-start | bytes 4456448 | tf_op jit(solution)/shard_map/all_gather | solution.py:67
  8.7 129.0 %all-gather.19.cloned.1.call-start = ((), (), s32[]{:S(2)}) async-start(), calls=%async_computation.9 | async-start | bytes 4456448 | tf_op jit(solution)/shard_map/all_gather | solution.py:68
  9.4 179.2 %all-gather.15.cloned.1.call-start = ((), (), s32[]{:S(2)}) async-start(), calls=%async_computation.7 | async-start | bytes 4456448 | tf_op jit(solution)/shard_map/all_gather | solution.py:69
  10.0 229.6 %all-gather.21.cloned.1.call-start = ((), (), s32[]{:S(2)}) async-start(), calls=%async_computation.10 | async-start | bytes 4456448 | tf_op jit(solution)/shard_map/all_gather | solution.py:70
  10.6 264.5 %reduce-scatter.9.cloned.1.call-start = ((), (), s32[]{:S(2)}) async-start(), calls=%async_computation.11 | async-start | bytes 3145728 | tf_op jit(solution)/shard_map/reduce_scatter | solution.py:24
  83.4 54.2 %copy-start.4 = (bf16[256,2048]{1,0:T(8,128)(2,1)S(1)}, bf16[256,2048]{1,0:T(8,128)(2,1)}, u32[]{:S(2)}) copy-start(bf16[256,2048]{1,0:T(8,128)(2,1)} %all-gather.13.cloned.1.call-done) | copy-start | bytes 3145732
  90.3 56.8 %copy-start.8 = (f32[256,1024]{1,0:T(8,128)}, f32[256,1024]{1,0:T(8,128)S(1)}, u32[]{:S(2)}) copy-start(f32[256,1024]{1,0:T(8,128)S(1)} %get-tuple-element.45) | copy-start | bytes 3145732
  141.1 9.1 copy-start.6
  193.4 51.0 %copy-start.23 = (bf16[8,128,256]{2,1,0:T(8,128)(2,1)}, bf16[8,128,256]{2,1,0:T(8,128)(2,1)S(1)}, u32[]{:S(2)}) copy-start(bf16[8,128,256]{2,1,0:T(8,128)(2,1)S(1)} %convolution_convert_fusion.1) | copy-start | bytes 1572868
  239.5 36.9 %copy-start.15 = (bf16[128,2048]{1,0:T(8,128)(2,1)S(1)}, bf16[128,2048]{1,0:T(8,128)(2,1)}, u32[]{:S(2)}) copy-start(bf16[128,2048]{1,0:T(8,128)(2,1)} %param.14) | copy-start | bytes 1572868
  244.4 55.7 %all-gather.23.cloned.1.call-start = ((), (), s32[]{:S(2)}) async-start(), calls=%async_computation.12 | async-start | bytes 1572864 | tf_op jit(solution)/shard_map/all_gather | solution.py:20
  278.7 150.1 %all-gather.25.cloned.1.call-start = ((), (), s32[]{:S(2)}) async-start(), calls=%async_computation.13 | async-start | bytes 17825792 | tf_op jit(solution)/shard_map/all_gather | solution.py:106
  279.5 276.1 %all-gather.27.cloned.1.call-start = ((), (), s32[]{:S(2)}) async-start(), calls=%async_computation.14 | async-start | bytes 17825792 | tf_op jit(solution)/shard_map/all_gather | solution.py:107
  280.2 402.0 %all-gather.29.cloned.1.call-start = ((), (), s32[]{:S(2)}) async-start(), calls=%async_computation.15 | async-start | bytes 17825792 | tf_op jit(solution)/shard_map/all_gather | solution.py:108
  280.8 444.0 %reduce-scatter.11.cloned.1.call-start = ((), (), s32[]{:S(2)}) async-start(), calls=%async_computation.16 | async-start | bytes 3145728 | tf_op jit(solution)/shard_map/reduce_scatter | solution.py:24
  300.1 255.4 %copy-start.13 = (bf16[256,2048]{1,0:T(8,128)(2,1)S(1)}, bf16[256,2048]{1,0:T(8,128)(2,1)}, u32[]{:S(2)}) copy-start(bf16[256,2048]{1,0:T(8,128)(2,1)} %all-gather.23.cloned.1.call-done) | copy-start | bytes 3145732
  682.2 44.0 %copy-start.2 = (bf16[128,2048]{1,0:T(8,128)(2,1)S(1)}, bf16[128,2048]{1,0:T(8,128)(2,1)}, u32[]{:S(2)}) copy-start(bf16[128,2048]{1,0:T(8,128)(2,1)} %param.27) | copy-start | bytes 1572868
  694.5 57.0 %all-gather.31.cloned.1.call-start = ((), (), s32[]{:S(2)}) async-start(), calls=%async_computation.17 | async-start | bytes 1572864 | tf_op jit(solution)/shard_map/all_gather | solution.py:20
  730.1 95.0 %reduce-scatter.13.cloned.1.call-start = ((), (), s32[]{:S(2)}) async-start(), calls=%async_computation.18 | async-start | bytes 3145728 | tf_op jit(solution)/shard_map/reduce_scatter | solution.py:24
  779.7 45.4 %copy-start.1 = (f32[128,2048]{1,0:T(8,128)S(1)}, f32[128,2048]{1,0:T(8,128)}, u32[]{:S(2)}) copy-start(f32[128,2048]{1,0:T(8,128)} %reduce-scatter.9.cloned.1.call-done) | copy-start | bytes 3145732
  793.0 58.6 %all-gather.33.cloned.1.call-start = ((), (), s32[]{:S(2)}) async-start(), calls=%async_computation.19 | async-start | bytes 1572864 | tf_op jit(solution)/shard_map/all_gather | solution.py:20
  830.1 204.4 %reduce-scatter.19.cloned.1.call-start = ((), (), s32[]{:S(2)}) async-start(), calls=%async_computation.22 | async-start | bytes 1081344
  855.4 4.9 copy-start.24
  857.7 5.9 copy-start.17
  860.3 4.6 copy-start.16
  861.7 4.7 copy-start.26
  866.4 6.3 copy-start.7
  867.7 4.6 copy-start.9
  869.3 2.9 copy-start.11
  872.7 9.8 copy-start.5
  880.8 1.7 copy-start.27
  887.1 11.1 copy-start.28
  897.9 166.7 %reduce-scatter.15.cloned.1.call-start = ((), (), s32[]{:S(2)}) async-start(), calls=%async_computation.20 | async-start | bytes 3145728 | tf_op jit(solution)/shard_map/reduce_scatter | solution.py:24
  901.6 4.5 copy-start.18
  906.1 1.3 copy-start.12
  907.4 4.5 copy-start.19
  941.5 1365.4 %reduce-scatter.17.cloned.1.call-start = ((), (), s32[]{:S(2)}) async-start(), calls=%async_computation.21 | async-start | bytes 142606336 | tf_op jit(solution)/shard_map/reduce_scatter | solution.py:208
  941.8 8.5 copy-start
  950.3 4.3 copy-start.25
  950.3 4.3 copy-start.29
  954.6 4.5 copy-start.14
  954.6 4.5 copy-start.22
  959.2 13.3 copy-start.21
  972.5 13.2 copy-start.20
  972.5 13.2 copy-start.30
  999.0 65.6 %copy-start.3 = (bf16[128,2048]{1,0:T(8,128)(2,1)S(1)}, bf16[128,2048]{1,0:T(8,128)(2,1)}, u32[]{:S(2)}) copy-start(bf16[128,2048]{1,0:T(8,128)(2,1)} %param.27) | copy-start | bytes 1572868
  999.0 65.6 %copy-start.10 = (f32[128,2048]{1,0:T(8,128)S(1)}, f32[128,2048]{1,0:T(8,128)}, u32[]{:S(2)}) copy-start(f32[128,2048]{1,0:T(8,128)} %reduce-scatter.13.cloned.1.call-done) | copy-start | bytes 3145732
  (1 other events, 0.8 us)
Sparse Core Ops, SparseCore 0:
  9.5 24.2 all-gather.12
  36.0 50.3 all-gather.16
  88.6 48.9 all-gather.18
  139.6 48.8 all-gather.14
  190.6 48.8 all-gather.20
  244.6 30.4 reduce-scatter.8
  278.8 21.2 all-gather.22
  302.3 126.4 all-gather.24
  430.9 124.5 all-gather.26
  557.6 124.5 all-gather.28
  694.7 30.0 reduce-scatter.10
  730.2 21.2 all-gather.30
  793.1 31.8 reduce-scatter.12
  830.3 21.2 all-gather.32
  898.0 136.5 reduce-scatter.18
  1036.7 27.8 reduce-scatter.14
  1068.7 1238.2 reduce-scatter.16
where the time goes:
time: 2330 us; the launch traced here: 2320 us
  waiting for transfers between devices  1950 us (84%)
  matrix products  173 us (7%)
  blocking collectives  80.9 us (3%)
  local copies, waits for them, and re-layouts  74.9 us (3%)
  other arithmetic  27.1 us (1%)
    reduce_scatter x1, waiting for transfers between devices, shards(): lax.psum_scatter(jnp.concatenate([jnp.concatenate([query_term, key_term,...  1240 us
    all_gather x1, waiting for transfers between devices, shards(): lax.all_gather(w_gate, 'dp', axis=0, tiled=True)  129 us
    reduce_scatter x4, waiting for transfers between devices, to_halves(): lax.psum_scatter(partial_value, 'tensor', scatter_dimension=0, tiled=True)  119 us
    all_gather x1, waiting for transfers between devices, shards(): lax.all_gather(w_up, 'dp', axis=0, tiled=True)  114 us
    all_gather x1, waiting for transfers between devices, shards(): lax.all_gather(w_down, 'dp', axis=0, tiled=True)  113 us
    all_gather x1, blocking collectives, shards(): lax.all_gather(jnp.stack([query_gain, key_gain, attn_gain, ffn_gain]), ('...  71 us
    all_gather x4, waiting for transfers between devices, whole_rows(): return lax.all_gather(halves, 'tensor', axis=0, tiled=True)  61.7 us
    all_gather x1, waiting for transfers between devices, shards(): lax.all_gather(w_key, 'dp', axis=0, tiled=True)  47.3 us
  transfers between devices with their start and end apart: 17, of which 16 were waited for; matrix products, arithmetic and copies ran while one was open for 7% of the time, Pallas kernels for 0%

commit v1 on v0

v1 whole, which is shorter than its diff:
```python
import math

import jax
import jax.numpy as jnp
from jax import lax
from jax.sharding import Mesh, PartitionSpec as P

HD = 128

EPSILON = 1e-06
NEGATIVE = -1e30
FLIP = [(0, 1), (1, 0)]
BF = jnp.bfloat16
F32 = jnp.float32


def swap(value, axis):
    return lax.ppermute(value, axis, FLIP)


def bit(axis):
    return lax.axis_index(axis)


def pick(axis, low, high):
    return jnp.where(bit(axis) == 0, low, high)


def ordered(axis, own, other, dim=0):
    return jnp.concatenate([pick(axis, own, other), pick(axis, other, own)], axis=dim)


def split(value, axis, dim):
    half = value.shape[dim] // 2
    low = lax.slice_in_dim(value, 0, half, axis=dim)
    high = lax.slice_in_dim(value, half, 2 * half, axis=dim)
    return pick(axis, low, high), pick(axis, high, low)


def dot(a, b):
    return jnp.dot(a, b, preferred_element_type=F32)


def dot_nt(a, b):
    return jnp.einsum("sc,rc->sr", a, b, preferred_element_type=F32)


def dot_tn(a, b):
    return jnp.einsum("sr,sc->rc", a, b, preferred_element_type=F32)


def rms_scale(values):
    return lax.rsqrt(jnp.mean(values * values, axis=1, keepdims=True) + EPSILON)


def build(high_bits):
    def to_relative(value):
        rows, width = value.shape
        count = 2 ** (len(high_bits) + 2)
        run = width // count
        pieces = [value[:, i * run : (i + 1) * run] for i in range(count)]
        names = list(high_bits) + ["zl", "x"]
        for position, name in enumerate(names):
            if name == "zl":
                continue
            mask = 1 << (len(names) - 1 - position)
            pieces = [pick(name, pieces[i], pieces[i ^ mask]) for i in range(count)]
        order = []
        for xr in range(2):
            for rest in range(count // 2):
                order.append(rest * 2 + xr)
        return jnp.concatenate([pieces[i] for i in order], axis=1)

    def to_natural(value):
        rows, width = value.shape
        count = 2 ** (len(high_bits) + 2)
        run = width // count
        moved = [value[:, i * run : (i + 1) * run] for i in range(count)]
        pieces = [None] * count
        place = 0
        for xr in range(2):
            for rest in range(count // 2):
                pieces[rest * 2 + xr] = moved[place]
                place += 1
        names = list(high_bits) + ["zl", "x"]
        for position, name in enumerate(names):
            if name == "zl":
                continue
            mask = 1 << (len(names) - 1 - position)
            pieces = [pick(name, pieces[i], pieces[i ^ mask]) for i in range(count)]
        return jnp.concatenate(pieces, axis=1)

    def gather_attn_weight(w):
        own, sent = split(w, "core", 1)
        rows = ordered("core", own, swap(sent, "core"))
        for name in high_bits[::-1]:
            rows = jnp.concatenate([rows, swap(rows, name)], axis=0)
        blocks = 2 ** len(high_bits)
        run = rows.shape[0] // blocks
        other = swap(rows, "zl")
        parts = []
        for b in range(blocks):
            parts.append(ordered("zl", rows[b * run : (b + 1) * run], other[b * run : (b + 1) * run]))
        rows = jnp.concatenate(parts, axis=0)
        return rows, swap(rows, "x")

    def gather_ffn_weight(w):
        own, sent = split(w, "core", 1)
        rows = ordered("core", own, swap(sent, "core"))
        own, sent = split(rows, "zl", 1)
        rows = ordered("zl", own, swap(sent, "zl"))
        for name in high_bits[::-1]:
            rows = jnp.concatenate([rows, swap(rows, name)], axis=0)
        return rows, swap(rows, "x")

    def scatter_high(total):
        for name in high_bits:
            half = total.shape[0] // 2
            total = total[:half] + swap(total[half:].astype(BF), name).astype(F32)
        return total

    def scatter_attn_grad(keep, send):
        total = keep + swap(send.astype(BF), "x").astype(F32)
        blocks = 2 ** len(high_bits)
        run = total.shape[0] // blocks
        pairs = [split(total[b * run : (b + 1) * run], "zl", 0) for b in range(blocks)]
        own = jnp.concatenate([p[0] for p in pairs], axis=0)
        sent = jnp.concatenate([p[1] for p in pairs], axis=0)
        total = own + swap(sent.astype(BF), "zl").astype(F32)
        total = scatter_high(total)
        own, sent = split(total, "core", 0)
        return ordered("core", own, swap(sent, "core"), dim=1)

    def scatter_ffn_grad(keep, send):
        total = keep + swap(send.astype(BF), "x").astype(F32)
        total = scatter_high(total)
        own, sent = split(total, "zl", 0)
        total = ordered("zl", own, swap(sent.astype(BF), "zl").astype(F32), dim=1)
        own, sent = split(total, "core", 0)
        return ordered("core", own, swap(sent.astype(BF), "core").astype(F32), dim=1)

    def gather_pair(value):
        value = ordered("tensor", value, swap(value, "tensor"))
        return jnp.concatenate([value, swap(value, "core")], axis=0)

    def scatter_pair(low, high):
        total = low + swap(high.astype(BF), "core").astype(F32)
        own, sent = split(total, "tensor", 0)
        return own + swap(sent.astype(BF), "tensor").astype(F32)

    def gather_ffn_rows(value):
        half = value.shape[1] // 2
        left, right = value[:, :half], value[:, half:]
        left = jnp.concatenate([left, swap(left, "tensor")], axis=0)
        left = jnp.concatenate([left, swap(left, "zl")], axis=0)
        rows = right.shape[0]
        right = jnp.concatenate([right, swap(right, "zl")], axis=0)
        right_other = swap(right, "tensor")
        right = jnp.concatenate(
            [right[:rows], right_other[:rows], right[rows:], right_other[rows:]], axis=0
        )
        both = jnp.concatenate([left, right], axis=1)
        return jnp.concatenate([both, swap(both, "core")], axis=0)

    def scatter_ffn_rows(low, high):
        quarter = low.shape[0] // 2
        left = low[:quarter] + swap(low[quarter:].astype(BF), "core").astype(F32)
        right = high[:quarter] + swap(high[quarter:].astype(BF), "core").astype(F32)
        half = quarter // 2
        left = left[:half] + swap(left[half:].astype(BF), "zl").astype(F32)
        half = half // 2
        left = left[:half] + swap(left[half:].astype(BF), "tensor").astype(F32)
        own = jnp.concatenate([right[:half], right[2 * half : 3 * half]], axis=0)
        sent = jnp.concatenate([right[half : 2 * half], right[3 * half :]], axis=0)
        right = own + swap(sent.astype(BF), "tensor").astype(F32)
        right = right[:half] + swap(right[half:].astype(BF), "zl").astype(F32)
        return jnp.concatenate([left, right], axis=1)

    def pair_sum(values):
        half = values.shape[1] // 2
        other = swap(values, "core")
        values = values + jnp.concatenate([other[:, half:], other[:, :half]], axis=1)
        return values + swap(values, "tensor")

    def gather_gains(gains):
        gains = ordered("tensor", gains, swap(gains, "tensor"), dim=1)
        gains = ordered("core", gains, swap(gains, "core"), dim=1)
        gains = ordered("zl", gains, swap(gains, "zl"), dim=1)
        for name in list(high_bits)[::-1] + ["x"]:
            gains = jnp.concatenate([gains, swap(gains, name)], axis=1)
        return gains

    def scatter_gains(gains):
        for name in ["x"] + list(high_bits):
            half = gains.shape[1] // 2
            gains = gains[:, :half] + swap(gains[:, half:], name)
        for name in ("zl", "core", "tensor"):
            own, sent = split(gains, name, 1)
            gains = own + swap(sent, name)
        return gains

    def shards(
        tokens,
        segment_ids,
        w_query,
        w_key,
        w_value,
        w_output,
        w_gate,
        w_up,
        w_down,
        query_gain,
        key_gain,
        attn_gain,
        ffn_gain,
        cotangent,
    ):
        own_tokens, model_width = tokens.shape
        half_width = model_width // 2
        seq_length = own_tokens * 2
        pair_tokens = seq_length * 2
        head_width = w_query.shape[1] // 2
        local_heads = head_width // HD
        score_scale = 1.0 / math.sqrt(HD)

        tokens_rel = to_relative(tokens)
        tokens_f = tokens_rel.astype(F32)
        whole_input = gather_pair(tokens_rel)
        wq0, wq1 = gather_attn_weight(w_query)
        wk0, wk1 = gather_attn_weight(w_key)
        wv0, wv1 = gather_attn_weight(w_value)
        wo0, wo1 = gather_attn_weight(w_output)
        wg0, wg1 = gather_ffn_weight(w_gate)
        wu0, wu1 = gather_ffn_weight(w_up)
        wd0, wd1 = gather_ffn_weight(w_down)
        gains = gather_gains(jnp.stack([query_gain, key_gain, attn_gain, ffn_gain]))
        attn_scale = gains[2]
        ffn_scale = gains[3]
        head_gains = to_natural(gains[:2])
        head_start = (bit("tensor") * 2 + bit("core")) * head_width
        head_gains = lax.dynamic_slice_in_dim(head_gains, head_start, head_width, axis=1)
        query_scale, key_scale = head_gains[0], head_gains[1]
        d_out = to_relative(cotangent).astype(F32)

        seq_ids = jnp.concatenate([segment_ids, swap(segment_ids, "core")], axis=0)
        positions = jnp.arange(seq_length)
        visible = (positions[:, None] >= positions[None, :])[None] & (
            seq_ids[:, :, None] == seq_ids[:, None, :]
        )
        visible = visible[:, None]

        in0, in1 = whole_input[:, :half_width], whole_input[:, half_width:]
        query = dot(in0, wq0) + dot(in1, wq1)
        key_proj = dot(in0, wk0) + dot(in1, wk1)
        value_bf = (dot(in0, wv0) + dot(in1, wv1)).astype(BF)
        squares = pair_sum(
            jnp.stack([jnp.sum(query * query, axis=1), jnp.sum(key_proj * key_proj, axis=1)])
        )
        q_rms = lax.rsqrt(squares[0] / model_width + EPSILON)[:, None]
        k_rms = lax.rsqrt(squares[1] / model_width + EPSILON)[:, None]
        normed_query = (query * q_rms * query_scale).astype(BF)
        normed_key = (key_proj * k_rms * key_scale).astype(BF)
        heads = (2, seq_length, local_heads, HD)
        query_heads = normed_query.reshape(heads)
        key_heads = normed_key.reshape(heads)
        value_heads = value_bf.reshape(heads)
        scores = (
            jnp.einsum("bqhd,bkhd->bhqk", query_heads, key_heads, preferred_element_type=F32)
            * score_scale
        )
        scores = jnp.where(visible, scores, NEGATIVE)
        peak = jnp.max(scores, axis=-1, keepdims=True)
        expo = jnp.exp(scores - peak)
        total = jnp.sum(expo, axis=-1, keepdims=True)
        prob = expo / total
        prob_bf = prob.astype(BF)
        attn_heads = jnp.einsum(
            "bhqk,bkhd->bqhd", prob_bf, value_heads, preferred_element_type=F32
        ).astype(BF)
        attn = attn_heads.reshape(pair_tokens, head_width)

        def out_proj(rows, w0, w1):
            return jnp.concatenate([dot_nt(rows, w0), dot_nt(rows, w1)], axis=1)

        proj = scatter_pair(
            out_proj(attn[:seq_length], wo0, wo1), out_proj(attn[seq_length:], wo0, wo1)
        )
        attn_rms = rms_scale(proj)
        resid = tokens_f + proj * attn_rms * attn_scale
        hidden = gather_ffn_rows(resid.astype(BF))
        h0, h1 = hidden[:, :half_width], hidden[:, half_width:]
        gate = dot(h0, wg0) + dot(h1, wg1)
        up = dot(h0, wu0) + dot(h1, wu1)
        sigma = jax.nn.sigmoid(gate)
        act = (gate * sigma * up).astype(BF)
        ffn = scatter_ffn_rows(dot_nt(act, wd0), dot_nt(act, wd1))
        ffn_rms = rms_scale(ffn)
        output = to_natural((resid + ffn * ffn_rms * ffn_scale).astype(BF))
        ffn_gain_term = jnp.sum(d_out * ffn * ffn_rms, axis=0)
        scaled_out = d_out * ffn_scale
        d_ffn = (
            ffn_rms
            * (
                scaled_out
                - ffn * ffn_rms * ffn_rms * jnp.mean(scaled_out * ffn, axis=1, keepdims=True)
            )
        ).astype(BF)
        whole_dffn = gather_ffn_rows(d_ffn)
        f0, f1 = whole_dffn[:, :half_width], whole_dffn[:, half_width:]
        grad_down = scatter_ffn_grad(dot_tn(f0, act), dot_tn(f1, act))
        d_act = dot(f0, wd0) + dot(f1, wd1)
        d_gate = (d_act * up * sigma * (1.0 + gate * (1.0 - sigma))).astype(BF)
        d_up = (d_act * gate * sigma).astype(BF)
        d_hidden = scatter_ffn_rows(
            dot_nt(d_gate, wg0) + dot_nt(d_up, wu0), dot_nt(d_gate, wg1) + dot_nt(d_up, wu1)
        )
        grad_gate = scatter_ffn_grad(dot_tn(h0, d_gate), dot_tn(h1, d_gate))
        grad_up = scatter_ffn_grad(dot_tn(h0, d_up), dot_tn(h1, d_up))
        d_resid = d_out + d_hidden
        attn_gain_term = jnp.sum(d_resid * proj * attn_rms, axis=0)
        scaled_resid = d_resid * attn_scale
        d_proj = (
            attn_rms
            * (
                scaled_resid
                - proj * attn_rms * attn_rms * jnp.mean(scaled_resid * proj, axis=1, keepdims=True)
            )
        ).astype(BF)
        whole_dproj = gather_pair(d_proj)
        p0, p1 = whole_dproj[:, :half_width], whole_dproj[:, half_width:]
        d_attn = (dot(p0, wo0) + dot(p1, wo1)).astype(BF)
        grad_output = scatter_attn_grad(dot_tn(p0, attn), dot_tn(p1, attn))
        d_attn_heads = d_attn.reshape(heads)
        d_value = (
            jnp.einsum("bhqk,bqhd->bkhd", prob_bf, d_attn_heads, preferred_element_type=F32)
            .reshape(pair_tokens, head_width)
            .astype(BF)
        )
        grad_value = scatter_attn_grad(dot_tn(in0, d_value), dot_tn(in1, d_value))
        d_prob = jnp.einsum(
            "bqhd,bkhd->bhqk", d_attn_heads, value_heads, preferred_element_type=F32
        )
        delta = jnp.einsum(
            "bqhd,bqhd->bhq", d_attn_heads, attn_heads, preferred_element_type=F32
        )[..., None]
        d_score = (prob * (d_prob - delta)).astype(BF)
        d_nq = (
            jnp.einsum("bhqk,bkhd->bqhd", d_score, key_heads, preferred_element_type=F32).reshape(
                pair_tokens, head_width
            )
            * score_scale
        )
        d_nk = (
            jnp.einsum("bhqk,bqhd->bkhd", d_score, query_heads, preferred_element_type=F32).reshape(
                pair_tokens, head_width
            )
            * score_scale
        )
        query_gain_term = jnp.sum(d_nq * query * q_rms, axis=0)
        key_gain_term = jnp.sum(d_nk * key_proj * k_rms, axis=0)
        scaled_q = d_nq * query_scale
        scaled_k = d_nk * key_scale
        inner = pair_sum(
            jnp.stack([jnp.sum(scaled_q * query, axis=1), jnp.sum(scaled_k * key_proj, axis=1)])
        )
        d_query = (
            q_rms * (scaled_q - query * q_rms * q_rms * (inner[0] / model_width)[:, None])
        ).astype(BF)
        d_key = (
            k_rms * (scaled_k - key_proj * k_rms * k_rms * (inner[1] / model_width)[:, None])
        ).astype(BF)
        grad_query = scatter_attn_grad(dot_tn(in0, d_query), dot_tn(in1, d_query))
        grad_key = scatter_attn_grad(dot_tn(in0, d_key), dot_tn(in1, d_key))

        def in_proj(rows):
            return jnp.concatenate(
                [
                    dot_nt(d_query[rows], wq) + dot_nt(d_key[rows], wk) + dot_nt(d_value[rows], wv)
                    for wq, wk, wv in ((wq0, wk0, wv0), (wq1, wk1, wv1))
                ],
                axis=1,
            )

        d_tokens = scatter_pair(
            in_proj(slice(0, seq_length)), in_proj(slice(seq_length, pair_tokens))
        )
        grad_tokens = to_natural(d_resid + d_tokens)

        zero = jnp.zeros((2, model_width), F32)
        placed = lax.dynamic_update_slice_in_dim(
            zero, jnp.stack([query_gain_term, key_gain_term]), head_start, 1
        )
        gain_parts = scatter_gains(
            jnp.concatenate(
                [to_relative(placed), jnp.stack([attn_gain_term, ffn_gain_term])], axis=0
            )
        )
        return (
            output,
            grad_tokens,
            grad_query,
            grad_key,
            grad_value,
            grad_output,
            grad_gate,
            grad_up,
            grad_down,
            gain_parts[0],
            gain_parts[1],
            gain_parts[2],
            gain_parts[3],
        )

    return shards


def solution(mesh):
    dp = mesh.shape["dp"]
    high = max(dp.bit_length() - 4, 0)
    high_bits = tuple(f"z{i}" for i in range(high))
    names = high_bits + ("zl", "x", "core", "tensor")
    fine = Mesh(mesh.devices.reshape((2,) * len(names)), names)
    rows = names[:-1]
    both = names
    mapped = jax.shard_map(
        build(high_bits),
        mesh=fine,
        in_specs=(
            P(both, None),
            P(rows, None),
            P(rows, "tensor"),
            P(rows, "tensor"),
            P(rows, "tensor"),
            P(rows, "tensor"),
            P(rows, "tensor"),
            P(rows, "tensor"),
            P(rows, "tensor"),
            P(both),
            P(both),
            P(both),
            P(both),
            P(both, None),
        ),
        out_specs=(
            P(both, None),
            P(both, None),
            P(rows, "tensor"),
            P(rows, "tensor"),
            P(rows, "tensor"),
            P(rows, "tensor"),
            P(rows, "tensor"),
            P(rows, "tensor"),
            P(rows, "tensor"),
            P(both),
            P(both),
            P(both),
            P(both),
        ),
        check_vma=False,
    )
    return mapped
```

time: 2330 us -> 949 us (0.41)
  waiting for transfers between devices: 1950 us -> 605 us
  starting transfers between devices: 1.45 us -> 103 us
  blocking collectives: 80.9 us -> 0 us
  matrix products: 173 us -> 100 us
  other arithmetic: 27.1 us -> 82.8 us
  local copies, waits for them, and re-layouts: 74.9 us -> 42.2 us
    reduce_scatter x5 -> x0, waiting for transfers between devices: 1360 us -> none  [the longest x1 1240 us: shards(): lax.psum_scatter(jnp.concatenate([jnp.concatenate([query_term, key_term,...]
    ppermute x0 -> x101, waiting for transfers between devices: none -> 605 us  [swap(): return lax.ppermute(value, axis, FLIP)]
    all_gather x11 -> x0, waiting for transfers between devices: 550 us -> none  [the longest x1 129 us: shards(): lax.all_gather(w_gate, 'dp', axis=0, tiled=True)]
    ppermute x0 -> x101, starting transfers between devices: none -> 103 us  [swap(): return lax.ppermute(value, axis, FLIP)]
    dot_general x27 -> x55, matrix products: 173 us -> 97.8 us  [the longest x14 34.8 us: dot(): return jnp.dot(a, b, preferred_element_type=F32)]
    all_gather x1 -> x0, blocking collectives: 71 us -> none  [shards(): lax.all_gather(jnp.stack([query_gain, key_gain, attn_gain, ffn_gain]), ('...]
    concatenate x0 -> x57, other arithmetic: none -> 43.6 us  [the longest x2 25.7 us: gather_ffn_rows(): both = jnp.concatenate([left, right], axis=1)]
    unnamed x18 -> x0, waiting for transfers between devices: 40.7 us -> none
  transfers between devices with their start and end apart: 17 -> 101, of which waited for: 16 -> 51; matrix products, arithmetic and copies ran while one was open for 7% -> 19% of each run, Pallas kernels for 0% -> 0%
where the time goes in v1:
time: 949 us; the launch traced here: 939 us
  waiting for transfers between devices  605 us (64%)
  starting transfers between devices  103 us (11%)
  matrix products  100 us (11%)
  other arithmetic  82.8 us (9%)
  local copies, waits for them, and re-layouts  42.2 us (4%)
    ppermute x101, waiting for transfers between devices, swap(): return lax.ppermute(value, axis, FLIP)  605 us
    ppermute x101, starting transfers between devices, swap(): return lax.ppermute(value, axis, FLIP)  103 us
    dot_general x14, matrix products, dot(): return jnp.dot(a, b, preferred_element_type=F32)  34.8 us
    dot_general x14, matrix products, dot_tn(): return jnp.einsum('sr,sc->rc', a, b, preferred_element_type=F32)  30.2 us
    dot_general x22, matrix products, dot_nt(): return jnp.einsum('sc,rc->sr', a, b, preferred_element_type=F32)  26.5 us
    concatenate x2, other arithmetic, gather_ffn_rows(): both = jnp.concatenate([left, right], axis=1)  25.7 us
    unnamed x296, local copies, waits for them, and re-layouts  25 us
    select_n x50, other arithmetic, pick(): return jnp.where(bit(axis) == 0, low, high)  19.3 us
  transfers between devices with their start and end apart: 101, of which 51 were waited for; matrix products, arithmetic and copies ran while one was open for 19% of the time, Pallas kernels for 0%

profile of v1, /device:TPU:0, one launch (start us, length us, event | category | flops | bytes accessed | tf_op | source)
XLA Modules:
  0.0 938.5 jit_solution(13256091217500272397)
XLA Ops:
  5.1 3.1 collective-permute-start
  13.5 6.9 collective-permute-done.17
  44.1 20.0 %collective-permute-done.8 = bf16[256,512]{1,0:T(8,128)(2,1)S(1)} collective-permute-done((bf16[256,512]{1,0:T(8,128)(2,1)S(1)}, bf16[256,512]{1,0:T(8,128)(2,1)S(1)}, u32[]{:S(2)}, u32[]{:S(2)}) %collective-permute-start.8) | collective-permute-done | bytes 262176 | tf_op jit(solution)/shard_map/ppermute | solution.py:18
  64.1 11.2 %collective-permute-done.12 = bf16[256,512]{1,0:T(8,128)(2,1)S(1)} collective-permute-done((bf16[256,512]{1,0:T(8,128)(2,1)S(1)}, bf16[256,512]{1,0:T(8,128)(2,1)S(1)}, u32[]{:S(2)}, u32[]{:S(2)}) %collective-permute-start.12) | collective-permute-done | bytes 262176 | tf_op jit(solution)/shard_map/ppermute | solution.py:18
  75.3 5.7 collective-permute-done.3
  81.0 4.8 collective-permute-done.23
  89.2 7.9 collective-permute-done.9
  97.4 10.9 %collective-permute-done.13 = bf16[512,512]{1,0:T(8,128)(2,1)S(1)} collective-permute-done((bf16[512,512]{1,0:T(8,128)(2,1)S(1)}, bf16[512,512]{1,0:T(8,128)(2,1)S(1)}, u32[]{:S(2)}, u32[]{:S(2)}) %collective-permute-start.13) | collective-permute-done | bytes 524320 | tf_op jit(solution)/shard_map/ppermute | solution.py:18
  110.2 9.4 collective-permute-done.4
  121.4 9.3 collective-permute-done.24
  136.6 20.2 %collective-permute-done.14 = bf16[1024,512]{1,0:T(8,128)(2,1)S(1)} collective-permute-done((bf16[1024,512]{1,0:T(8,128)(2,1)S(1)}, bf16[1024,512]{1,0:T(8,128)(2,1)S(1)}, u32[]{:S(2)}, u32[]{:S(2)}) %collective-permute-start.14) | collective-permute-done | bytes 1048608 | tf_op jit(solution)/shard_map/ppermute | solution.py:18
  160.8 18.5 %collective-permute-done.5 = bf16[1024,512]{1,0:T(8,128)(2,1)S(1)} collective-permute-done((bf16[1024,512]{1,0:T(8,128)(2,1)S(1)}, bf16[1024,512]{1,0:T(8,128)(2,1)S(1)}, u32[]{:S(2)}, u32[]{:S(2)}) %collective-permute-start.5) | collective-permute-done | bytes 1048608 | tf_op jit(solution)/shard_map/ppermute | solution.py:18
  195.5 5.4 collective-permute-done.25
  211.8 9.3 collective-permute-done.27
  226.8 8.9 collective-permute-done.30
  238.0 4.1 collective-permute-start.35
  242.1 6.7 collective-permute-done.31
  248.8 27.0 %collective-permute-done.29 = bf16[256,1024]{1,0:T(8,128)(2,1)S(1)} collective-permute-done((bf16[256,1024]{1,0:T(8,128)(2,1)S(1)}, bf16[256,1024]{1,0:T(8,128)(2,1)S(1)}, u32[]{:S(2)}, u32[]{:S(2)}) %collective-permute-start.29) | collective-permute-done | bytes 524320 | tf_op jit(solution)/shard_map/ppermute | solution.py:18
  275.8 12.2 %maximum_maximum_fusion = bf16[512,2048]{1,0:T(8,128)(2,1)S(1)} fusion(bf16[128,1024]{1,0:T(8,128)(2,1)S(1)} %get-tuple-element.148, bf16[128,1024]{1,0:T(8,128)(2,1)S(1)} %collective-permute-done.30, bf16[128,1024]{1,0:T(8,128)(2,1)S(1)} %get-tuple-element.147, bf16[128,1024]{1,0:T(8,128)(2,1)S(1)} %get-tuple-element.146, ...), kind=kLoop, calls=%fused_computation.26 | loop fusion | flops 14680064 | bytes 4194304 | tf_op jit(solution)/shard_map/concatenate | solution.py:162
  290.9 3.0 collective-permute-start.43
  294.1 64.9 %collective-permute-done.39 = bf16[512,1024]{0,1:T(8,128)(2,1)S(1)} collective-permute-done((bf16[512,1024]{0,1:T(8,128)(2,1)S(1)}, bf16[512,1024]{0,1:T(8,128)(2,1)S(1)}, u32[]{:S(2)}, u32[]{:S(2)}) %collective-permute-start.39) | collective-permute-done | bytes 1048608 | tf_op jit(solution)/shard_map/ppermute | solution.py:18
  360.9 20.5 %collective-permute-done.43 = bf16[512,1024]{0,1:T(8,128)(2,1)S(1)} collective-permute-done((bf16[512,1024]{0,1:T(8,128)(2,1)S(1)}, bf16[512,1024]{0,1:T(8,128)(2,1)S(1)}, u32[]{:S(2)}, u32[]{:S(2)}) %collective-permute-start.43) | collective-permute-done | bytes 1048608 | tf_op jit(solution)/shard_map/ppermute | solution.py:18
  383.3 2.9 pad_maximum_fusion
  389.0 4.5 convolution_add_fusion.4
  393.5 14.4 %collective-permute-done.40 = bf16[1024,1024]{0,1:T(8,128)(2,1)S(1)} collective-permute-done((bf16[1024,1024]{0,1:T(8,128)(2,1)S(1)}, bf16[1024,1024]{0,1:T(8,128)(2,1)S(1)}, u32[]{:S(2)}, u32[]{:S(2)}) %collective-permute-start.40) | collective-permute-done | bytes 2097184 | tf_op jit(solution)/shard_map/ppermute | solution.py:18
  407.9 4.3 fusion.13
  412.2 6.6 multiply_convert_fusion.2
  421.5 30.4 %collective-permute-done.47 = bf16[1024,1024]{0,1:T(8,128)(2,1)S(1)} collective-permute-done((bf16[1024,1024]{0,1:T(8,128)(2,1)S(1)}, bf16[1024,1024]{0,1:T(8,128)(2,1)S(1)}, u32[]{:S(2)}, u32[]{:S(2)}) %collective-permute-start.47) | collective-permute-done | bytes 2097184 | tf_op jit(solution)/shard_map/ppermute | solution.py:18
  460.5 9.1 collective-permute-done.45
  473.2 5.3 collective-permute-done.46
  483.5 5.1 collective-permute-done.53
  491.2 9.2 collective-permute-done.54
  501.1 13.5 %maximum_maximum_fusion.1 = bf16[512,2048]{1,0:T(8,128)(2,1)} fusion(bf16[128,1024]{1,0:T(8,128)(2,1)S(1)} %get-tuple-element.144, bf16[128,1024]{1,0:T(8,128)(2,1)S(1)} %collective-permute-done.53, bf16[128,1024]{1,0:T(8,128)(2,1)S(1)} %get-tuple-element.143, bf16[128,1024]{1,0:T(8,128)(2,1)S(1)} %get-tuple-element.142, ...), kind=kLoop, calls=%fused_computation.30 | loop fusion | flops 14680064 | bytes 4194304 | tf_op jit(solution)/shard_map/concatenate | solution.py:162
  515.9 3.4 collective-permute-done.55
  519.3 3.2 pad_maximum_fusion.1
  525.4 5.9 multiply_convert_fusion.1
  552.1 11.5 %collective-permute-done.57 = bf16[256,1024]{1,0:T(8,128)(2,1)S(1)} collective-permute-done((bf16[256,1024]{1,0:T(8,128)(2,1)S(1)}, bf16[256,1024]{1,0:T(8,128)(2,1)S(1)}, u32[]{:S(2)}, u32[]{:S(2)}) %collective-permute-start.57) | collective-permute-done | bytes 524320 | tf_op jit(solution)/shard_map/ppermute | solution.py:18
  575.6 41.6 %collective-permute-done.92 = bf16[1024,1024]{0,1:T(8,128)(2,1)S(1)} collective-permute-done((bf16[1024,1024]{0,1:T(8,128)(2,1)S(1)}, bf16[1024,1024]{0,1:T(8,128)(2,1)S(1)}, u32[]{:S(2)}, u32[]{:S(2)}) %collective-permute-start.92) | collective-permute-done | bytes 2097184 | tf_op jit(solution)/shard_map/ppermute | solution.py:18
  621.7 40.5 %collective-permute-done.88 = bf16[1024,1024]{0,1:T(8,128)(2,1)S(1)} collective-permute-done((bf16[1024,1024]{0,1:T(8,128)(2,1)S(1)}, bf16[1024,1024]{0,1:T(8,128)(2,1)S(1)}, u32[]{:S(2)}, u32[]{:S(2)}) %collective-permute-start.88) | collective-permute-done | bytes 2097184 | tf_op jit(solution)/shard_map/ppermute | solution.py:18
  666.6 38.2 %collective-permute-done.84 = bf16[1024,1024]{0,1:T(8,128)(2,1)S(1)} collective-permute-done((bf16[1024,1024]{0,1:T(8,128)(2,1)S(1)}, bf16[1024,1024]{0,1:T(8,128)(2,1)S(1)}, u32[]{:S(2)}, u32[]{:S(2)}) %collective-permute-start.84) | collective-permute-done | bytes 2097184 | tf_op jit(solution)/shard_map/ppermute | solution.py:18
  714.5 39.6 %collective-permute-done.85 = bf16[512,1024]{0,1:T(8,128)(2,1)S(1)} collective-permute-done((bf16[512,1024]{0,1:T(8,128)(2,1)S(1)}, bf16[512,1024]{0,1:T(8,128)(2,1)S(1)}, u32[]{:S(2)}, u32[]{:S(2)}) %collective-permute-start.85) | collective-permute-done | bytes 1048608 | tf_op jit(solution)/shard_map/ppermute | solution.py:18
  834.0 3.2 copy.88
  845.6 13.0 %collective-permute-done.72 = bf16[1024,512]{1,0:T(8,128)(2,1)} collective-permute-done((bf16[1024,512]{1,0:T(8,128)(2,1)}, bf16[1024,512]{1,0:T(8,128)(2,1)}, u32[]{:S(2)}, u32[]{:S(2)}) %collective-permute-start.72) | collective-permute-done | bytes 1048608 | tf_op jit(solution)/shard_map/ppermute | solution.py:18
  862.6 17.2 %collective-permute-done.68 = bf16[1024,512]{1,0:T(8,128)(2,1)} collective-permute-done((bf16[1024,512]{1,0:T(8,128)(2,1)}, bf16[1024,512]{1,0:T(8,128)(2,1)}, u32[]{:S(2)}, u32[]{:S(2)}) %collective-permute-start.68) | collective-permute-done | bytes 1048608 | tf_op jit(solution)/shard_map/ppermute | solution.py:18
  893.0 9.4 collective-permute-done.69
  903.5 16.5 %collective-permute-done.82 = bf16[256,512]{1,0:T(8,128)(2,1)S(1)} collective-permute-done((bf16[256,512]{1,0:T(8,128)(2,1)S(1)}, bf16[256,512]{1,0:T(8,128)(2,1)S(1)}, u32[]{:S(2)}, u32[]{:S(2)}) %collective-permute-start.82) | collective-permute-done | bytes 262176 | tf_op jit(solution)/shard_map/ppermute | solution.py:18
  920.2 5.4 collective-permute-done.78
  925.8 5.4 collective-permute-done.74
  (778 shorter events, 284.7 us)
Async XLA Ops:
  3.4 199.3 %collective-permute-start.37 = (bf16[128,2048]{0,1:T(8,128)(2,1)}, bf16[128,2048]{0,1:T(8,128)(2,1)}, u32[]{:S(2)}, u32[]{:S(2)}) collective-permute-start(bf16[128,2048]{0,1:T(8,128)(2,1)} %broadcast_select_fusion.9), channel_id=1, source_target_pairs={{0,2},{2,0},{1,3},{3,1},{4,6},{6,4},{5,7},{7,5},{8,10},{10,8},{9,1... | collective-permute-start | bytes 1572872 | tf_op jit(solution)/shard_map/ppermute | solution.py:18
  4.6 30.9 %collective-permute-start.7 = (bf16[128,512]{1,0:T(8,128)(2,1)}, bf16[128,512]{1,0:T(8,128)(2,1)}, u32[]{:S(2)}, u32[]{:S(2)}) collective-permute-start(bf16[128,512]{1,0:T(8,128)(2,1)} %broadcast_select_fusion.65), channel_id=1, source_target_pairs={{0,2},{2,0},{1,3},{3,1},{4,6},{6,4},{5,7},{7,5},{8,10},{10,8},{9,1... | collective-permute-start | bytes 393224 | tf_op jit(solution)/shard_map/ppermute | solution.py:18
  5.1 81.5 %collective-permute-start = (bf16[128,2048]{1,0:T(8,128)(2,1)S(1)}, bf16[128,2048]{1,0:T(8,128)(2,1)}, u32[]{:S(2)}, u32[]{:S(2)}) collective-permute-start(bf16[128,2048]{1,0:T(8,128)(2,1)S(1)} %constant_dynamic-update-slice_fusion), channel_id=1, source_target_pairs={{0,1},{1,0},{2,3},{3,2},{4,5},{5,4},{6,7},{7,6},{8,9},{9,8},{10,11... | collective-permute-start | bytes 1572872 | tf_op jit(solution)/shard_map/ppermute | solution.py:18
  8.8 28.3 %collective-permute-start.11 = (bf16[128,512]{1,0:T(8,128)(2,1)}, bf16[128,512]{1,0:T(8,128)(2,1)}, u32[]{:S(2)}, u32[]{:S(2)}) collective-permute-start(bf16[128,512]{1,0:T(8,128)(2,1)} %broadcast_select_fusion.61), channel_id=1, source_target_pairs={{0,2},{2,0},{1,3},{3,1},{4,6},{6,4},{5,7},{7,5},{8,10},{10,8},{9,1... | collective-permute-start | bytes 393224 | tf_op jit(solution)/shard_map/ppermute | solution.py:18
  40.9 34.4 %collective-permute-start.12 = (bf16[256,512]{1,0:T(8,128)(2,1)S(1)}, bf16[256,512]{1,0:T(8,128)(2,1)S(1)}, u32[]{:S(2)}, u32[]{:S(2)}) collective-permute-start(bf16[256,512]{1,0:T(8,128)(2,1)S(1)} %pad_maximum_fusion.48), channel_id=1, source_target_pairs={{0,16},{16,0},{1,17},{17,1},{2,18},{18,2},{3,19},{19,3},{4,20},{20... | collective-permute-start | bytes 786440 | tf_op jit(solution)/shard_map/ppermute | solution.py:18
  41.2 39.9 %collective-permute-start.3 = (bf16[256,512]{1,0:T(8,128)(2,1)S(1)}, bf16[256,512]{1,0:T(8,128)(2,1)S(1)}, u32[]{:S(2)}, u32[]{:S(2)}) collective-permute-start(bf16[256,512]{1,0:T(8,128)(2,1)S(1)} %pad_maximum_fusion.46), channel_id=1, source_target_pairs={{0,16},{16,0},{1,17},{17,1},{2,18},{18,2},{3,19},{19,3},{4,20},{20... | collective-permute-start | bytes 786440 | tf_op jit(solution)/shard_map/ppermute | solution.py:18
  85.8 33.7 %collective-permute-start.4 = (bf16[512,512]{1,0:T(8,128)(2,1)S(1)}, bf16[512,512]{1,0:T(8,128)(2,1)S(1)}, u32[]{:S(2)}, u32[]{:S(2)}) collective-permute-start(bf16[512,512]{1,0:T(8,128)(2,1)S(1)} %pad_maximum_fusion.28), channel_id=1, source_target_pairs={{0,8},{8,0},{1,9},{9,1},{2,10},{10,2},{3,11},{11,3},{4,12},{12,4},... | collective-permute-start | bytes 1572872 | tf_op jit(solution)/shard_map/ppermute | solution.py:18
  86.6 44.1 %collective-permute-start.24 = (bf16[512,512]{1,0:T(8,128)(2,1)S(1)}, bf16[512,512]{1,0:T(8,128)(2,1)S(1)}, u32[]{:S(2)}, u32[]{:S(2)}) collective-permute-start(bf16[512,512]{1,0:T(8,128)(2,1)S(1)} %pad_maximum_fusion.31), channel_id=1, source_target_pairs={{0,8},{8,0},{1,9},{9,1},{2,10},{10,2},{3,11},{11,3},{4,12},{12,4},... | collective-permute-start | bytes 1572872 | tf_op jit(solution)/shard_map/ppermute | solution.py:18
  97.1 33.9 %collective-permute-start.1 = (bf16[256,2048]{1,0:T(8,128)(2,1)S(1)}, bf16[256,2048]{1,0:T(8,128)(2,1)S(1)}, u32[]{:S(2)}, u32[]{:S(2)}) collective-permute-start(bf16[256,2048]{1,0:T(8,128)(2,1)S(1)} %pad_maximum_fusion.13), channel_id=1, source_target_pairs={{0,2},{2,0},{1,3},{3,1},{4,6},{6,4},{5,7},{7,5},{8,10},{10,8},{9,1... | collective-permute-start | bytes 3145736 | tf_op jit(solution)/shard_map/ppermute | solution.py:18
  119.5 37.3 %collective-permute-start.14 = (bf16[1024,512]{1,0:T(8,128)(2,1)S(1)}, bf16[1024,512]{1,0:T(8,128)(2,1)S(1)}, u32[]{:S(2)}, u32[]{:S(2)}) collective-permute-start(bf16[1024,512]{1,0:T(8,128)(2,1)S(1)} %pad_maximum_fusion.16), channel_id=1, source_target_pairs={{0,4},{4,0},{1,5},{5,1},{2,6},{6,2},{3,7},{7,3},{8,12},{12,8},{9,1... | collective-permute-start | bytes 3145736 | tf_op jit(solution)/shard_map/ppermute | solution.py:18
  130.7 77.7 %collective-permute-start.33 = (bf16[128,2048]{0,1:T(8,128)(2,1)}, bf16[128,2048]{0,1:T(8,128)(2,1)}, u32[]{:S(2)}, u32[]{:S(2)}) collective-permute-start(bf16[128,2048]{0,1:T(8,128)(2,1)} %broadcast_select_fusion.13), channel_id=1, source_target_pairs={{0,2},{2,0},{1,3},{3,1},{4,6},{6,4},{5,7},{7,5},{8,10},{10,8},{9,1... | collective-permute-start | bytes 1572872 | tf_op jit(solution)/shard_map/ppermute | solution.py:18
  131.0 94.1 %collective-permute-start.41 = (bf16[128,2048]{0,1:T(8,128)(2,1)}, bf16[128,2048]{0,1:T(8,128)(2,1)}, u32[]{:S(2)}, u32[]{:S(2)}) collective-permute-start(bf16[128,2048]{0,1:T(8,128)(2,1)} %broadcast_select_fusion.5), channel_id=1, source_target_pairs={{0,2},{2,0},{1,3},{3,1},{4,6},{6,4},{5,7},{7,5},{8,10},{10,8},{9,1... | collective-permute-start | bytes 1572872 | tf_op jit(solution)/shard_map/ppermute | solution.py:18
  134.3 44.9 %collective-permute-start.5 = (bf16[1024,512]{1,0:T(8,128)(2,1)S(1)}, bf16[1024,512]{1,0:T(8,128)(2,1)S(1)}, u32[]{:S(2)}, u32[]{:S(2)}) collective-permute-start(bf16[1024,512]{1,0:T(8,128)(2,1)S(1)} %pad_maximum_fusion.14), channel_id=1, source_target_pairs={{0,4},{4,0},{1,5},{5,1},{2,6},{6,2},{3,7},{7,3},{8,12},{12,8},{9,1... | collective-permute-start | bytes 3145736 | tf_op jit(solution)/shard_map/ppermute | solution.py:18
  156.8 44.0 %collective-permute-start.25 = (bf16[1024,512]{1,0:T(8,128)(2,1)S(1)}, bf16[1024,512]{1,0:T(8,128)(2,1)}, u32[]{:S(2)}, u32[]{:S(2)}) collective-permute-start(bf16[1024,512]{1,0:T(8,128)(2,1)S(1)} %pad_maximum_fusion.17), channel_id=1, source_target_pairs={{0,4},{4,0},{1,5},{5,1},{2,6},{6,2},{3,7},{7,3},{8,12},{12,8},{9,1... | collective-permute-start | bytes 3145736 | tf_op jit(solution)/shard_map/ppermute | solution.py:18
  204.0 84.0 %collective-permute-start.38 = (bf16[256,1024]{0,1:T(8,128)(2,1)S(1)}, bf16[256,1024]{0,1:T(8,128)(2,1)S(1)}, u32[]{:S(2)}, u32[]{:S(2)}) collective-permute-start(bf16[256,1024]{0,1:T(8,128)(2,1)S(1)} %broadcast_select_fusion.21), channel_id=1, source_target_pairs={{0,8},{8,0},{1,9},{9,1},{2,10},{10,2},{3,11},{11,3},{4,12},{12,4},... | collective-permute-start | bytes 1572872 | tf_op jit(solution)/shard_map/ppermute | solution.py:18
  226.4 62.2 %collective-permute-start.42 = (bf16[256,1024]{0,1:T(8,128)(2,1)S(1)}, bf16[256,1024]{0,1:T(8,128)(2,1)S(1)}, u32[]{:S(2)}, u32[]{:S(2)}) collective-permute-start(bf16[256,1024]{0,1:T(8,128)(2,1)S(1)} %broadcast_select_fusion.17), channel_id=1, source_target_pairs={{0,8},{8,0},{1,9},{9,1},{2,10},{10,2},{3,11},{11,3},{4,12},{12,4},... | collective-permute-start | bytes 1572872 | tf_op jit(solution)/shard_map/ppermute | solution.py:18
  237.5 38.4 %collective-permute-start.29 = (bf16[256,1024]{1,0:T(8,128)(2,1)S(1)}, bf16[256,1024]{1,0:T(8,128)(2,1)S(1)}, u32[]{:S(2)}, u32[]{:S(2)}) collective-permute-start(bf16[256,1024]{1,0:T(8,128)(2,1)S(1)} %pad_maximum_fusion.32), channel_id=1, source_target_pairs={{0,8},{8,0},{1,9},{9,1},{2,10},{10,2},{3,11},{11,3},{4,12},{12,4},... | collective-permute-start | bytes 1572872 | tf_op jit(solution)/shard_map/ppermute | solution.py:18
  238.0 51.0 %collective-permute-start.35 = (bf16[512,1024]{0,1:T(8,128)(2,1)S(1)}, bf16[512,1024]{0,1:T(8,128)(2,1)S(1)}, u32[]{:S(2)}, u32[]{:S(2)}) collective-permute-start(bf16[512,1024]{0,1:T(8,128)(2,1)S(1)} %pad_maximum_fusion.19), channel_id=1, source_target_pairs={{0,16},{16,0},{1,17},{17,1},{2,18},{18,2},{3,19},{19,3},{4,20},{20... | collective-permute-start | bytes 3145736 | tf_op jit(solution)/shard_map/ppermute | solution.py:18
  288.0 95.3 %collective-permute-start.32 = (bf16[512,2048]{1,0:T(8,128)(2,1)S(1)}, bf16[512,2048]{1,0:T(8,128)(2,1)S(1)}, u32[]{:S(2)}, u32[]{:S(2)}) collective-permute-start(bf16[512,2048]{1,0:T(8,128)(2,1)S(1)} %maximum_maximum_fusion), channel_id=1, source_target_pairs={{0,2},{2,0},{1,3},{3,1},{4,6},{6,4},{5,7},{7,5},{8,10},{10,8},{9,1... | collective-permute-start | bytes 6291464 | tf_op jit(solution)/shard_map/ppermute | solution.py:18
  288.5 70.5 %collective-permute-start.39 = (bf16[512,1024]{0,1:T(8,128)(2,1)S(1)}, bf16[512,1024]{0,1:T(8,128)(2,1)S(1)}, u32[]{:S(2)}, u32[]{:S(2)}) collective-permute-start(bf16[512,1024]{0,1:T(8,128)(2,1)S(1)} %pad_maximum_fusion.20), channel_id=1, source_target_pairs={{0,16},{16,0},{1,17},{17,1},{2,18},{18,2},{3,19},{19,3},{4,20},{20... | collective-permute-start | bytes 3145736 | tf_op jit(solution)/shard_map/ppermute | solution.py:18
  289.3 97.0 %collective-permute-start.36 = (bf16[1024,1024]{0,1:T(8,128)(2,1)S(1)}, bf16[1024,1024]{0,1:T(8,128)(2,1)S(1)}, u32[]{:S(2)}, u32[]{:S(2)}) collective-permute-start(bf16[1024,1024]{0,1:T(8,128)(2,1)S(1)} %pad_maximum_fusion.3), channel_id=1, source_target_pairs={{0,4},{4,0},{1,5},{5,1},{2,6},{6,2},{3,7},{7,3},{8,12},{12,8},{9,1... | collective-permute-start | bytes 6291464 | tf_op jit(solution)/shard_map/ppermute | solution.py:18
  290.9 90.5 %collective-permute-start.43 = (bf16[512,1024]{0,1:T(8,128)(2,1)S(1)}, bf16[512,1024]{0,1:T(8,128)(2,1)S(1)}, u32[]{:S(2)}, u32[]{:S(2)}) collective-permute-start(bf16[512,1024]{0,1:T(8,128)(2,1)S(1)} %pad_maximum_fusion.21), channel_id=1, source_target_pairs={{0,16},{16,0},{1,17},{17,1},{2,18},{18,2},{3,19},{19,3},{4,20},{20... | collective-permute-start | bytes 3145736 | tf_op jit(solution)/shard_map/ppermute | solution.py:18
  359.3 48.6 %collective-permute-start.40 = (bf16[1024,1024]{0,1:T(8,128)(2,1)S(1)}, bf16[1024,1024]{0,1:T(8,128)(2,1)S(1)}, u32[]{:S(2)}, u32[]{:S(2)}) collective-permute-start(bf16[1024,1024]{0,1:T(8,128)(2,1)S(1)} %pad_maximum_fusion.4), channel_id=1, source_target_pairs={{0,4},{4,0},{1,5},{5,1},{2,6},{6,2},{3,7},{7,3},{8,12},{12,8},{9,1... | collective-permute-start | bytes 6291464 | tf_op jit(solution)/shard_map/ppermute | solution.py:18
  381.7 70.1 %collective-permute-start.47 = (bf16[1024,1024]{0,1:T(8,128)(2,1)S(1)}, bf16[1024,1024]{0,1:T(8,128)(2,1)S(1)}, u32[]{:S(2)}, u32[]{:S(2)}) collective-permute-start(bf16[1024,1024]{0,1:T(8,128)(2,1)S(1)} %pad_maximum_fusion.5), channel_id=1, source_target_pairs={{0,4},{4,0},{1,5},{5,1},{2,6},{6,2},{3,7},{7,3},{8,12},{12,8},{9,1... | collective-permute-start | bytes 6291464 | tf_op jit(solution)/shard_map/ppermute | solution.py:18
  421.4 33.3 %collective-permute-start.44 = (bf16[512,1024]{1,0:T(8,128)(2,1)S(1)}, bf16[512,1024]{1,0:T(8,128)(2,1)S(1)}, u32[]{:S(2)}, u32[]{:S(2)}) collective-permute-start(bf16[512,1024]{1,0:T(8,128)(2,1)S(1)} %slice.2002), channel_id=1, source_target_pairs={{0,2},{2,0},{1,3},{3,1},{4,6},{6,4},{5,7},{7,5},{8,10},{10,8},{9,1... | collective-permute-start | bytes 3145736 | tf_op jit(solution)/shard_map/ppermute | solution.py:18
  568.6 48.6 %collective-permute-start.92 = (bf16[1024,1024]{0,1:T(8,128)(2,1)S(1)}, bf16[1024,1024]{0,1:T(8,128)(2,1)S(1)}, u32[]{:S(2)}, u32[]{:S(2)}) collective-permute-start(bf16[1024,1024]{0,1:T(8,128)(2,1)S(1)} %convolution_convert_fusion), channel_id=1, source_target_pairs={{0,4},{4,0},{1,5},{5,1},{2,6},{6,2},{3,7},{7,3},{8,12},{12,8},{9,1... | collective-permute-start | bytes 6291464 | tf_op jit(solution)/shard_map/ppermute | solution.py:18
  570.2 92.0 %collective-permute-start.88 = (bf16[1024,1024]{0,1:T(8,128)(2,1)S(1)}, bf16[1024,1024]{0,1:T(8,128)(2,1)S(1)}, u32[]{:S(2)}, u32[]{:S(2)}) collective-permute-start(bf16[1024,1024]{0,1:T(8,128)(2,1)S(1)} %convolution_convert_fusion.1), channel_id=1, source_target_pairs={{0,4},{4,0},{1,5},{5,1},{2,6},{6,2},{3,7},{7,3},{8,12},{12,8},{9,1... | collective-permute-start | bytes 6291464 | tf_op jit(solution)/shard_map/ppermute | solution.py:18
  570.7 134.1 %collective-permute-start.84 = (bf16[1024,1024]{0,1:T(8,128)(2,1)S(1)}, bf16[1024,1024]{0,1:T(8,128)(2,1)S(1)}, u32[]{:S(2)}, u32[]{:S(2)}) collective-permute-start(bf16[1024,1024]{0,1:T(8,128)(2,1)S(1)} %convolution_convert_fusion.2), channel_id=1, source_target_pairs={{0,4},{4,0},{1,5},{5,1},{2,6},{6,2},{3,7},{7,3},{8,12},{12,8},{9,1... | collective-permute-start | bytes 6291464 | tf_op jit(solution)/shard_map/ppermute | solution.py:18
  573.9 135.6 %collective-permute-start.62 = (bf16[128,2048]{1,0:T(8,128)(2,1)S(1)}, bf16[128,2048]{1,0:T(8,128)(2,1)S(1)}, u32[]{:S(2)}, u32[]{:S(2)}) collective-permute-start(bf16[128,2048]{1,0:T(8,128)(2,1)S(1)} %get-tuple-element.99), channel_id=1, source_target_pairs={{0,1},{1,0},{2,3},{3,2},{4,5},{5,4},{6,7},{7,6},{8,9},{9,8},{10,11... | collective-permute-start | bytes 1572872 | tf_op jit(solution)/shard_map/ppermute | solution.py:18
  619.8 89.9 %collective-permute-start.93 = (bf16[512,1024]{0,1:T(8,128)(2,1)S(1)}, bf16[512,1024]{0,1:T(8,128)(2,1)S(1)}, u32[]{:S(2)}, u32[]{:S(2)}) collective-permute-start(bf16[512,1024]{0,1:T(8,128)(2,1)S(1)} %slice.1996), channel_id=1, source_target_pairs={{0,16},{16,0},{1,17},{17,1},{2,18},{18,2},{3,19},{19,3},{4,20},{20... | collective-permute-start | bytes 3145736 | tf_op jit(solution)/shard_map/ppermute | solution.py:18
  664.7 47.4 %collective-permute-start.89 = (bf16[512,1024]{0,1:T(8,128)(2,1)S(1)}, bf16[512,1024]{0,1:T(8,128)(2,1)S(1)}, u32[]{:S(2)}, u32[]{:S(2)}) collective-permute-start(bf16[512,1024]{0,1:T(8,128)(2,1)S(1)} %slice.1997), channel_id=1, source_target_pairs={{0,16},{16,0},{1,17},{17,1},{2,18},{18,2},{3,19},{19,3},{4,20},{20... | collective-permute-start | bytes 3145736 | tf_op jit(solution)/shard_map/ppermute | solution.py:18
  707.6 46.5 %collective-permute-start.85 = (bf16[512,1024]{0,1:T(8,128)(2,1)S(1)}, bf16[512,1024]{0,1:T(8,128)(2,1)S(1)}, u32[]{:S(2)}, u32[]{:S(2)}) collective-permute-start(bf16[512,1024]{0,1:T(8,128)(2,1)S(1)} %slice.1998), channel_id=1, source_target_pairs={{0,16},{16,0},{1,17},{17,1},{2,18},{18,2},{3,19},{19,3},{4,20},{20... | collective-permute-start | bytes 3145736 | tf_op jit(solution)/shard_map/ppermute | solution.py:18
  709.7 47.0 %collective-permute-start.63 = (bf16[256,2048]{1,0:T(8,128)(2,1)S(1)}, bf16[256,2048]{1,0:T(8,128)(2,1)S(1)}, u32[]{:S(2)}, u32[]{:S(2)}) collective-permute-start(bf16[256,2048]{1,0:T(8,128)(2,1)S(1)} %pad_maximum_fusion.23), channel_id=1, source_target_pairs={{0,2},{2,0},{1,3},{3,1},{4,6},{6,4},{5,7},{7,5},{8,10},{10,8},{9,1... | collective-permute-start | bytes 3145736 | tf_op jit(solution)/shard_map/ppermute | solution.py:18
  711.1 100.7 %collective-permute-start.94 = (bf16[256,1024]{0,1:T(8,128)(2,1)}, bf16[256,1024]{0,1:T(8,128)(2,1)}, u32[]{:S(2)}, u32[]{:S(2)}) collective-permute-start(bf16[256,1024]{0,1:T(8,128)(2,1)} %select_convert_fusion.1), channel_id=1, source_target_pairs={{0,8},{8,0},{1,9},{9,1},{2,10},{10,2},{3,11},{11,3},{4,12},{12,4},... | collective-permute-start | bytes 1572872 | tf_op jit(solution)/shard_map/ppermute | solution.py:18
  713.4 100.4 %collective-permute-start.90 = (bf16[256,1024]{0,1:T(8,128)(2,1)}, bf16[256,1024]{0,1:T(8,128)(2,1)}, u32[]{:S(2)}, u32[]{:S(2)}) collective-permute-start(bf16[256,1024]{0,1:T(8,128)(2,1)} %select_convert_fusion.3), channel_id=1, source_target_pairs={{0,8},{8,0},{1,9},{9,1},{2,10},{10,2},{3,11},{11,3},{4,12},{12,4},... | collective-permute-start | bytes 1572872 | tf_op jit(solution)/shard_map/ppermute | solution.py:18
  756.6 60.1 %collective-permute-start.86 = (bf16[256,1024]{0,1:T(8,128)(2,1)}, bf16[256,1024]{0,1:T(8,128)(2,1)}, u32[]{:S(2)}, u32[]{:S(2)}) collective-permute-start(bf16[256,1024]{0,1:T(8,128)(2,1)} %select_convert_fusion.5), channel_id=1, source_target_pairs={{0,8},{8,0},{1,9},{9,1},{2,10},{10,2},{3,11},{11,3},{4,12},{12,4},... | collective-permute-start | bytes 1572872 | tf_op jit(solution)/shard_map/ppermute | solution.py:18
  787.3 49.9 %collective-permute-start.80 = (bf16[1024,512]{1,0:T(8,128)(2,1)}, bf16[1024,512]{1,0:T(8,128)(2,1)}, u32[]{:S(2)}, u32[]{:S(2)}) collective-permute-start(bf16[1024,512]{1,0:T(8,128)(2,1)} %convolution_convert_fusion.3), channel_id=1, source_target_pairs={{0,4},{4,0},{1,5},{5,1},{2,6},{6,2},{3,7},{7,3},{8,12},{12,8},{9,1... | collective-permute-start | bytes 3145736 | tf_op jit(solution)/shard_map/ppermute | solution.py:18
  809.8 31.8 %collective-permute-start.76 = (bf16[1024,512]{1,0:T(8,128)(2,1)}, bf16[1024,512]{1,0:T(8,128)(2,1)}, u32[]{:S(2)}, u32[]{:S(2)}) collective-permute-start(bf16[1024,512]{1,0:T(8,128)(2,1)} %convolution_convert_fusion.4), channel_id=1, source_target_pairs={{0,4},{4,0},{1,5},{5,1},{2,6},{6,2},{3,7},{7,3},{8,12},{12,8},{9,1... | collective-permute-start | bytes 3145736 | tf_op jit(solution)/shard_map/ppermute | solution.py:18
  811.9 46.7 %collective-permute-start.72 = (bf16[1024,512]{1,0:T(8,128)(2,1)}, bf16[1024,512]{1,0:T(8,128)(2,1)}, u32[]{:S(2)}, u32[]{:S(2)}) collective-permute-start(bf16[1024,512]{1,0:T(8,128)(2,1)} %convolution_convert_fusion.5), channel_id=1, source_target_pairs={{0,4},{4,0},{1,5},{5,1},{2,6},{6,2},{3,7},{7,3},{8,12},{12,8},{9,1... | collective-permute-start | bytes 3145736 | tf_op jit(solution)/shard_map/ppermute | solution.py:18
  820.3 59.6 %collective-permute-start.68 = (bf16[1024,512]{1,0:T(8,128)(2,1)}, bf16[1024,512]{1,0:T(8,128)(2,1)}, u32[]{:S(2)}, u32[]{:S(2)}) collective-permute-start(bf16[1024,512]{1,0:T(8,128)(2,1)} %convolution_convert_fusion.6), channel_id=1, source_target_pairs={{0,4},{4,0},{1,5},{5,1},{2,6},{6,2},{3,7},{7,3},{8,12},{12,8},{9,1... | collective-permute-start | bytes 3145736 | tf_op jit(solution)/shard_map/ppermute | solution.py:18
  830.9 53.0 %collective-permute-start.66 = (bf16[256,2048]{1,0:T(8,128)(2,1)}, bf16[256,2048]{1,0:T(8,128)(2,1)}, u32[]{:S(2)}, u32[]{:S(2)}) collective-permute-start(bf16[256,2048]{1,0:T(8,128)(2,1)} %pad_maximum_fusion.24), channel_id=1, source_target_pairs={{0,2},{2,0},{1,3},{3,1},{4,6},{6,4},{5,7},{7,5},{8,10},{10,8},{9,1... | collective-permute-start | bytes 3145736 | tf_op jit(solution)/shard_map/ppermute | solution.py:18
  839.7 47.5 %collective-permute-start.81 = (bf16[512,512]{1,0:T(8,128)(2,1)S(1)}, bf16[512,512]{1,0:T(8,128)(2,1)S(1)}, u32[]{:S(2)}, u32[]{:S(2)}) collective-permute-start(bf16[512,512]{1,0:T(8,128)(2,1)S(1)} %pad_maximum_fusion.44), channel_id=1, source_target_pairs={{0,8},{8,0},{1,9},{9,1},{2,10},{10,2},{3,11},{11,3},{4,12},{12,4},... | collective-permute-start | bytes 1572872 | tf_op jit(solution)/shard_map/ppermute | solution.py:18
  843.9 45.6 %collective-permute-start.77 = (bf16[512,512]{1,0:T(8,128)(2,1)S(1)}, bf16[512,512]{1,0:T(8,128)(2,1)S(1)}, u32[]{:S(2)}, u32[]{:S(2)}) collective-permute-start(bf16[512,512]{1,0:T(8,128)(2,1)S(1)} %pad_maximum_fusion.42), channel_id=1, source_target_pairs={{0,8},{8,0},{1,9},{9,1},{2,10},{10,2},{3,11},{11,3},{4,12},{12,4},... | collective-permute-start | bytes 1572872 | tf_op jit(solution)/shard_map/ppermute | solution.py:18
  860.8 29.9 %collective-permute-start.73 = (bf16[512,512]{1,0:T(8,128)(2,1)S(1)}, bf16[512,512]{1,0:T(8,128)(2,1)S(1)}, u32[]{:S(2)}, u32[]{:S(2)}) collective-permute-start(bf16[512,512]{1,0:T(8,128)(2,1)S(1)} %pad_maximum_fusion.40), channel_id=1, source_target_pairs={{0,8},{8,0},{1,9},{9,1},{2,10},{10,2},{3,11},{11,3},{4,12},{12,4},... | collective-permute-start | bytes 1572872 | tf_op jit(solution)/shard_map/ppermute | solution.py:18
  887.4 32.6 %collective-permute-start.82 = (bf16[256,512]{1,0:T(8,128)(2,1)S(1)}, bf16[256,512]{1,0:T(8,128)(2,1)S(1)}, u32[]{:S(2)}, u32[]{:S(2)}) collective-permute-start(bf16[256,512]{1,0:T(8,128)(2,1)S(1)} %slice.2005), channel_id=1, source_target_pairs={{0,16},{16,0},{1,17},{17,1},{2,18},{18,2},{3,19},{19,3},{4,20},{20... | collective-permute-start | bytes 786440 | tf_op jit(solution)/shard_map/ppermute | solution.py:18
  889.7 35.9 %collective-permute-start.78 = (bf16[256,512]{1,0:T(8,128)(2,1)S(1)}, bf16[256,512]{1,0:T(8,128)(2,1)S(1)}, u32[]{:S(2)}, u32[]{:S(2)}) collective-permute-start(bf16[256,512]{1,0:T(8,128)(2,1)S(1)} %slice.2006), channel_id=1, source_target_pairs={{0,16},{16,0},{1,17},{17,1},{2,18},{18,2},{3,19},{19,3},{4,20},{20... | collective-permute-start | bytes 786440 | tf_op jit(solution)/shard_map/ppermute | solution.py:18
  890.9 40.4 %collective-permute-start.74 = (bf16[256,512]{1,0:T(8,128)(2,1)S(1)}, bf16[256,512]{1,0:T(8,128)(2,1)S(1)}, u32[]{:S(2)}, u32[]{:S(2)}) collective-permute-start(bf16[256,512]{1,0:T(8,128)(2,1)S(1)} %slice.2007), channel_id=1, source_target_pairs={{0,16},{16,0},{1,17},{17,1},{2,18},{18,2},{3,19},{19,3},{4,20},{20... | collective-permute-start | bytes 786440 | tf_op jit(solution)/shard_map/ppermute | solution.py:18
  902.5 31.7 %collective-permute-start.70 = (bf16[256,512]{1,0:T(8,128)(2,1)S(1)}, bf16[256,512]{1,0:T(8,128)(2,1)S(1)}, u32[]{:S(2)}, u32[]{:S(2)}) collective-permute-start(bf16[256,512]{1,0:T(8,128)(2,1)S(1)} %slice.2008), channel_id=1, source_target_pairs={{0,16},{16,0},{1,17},{17,1},{2,18},{18,2},{3,19},{19,3},{4,20},{20... | collective-permute-start | bytes 786440 | tf_op jit(solution)/shard_map/ppermute | solution.py:18
  (195 other events, 3401.7 us)

commit v2 on v1

v2 whole, which is shorter than its diff:
```python
import math

import jax
import jax.numpy as jnp
from jax import lax
from jax.sharding import Mesh, PartitionSpec as P

HD = 128

EPSILON = 1e-06
NEGATIVE = -1e30
FLIP = [(0, 1), (1, 0)]
BF = jnp.bfloat16
F32 = jnp.float32


def swap(value, axis):
    return lax.ppermute(value, axis, FLIP)


def bit(axis):
    return lax.axis_index(axis)


def pick(axis, low, high):
    return jnp.where(bit(axis) == 0, low, high)


def ordered(axis, own, other, dim=0):
    return jnp.concatenate([pick(axis, own, other), pick(axis, other, own)], axis=dim)


def split(value, axis, dim):
    half = value.shape[dim] // 2
    low = lax.slice_in_dim(value, 0, half, axis=dim)
    high = lax.slice_in_dim(value, half, 2 * half, axis=dim)
    return pick(axis, low, high), pick(axis, high, low)


def dot(a, b):
    return jnp.dot(a, b, preferred_element_type=F32)


def dot_nt(a, b):
    return jnp.einsum("sc,rc->sr", a, b, preferred_element_type=F32)


def dot_tn(a, b):
    return jnp.einsum("sr,sc->rc", a, b, preferred_element_type=F32)


def rms_scale(values):
    return lax.rsqrt(jnp.mean(values * values, axis=1, keepdims=True) + EPSILON)


def build(high_bits):
    def to_relative(value):
        rows, width = value.shape
        count = 2 ** (len(high_bits) + 2)
        run = width // count
        pieces = [value[:, i * run : (i + 1) * run] for i in range(count)]
        names = list(high_bits) + ["zl", "x"]
        for position, name in enumerate(names):
            if name == "zl":
                continue
            mask = 1 << (len(names) - 1 - position)
            pieces = [pick(name, pieces[i], pieces[i ^ mask]) for i in range(count)]
        order = []
        for xr in range(2):
            for rest in range(count // 2):
                order.append(rest * 2 + xr)
        return jnp.concatenate([pieces[i] for i in order], axis=1)

    def to_natural(value):
        rows, width = value.shape
        count = 2 ** (len(high_bits) + 2)
        run = width // count
        moved = [value[:, i * run : (i + 1) * run] for i in range(count)]
        pieces = [None] * count
        place = 0
        for xr in range(2):
            for rest in range(count // 2):
                pieces[rest * 2 + xr] = moved[place]
                place += 1
        names = list(high_bits) + ["zl", "x"]
        for position, name in enumerate(names):
            if name == "zl":
                continue
            mask = 1 << (len(names) - 1 - position)
            pieces = [pick(name, pieces[i], pieces[i ^ mask]) for i in range(count)]
        return jnp.concatenate(pieces, axis=1)

    class Chain:
        def __init__(self, token):
            self.token = token

        def sync(self, *values):
            out = lax.optimization_barrier((self.token,) + values)
            self.token = out[0]
            return out[1] if len(values) == 1 else out[1:]

        def start(self, value, axis):
            return swap(self.sync(value), axis)

        def start_high(self, rows):
            for name in high_bits[:0:-1]:
                rows = jnp.concatenate([rows, self.sync(self.start(rows, name))], axis=0)
            return rows, (self.start(rows, high_bits[0]) if high_bits else None)

        def end_high(self, pending):
            rows, sent = pending
            return rows if sent is None else jnp.concatenate([rows, self.sync(sent)], axis=0)

        def start_high_sum(self, total):
            for name in high_bits[:-1]:
                half = total.shape[0] // 2
                total = total[:half] + self.sync(self.start(total[half:].astype(BF), name)).astype(F32)
            if not high_bits:
                return total, None
            half = total.shape[0] // 2
            return total[:half], self.start(total[half:].astype(BF), high_bits[-1])

        def end_high_sum(self, pending):
            total, sent = pending
            return total if sent is None else total + self.sync(sent).astype(F32)

    high_blocks = 2 ** len(high_bits)

    def split_lines(rows, outer):
        run = rows.shape[0] // outer
        pairs = [split(rows[b * run : (b + 1) * run], "zl", 0) for b in range(outer)]
        if outer == 1:
            return pairs[0]
        return tuple(jnp.concatenate([p[i] for p in pairs], axis=0) for i in range(2))

    def join_lines(own, other, outer):
        run = own.shape[0] // outer
        parts = [
            ordered("zl", own[b * run : (b + 1) * run], other[b * run : (b + 1) * run])
            for b in range(outer)
        ]
        return parts[0] if outer == 1 else jnp.concatenate(parts, axis=0)

    def gather_gains(c, gains):
        gains = ordered("tensor", gains, c.sync(c.start(gains, "tensor")), dim=1)
        gains = ordered("core", gains, c.sync(c.start(gains, "core")), dim=1)
        gains = ordered("zl", gains, c.sync(c.start(gains, "zl")), dim=1)
        for name in list(high_bits)[::-1] + ["x"]:
            gains = jnp.concatenate([gains, c.sync(c.start(gains, name))], axis=1)
        return gains

    def pair_sum(c, values):
        half = values.shape[1] // 2
        other = c.sync(c.start(values, "core"))
        values = values + jnp.concatenate([other[:, half:], other[:, :half]], axis=1)
        return values + c.sync(c.start(values, "tensor"))

    def scatter_gains(c, gains):
        for name in ["x"] + list(high_bits):
            half = gains.shape[1] // 2
            gains = gains[:, :half] + c.sync(c.start(gains[:, half:], name))
        for name in ("zl", "core", "tensor"):
            own, sent = split(gains, name, 1)
            gains = own + c.sync(c.start(sent, name))
        return gains

    def stack2(low, high):
        return jnp.concatenate([low, high], axis=0)

    def shards(
        tokens,
        segment_ids,
        w_query,
        w_key,
        w_value,
        w_output,
        w_gate,
        w_up,
        w_down,
        query_gain,
        key_gain,
        attn_gain,
        ffn_gain,
        cotangent,
    ):
        own_tokens, model_width = tokens.shape
        half_width = model_width // 2
        seq_length = own_tokens * 2
        pair_tokens = seq_length * 2
        head_width = w_query.shape[1] // 2
        ffn_width = w_gate.shape[1] // 4
        local_heads = head_width // HD
        score_scale = 1.0 / math.sqrt(HD)
        c = Chain(query_gain)

        attn_split = [split(w, "core", 1) for w in (w_query, w_key, w_value, w_output)]
        attn_sent = c.start(jnp.concatenate([s[1] for s in attn_split], axis=1), "core")
        tokens_rel = to_relative(tokens)
        tokens_sent = c.start(tokens_rel, "tensor")
        ffn_split = [split(w, "core", 1) for w in (w_gate, w_up, w_down)]
        ffn_sent = c.start(jnp.concatenate([s[1] for s in ffn_split], axis=1), "core")

        attn_sent = c.sync(attn_sent)
        q_rows, k_rows, v_rows, o_rows = [
            ordered("core", s[0], attn_sent[:, i * head_width : (i + 1) * head_width])
            for i, s in enumerate(attn_split)
        ]
        k_high = c.start_high(k_rows)
        q_x = c.start(q_rows, "x")
        ffn_sent = c.sync(ffn_sent)
        g_rows, u_rows, d_rows = [
            split(
                ordered("core", s[0], ffn_sent[:, i * 2 * ffn_width : (i + 1) * 2 * ffn_width]),
                "zl",
                1,
            )
            for i, s in enumerate(ffn_split)
        ]
        g_line = c.start(g_rows[1], "zl")
        q_x = c.sync(q_x)
        q_rows2 = jnp.concatenate([q_rows, q_x], axis=1)
        segments_other = swap(segment_ids, "core")
        gains = gather_gains(c, jnp.stack([query_gain, key_gain, attn_gain, ffn_gain]))
        tokens_sent = c.sync(tokens_sent)
        own_seq = ordered("tensor", tokens_rel, tokens_sent)
        tokens_sent = c.start(own_seq, "core")
        k_rows = c.end_high(k_high)
        v_high = c.start_high(v_rows)
        g_rows = ordered("zl", g_rows[0], c.sync(g_line))
        k_line = c.start(k_rows, "zl")
        whole_input = stack2(own_seq, c.sync(tokens_sent))
        k_rows = join_lines(k_rows, c.sync(k_line), high_blocks)
        k_x = c.start(k_rows, "x")
        v_rows = c.end_high(v_high)
        q_high = c.start_high(q_rows2)
        v_line = c.start(v_rows, "zl")
        v_rows = join_lines(v_rows, c.sync(v_line), high_blocks)
        u_line = c.start(u_rows[1], "zl")

        attn_scale = gains[2]
        ffn_scale = gains[3]
        head_gains = to_natural(gains[:2])
        head_start = (bit("tensor") * 2 + bit("core")) * head_width
        head_gains = lax.dynamic_slice_in_dim(head_gains, head_start, head_width, axis=1)
        query_scale, key_scale = head_gains[0], head_gains[1]
        tokens_f = tokens_rel.astype(F32)
        d_out = to_relative(cotangent).astype(F32)
        seq_ids = stack2(segment_ids, segments_other)
        positions = jnp.arange(seq_length)
        visible = (positions[:, None] >= positions[None, :])[None] & (
            seq_ids[:, :, None] == seq_ids[:, None, :]
        )
        visible = visible[:, None]
        in0, in1 = whole_input[:, :half_width], whole_input[:, half_width:]

        k_x = c.sync(k_x)
        v_x = c.start(v_rows, "x")
        key_proj = dot(in0, k_rows) + dot(in1, k_x)
        q_rows2 = c.end_high(q_high)
        u_rows = ordered("zl", u_rows[0], c.sync(u_line))
        q_line = c.start(q_rows2, "zl")
        o_high = c.start_high(o_rows)
        o_rows = c.end_high(o_high)
        g_high = c.start_high(g_rows)
        q_rows2 = join_lines(q_rows2, c.sync(q_line), high_blocks)
        o_line = c.start(o_rows, "zl")
        wq0, wq1 = q_rows2[:, :head_width], q_rows2[:, head_width:]
        query = dot(in0, wq0) + dot(in1, wq1)
        v_x = c.sync(v_x)
        wk0, wk1, wv0, wv1 = k_rows, k_x, v_rows, v_x
        value_bf = (dot(in0, wv0) + dot(in1, wv1)).astype(BF)
        squares = pair_sum(
            c, jnp.stack([jnp.sum(query * query, axis=1), jnp.sum(key_proj * key_proj, axis=1)])
        )
        o_rows = join_lines(o_rows, c.sync(o_line), high_blocks)
        o_x = c.start(o_rows, "x")
        d_line = c.start(d_rows[1], "zl")
        q_rms = lax.rsqrt(squares[0] / model_width + EPSILON)[:, None]
        k_rms = lax.rsqrt(squares[1] / model_width + EPSILON)[:, None]
        normed_query = (query * q_rms * query_scale).astype(BF)
        normed_key = (key_proj * k_rms * key_scale).astype(BF)
        heads = (2, seq_length, local_heads, HD)
        query_heads = normed_query.reshape(heads)
        key_heads = normed_key.reshape(heads)
        value_heads = value_bf.reshape(heads)
        scores = (
            jnp.einsum("bqhd,bkhd->bhqk", query_heads, key_heads, preferred_element_type=F32)
            * score_scale
        )
        scores = jnp.where(visible, scores, NEGATIVE)
        peak = jnp.max(scores, axis=-1, keepdims=True)
        expo = jnp.exp(scores - peak)
        total = jnp.sum(expo, axis=-1, keepdims=True)
        prob = expo / total
        prob_bf = prob.astype(BF)
        attn_heads = jnp.einsum(
            "bhqk,bkhd->bqhd", prob_bf, value_heads, preferred_element_type=F32
        ).astype(BF)
        attn = c.sync(attn_heads.reshape(pair_tokens, head_width))
        d_rows = ordered("zl", d_rows[0], c.sync(d_line))
        o_x = c.sync(o_x)
        wo0, wo1 = o_rows, o_x
        g_rows = c.end_high(g_high)
        g_x = c.start(g_rows, "x")
        u_high = c.start_high(u_rows)

        def columns(parts):
            return jnp.concatenate(parts, axis=1)

        def scatter_pair(low, high):
            sent = c.start(high().astype(BF), "core")
            total = low() + c.sync(sent).astype(F32)
            own, sent = split(total, "tensor", 0)
            return own + c.sync(c.start(sent.astype(BF), "tensor")).astype(F32)

        def out_proj(rows):
            return columns([dot_nt(rows, wo0), dot_nt(rows, wo1)])

        proj = scatter_pair(
            lambda: out_proj(attn[:seq_length]), lambda: out_proj(attn[seq_length:])
        )
        attn_rms = rms_scale(proj)
        resid = tokens_f + proj * attn_rms * attn_scale

        def gather_rows(value):
            left, right = value[:, :half_width], value[:, half_width:]
            left_sent = c.start(left, "tensor")
            right_sent = c.start(right, "zl")
            left = stack2(left, c.sync(left_sent))
            right = stack2(right, c.sync(right_sent))
            left_sent = c.start(left, "zl")
            right_sent = c.start(right, "tensor")
            left = stack2(left, c.sync(left_sent))
            right_sent = c.sync(right_sent)
            rows = own_tokens
            right = jnp.concatenate(
                [right[:rows], right_sent[:rows], right[rows:], right_sent[rows:]], axis=0
            )
            left_sent = c.start(left, "core")
            right_sent = c.start(right, "core")
            return left, right, left_sent, right_sent

        h0a, h1a, h0b, h1b = gather_rows(resid.astype(BF))
        h0b, h1b = c.sync(h0b, h1b)
        g_x = c.sync(g_x)
        u_rows = c.end_high(u_high)
        u_x = c.start(u_rows, "x")
        d_high = c.start_high(d_rows)
        wg0, wg1, wu0 = g_rows, g_x, u_rows
        gate_a = dot(h0a, wg0) + dot(h1a, wg1)
        gate_b = dot(h0b, wg0) + dot(h1b, wg1)
        gate_a, gate_b = c.sync(gate_a, gate_b)
        wd0 = c.end_high(d_high)
        wu1 = c.sync(u_x)
        d_x = c.start(wd0, "x")
        up_a = dot(h0a, wu0) + dot(h1a, wu1)
        up_b = dot(h0b, wu0) + dot(h1b, wu1)
        sigma_a, sigma_b = jax.nn.sigmoid(gate_a), jax.nn.sigmoid(gate_b)
        act_a = (gate_a * sigma_a * up_a).astype(BF)
        act_b = (gate_b * sigma_b * up_b).astype(BF)

        def halve(total, axis):
            half = total.shape[0] // 2
            return total[:half], c.start(total[half:].astype(BF), axis)

        def added(pair):
            return pair[0] + c.sync(pair[1]).astype(F32)

        def cross(total):
            rows = own_tokens
            own = stack2(total[:rows], total[2 * rows : 3 * rows])
            sent = stack2(total[rows : 2 * rows], total[3 * rows :])
            return own, c.start(sent.astype(BF), "tensor")

        left_sent = c.start(dot_nt(act_b, wd0).astype(BF), "core")
        left = dot_nt(act_a, wd0) + c.sync(left_sent).astype(F32)
        left = added(halve(left, "zl"))
        left = added(halve(left, "tensor"))
        wd1 = c.sync(d_x)
        right_sent = c.start(dot_nt(act_b, wd1).astype(BF), "core")
        right = dot_nt(act_a, wd1) + c.sync(right_sent).astype(F32)
        right = added(cross(right))
        right = added(halve(right, "zl"))
        ffn = columns([left, right])

        ffn_rms = rms_scale(ffn)
        output = to_natural((resid + ffn * ffn_rms * ffn_scale).astype(BF))
        ffn_gain_term = jnp.sum(d_out * ffn * ffn_rms, axis=0)
        scaled_out = d_out * ffn_scale
        d_ffn = (
            ffn_rms
            * (
                scaled_out
                - ffn * ffn_rms * ffn_rms * jnp.mean(scaled_out * ffn, axis=1, keepdims=True)
            )
        ).astype(BF)
        f0a, f1a, f0b, f1b = gather_rows(d_ffn)
        f0b, f1b = c.sync(f0b, f1b)
        part = ffn_width // 2

        class FfnGrad:
            def __init__(self, kept, sent):
                self.kept, self.sent = kept, sent
                self.moving, self.high, self.sums = [None, None], [None, None], [None, None]

            def product(self, pair, i):
                left, right = pair
                cols = slice(i * part, (i + 1) * part)
                return dot_tn(left[0], right[0][:, cols]) + dot_tn(left[1], right[1][:, cols])

            def start_x(self, i):
                self.moving[i] = c.start(self.product(self.sent, i).astype(BF), "x")

            def end_x(self, i):
                moved = c.sync(self.moving[i])
                self.sums[i] = self.product(self.kept, i) + moved.astype(F32)

            def start_high(self, i):
                self.high[i] = c.start_high_sum(self.sums[i])

            def end_high(self, i):
                self.sums[i] = c.end_high_sum(self.high[i])

            def start_line(self):
                self.own, sent = split(columns(self.sums), "zl", 0)
                self.line = c.start(sent.astype(BF), "zl")

            def end_line(self):
                moved = c.sync(self.line).astype(F32)
                total = ordered("zl", self.own, moved, dim=1)
                self.own, sent = split(total, "core", 0)
                self.core = c.start(sent.astype(BF), "core")

            def result(self):
                return ordered("core", self.own, c.sync(self.core).astype(F32), dim=1)

        class AttnGrad:
            def __init__(self, kept, sent, right):
                self.kept, self.sent = kept, sent
                self.right = right

            def start_x(self):
                self.x = c.start(dot_tn(self.sent, self.right).astype(BF), "x")

            def end_x(self):
                moved = c.sync(self.x)
                self.total = dot_tn(self.kept, self.right) + moved.astype(F32)

            def start_line(self):
                self.own, sent = split_lines(self.total, high_blocks)
                self.line = c.start(sent.astype(BF), "zl")

            def end_line(self):
                self.total = self.own + c.sync(self.line).astype(F32)

            def start_high(self):
                self.high = c.start_high_sum(self.total)

            def end_high(self):
                self.total = c.end_high_sum(self.high)

            def start_core(self):
                self.own, sent = split(self.total, "core", 0)
                self.core = c.start(sent.astype(BF), "core")

            def result(self):
                return ordered("core", self.own, c.sync(self.core).astype(F32), dim=1)

        down = FfnGrad(((f0a, f0b), (act_a, act_b)), ((f1a, f1b), (act_a, act_b)))
        down.start_x(0)

        def backward_gate(f0, f1, gate, up, sigma):
            d_act = dot(f0, wd0) + dot(f1, wd1)
            d_gate = (d_act * up * sigma * (1.0 + gate * (1.0 - sigma))).astype(BF)
            return d_gate, (d_act * gate * sigma).astype(BF)

        dg_b, du_b = backward_gate(f0b, f1b, gate_b, up_b, sigma_b)
        left_sent = c.start((dot_nt(dg_b, wg0) + dot_nt(du_b, wu0)).astype(BF), "core")
        right_sent = c.start((dot_nt(dg_b, wg1) + dot_nt(du_b, wu1)).astype(BF), "core")
        dg_a, du_a = backward_gate(f0a, f1a, gate_a, up_a, sigma_a)
        left = dot_nt(dg_a, wg0) + dot_nt(du_a, wu0)
        right = dot_nt(dg_a, wg1) + dot_nt(du_a, wu1)
        left = left + c.sync(left_sent).astype(F32)
        right = right + c.sync(right_sent).astype(F32)
        down.end_x(0)
        down.start_x(1)
        left_pair = halve(left, "zl")
        right_pair = cross(right)
        down.start_high(0)
        left = added(left_pair)
        right = added(right_pair)
        left_pair = halve(left, "tensor")
        right_pair = halve(right, "zl")
        gate_grad = FfnGrad(((h0a, h0b), (dg_a, dg_b)), ((h1a, h1b), (dg_a, dg_b)))
        up_grad = FfnGrad(((h0a, h0b), (du_a, du_b)), ((h1a, h1b), (du_a, du_b)))
        left = added(left_pair)
        right = added(right_pair)
        d_resid = d_out + columns([left, right])
        attn_gain_term = jnp.sum(d_resid * proj * attn_rms, axis=0)
        scaled_resid = d_resid * attn_scale
        d_proj = (
            attn_rms
            * (
                scaled_resid
                - proj * attn_rms * attn_rms * jnp.mean(scaled_resid * proj, axis=1, keepdims=True)
            )
        ).astype(BF)
        dproj_sent = c.start(d_proj, "tensor")
        down.end_high(0)
        down.end_x(1)
        gate_grad.start_x(0)
        down.start_high(1)
        own_dproj = ordered("tensor", d_proj, c.sync(dproj_sent))
        dproj_sent = c.start(own_dproj, "core")
        whole_dproj = stack2(own_dproj, c.sync(dproj_sent))
        p0, p1 = whole_dproj[:, :half_width], whole_dproj[:, half_width:]
        d_attn = (dot(p0, wo0) + dot(p1, wo1)).astype(BF)
        d_attn = c.sync(d_attn)
        gate_grad.end_x(0)
        gate_grad.start_x(1)
        down.end_high(1)
        gate_grad.start_high(0)
        down.start_line()

        d_attn_heads = d_attn.reshape(heads)
        d_value = (
            jnp.einsum("bhqk,bqhd->bkhd", prob_bf, d_attn_heads, preferred_element_type=F32)
            .reshape(pair_tokens, head_width)
            .astype(BF)
        )
        d_prob = jnp.einsum(
            "bqhd,bkhd->bhqk", d_attn_heads, value_heads, preferred_element_type=F32
        )
        delta = jnp.einsum(
            "bqhd,bqhd->bhq", d_attn_heads, attn.reshape(heads), preferred_element_type=F32
        )[..., None]
        d_score = (prob * (d_prob - delta)).astype(BF)
        d_nq = (
            jnp.einsum("bhqk,bkhd->bqhd", d_score, key_heads, preferred_element_type=F32).reshape(
                pair_tokens, head_width
            )
            * score_scale
        )
        d_nk = (
            jnp.einsum("bhqk,bqhd->bkhd", d_score, query_heads, preferred_element_type=F32).reshape(
                pair_tokens, head_width
            )
            * score_scale
        )
        query_gain_term = jnp.sum(d_nq * query * q_rms, axis=0)
        key_gain_term = jnp.sum(d_nk * key_proj * k_rms, axis=0)
        scaled_q = d_nq * query_scale
        scaled_k = d_nk * key_scale
        inner = pair_sum(
            c, jnp.stack([jnp.sum(scaled_q * query, axis=1), jnp.sum(scaled_k * key_proj, axis=1)])
        )
        d_query = (
            q_rms * (scaled_q - query * q_rms * q_rms * (inner[0] / model_width)[:, None])
        ).astype(BF)
        d_key = (
            k_rms * (scaled_k - key_proj * k_rms * k_rms * (inner[1] / model_width)[:, None])
        ).astype(BF)
        query_grad = AttnGrad(in0, in1, d_query)
        key_grad = AttnGrad(in0, in1, d_key)
        value_grad = AttnGrad(in0, in1, d_value)
        output_grad = AttnGrad(p0, p1, attn)

        def in_proj(rows):
            return columns(
                [
                    dot_nt(d_query[rows], wq) + dot_nt(d_key[rows], wk) + dot_nt(d_value[rows], wv)
                    for wq, wk, wv in ((wq0, wk0, wv0), (wq1, wk1, wv1))
                ]
            )

        query_whole = stack2(
            dot_tn(query_grad.kept, query_grad.right), dot_tn(query_grad.sent, query_grad.right)
        )
        query_own, query_sent = split_lines(query_whole, 2 * high_blocks)
        query_line = c.start(query_sent.astype(BF), "zl")
        tok_sent = c.start(in_proj(slice(seq_length, pair_tokens)).astype(BF), "core")
        gate_grad.end_x(1)
        up_grad.start_x(0)
        gate_grad.end_high(0)
        gate_grad.start_high(1)
        total = in_proj(slice(0, seq_length)) + c.sync(tok_sent).astype(F32)
        own, sent = split(total, "tensor", 0)
        tok_sent = c.start(sent.astype(BF), "tensor")
        down.end_line()
        query_total = query_own + c.sync(query_line).astype(F32)
        d_tokens = own + c.sync(tok_sent).astype(F32)
        grad_tokens = to_natural(d_resid + d_tokens)
        grad_down = down.result()
        up_grad.end_x(0)
        up_grad.start_x(1)
        gate_grad.end_high(1)
        up_grad.start_high(0)
        gate_grad.start_line()

        zero = jnp.zeros((2, model_width), F32)
        placed = lax.dynamic_update_slice_in_dim(
            zero, jnp.stack([query_gain_term, key_gain_term]), head_start, 1
        )
        gain_parts = scatter_gains(
            c,
            jnp.concatenate(
                [to_relative(placed), jnp.stack([attn_gain_term, ffn_gain_term])], axis=0
            ),
        )
        gate_grad.end_line()
        grad_gate = gate_grad.result()
        up_grad.end_x(1)
        output_grad.start_x()
        up_grad.end_high(0)
        up_grad.start_high(1)
        output_grad.end_x()
        value_grad.start_x()
        output_grad.start_line()
        up_grad.end_high(1)
        half = query_total.shape[0] // 2
        query_high = [
            c.start_high_sum(
                columns([query_total[:half], query_total[half:]])
            )
        ]
        output_grad.end_line()
        up_grad.start_line()
        up_grad.end_line()
        value_grad.end_x()
        key_grad.start_x()
        value_grad.start_line()
        query_total = c.end_high_sum(query_high[0])
        output_grad.start_high()
        query_x = c.start(query_total[:, head_width:].astype(BF), "x")
        grad_up = up_grad.result()
        value_grad.end_line()
        output_grad.end_high()
        value_grad.start_high()
        output_grad.start_core()
        key_grad.end_x()
        key_grad.start_line()
        query_grad.total = query_total[:, :head_width] + c.sync(query_x).astype(F32)
        query_grad.start_core()
        grad_output = output_grad.result()
        value_grad.end_high()
        value_grad.start_core()
        key_grad.end_line()
        key_grad.start_high()
        grad_query = query_grad.result()
        grad_value = value_grad.result()
        key_grad.end_high()
        key_grad.start_core()
        grad_key = key_grad.result()
        return (
            output,
            grad_tokens,
            grad_query,
            grad_key,
            grad_value,
            grad_output,
            grad_gate,
            grad_up,
            grad_down,
            gain_parts[0],
            gain_parts[1],
            gain_parts[2],
            gain_parts[3],
        )

    return shards


def solution(mesh):
    dp = mesh.shape["dp"]
    high = max(dp.bit_length() - 4, 0)
    high_bits = tuple(f"z{i}" for i in range(high))
    names = high_bits + ("zl", "x", "core", "tensor")
    fine = Mesh(mesh.devices.reshape((2,) * len(names)), names)
    rows = names[:-1]
    both = names
    mapped = jax.shard_map(
        build(high_bits),
        mesh=fine,
        in_specs=(
            P(both, None),
            P(rows, None),
            P(rows, "tensor"),
            P(rows, "tensor"),
            P(rows, "tensor"),
            P(rows, "tensor"),
            P(rows, "tensor"),
            P(rows, "tensor"),
            P(rows, "tensor"),
            P(both),
            P(both),
            P(both),
            P(both),
            P(both, None),
        ),
        out_specs=(
            P(both, None),
            P(both, None),
            P(rows, "tensor"),
            P(rows, "tensor"),
            P(rows, "tensor"),
            P(rows, "tensor"),
            P(rows, "tensor"),
            P(rows, "tensor"),
            P(rows, "tensor"),
            P(both),
            P(both),
            P(both),
            P(both),
        ),
        check_vma=False,
    )
    return mapped
```

time: 949 us -> 889 us (0.937)
  waiting for transfers between devices: 605 us -> 559 us
  matrix products: 100 us -> 123 us
  starting transfers between devices: 103 us -> 90.9 us
  local copies, waits for them, and re-layouts: 42.2 us -> 30.3 us
  other arithmetic: 82.8 us -> 71.7 us
    ppermute x101 -> x104, waiting for transfers between devices: 605 us -> 559 us  [swap(): return lax.ppermute(value, axis, FLIP)]
    concatenate x31 -> x34, other arithmetic: 35.1 us -> 12.1 us  [the longest x11 3.58 us: stack2(): return jnp.concatenate([low, high], axis=0)]
    unnamed x296 -> x329, local copies, waits for them, and re-layouts: 25 us -> 11.9 us
    dot_general x14 -> x32, matrix products: 30.2 us -> 42.9 us  [dot_tn(): return jnp.einsum('sr,sc->rc', a, b, preferred_element_type=F32)]
    ppermute x101 -> x104, starting transfers between devices: 103 us -> 90.9 us  [swap(): return lax.ppermute(value, axis, FLIP)]
    dot_general x22 -> x28, matrix products: 26.5 us -> 33.3 us  [dot_nt(): return jnp.einsum('sc,rc->sr', a, b, preferred_element_type=F32)]
    select_n x50 -> x40, other arithmetic: 19.3 us -> 16.4 us  [pick(): return jnp.where(bit(axis) == 0, low, high)]
    dot_general x14 -> x20, matrix products: 34.8 us -> 34.8 us  [dot(): return jnp.dot(a, b, preferred_element_type=F32)]
  transfers between devices with their start and end apart: 101 -> 104, of which waited for: 51 -> 65; matrix products, arithmetic and copies ran while one was open for 19% -> 14% of each run, Pallas kernels for 0% -> 0%
where the time goes in v2:
time: 889 us; the launch traced here: 879 us
  waiting for transfers between devices  559 us (63%)
  matrix products  123 us (14%)
  starting transfers between devices  90.9 us (10%)
  other arithmetic  71.7 us (8%)
  local copies, waits for them, and re-layouts  30.3 us (3%)
    ppermute x104, waiting for transfers between devices, swap(): return lax.ppermute(value, axis, FLIP)  559 us
    ppermute x104, starting transfers between devices, swap(): return lax.ppermute(value, axis, FLIP)  90.9 us
    dot_general x32, matrix products, dot_tn(): return jnp.einsum('sr,sc->rc', a, b, preferred_element_type=F32)  42.9 us
    dot_general x20, matrix products, dot(): return jnp.dot(a, b, preferred_element_type=F32)  34.8 us
    dot_general x28, matrix products, dot_nt(): return jnp.einsum('sc,rc->sr', a, b, preferred_element_type=F32)  33.3 us
  transfers between devices with their start and end apart: 104, of which 65 were waited for; matrix products, arithmetic and copies ran while one was open for 14% of the time, Pallas kernels for 0%

profile of v2, /device:TPU:0, one launch (start us, length us, event | category | flops | bytes accessed | tf_op | source)
XLA Modules:
  0.0 879.2 jit_solution(5904948095240114858)
XLA Ops:
  11.7 3.0 collective-permute-start.8
  35.2 12.5 %collective-permute-done.5 = f32[4,256]{1,0:T(4,128)S(1)} collective-permute-done((f32[4,256]{1,0:T(4,128)S(1)}, f32[4,256]{1,0:T(4,128)S(1)}, u32[]{:S(2)}, u32[]{:S(2)}) %collective-permute-start.5) | collective-permute-done | bytes 4128 | tf_op jit(solution)/shard_map/ppermute | solution.py:18
  61.7 16.9 %collective-permute-done.12 = bf16[512,512]{1,0:T(8,128)(2,1)S(1)} collective-permute-done((bf16[512,512]{1,0:T(8,128)(2,1)S(1)}, bf16[512,512]{1,0:T(8,128)(2,1)S(1)}, u32[]{:S(2)}, u32[]{:S(2)}) %collective-permute-start.12) | collective-permute-done | bytes 524320 | tf_op jit(solution)/shard_map/ppermute | solution.py:18
  84.3 16.2 %collective-permute-done.14 = bf16[512,512]{1,0:T(8,128)(2,1)S(1)} collective-permute-done((bf16[512,512]{1,0:T(8,128)(2,1)S(1)}, bf16[512,512]{1,0:T(8,128)(2,1)S(1)}, u32[]{:S(2)}, u32[]{:S(2)}) %collective-permute-start.14) | collective-permute-done | bytes 524320 | tf_op jit(solution)/shard_map/ppermute | solution.py:18
  104.0 3.7 collective-permute-done.16
  107.7 8.5 collective-permute-done.17
  122.3 20.7 %collective-permute-done.18 = bf16[256,512]{1,0:T(8,128)(2,1)S(1)} collective-permute-done((bf16[256,512]{1,0:T(8,128)(2,1)S(1)}, bf16[256,512]{1,0:T(8,128)(2,1)S(1)}, u32[]{:S(2)}, u32[]{:S(2)}) %collective-permute-start.18) | collective-permute-done | bytes 262176 | tf_op jit(solution)/shard_map/ppermute | solution.py:18
  158.4 27.0 %collective-permute-done.23 = bf16[512,512]{1,0:T(8,128)(2,1)} collective-permute-done((bf16[512,512]{1,0:T(8,128)(2,1)}, bf16[512,512]{1,0:T(8,128)(2,1)}, u32[]{:S(2)}, u32[]{:S(2)}) %collective-permute-start.23) | collective-permute-done | bytes 524320 | tf_op jit(solution)/shard_map/ppermute | solution.py:18
  198.3 2.9 fusion.8
  204.4 5.5 collective-permute-done.25
  209.9 3.9 collective-permute-done.26
  221.0 12.4 %collective-permute-done.29 = bf16[128,2048]{1,0:T(8,128)(2,1)S(1)} collective-permute-done((bf16[128,2048]{1,0:T(8,128)(2,1)S(1)}, bf16[128,2048]{1,0:T(8,128)(2,1)S(1)}, u32[]{:S(2)}, u32[]{:S(2)}) %collective-permute-start.29) | collective-permute-done | bytes 524320 | tf_op jit(solution)/shard_map/ppermute | solution.py:18
  246.0 10.0 %collective-permute-done.32 = bf16[256,1024]{1,0:T(8,128)(2,1)S(1)} collective-permute-done((bf16[256,1024]{1,0:T(8,128)(2,1)S(1)}, bf16[256,1024]{1,0:T(8,128)(2,1)S(1)}, u32[]{:S(2)}, u32[]{:S(2)}) %collective-permute-start.32) | collective-permute-done | bytes 524320 | tf_op jit(solution)/shard_map/ppermute | solution.py:18
  261.6 22.7 %collective-permute-done.36 = bf16[1024,1024]{1,0:T(8,128)(2,1)S(1)} collective-permute-done((bf16[1024,1024]{1,0:T(8,128)(2,1)S(1)}, bf16[1024,1024]{1,0:T(8,128)(2,1)S(1)}, u32[]{:S(2)}, u32[]{:S(2)}) %collective-permute-start.36) | collective-permute-done | bytes 2097184 | tf_op jit(solution)/shard_map/ppermute | solution.py:18
  284.3 22.2 %collective-permute-done.37 = bf16[512,1024]{1,0:T(8,128)(2,1)S(1)} collective-permute-done((bf16[512,1024]{1,0:T(8,128)(2,1)S(1)}, bf16[512,1024]{1,0:T(8,128)(2,1)S(1)}, u32[]{:S(2)}, u32[]{:S(2)}) %collective-permute-start.37) | collective-permute-done | bytes 1048608 | tf_op jit(solution)/shard_map/ppermute | solution.py:18
  314.3 3.2 fusion.167
  317.6 39.6 %collective-permute-done.38 = bf16[512,1024]{1,0:T(8,128)(2,1)S(1)} collective-permute-done((bf16[512,1024]{1,0:T(8,128)(2,1)S(1)}, bf16[512,1024]{1,0:T(8,128)(2,1)S(1)}, u32[]{:S(2)}, u32[]{:S(2)}) %collective-permute-start.38) | collective-permute-done | bytes 1048608 | tf_op jit(solution)/shard_map/ppermute | solution.py:18
  369.4 14.0 %collective-permute-done.41 = bf16[256,1024]{1,0:T(8,128)(2,1)S(1)} collective-permute-done((bf16[256,1024]{1,0:T(8,128)(2,1)S(1)}, bf16[256,1024]{1,0:T(8,128)(2,1)S(1)}, u32[]{:S(2)}, u32[]{:S(2)}) %collective-permute-start.41) | collective-permute-done | bytes 524320 | tf_op jit(solution)/shard_map/ppermute | solution.py:18
  384.2 7.0 collective-permute-done.42
  391.2 19.6 %collective-permute-done.43 = bf16[1024,1024]{1,0:T(8,128)(2,1)S(1)} collective-permute-done((bf16[1024,1024]{1,0:T(8,128)(2,1)S(1)}, bf16[1024,1024]{1,0:T(8,128)(2,1)S(1)}, u32[]{:S(2)}, u32[]{:S(2)}) %collective-permute-start.43) | collective-permute-done | bytes 2097184 | tf_op jit(solution)/shard_map/ppermute | solution.py:18
  416.8 13.4 %collective-permute-done.45 = bf16[256,1024]{1,0:T(8,128)(2,1)S(1)} collective-permute-done((bf16[256,1024]{1,0:T(8,128)(2,1)S(1)}, bf16[256,1024]{1,0:T(8,128)(2,1)S(1)}, u32[]{:S(2)}, u32[]{:S(2)}) %collective-permute-start.45) | collective-permute-done | bytes 524320 | tf_op jit(solution)/shard_map/ppermute | solution.py:18
  430.6 7.4 collective-permute-done.46
  442.0 5.8 collective-permute-done.47
  453.8 7.5 collective-permute-done.49
  471.7 3.0 multiply_convert_fusion.3
  500.0 3.9 multiply_convert_fusion.2
  515.7 3.3 add_convert_fusion.6
  533.3 14.4 %collective-permute-done.55 = bf16[1024,512]{1,0:T(8,128)(2,1)S(1)} collective-permute-done((bf16[1024,512]{1,0:T(8,128)(2,1)S(1)}, bf16[1024,512]{1,0:T(8,128)(2,1)S(1)}, u32[]{:S(2)}, u32[]{:S(2)}) %collective-permute-start.55) | collective-permute-done | bytes 1048608 | tf_op jit(solution)/shard_map/ppermute | solution.py:18
  554.0 9.6 %collective-permute-done.56 = bf16[256,1024]{1,0:T(8,128)(2,1)S(1)} collective-permute-done((bf16[256,1024]{1,0:T(8,128)(2,1)S(1)}, bf16[256,1024]{1,0:T(8,128)(2,1)S(1)}, u32[]{:S(2)}, u32[]{:S(2)}) %collective-permute-start.56) | collective-permute-done | bytes 524320 | tf_op jit(solution)/shard_map/ppermute | solution.py:18
  571.5 4.2 collective-permute-done.59
  579.1 13.9 %collective-permute-done.60 = bf16[512,512]{1,0:T(8,128)(2,1)S(1)} collective-permute-done((bf16[512,512]{1,0:T(8,128)(2,1)S(1)}, bf16[512,512]{1,0:T(8,128)(2,1)S(1)}, u32[]{:S(2)}, u32[]{:S(2)}) %collective-permute-start.60) | collective-permute-done | bytes 524320 | tf_op jit(solution)/shard_map/ppermute | solution.py:18
  595.2 9.6 %collective-permute-done.62 = bf16[128,2048]{1,0:T(8,128)(2,1)S(1)} collective-permute-done((bf16[128,2048]{1,0:T(8,128)(2,1)S(1)}, bf16[128,2048]{1,0:T(8,128)(2,1)S(1)}, u32[]{:S(2)}, u32[]{:S(2)}) %collective-permute-start.62) | collective-permute-done | bytes 524320 | tf_op jit(solution)/shard_map/ppermute | solution.py:18
  621.0 10.4 %collective-permute-done.64 = bf16[1024,512]{1,0:T(8,128)(2,1)} collective-permute-done((bf16[1024,512]{1,0:T(8,128)(2,1)}, bf16[1024,512]{1,0:T(8,128)(2,1)}, u32[]{:S(2)}, u32[]{:S(2)}) %collective-permute-start.64) | collective-permute-done | bytes 1048608 | tf_op jit(solution)/shard_map/ppermute | solution.py:18
  649.6 2.9 collective-permute-done.67
  665.5 4.3 collective-permute-done.68
  670.4 21.3 %collective-permute-done.90 = bf16[1024,512]{1,0:T(8,128)(2,1)S(1)} collective-permute-done((bf16[1024,512]{1,0:T(8,128)(2,1)S(1)}, bf16[1024,512]{1,0:T(8,128)(2,1)S(1)}, u32[]{:S(2)}, u32[]{:S(2)}) %collective-permute-start.90) | collective-permute-done | bytes 1048608 | tf_op jit(solution)/shard_map/ppermute | solution.py:18
  700.8 17.0 %collective-permute-done.94 = bf16[1024,512]{1,0:T(8,128)(2,1)S(1)} collective-permute-done((bf16[1024,512]{1,0:T(8,128)(2,1)S(1)}, bf16[1024,512]{1,0:T(8,128)(2,1)S(1)}, u32[]{:S(2)}, u32[]{:S(2)}) %collective-permute-start.94) | collective-permute-done | bytes 1048608 | tf_op jit(solution)/shard_map/ppermute | solution.py:18
  722.8 21.8 %collective-permute-done.91 = bf16[256,1024]{1,0:T(8,128)(2,1)S(1)} collective-permute-done((bf16[256,1024]{1,0:T(8,128)(2,1)S(1)}, bf16[256,1024]{1,0:T(8,128)(2,1)S(1)}, u32[]{:S(2)}, u32[]{:S(2)}) %collective-permute-start.91) | collective-permute-done | bytes 524320 | tf_op jit(solution)/shard_map/ppermute | solution.py:18
  746.4 2.9 collective-permute-start.96
  751.2 10.9 %collective-permute-done.101 = bf16[256,512]{1,0:T(8,128)(2,1)S(1)} collective-permute-done((bf16[256,512]{1,0:T(8,128)(2,1)S(1)}, bf16[256,512]{1,0:T(8,128)(2,1)S(1)}, u32[]{:S(2)}, u32[]{:S(2)}) %collective-permute-start.101) | collective-permute-done | bytes 262176 | tf_op jit(solution)/shard_map/ppermute | solution.py:18
  763.0 4.6 collective-permute-done.96
  773.6 3.7 collective-permute-done.78
  777.4 3.5 collective-permute-done.79
  786.6 17.3 %collective-permute-done.82 = bf16[256,1024]{1,0:T(8,128)(2,1)S(1)} collective-permute-done((bf16[256,1024]{1,0:T(8,128)(2,1)S(1)}, bf16[256,1024]{1,0:T(8,128)(2,1)S(1)}, u32[]{:S(2)}, u32[]{:S(2)}) %collective-permute-start.82) | collective-permute-done | bytes 524320 | tf_op jit(solution)/shard_map/ppermute | solution.py:18
  814.3 22.3 %collective-permute-done.87 = bf16[512,512]{1,0:T(8,128)(2,1)S(1)} collective-permute-done((bf16[512,512]{1,0:T(8,128)(2,1)S(1)}, bf16[512,512]{1,0:T(8,128)(2,1)S(1)}, u32[]{:S(2)}, u32[]{:S(2)}) %collective-permute-start.87) | collective-permute-done | bytes 524320 | tf_op jit(solution)/shard_map/ppermute | solution.py:18
  839.9 11.8 %collective-permute-done.89 = bf16[256,1024]{1,0:T(8,128)(2,1)S(1)} collective-permute-done((bf16[256,1024]{1,0:T(8,128)(2,1)S(1)}, bf16[256,1024]{1,0:T(8,128)(2,1)S(1)}, u32[]{:S(2)}, u32[]{:S(2)}) %collective-permute-start.89) | collective-permute-done | bytes 524320 | tf_op jit(solution)/shard_map/ppermute | solution.py:18
  852.5 9.5 %collective-permute-done.88 = bf16[512,512]{1,0:T(8,128)(2,1)S(1)} collective-permute-done((bf16[512,512]{1,0:T(8,128)(2,1)S(1)}, bf16[512,512]{1,0:T(8,128)(2,1)S(1)}, u32[]{:S(2)}, u32[]{:S(2)}) %collective-permute-start.88) | collective-permute-done | bytes 524320 | tf_op jit(solution)/shard_map/ppermute | solution.py:18
  863.2 13.0 %collective-permute-done.100 = bf16[256,512]{1,0:T(8,128)(2,1)S(1)} collective-permute-done((bf16[256,512]{1,0:T(8,128)(2,1)S(1)}, bf16[256,512]{1,0:T(8,128)(2,1)S(1)}, u32[]{:S(2)}, u32[]{:S(2)}) %collective-permute-start.100) | collective-permute-done | bytes 262176 | tf_op jit(solution)/shard_map/ppermute | solution.py:18
  (850 shorter events, 329.4 us)
Async XLA Ops:
  11.7 44.4 %collective-permute-start.8 = (bf16[128,2048]{1,0:T(8,128)(2,1)S(1)}, bf16[128,2048]{1,0:T(8,128)(2,1)}, u32[]{:S(2)}, u32[]{:S(2)}) collective-permute-start(bf16[128,2048]{1,0:T(8,128)(2,1)S(1)} %get-tuple-element.434), channel_id=1, source_target_pairs={{0,1},{1,0},{2,3},{3,2},{4,5},{5,4},{6,7},{7,6},{8,9},{9,8},{10,11... | collective-permute-start | bytes 1572872 | tf_op jit(solution)/shard_map/ppermute | solution.py:18
  21.8 35.5 %collective-permute-start.9 = (bf16[256,512]{1,0:T(8,128)(2,1)S(1)}, bf16[256,512]{1,0:T(8,128)(2,1)S(1)}, u32[]{:S(2)}, u32[]{:S(2)}) collective-permute-start(bf16[256,512]{1,0:T(8,128)(2,1)S(1)} %pad_maximum_fusion.55), channel_id=1, source_target_pairs={{0,16},{16,0},{1,17},{17,1},{2,18},{18,2},{3,19},{19,3},{4,20},{20... | collective-permute-start | bytes 786440 | tf_op jit(solution)/shard_map/ppermute | solution.py:18
  32.1 27.2 %collective-permute-start.10 = (bf16[256,1024]{1,0:T(8,128)(2,1)S(1)}, bf16[256,1024]{1,0:T(8,128)(2,1)S(1)}, u32[]{:S(2)}, u32[]{:S(2)}) collective-permute-start(bf16[256,1024]{1,0:T(8,128)(2,1)S(1)} %broadcast_select_fusion.18), channel_id=1, source_target_pairs={{0,8},{8,0},{1,9},{9,1},{2,10},{10,2},{3,11},{11,3},{4,12},{12,4},... | collective-permute-start | bytes 1572872 | tf_op jit(solution)/shard_map/ppermute | solution.py:18
  57.4 21.5 %collective-permute-start.13 = (bf16[256,512]{1,0:T(8,128)(2,1)S(1)}, bf16[256,512]{1,0:T(8,128)(2,1)S(1)}, u32[]{:S(2)}, u32[]{:S(2)}) collective-permute-start(bf16[256,512]{1,0:T(8,128)(2,1)S(1)} %pad_maximum_fusion.57), channel_id=1, source_target_pairs={{0,16},{16,0},{1,17},{17,1},{2,18},{18,2},{3,19},{19,3},{4,20},{20... | collective-permute-start | bytes 786440 | tf_op jit(solution)/shard_map/ppermute | solution.py:18
  59.3 19.3 %collective-permute-start.12 = (bf16[512,512]{1,0:T(8,128)(2,1)S(1)}, bf16[512,512]{1,0:T(8,128)(2,1)S(1)}, u32[]{:S(2)}, u32[]{:S(2)}) collective-permute-start(bf16[512,512]{1,0:T(8,128)(2,1)S(1)} %pad_maximum_fusion.38), channel_id=1, source_target_pairs={{0,8},{8,0},{1,9},{9,1},{2,10},{10,2},{3,11},{11,3},{4,12},{12,4},... | collective-permute-start | bytes 1572872 | tf_op jit(solution)/shard_map/ppermute | solution.py:18
  78.9 21.6 %collective-permute-start.14 = (bf16[512,512]{1,0:T(8,128)(2,1)S(1)}, bf16[512,512]{1,0:T(8,128)(2,1)S(1)}, u32[]{:S(2)}, u32[]{:S(2)}) collective-permute-start(bf16[512,512]{1,0:T(8,128)(2,1)S(1)} %pad_maximum_fusion.40), channel_id=1, source_target_pairs={{0,8},{8,0},{1,9},{9,1},{2,10},{10,2},{3,11},{11,3},{4,12},{12,4},... | collective-permute-start | bytes 1572872 | tf_op jit(solution)/shard_map/ppermute | solution.py:18
  79.6 24.4 %collective-permute-start.15 = (bf16[1024,512]{1,0:T(8,128)(2,1)S(1)}, bf16[1024,512]{1,0:T(8,128)(2,1)S(1)}, u32[]{:S(2)}, u32[]{:S(2)}) collective-permute-start(bf16[1024,512]{1,0:T(8,128)(2,1)S(1)} %pad_maximum_fusion.18), channel_id=1, source_target_pairs={{0,4},{4,0},{1,5},{5,1},{2,6},{6,2},{3,7},{7,3},{8,12},{12,8},{9,1... | collective-permute-start | bytes 3145736 | tf_op jit(solution)/shard_map/ppermute | solution.py:18
  82.6 25.1 %collective-permute-start.16 = (bf16[256,1024]{1,0:T(8,128)(2,1)S(1)}, bf16[256,1024]{1,0:T(8,128)(2,1)S(1)}, u32[]{:S(2)}, u32[]{:S(2)}) collective-permute-start(bf16[256,1024]{1,0:T(8,128)(2,1)S(1)} %pad_maximum_fusion.39), channel_id=1, source_target_pairs={{0,16},{16,0},{1,17},{17,1},{2,18},{18,2},{3,19},{19,3},{4,20},{20... | collective-permute-start | bytes 1572872 | tf_op jit(solution)/shard_map/ppermute | solution.py:18
  100.6 15.6 %collective-permute-start.17 = (bf16[256,1024]{1,0:T(8,128)(2,1)S(1)}, bf16[256,1024]{1,0:T(8,128)(2,1)S(1)}, u32[]{:S(2)}, u32[]{:S(2)}) collective-permute-start(bf16[256,1024]{1,0:T(8,128)(2,1)S(1)} %broadcast_select_fusion.17), channel_id=1, source_target_pairs={{0,8},{8,0},{1,9},{9,1},{2,10},{10,2},{3,11},{11,3},{4,12},{12,4},... | collective-permute-start | bytes 1572872 | tf_op jit(solution)/shard_map/ppermute | solution.py:18
  116.3 28.9 %collective-permute-start.19 = (bf16[512,1024]{1,0:T(8,128)(2,1)S(1)}, bf16[512,1024]{1,0:T(8,128)(2,1)S(1)}, u32[]{:S(2)}, u32[]{:S(2)}) collective-permute-start(bf16[512,1024]{1,0:T(8,128)(2,1)S(1)} %pad_maximum_fusion.20), channel_id=1, source_target_pairs={{0,8},{8,0},{1,9},{9,1},{2,10},{10,2},{3,11},{11,3},{4,12},{12,4},... | collective-permute-start | bytes 3145736 | tf_op jit(solution)/shard_map/ppermute | solution.py:18
  116.4 28.9 %collective-permute-start.20 = (bf16[1024,512]{1,0:T(8,128)(2,1)S(1)}, bf16[1024,512]{1,0:T(8,128)(2,1)S(1)}, u32[]{:S(2)}, u32[]{:S(2)}) collective-permute-start(bf16[1024,512]{1,0:T(8,128)(2,1)S(1)} %pad_maximum_fusion.19), channel_id=1, source_target_pairs={{0,4},{4,0},{1,5},{5,1},{2,6},{6,2},{3,7},{7,3},{8,12},{12,8},{9,1... | collective-permute-start | bytes 3145736 | tf_op jit(solution)/shard_map/ppermute | solution.py:18
  118.6 24.4 %collective-permute-start.18 = (bf16[256,512]{1,0:T(8,128)(2,1)S(1)}, bf16[256,512]{1,0:T(8,128)(2,1)S(1)}, u32[]{:S(2)}, u32[]{:S(2)}) collective-permute-start(bf16[256,512]{1,0:T(8,128)(2,1)S(1)} %pad_maximum_fusion.58), channel_id=1, source_target_pairs={{0,16},{16,0},{1,17},{17,1},{2,18},{18,2},{3,19},{19,3},{4,20},{20... | collective-permute-start | bytes 786440 | tf_op jit(solution)/shard_map/ppermute | solution.py:18
  148.8 65.0 %collective-permute-start.27 = (bf16[512,1024]{1,0:T(8,128)(2,1)}, bf16[512,1024]{1,0:T(8,128)(2,1)}, u32[]{:S(2)}, u32[]{:S(2)}) collective-permute-start(bf16[512,1024]{1,0:T(8,128)(2,1)} %pad_maximum_fusion.21), channel_id=1, source_target_pairs={{0,16},{16,0},{1,17},{17,1},{2,18},{18,2},{3,19},{19,3},{4,20},{20... | collective-permute-start | bytes 3145736 | tf_op jit(solution)/shard_map/ppermute | solution.py:18
  150.9 34.5 %collective-permute-start.23 = (bf16[512,512]{1,0:T(8,128)(2,1)}, bf16[512,512]{1,0:T(8,128)(2,1)}, u32[]{:S(2)}, u32[]{:S(2)}) collective-permute-start(bf16[512,512]{1,0:T(8,128)(2,1)} %pad_maximum_fusion.41), channel_id=1, source_target_pairs={{0,8},{8,0},{1,9},{9,1},{2,10},{10,2},{3,11},{11,3},{4,12},{12,4},... | collective-permute-start | bytes 1572872 | tf_op jit(solution)/shard_map/ppermute | solution.py:18
  189.1 24.7 %collective-permute-start.26 = (bf16[1024,512]{1,0:T(8,128)(2,1)}, bf16[1024,512]{1,0:T(8,128)(2,1)S(1)}, u32[]{:S(2)}, u32[]{:S(2)}) collective-permute-start(bf16[1024,512]{1,0:T(8,128)(2,1)} %pad_maximum_fusion.22), channel_id=1, source_target_pairs={{0,4},{4,0},{1,5},{5,1},{2,6},{6,2},{3,7},{7,3},{8,12},{12,8},{9,1... | collective-permute-start | bytes 3145736 | tf_op jit(solution)/shard_map/ppermute | solution.py:18
  238.1 46.3 %collective-permute-start.36 = (bf16[1024,1024]{1,0:T(8,128)(2,1)S(1)}, bf16[1024,1024]{1,0:T(8,128)(2,1)S(1)}, u32[]{:S(2)}, u32[]{:S(2)}) collective-permute-start(bf16[1024,1024]{1,0:T(8,128)(2,1)S(1)} %pad_maximum_fusion.2), channel_id=1, source_target_pairs={{0,4},{4,0},{1,5},{5,1},{2,6},{6,2},{3,7},{7,3},{8,12},{12,8},{9,1... | collective-permute-start | bytes 6291464 | tf_op jit(solution)/shard_map/ppermute | solution.py:18
  258.6 47.9 %collective-permute-start.37 = (bf16[512,1024]{1,0:T(8,128)(2,1)S(1)}, bf16[512,1024]{1,0:T(8,128)(2,1)S(1)}, u32[]{:S(2)}, u32[]{:S(2)}) collective-permute-start(bf16[512,1024]{1,0:T(8,128)(2,1)S(1)} %copy-done.77), channel_id=1, source_target_pairs={{0,16},{16,0},{1,17},{17,1},{2,18},{18,2},{3,19},{19,3},{4,20},{20... | collective-permute-start | bytes 3145736 | tf_op jit(solution)/shard_map/ppermute | solution.py:18
  306.7 50.7 %collective-permute-start.39 = (bf16[1024,1024]{1,0:T(8,128)(2,1)S(1)}, bf16[1024,1024]{1,0:T(8,128)(2,1)S(1)}, u32[]{:S(2)}, u32[]{:S(2)}) collective-permute-start(bf16[1024,1024]{1,0:T(8,128)(2,1)S(1)} %pad_maximum_fusion.3), channel_id=1, source_target_pairs={{0,4},{4,0},{1,5},{5,1},{2,6},{6,2},{3,7},{7,3},{8,12},{12,8},{9,1... | collective-permute-start | bytes 6291464 | tf_op jit(solution)/shard_map/ppermute | solution.py:18
  309.2 48.0 %collective-permute-start.38 = (bf16[512,1024]{1,0:T(8,128)(2,1)S(1)}, bf16[512,1024]{1,0:T(8,128)(2,1)S(1)}, u32[]{:S(2)}, u32[]{:S(2)}) collective-permute-start(bf16[512,1024]{1,0:T(8,128)(2,1)S(1)} %pad_maximum_fusion.27), channel_id=1, source_target_pairs={{0,16},{16,0},{1,17},{17,1},{2,18},{18,2},{3,19},{19,3},{4,20},{20... | collective-permute-start | bytes 3145736 | tf_op jit(solution)/shard_map/ppermute | solution.py:18
  362.8 48.0 %collective-permute-start.43 = (bf16[1024,1024]{1,0:T(8,128)(2,1)S(1)}, bf16[1024,1024]{1,0:T(8,128)(2,1)S(1)}, u32[]{:S(2)}, u32[]{:S(2)}) collective-permute-start(bf16[1024,1024]{1,0:T(8,128)(2,1)S(1)} %pad_maximum_fusion.4), channel_id=1, source_target_pairs={{0,4},{4,0},{1,5},{5,1},{2,6},{6,2},{3,7},{7,3},{8,12},{12,8},{9,1... | collective-permute-start | bytes 6291464 | tf_op jit(solution)/shard_map/ppermute | solution.py:18
  522.5 25.1 %collective-permute-start.55 = (bf16[1024,512]{1,0:T(8,128)(2,1)S(1)}, bf16[1024,512]{1,0:T(8,128)(2,1)S(1)}, u32[]{:S(2)}, u32[]{:S(2)}) collective-permute-start(bf16[1024,512]{1,0:T(8,128)(2,1)S(1)} %add_convert_fusion.7), channel_id=1, source_target_pairs={{0,4},{4,0},{1,5},{5,1},{2,6},{6,2},{3,7},{7,3},{8,12},{12,8},{9,1... | collective-permute-start | bytes 3145736 | tf_op jit(solution)/shard_map/ppermute | solution.py:18
  569.4 23.5 %collective-permute-start.60 = (bf16[512,512]{1,0:T(8,128)(2,1)S(1)}, bf16[512,512]{1,0:T(8,128)(2,1)S(1)}, u32[]{:S(2)}, u32[]{:S(2)}) collective-permute-start(bf16[512,512]{1,0:T(8,128)(2,1)S(1)} %slice.2227), channel_id=1, source_target_pairs={{0,16},{16,0},{1,17},{17,1},{2,18},{18,2},{3,19},{19,3},{4,20},{20... | collective-permute-start | bytes 1572872 | tf_op jit(solution)/shard_map/ppermute | solution.py:18
  570.6 23.1 %collective-permute-start.61 = (bf16[1024,512]{1,0:T(8,128)(2,1)S(1)}, bf16[1024,512]{1,0:T(8,128)(2,1)S(1)}, u32[]{:S(2)}, u32[]{:S(2)}) collective-permute-start(bf16[1024,512]{1,0:T(8,128)(2,1)S(1)} %add_convert_fusion.4), channel_id=1, source_target_pairs={{0,4},{4,0},{1,5},{5,1},{2,6},{6,2},{3,7},{7,3},{8,12},{12,8},{9,1... | collective-permute-start | bytes 3145736 | tf_op jit(solution)/shard_map/ppermute | solution.py:18
  605.5 25.9 %collective-permute-start.64 = (bf16[1024,512]{1,0:T(8,128)(2,1)}, bf16[1024,512]{1,0:T(8,128)(2,1)}, u32[]{:S(2)}, u32[]{:S(2)}) collective-permute-start(bf16[1024,512]{1,0:T(8,128)(2,1)} %add_convert_fusion.3), channel_id=1, source_target_pairs={{0,4},{4,0},{1,5},{5,1},{2,6},{6,2},{3,7},{7,3},{8,12},{12,8},{9,1... | collective-permute-start | bytes 3145736 | tf_op jit(solution)/shard_map/ppermute | solution.py:18
  606.6 29.6 %collective-permute-start.65 = (bf16[512,512]{1,0:T(8,128)(2,1)}, bf16[512,512]{1,0:T(8,128)(2,1)}, u32[]{:S(2)}, u32[]{:S(2)}) collective-permute-start(bf16[512,512]{1,0:T(8,128)(2,1)} %slice.2226), channel_id=1, source_target_pairs={{0,16},{16,0},{1,17},{17,1},{2,18},{18,2},{3,19},{19,3},{4,20},{20... | collective-permute-start | bytes 1572872 | tf_op jit(solution)/shard_map/ppermute | solution.py:18
  643.7 26.1 %collective-permute-start.68 = (bf16[1024,512]{1,0:T(8,128)(2,1)S(1)}, bf16[1024,512]{1,0:T(8,128)(2,1)S(1)}, u32[]{:S(2)}, u32[]{:S(2)}) collective-permute-start(bf16[1024,512]{1,0:T(8,128)(2,1)S(1)} %copy-done.84), channel_id=1, source_target_pairs={{0,4},{4,0},{1,5},{5,1},{2,6},{6,2},{3,7},{7,3},{8,12},{12,8},{9,1... | collective-permute-start | bytes 3145736 | tf_op jit(solution)/shard_map/ppermute | solution.py:18
  644.8 48.9 %collective-permute-start.69 = (bf16[512,512]{1,0:T(8,128)(2,1)S(1)}, bf16[512,512]{1,0:T(8,128)(2,1)S(1)}, u32[]{:S(2)}, u32[]{:S(2)}) collective-permute-start(bf16[512,512]{1,0:T(8,128)(2,1)S(1)} %slice.2225), channel_id=1, source_target_pairs={{0,16},{16,0},{1,17},{17,1},{2,18},{18,2},{3,19},{19,3},{4,20},{20... | collective-permute-start | bytes 1572872 | tf_op jit(solution)/shard_map/ppermute | solution.py:18
  644.8 52.2 %collective-permute-start.71 = (bf16[256,1024]{1,0:T(8,128)(2,1)S(1)}, bf16[256,1024]{1,0:T(8,128)(2,1)S(1)}, u32[]{:S(2)}, u32[]{:S(2)}) collective-permute-start(bf16[256,1024]{1,0:T(8,128)(2,1)S(1)} %select_convert_fusion.6), channel_id=1, source_target_pairs={{0,8},{8,0},{1,9},{9,1},{2,10},{10,2},{3,11},{11,3},{4,12},{12,4},... | collective-permute-start | bytes 1572872 | tf_op jit(solution)/shard_map/ppermute | solution.py:18
  647.4 44.3 %collective-permute-start.90 = (bf16[1024,512]{1,0:T(8,128)(2,1)S(1)}, bf16[1024,512]{1,0:T(8,128)(2,1)S(1)}, u32[]{:S(2)}, u32[]{:S(2)}) collective-permute-start(bf16[1024,512]{1,0:T(8,128)(2,1)S(1)} %convolution_convert_fusion.3), channel_id=1, source_target_pairs={{0,4},{4,0},{1,5},{5,1},{2,6},{6,2},{3,7},{7,3},{8,12},{12,8},{9,1... | collective-permute-start | bytes 3145736 | tf_op jit(solution)/shard_map/ppermute | solution.py:18
  664.4 30.0 %collective-permute-start.70 = (bf16[256,2048]{1,0:T(8,128)(2,1)S(1)}, bf16[256,2048]{1,0:T(8,128)(2,1)S(1)}, u32[]{:S(2)}, u32[]{:S(2)}) collective-permute-start(bf16[256,2048]{1,0:T(8,128)(2,1)S(1)} %pad_maximum_fusion.33), channel_id=1, source_target_pairs={{0,2},{2,0},{1,3},{3,1},{4,6},{6,4},{5,7},{7,5},{8,10},{10,8},{9,1... | collective-permute-start | bytes 3145736 | tf_op jit(solution)/shard_map/ppermute | solution.py:18
  669.8 29.7 %collective-permute-start.72 = (bf16[1024,512]{1,0:T(8,128)(2,1)S(1)}, bf16[1024,512]{1,0:T(8,128)(2,1)S(1)}, u32[]{:S(2)}, u32[]{:S(2)}) collective-permute-start(bf16[1024,512]{1,0:T(8,128)(2,1)S(1)} %pad_maximum_fusion.32), channel_id=1, source_target_pairs={{0,8},{8,0},{1,9},{9,1},{2,10},{10,2},{3,11},{11,3},{4,12},{12,4},... | collective-permute-start | bytes 3145736 | tf_op jit(solution)/shard_map/ppermute | solution.py:18
  691.7 26.0 %collective-permute-start.94 = (bf16[1024,512]{1,0:T(8,128)(2,1)S(1)}, bf16[1024,512]{1,0:T(8,128)(2,1)S(1)}, u32[]{:S(2)}, u32[]{:S(2)}) collective-permute-start(bf16[1024,512]{1,0:T(8,128)(2,1)S(1)} %convolution_convert_fusion.2), channel_id=1, source_target_pairs={{0,4},{4,0},{1,5},{5,1},{2,6},{6,2},{3,7},{7,3},{8,12},{12,8},{9,1... | collective-permute-start | bytes 3145736 | tf_op jit(solution)/shard_map/ppermute | solution.py:18
  693.9 25.0 %collective-permute-start.99 = (bf16[512,512]{1,0:T(8,128)(2,1)S(1)}, bf16[512,512]{1,0:T(8,128)(2,1)S(1)}, u32[]{:S(2)}, u32[]{:S(2)}) collective-permute-start(bf16[512,512]{1,0:T(8,128)(2,1)S(1)} %pad_maximum_fusion.51), channel_id=1, source_target_pairs={{0,8},{8,0},{1,9},{9,1},{2,10},{10,2},{3,11},{11,3},{4,12},{12,4},... | collective-permute-start | bytes 1572872 | tf_op jit(solution)/shard_map/ppermute | solution.py:18
  695.5 72.4 %collective-permute-start.75 = (bf16[1024,512]{1,0:T(8,128)(2,1)S(1)}, bf16[1024,512]{1,0:T(8,128)(2,1)S(1)}, u32[]{:S(2)}, u32[]{:S(2)}) collective-permute-start(bf16[1024,512]{1,0:T(8,128)(2,1)S(1)} %copy-done.83), channel_id=1, source_target_pairs={{0,4},{4,0},{1,5},{5,1},{2,6},{6,2},{3,7},{7,3},{8,12},{12,8},{9,1... | collective-permute-start | bytes 3145736 | tf_op jit(solution)/shard_map/ppermute | solution.py:18
  696.9 70.9 %collective-permute-start.76 = (bf16[512,512]{1,0:T(8,128)(2,1)S(1)}, bf16[512,512]{1,0:T(8,128)(2,1)S(1)}, u32[]{:S(2)}, u32[]{:S(2)}) collective-permute-start(bf16[512,512]{1,0:T(8,128)(2,1)S(1)} %slice.2224), channel_id=1, source_target_pairs={{0,16},{16,0},{1,17},{17,1},{2,18},{18,2},{3,19},{19,3},{4,20},{20... | collective-permute-start | bytes 1572872 | tf_op jit(solution)/shard_map/ppermute | solution.py:18
  699.5 21.7 %collective-permute-start.73 = (bf16[128,2048]{1,0:T(8,128)(2,1)S(1)}, bf16[128,2048]{1,0:T(8,128)(2,1)S(1)}, u32[]{:S(2)}, u32[]{:S(2)}) collective-permute-start(bf16[128,2048]{1,0:T(8,128)(2,1)S(1)} %select_convert_fusion.5), channel_id=1, source_target_pairs={{0,1},{1,0},{2,3},{3,2},{4,5},{5,4},{6,7},{7,6},{8,9},{9,8},{10,11... | collective-permute-start | bytes 1572872 | tf_op jit(solution)/shard_map/ppermute | solution.py:18
  717.8 26.8 %collective-permute-start.91 = (bf16[256,1024]{1,0:T(8,128)(2,1)S(1)}, bf16[256,1024]{1,0:T(8,128)(2,1)S(1)}, u32[]{:S(2)}, u32[]{:S(2)}) collective-permute-start(bf16[256,1024]{1,0:T(8,128)(2,1)S(1)} %fusion.23), channel_id=1, source_target_pairs={{0,16},{16,0},{1,17},{17,1},{2,18},{18,2},{3,19},{19,3},{4,20},{20... | collective-permute-start | bytes 1572872 | tf_op jit(solution)/shard_map/ppermute | solution.py:18
  718.9 26.5 %collective-permute-start.95 = (bf16[512,512]{1,0:T(8,128)(2,1)S(1)}, bf16[512,512]{1,0:T(8,128)(2,1)S(1)}, u32[]{:S(2)}, u32[]{:S(2)}) collective-permute-start(bf16[512,512]{1,0:T(8,128)(2,1)S(1)} %pad_maximum_fusion.49), channel_id=1, source_target_pairs={{0,8},{8,0},{1,9},{9,1},{2,10},{10,2},{3,11},{11,3},{4,12},{12,4},... | collective-permute-start | bytes 1572872 | tf_op jit(solution)/shard_map/ppermute | solution.py:18
  721.3 25.2 %collective-permute-start.74 = (bf16[128,2048]{1,0:T(8,128)(2,1)S(1)}, bf16[128,2048]{1,0:T(8,128)(2,1)S(1)}, u32[]{:S(2)}, u32[]{:S(2)}) collective-permute-start(bf16[128,2048]{1,0:T(8,128)(2,1)S(1)} %select_convert_fusion.4), channel_id=1, source_target_pairs={{0,2},{2,0},{1,3},{3,1},{4,6},{6,4},{5,7},{7,5},{8,10},{10,8},{9,1... | collective-permute-start | bytes 1572872 | tf_op jit(solution)/shard_map/ppermute | solution.py:18
  744.6 17.5 %collective-permute-start.101 = (bf16[256,512]{1,0:T(8,128)(2,1)S(1)}, bf16[256,512]{1,0:T(8,128)(2,1)S(1)}, u32[]{:S(2)}, u32[]{:S(2)}) collective-permute-start(bf16[256,512]{1,0:T(8,128)(2,1)S(1)} %slice.2231), channel_id=1, source_target_pairs={{0,16},{16,0},{1,17},{17,1},{2,18},{18,2},{3,19},{19,3},{4,20},{20... | collective-permute-start | bytes 786440 | tf_op jit(solution)/shard_map/ppermute | solution.py:18
  745.4 16.9 %collective-permute-start.92 = (bf16[256,512]{1,0:T(8,128)(2,1)S(1)}, bf16[256,512]{1,0:T(8,128)(2,1)S(1)}, u32[]{:S(2)}, u32[]{:S(2)}) collective-permute-start(bf16[256,512]{1,0:T(8,128)(2,1)S(1)} %slice.2233), channel_id=1, source_target_pairs={{0,4},{4,0},{1,5},{5,1},{2,6},{6,2},{3,7},{7,3},{8,12},{12,8},{9,1... | collective-permute-start | bytes 786440 | tf_op jit(solution)/shard_map/ppermute | solution.py:18
  746.4 21.2 %collective-permute-start.96 = (bf16[256,512]{1,0:T(8,128)(2,1)S(1)}, bf16[256,512]{1,0:T(8,128)(2,1)S(1)}, u32[]{:S(2)}, u32[]{:S(2)}) collective-permute-start(bf16[256,512]{1,0:T(8,128)(2,1)S(1)} %slice.2232), channel_id=1, source_target_pairs={{0,16},{16,0},{1,17},{17,1},{2,18},{18,2},{3,19},{19,3},{4,20},{20... | collective-permute-start | bytes 786440 | tf_op jit(solution)/shard_map/ppermute | solution.py:18
  781.1 22.8 %collective-permute-start.82 = (bf16[256,1024]{1,0:T(8,128)(2,1)S(1)}, bf16[256,1024]{1,0:T(8,128)(2,1)S(1)}, u32[]{:S(2)}, u32[]{:S(2)}) collective-permute-start(bf16[256,1024]{1,0:T(8,128)(2,1)S(1)} %select_convert_fusion.3), channel_id=1, source_target_pairs={{0,8},{8,0},{1,9},{9,1},{2,10},{10,2},{3,11},{11,3},{4,12},{12,4},... | collective-permute-start | bytes 1572872 | tf_op jit(solution)/shard_map/ppermute | solution.py:18
  783.7 25.0 %collective-permute-start.84 = (bf16[1024,512]{1,0:T(8,128)(2,1)S(1)}, bf16[1024,512]{1,0:T(8,128)(2,1)S(1)}, u32[]{:S(2)}, u32[]{:S(2)}) collective-permute-start(bf16[1024,512]{1,0:T(8,128)(2,1)S(1)} %copy-done.82), channel_id=1, source_target_pairs={{0,4},{4,0},{1,5},{5,1},{2,6},{6,2},{3,7},{7,3},{8,12},{12,8},{9,1... | collective-permute-start | bytes 3145736 | tf_op jit(solution)/shard_map/ppermute | solution.py:18
  784.6 25.6 %collective-permute-start.85 = (bf16[512,512]{1,0:T(8,128)(2,1)S(1)}, bf16[512,512]{1,0:T(8,128)(2,1)S(1)}, u32[]{:S(2)}, u32[]{:S(2)}) collective-permute-start(bf16[512,512]{1,0:T(8,128)(2,1)S(1)} %slice.2223), channel_id=1, source_target_pairs={{0,16},{16,0},{1,17},{17,1},{2,18},{18,2},{3,19},{19,3},{4,20},{20... | collective-permute-start | bytes 1572872 | tf_op jit(solution)/shard_map/ppermute | solution.py:18
  810.9 26.1 %collective-permute-start.86 = (bf16[1024,512]{1,0:T(8,128)(2,1)S(1)}, bf16[1024,512]{1,0:T(8,128)(2,1)S(1)}, u32[]{:S(2)}, u32[]{:S(2)}) collective-permute-start(bf16[1024,512]{1,0:T(8,128)(2,1)S(1)} %convolution_convert_fusion.4), channel_id=1, source_target_pairs={{0,4},{4,0},{1,5},{5,1},{2,6},{6,2},{3,7},{7,3},{8,12},{12,8},{9,1... | collective-permute-start | bytes 3145736 | tf_op jit(solution)/shard_map/ppermute | solution.py:18
  812.4 24.2 %collective-permute-start.87 = (bf16[512,512]{1,0:T(8,128)(2,1)S(1)}, bf16[512,512]{1,0:T(8,128)(2,1)S(1)}, u32[]{:S(2)}, u32[]{:S(2)}) collective-permute-start(bf16[512,512]{1,0:T(8,128)(2,1)S(1)} %slice.2222), channel_id=1, source_target_pairs={{0,16},{16,0},{1,17},{17,1},{2,18},{18,2},{3,19},{19,3},{4,20},{20... | collective-permute-start | bytes 1572872 | tf_op jit(solution)/shard_map/ppermute | solution.py:18
  837.9 24.1 %collective-permute-start.88 = (bf16[512,512]{1,0:T(8,128)(2,1)S(1)}, bf16[512,512]{1,0:T(8,128)(2,1)S(1)}, u32[]{:S(2)}, u32[]{:S(2)}) collective-permute-start(bf16[512,512]{1,0:T(8,128)(2,1)S(1)} %pad_maximum_fusion.53), channel_id=1, source_target_pairs={{0,8},{8,0},{1,9},{9,1},{2,10},{10,2},{3,11},{11,3},{4,12},{12,4},... | collective-permute-start | bytes 1572872 | tf_op jit(solution)/shard_map/ppermute | solution.py:18
  (219 other events, 3106.6 us)

commit v3 on v1

v3 whole, which is shorter than its diff:
```python
import math

import jax
import jax.numpy as jnp
from jax import lax
from jax.sharding import Mesh, PartitionSpec as P

HD = 128

EPSILON = 1e-06
NEGATIVE = -1e30
FLIP = [(0, 1), (1, 0)]
BF = jnp.bfloat16
F32 = jnp.float32


def swap(value, axis):
    return lax.ppermute(value, axis, FLIP)


def bit(axis):
    return lax.axis_index(axis)


def pick(axis, low, high):
    return jnp.where(bit(axis) == 0, low, high)


def ordered(axis, own, other, dim=0):
    return jnp.concatenate([pick(axis, own, other), pick(axis, other, own)], axis=dim)


def split(value, axis, dim):
    half = value.shape[dim] // 2
    low = lax.slice_in_dim(value, 0, half, axis=dim)
    high = lax.slice_in_dim(value, half, 2 * half, axis=dim)
    return pick(axis, low, high), pick(axis, high, low)


def dot(a, b):
    return jnp.dot(a, b, preferred_element_type=F32)


def dot_nt(a, b):
    return jnp.einsum("sc,rc->sr", a, b, preferred_element_type=F32)


def dot_tn(a, b):
    return jnp.einsum("sr,sc->rc", a, b, preferred_element_type=F32)


def rms_scale(values):
    return lax.rsqrt(jnp.mean(values * values, axis=1, keepdims=True) + EPSILON)


def build(high_bits):
    def to_relative(value):
        rows, width = value.shape
        count = 2 ** (len(high_bits) + 2)
        run = width // count
        pieces = [value[:, i * run : (i + 1) * run] for i in range(count)]
        names = list(high_bits) + ["zl", "x"]
        for position, name in enumerate(names):
            if name == "zl":
                continue
            mask = 1 << (len(names) - 1 - position)
            pieces = [pick(name, pieces[i], pieces[i ^ mask]) for i in range(count)]
        order = []
        for xr in range(2):
            for rest in range(count // 2):
                order.append(rest * 2 + xr)
        return jnp.concatenate([pieces[i] for i in order], axis=1)

    def to_natural(value):
        rows, width = value.shape
        count = 2 ** (len(high_bits) + 2)
        run = width // count
        moved = [value[:, i * run : (i + 1) * run] for i in range(count)]
        pieces = [None] * count
        place = 0
        for xr in range(2):
            for rest in range(count // 2):
                pieces[rest * 2 + xr] = moved[place]
                place += 1
        names = list(high_bits) + ["zl", "x"]
        for position, name in enumerate(names):
            if name == "zl":
                continue
            mask = 1 << (len(names) - 1 - position)
            pieces = [pick(name, pieces[i], pieces[i ^ mask]) for i in range(count)]
        return jnp.concatenate(pieces, axis=1)

    class Chain:
        def __init__(self, token):
            self.token = token

        def sync(self, *values):
            out = lax.optimization_barrier((self.token,) + values)
            self.token = out[0]
            return out[1] if len(values) == 1 else out[1:]

        def start(self, value, axis):
            return swap(self.sync(value), axis)

        def start_high(self, rows):
            for name in high_bits[:0:-1]:
                rows = jnp.concatenate([rows, self.sync(self.start(rows, name))], axis=0)
            return rows, (self.start(rows, high_bits[0]) if high_bits else None)

        def end_high(self, pending):
            rows, sent = pending
            return rows if sent is None else jnp.concatenate([rows, self.sync(sent)], axis=0)

        def start_high_sum(self, total):
            for name in high_bits[:-1]:
                half = total.shape[0] // 2
                total = total[:half] + self.sync(self.start(total[half:].astype(BF), name)).astype(F32)
            if not high_bits:
                return total, None
            half = total.shape[0] // 2
            return total[:half], self.start(total[half:].astype(BF), high_bits[-1])

        def end_high_sum(self, pending):
            total, sent = pending
            return total if sent is None else total + self.sync(sent).astype(F32)

    def gather_gains(c, gains):
        gains = ordered("tensor", gains, c.sync(c.start(gains, "tensor")), dim=1)
        gains = ordered("core", gains, c.sync(c.start(gains, "core")), dim=1)
        gains = ordered("zl", gains, c.sync(c.start(gains, "zl")), dim=1)
        for name in list(high_bits)[::-1] + ["x"]:
            gains = jnp.concatenate([gains, c.sync(c.start(gains, name))], axis=1)
        return gains

    def pair_sum(c, values):
        count, width = values.shape
        for level, axis in enumerate(("core", "zl", "tensor")):
            run = width >> (level + 1)
            other = c.sync(c.start(values, axis))
            blocks = [other[:, i * run : (i + 1) * run] for i in range(width // run)]
            values = values + jnp.concatenate([blocks[i ^ 1] for i in range(len(blocks))], axis=1)
        return values

    def scatter_gains(c, gains):
        for name in ["x"] + list(high_bits):
            half = gains.shape[1] // 2
            gains = gains[:, :half] + c.sync(c.start(gains[:, half:], name))
        for name in ("zl", "core", "tensor"):
            own, sent = split(gains, name, 1)
            gains = own + c.sync(c.start(sent, name))
        return gains

    def stack2(low, high):
        return jnp.concatenate([low, high], axis=0)

    def shards(
        tokens,
        segment_ids,
        w_query,
        w_key,
        w_value,
        w_output,
        w_gate,
        w_up,
        w_down,
        query_gain,
        key_gain,
        attn_gain,
        ffn_gain,
        cotangent,
    ):
        own_tokens, model_width = tokens.shape
        half_width = model_width // 2
        seq_length = own_tokens * 2
        core_tokens = seq_length * 2
        group_tokens = core_tokens * 2
        head_width = w_query.shape[1] // 4
        part = w_gate.shape[1] // 8
        local_heads = head_width // HD
        score_scale = 1.0 / math.sqrt(HD)
        c = Chain(query_gain)

        def columns(parts):
            return jnp.concatenate(parts, axis=1)

        attn_split = [split(w, "core", 1) for w in (w_query, w_key, w_value, w_output)]
        attn_sent = c.start(columns([s[1] for s in attn_split]), "core")
        tokens_rel = to_relative(tokens)
        left, right = tokens_rel[:, :half_width], tokens_rel[:, half_width:]
        left_sent = c.start(left, "tensor")
        ffn_split = [split(w, "core", 1) for w in (w_gate, w_up, w_down)]
        ffn_sent = c.start(columns([s[1] for s in ffn_split]), "core")

        attn_sent = c.sync(attn_sent)
        attn_pairs = [
            split(
                ordered("core", s[0], attn_sent[:, i * 2 * head_width : (i + 1) * 2 * head_width]),
                "zl",
                1,
            )
            for i, s in enumerate(attn_split)
        ]
        qk_line = c.start(columns([p[1] for p in attn_pairs[:2]]), "zl")
        right_sent = c.start(right, "zl")

        def line_rows(pairs, sent):
            own = columns([p[0] for p in pairs])
            return ordered("zl", own, sent)

        class WeightStream:
            def __init__(self):
                self.waiting, self.high, self.x, self.rows = [], [], [], []

            def add(self, *chunks):
                self.waiting.extend(chunks)

            def feed(self):
                self.high.append(c.start_high(self.waiting[len(self.high)]))

            def step(self):
                k = len(self.rows)
                rows = c.end_high(self.high[k])
                if len(self.high) < len(self.waiting):
                    self.feed()
                self.rows.append(rows)
                if k > 0:
                    self.x[k - 1] = c.sync(self.x[k - 1])
                self.x.append(c.start(rows, "x"))

            def end(self):
                self.x[-1] = c.sync(self.x[-1])

        stream = WeightStream()
        qk_rows = line_rows(attn_pairs[:2], c.sync(qk_line))
        stream.add(qk_rows)
        stream.feed()
        vo_line = c.start(columns([p[1] for p in attn_pairs[2:]]), "zl")
        ffn_sent = c.sync(ffn_sent)
        g_pair, u_pair, d_pair = [
            split(
                ordered("core", s[0], ffn_sent[:, i * 4 * part : (i + 1) * 4 * part]),
                "zl",
                1,
            )
            for i, s in enumerate(ffn_split)
        ]
        g_line = c.start(g_pair[1], "zl")
        left = stack2(left, c.sync(left_sent))
        right = stack2(right, c.sync(right_sent))

        def rows_second(left, right):
            left_sent = c.start(left, "zl")
            right_sent = c.start(right, "tensor")
            left = stack2(left, c.sync(left_sent))
            right_sent = c.sync(right_sent)
            rows = own_tokens
            right = jnp.concatenate(
                [right[:rows], right_sent[:rows], right[rows:], right_sent[rows:]], axis=0
            )
            left_sent = c.start(left, "core")
            right_sent = c.start(right, "core")
            return stack2(left, c.sync(left_sent)), stack2(right, c.sync(right_sent))

        def gather_rows(value):
            left, right = value[:, :half_width], value[:, half_width:]
            left_sent = c.start(left, "tensor")
            right_sent = c.start(right, "zl")
            left = stack2(left, c.sync(left_sent))
            right = stack2(right, c.sync(right_sent))
            return rows_second(left, right)

        vo_rows = line_rows(attn_pairs[2:], c.sync(vo_line))
        stream.add(vo_rows)
        stream.feed()
        in0, in1 = rows_second(left, right)
        g_rows = line_rows([g_pair], c.sync(g_line))
        stream.add(g_rows[:, :part], g_rows[:, part:])
        u_line = c.start(u_pair[1], "zl")
        ids = jnp.concatenate(
            [
                pick("tensor", segment_ids[:, :own_tokens], segment_ids[:, own_tokens:]),
                pick("tensor", segment_ids[:, own_tokens:], segment_ids[:, :own_tokens]),
            ],
            axis=1,
        )
        gains = jnp.stack([query_gain, key_gain, attn_gain, ffn_gain])
        gains = gather_gains(c, gains)
        stream.step()
        seq_ids = stack2(ids, c.sync(c.start(ids, "zl")))
        seq_ids = stack2(seq_ids, c.sync(c.start(seq_ids, "core")))
        u_rows = line_rows([u_pair], c.sync(u_line))
        stream.add(u_rows[:, :part], u_rows[:, part:])
        d_line = c.start(d_pair[1], "zl")

        attn_scale = gains[2]
        ffn_scale = gains[3]
        head_gains = to_natural(gains[:2])
        head_start = (bit("tensor") * 4 + bit("core") * 2 + bit("zl")) * head_width
        head_gains = lax.dynamic_slice_in_dim(head_gains, head_start, head_width, axis=1)
        query_scale, key_scale = head_gains[0], head_gains[1]
        tokens_f = tokens_rel.astype(F32)
        d_out = to_relative(cotangent).astype(F32)
        places = jnp.arange(own_tokens)
        positions = jnp.concatenate(
            [places + bit("tensor") * own_tokens, places + (1 - bit("tensor")) * own_tokens]
        )
        visible = (positions[:, None] >= positions[None, :])[None] & (
            seq_ids[:, :, None] == seq_ids[:, None, :]
        )
        visible = visible[:, None]

        d_rows = line_rows([d_pair], c.sync(d_line))
        stream.add(d_rows[:, :part], d_rows[:, part:])
        stream.step()
        wqk0, wqk1 = stream.rows[0], stream.x[0]
        qk = dot(in0, wqk0) + dot(in1, wqk1)
        query, key_proj = qk[:, :head_width], qk[:, head_width:]
        squares = pair_sum(
            c, jnp.stack([jnp.sum(query * query, axis=1), jnp.sum(key_proj * key_proj, axis=1)])
        )
        q_rms = lax.rsqrt(squares[0] / model_width + EPSILON)[:, None]
        k_rms = lax.rsqrt(squares[1] / model_width + EPSILON)[:, None]
        normed_query = (query * q_rms * query_scale).astype(BF)
        normed_key = (key_proj * k_rms * key_scale).astype(BF)
        stream.step()
        wv0, wo0 = stream.rows[1][:, :head_width], stream.rows[1][:, head_width:]
        wv1, wo1 = stream.x[1][:, :head_width], stream.x[1][:, head_width:]
        value_bf = (dot(in0, wv0) + dot(in1, wv1)).astype(BF)
        heads = (4, seq_length, local_heads, HD)
        query_heads = normed_query.reshape(heads)
        key_heads = normed_key.reshape(heads)
        value_heads = value_bf.reshape(heads)
        scores = (
            jnp.einsum("bqhd,bkhd->bhqk", query_heads, key_heads, preferred_element_type=F32)
            * score_scale
        )
        scores = jnp.where(visible, scores, NEGATIVE)
        peak = jnp.max(scores, axis=-1, keepdims=True)
        expo = jnp.exp(scores - peak)
        total = jnp.sum(expo, axis=-1, keepdims=True)
        prob = expo / total
        prob_bf = prob.astype(BF)
        attn_heads = jnp.einsum(
            "bhqk,bkhd->bqhd", prob_bf, value_heads, preferred_element_type=F32
        ).astype(BF)
        attn = attn_heads.reshape(group_tokens, head_width)

        def halve(total, axis):
            half = total.shape[0] // 2
            return total[:half], c.start(total[half:].astype(BF), axis)

        def added(pair):
            return pair[0] + c.sync(pair[1]).astype(F32)

        def cross(total):
            rows = own_tokens
            own = stack2(total[:rows], total[2 * rows : 3 * rows])
            sent = stack2(total[rows : 2 * rows], total[3 * rows :])
            return own, c.start(sent.astype(BF), "tensor")

        def scatter_rows(left_of, right_of, between=None):
            own, other = slice(0, core_tokens), slice(core_tokens, group_tokens)
            left_sent = c.start(left_of(other).astype(BF), "core")
            right_sent = c.start(right_of(other).astype(BF), "core")
            left = halve(left_of(own) + c.sync(left_sent).astype(F32), "zl")
            right = cross(right_of(own) + c.sync(right_sent).astype(F32))
            if between:
                between()
            left, right = added(left), added(right)
            left, right = halve(left, "tensor"), halve(right, "zl")
            return columns([added(left), added(right)])

        proj = scatter_rows(
            lambda rows: dot_nt(attn[rows], wo0), lambda rows: dot_nt(attn[rows], wo1), stream.step
        )
        attn_rms = rms_scale(proj)
        resid = tokens_f + proj * attn_rms * attn_scale
        h0, h1 = gather_rows(resid.astype(BF))
        stream.step()
        chunks = range(2)
        wg0, wu0, wd0 = [None, None], [None, None], [None, None]
        wg1, wu1, wd1 = [None, None], [None, None], [None, None]
        gate, up = [None, None], [None, None]
        wg0[0], wg1[0] = stream.rows[2], stream.x[2]
        gate[0] = dot(h0, wg0[0]) + dot(h1, wg1[0])
        stream.step()
        wg0[1], wg1[1] = stream.rows[3], stream.x[3]
        gate[1] = dot(h0, wg0[1]) + dot(h1, wg1[1])
        stream.step()
        wu0[0], wu1[0] = stream.rows[4], stream.x[4]
        up[0] = dot(h0, wu0[0]) + dot(h1, wu1[0])
        stream.step()
        wu0[1], wu1[1] = stream.rows[5], stream.x[5]
        up[1] = dot(h0, wu0[1]) + dot(h1, wu1[1])
        sigma = [jax.nn.sigmoid(g) for g in gate]
        act = [(gate[j] * sigma[j] * up[j]).astype(BF) for j in chunks]
        wd0[0], wd0[1] = stream.rows[6], stream.rows[7]

        own, other = slice(0, core_tokens), slice(core_tokens, group_tokens)

        def down(rows, w):
            return dot_nt(act[0][rows], w[0]) + dot_nt(act[1][rows], w[1])

        left_sent = c.start(down(other, wd0).astype(BF), "core")
        left = halve(down(own, wd0) + c.sync(left_sent).astype(F32), "zl")
        wd1[0] = stream.x[6]
        left = halve(added(left), "tensor")
        left = added(left)
        stream.end()
        wd1[1] = stream.x[7]
        right_sent = c.start(down(other, wd1).astype(BF), "core")
        right = cross(down(own, wd1) + c.sync(right_sent).astype(F32))
        right = halve(added(right), "zl")
        ffn = columns([left, added(right)])

        ffn_rms = rms_scale(ffn)
        output = to_natural((resid + ffn * ffn_rms * ffn_scale).astype(BF))
        ffn_gain_term = jnp.sum(d_out * ffn * ffn_rms, axis=0)
        scaled_out = d_out * ffn_scale
        d_ffn = (
            ffn_rms
            * (
                scaled_out
                - ffn * ffn_rms * ffn_rms * jnp.mean(scaled_out * ffn, axis=1, keepdims=True)
            )
        ).astype(BF)
        f0, f1 = gather_rows(d_ffn)

        class Grad:
            def __init__(self, count):
                self.parts, self.count = [], count

            def collect(self, total):
                self.parts.append(total)
                if len(self.parts) < self.count:
                    return False
                total = self.parts[0] if self.count == 1 else columns(self.parts)
                self.own, sent = split(total, "zl", 0)
                self.line = c.start(sent.astype(BF), "zl")
                return True

            def end_line(self):
                moved = c.sync(self.line).astype(F32)
                total = ordered("zl", self.own, moved, dim=1)
                self.own, sent = split(total, "core", 0)
                self.core = c.start(sent.astype(BF), "core")

            def end(self):
                self.result = ordered("core", self.own, c.sync(self.core).astype(F32), dim=1)

        class GradStream:
            def __init__(self):
                self.jobs, self.x = [], []
                self.at, self.high, self.lines, self.cores = 0, None, [], []

            def add(self, grad, kept, sent, right):
                self.jobs.append((grad, kept, sent, right))

            def feed(self):
                grad, kept, sent, right = self.jobs[len(self.x)]
                self.x.append(c.start(dot_tn(sent, right).astype(BF), "x"))

            def step(self):
                if self.at < len(self.x):
                    grad, kept, sent, right = self.jobs[self.at]
                    moved = c.sync(self.x[self.at])
                    if len(self.x) < len(self.jobs):
                        self.feed()
                    total = dot_tn(kept, right) + moved.astype(F32)
                    high = (grad, c.start_high_sum(total))
                    self.at += 1
                else:
                    high = None
                cores, lines = self.cores, self.lines
                self.cores, self.lines = [], []
                for grad in cores:
                    grad.end()
                for grad in lines:
                    grad.end_line()
                    self.cores.append(grad)
                if self.high is not None:
                    grad, pending = self.high
                    if grad.collect(c.end_high_sum(pending)):
                        self.lines.append(grad)
                self.high = high

            def idle(self):
                return self.high is None and not self.lines and not self.cores

        grads = GradStream()
        down_grad, gate_grad, up_grad = Grad(2), Grad(2), Grad(2)
        for j in chunks:
            grads.add(down_grad, f0, f1, act[j])
        grads.feed()
        grads.feed()
        d_gate, d_up = [None, None], [None, None]
        for j in chunks:
            d_act = dot(f0, wd0[j]) + dot(f1, wd1[j])
            d_gate[j] = (d_act * up[j] * sigma[j] * (1.0 + gate[j] * (1.0 - sigma[j]))).astype(BF)
            d_up[j] = (d_act * gate[j] * sigma[j]).astype(BF)
        for j in chunks:
            grads.add(gate_grad, h0, h1, d_gate[j])
            grads.add(up_grad, h0, h1, d_up[j])

        def hidden(rows, wg, wu):
            return (
                dot_nt(d_gate[0][rows], wg[0])
                + dot_nt(d_up[0][rows], wu[0])
                + dot_nt(d_gate[1][rows], wg[1])
                + dot_nt(d_up[1][rows], wu[1])
            )

        d_resid = d_out + scatter_rows(
            lambda rows: hidden(rows, wg0, wu0), lambda rows: hidden(rows, wg1, wu1), grads.step
        )
        attn_gain_term = jnp.sum(d_resid * proj * attn_rms, axis=0)
        scaled_resid = d_resid * attn_scale
        d_proj = (
            attn_rms
            * (
                scaled_resid
                - proj * attn_rms * attn_rms * jnp.mean(scaled_resid * proj, axis=1, keepdims=True)
            )
        ).astype(BF)
        grads.step()
        p0, p1 = gather_rows(d_proj)
        out_grad, value_grad, query_grad, key_grad = Grad(1), Grad(1), Grad(1), Grad(1)
        grads.add(out_grad, p0, p1, attn)
        d_attn = (dot(p0, wo0) + dot(p1, wo1)).astype(BF)
        grads.step()

        d_attn_heads = d_attn.reshape(heads)
        d_value = (
            jnp.einsum("bhqk,bqhd->bkhd", prob_bf, d_attn_heads, preferred_element_type=F32)
            .reshape(group_tokens, head_width)
            .astype(BF)
        )
        grads.add(value_grad, in0, in1, d_value)
        d_prob = jnp.einsum(
            "bqhd,bkhd->bhqk", d_attn_heads, value_heads, preferred_element_type=F32
        )
        delta = jnp.einsum(
            "bqhd,bqhd->bhq", d_attn_heads, attn.reshape(heads), preferred_element_type=F32
        )[..., None]
        d_score = (prob * (d_prob - delta)).astype(BF)
        d_nq = (
            jnp.einsum("bhqk,bkhd->bqhd", d_score, key_heads, preferred_element_type=F32).reshape(
                group_tokens, head_width
            )
            * score_scale
        )
        d_nk = (
            jnp.einsum("bhqk,bqhd->bkhd", d_score, query_heads, preferred_element_type=F32).reshape(
                group_tokens, head_width
            )
            * score_scale
        )
        query_gain_term = jnp.sum(d_nq * query * q_rms, axis=0)
        key_gain_term = jnp.sum(d_nk * key_proj * k_rms, axis=0)
        scaled_q = d_nq * query_scale
        scaled_k = d_nk * key_scale
        inner = pair_sum(
            c, jnp.stack([jnp.sum(scaled_q * query, axis=1), jnp.sum(scaled_k * key_proj, axis=1)])
        )
        grads.step()
        d_query = (
            q_rms * (scaled_q - query * q_rms * q_rms * (inner[0] / model_width)[:, None])
        ).astype(BF)
        d_key = (
            k_rms * (scaled_k - key_proj * k_rms * k_rms * (inner[1] / model_width)[:, None])
        ).astype(BF)
        grads.add(query_grad, in0, in1, d_query)
        grads.add(key_grad, in0, in1, d_key)
        d_qk = columns([d_query, d_key])

        d_tokens = scatter_rows(
            lambda rows: dot_nt(d_qk[rows], wqk0) + dot_nt(d_value[rows], wv0),
            lambda rows: dot_nt(d_qk[rows], wqk1) + dot_nt(d_value[rows], wv1),
            grads.step,
        )
        grad_tokens = to_natural(d_resid + d_tokens)
        grads.step()

        zero = jnp.zeros((2, model_width), F32)
        placed = lax.dynamic_update_slice_in_dim(
            zero, jnp.stack([query_gain_term, key_gain_term]), head_start, 1
        )
        gain_parts = scatter_gains(
            c,
            jnp.concatenate(
                [to_relative(placed), jnp.stack([attn_gain_term, ffn_gain_term])], axis=0
            ),
        )
        while grads.at < len(grads.jobs) or not grads.idle():
            grads.step()
        return (
            output,
            grad_tokens,
            query_grad.result,
            key_grad.result,
            value_grad.result,
            out_grad.result,
            gate_grad.result,
            up_grad.result,
            down_grad.result,
            gain_parts[0],
            gain_parts[1],
            gain_parts[2],
            gain_parts[3],
        )

    return shards


def solution(mesh):
    dp = mesh.shape["dp"]
    high = max(dp.bit_length() - 4, 0)
    high_bits = tuple(f"z{i}" for i in range(high))
    names = high_bits + ("zl", "x", "core", "tensor")
    fine = Mesh(mesh.devices.reshape((2,) * len(names)), names)
    rows = names[:-1]
    both = names
    mapped = jax.shard_map(
        build(high_bits),
        mesh=fine,
        in_specs=(
            P(both, None),
            P(rows, None),
            P(rows, "tensor"),
            P(rows, "tensor"),
            P(rows, "tensor"),
            P(rows, "tensor"),
            P(rows, "tensor"),
            P(rows, "tensor"),
            P(rows, "tensor"),
            P(both),
            P(both),
            P(both),
            P(both),
            P(both, None),
        ),
        out_specs=(
            P(both, None),
            P(both, None),
            P(rows, "tensor"),
            P(rows, "tensor"),
            P(rows, "tensor"),
            P(rows, "tensor"),
            P(rows, "tensor"),
            P(rows, "tensor"),
            P(rows, "tensor"),
            P(both),
            P(both),
            P(both),
            P(both),
        ),
        check_vma=False,
    )
    return mapped
```

time: 949 us -> 851 us (0.90)
  waiting for transfers between devices: 605 us -> 492 us
  matrix products: 100 us -> 119 us
    ppermute x101 -> x123, waiting for transfers between devices: 605 us -> 492 us  [swap(): return lax.ppermute(value, axis, FLIP)]
    concatenate x31 -> x38, other arithmetic: 35.1 us -> 13.6 us  [the longest x19 5.28 us: stack2(): return jnp.concatenate([low, high], axis=0)]
    dot_general x22 -> x36, matrix products: 26.5 us -> 39.6 us  [dot_nt(): return jnp.einsum('sc,rc->sr', a, b, preferred_element_type=F32)]
    unnamed x43 -> x44, other arithmetic: 1.41 us -> 11.5 us
    dot_general x14 -> x20, matrix products: 30.2 us -> 35.4 us  [dot_tn(): return jnp.einsum('sr,sc->rc', a, b, preferred_element_type=F32)]
    select_n x50 -> x40, other arithmetic: 19.3 us -> 14.4 us  [pick(): return jnp.where(bit(axis) == 0, low, high)]
    ppermute x101 -> x123, starting transfers between devices: 103 us -> 105 us  [swap(): return lax.ppermute(value, axis, FLIP)]
    unnamed x296 -> x382, local copies, waits for them, and re-layouts: 25 us -> 23.5 us
  transfers between devices with their start and end apart: 101 -> 123, of which waited for: 51 -> 69; matrix products, arithmetic and copies ran while one was open for 19% -> 20% of each run, Pallas kernels for 0% -> 0%
where the time goes in v3:
time: 851 us; the launch traced here: 845 us
  waiting for transfers between devices  492 us (58%)
  matrix products  119 us (14%)
  starting transfers between devices  105 us (12%)
  other arithmetic  75.7 us (9%)
  local copies, waits for them, and re-layouts  47.4 us (6%)
    ppermute x123, waiting for transfers between devices, swap(): return lax.ppermute(value, axis, FLIP)  492 us
    ppermute x123, starting transfers between devices, swap(): return lax.ppermute(value, axis, FLIP)  105 us
    dot_general x36, matrix products, dot_nt(): return jnp.einsum('sc,rc->sr', a, b, preferred_element_type=F32)  39.6 us
    dot_general x20, matrix products, dot_tn(): return jnp.einsum('sr,sc->rc', a, b, preferred_element_type=F32)  35.4 us
    dot_general x18, matrix products, dot(): return jnp.dot(a, b, preferred_element_type=F32)  33.6 us
    unnamed x382, local copies, waits for them, and re-layouts  23.5 us
  transfers between devices with their start and end apart: 123, of which 69 were waited for; matrix products, arithmetic and copies ran while one was open for 20% of the time, Pallas kernels for 0%

profile of v3, /device:TPU:0, one launch (start us, length us, event | category | flops | bytes accessed | tf_op | source)
XLA Modules:
  0.0 844.9 jit_solution(11313561086909699914)
XLA Ops:
  21.0 7.0 collective-permute-done.1
  33.7 4.4 collective-permute-done.5
  41.3 10.6 %collective-permute-done.6 = bf16[256,1024]{1,0:T(8,128)(2,1)S(1)} collective-permute-done((bf16[256,1024]{1,0:T(8,128)(2,1)S(1)}, bf16[256,1024]{1,0:T(8,128)(2,1)S(1)}, u32[]{:S(2)}, u32[]{:S(2)}) %collective-permute-start.6) | collective-permute-done | bytes 524320 | tf_op jit(solution)/shard_map/ppermute | solution.py:18
  60.7 22.7 %collective-permute-done.10 = bf16[256,1024]{1,0:T(8,128)(2,1)S(1)} collective-permute-done((bf16[256,1024]{1,0:T(8,128)(2,1)}, bf16[256,1024]{1,0:T(8,128)(2,1)S(1)}, u32[]{:S(2)}, u32[]{:S(2)}) %collective-permute-start.10) | collective-permute-done | bytes 524320 | tf_op jit(solution)/shard_map/ppermute | solution.py:18
  90.2 17.6 %collective-permute-done.13 = f32[4,256]{1,0:T(4,128)S(1)} collective-permute-done((f32[4,256]{1,0:T(4,128)S(1)}, f32[4,256]{1,0:T(4,128)S(1)}, u32[]{:S(2)}, u32[]{:S(2)}) %collective-permute-start.13) | collective-permute-done | bytes 4128 | tf_op jit(solution)/shard_map/ppermute | solution.py:18
  122.8 22.4 %collective-permute-done.20 = bf16[256,1024]{1,0:T(8,128)(2,1)S(1)} collective-permute-done((bf16[256,1024]{1,0:T(8,128)(2,1)S(1)}, bf16[256,1024]{1,0:T(8,128)(2,1)S(1)}, u32[]{:S(2)}, u32[]{:S(2)}) %collective-permute-start.20) | collective-permute-done | bytes 524320 | tf_op jit(solution)/shard_map/ppermute | solution.py:18
  167.7 3.4 fusion.211
  171.1 12.2 %collective-permute-done.27 = bf16[1024,512]{1,0:T(8,128)(2,1)} collective-permute-done((bf16[1024,512]{1,0:T(8,128)(2,1)}, bf16[1024,512]{1,0:T(8,128)(2,1)}, u32[]{:S(2)}, u32[]{:S(2)}) %collective-permute-start.27) | collective-permute-done | bytes 1048608 | tf_op jit(solution)/shard_map/ppermute | solution.py:18
  205.8 18.0 %collective-permute-done.30 = bf16[512,512]{1,0:T(8,128)(2,1)S(1)} collective-permute-done((bf16[512,512]{1,0:T(8,128)(2,1)S(1)}, bf16[512,512]{1,0:T(8,128)(2,1)S(1)}, u32[]{:S(2)}, u32[]{:S(2)}) %collective-permute-start.30) | collective-permute-done | bytes 524320 | tf_op jit(solution)/shard_map/ppermute | solution.py:18
  224.0 3.9 collective-permute-done.32
  229.4 6.7 collective-permute-done.34
  239.8 4.4 collective-permute-done.36
  247.3 9.8 %collective-permute-done.38 = bf16[256,1024]{1,0:T(8,128)(2,1)S(1)} collective-permute-done((bf16[256,1024]{1,0:T(8,128)(2,1)S(1)}, bf16[256,1024]{1,0:T(8,128)(2,1)S(1)}, u32[]{:S(2)}, u32[]{:S(2)}) %collective-permute-start.38) | collective-permute-done | bytes 524320 | tf_op jit(solution)/shard_map/ppermute | solution.py:18
  262.4 34.2 %collective-permute-done.42 = bf16[512,512]{1,0:T(8,128)(2,1)S(1)} collective-permute-done((bf16[512,512]{1,0:T(8,128)(2,1)S(1)}, bf16[512,512]{1,0:T(8,128)(2,1)S(1)}, u32[]{:S(2)}, u32[]{:S(2)}) %collective-permute-start.42) | collective-permute-done | bytes 524320 | tf_op jit(solution)/shard_map/ppermute | solution.py:18
  296.7 10.5 %collective-permute-done.44 = bf16[512,512]{1,0:T(8,128)(2,1)S(1)} collective-permute-done((bf16[512,512]{1,0:T(8,128)(2,1)S(1)}, bf16[512,512]{1,0:T(8,128)(2,1)S(1)}, u32[]{:S(2)}, u32[]{:S(2)}) %collective-permute-start.44) | collective-permute-done | bytes 524320 | tf_op jit(solution)/shard_map/ppermute | solution.py:18
  317.5 14.3 %collective-permute-done.45 = bf16[1024,512]{1,0:T(8,128)(2,1)S(1)} collective-permute-done((bf16[1024,512]{1,0:T(8,128)(2,1)S(1)}, bf16[1024,512]{1,0:T(8,128)(2,1)S(1)}, u32[]{:S(2)}, u32[]{:S(2)}) %collective-permute-start.45) | collective-permute-done | bytes 1048608 | tf_op jit(solution)/shard_map/ppermute | solution.py:18
  336.9 6.6 collective-permute-done.46
  344.4 11.1 %collective-permute-done.47 = bf16[1024,512]{1,0:T(8,128)(2,1)S(1)} collective-permute-done((bf16[1024,512]{1,0:T(8,128)(2,1)S(1)}, bf16[1024,512]{1,0:T(8,128)(2,1)S(1)}, u32[]{:S(2)}, u32[]{:S(2)}) %collective-permute-start.47) | collective-permute-done | bytes 1048608 | tf_op jit(solution)/shard_map/ppermute | solution.py:18
  361.5 18.3 %collective-permute-done.49 = bf16[1024,512]{1,0:T(8,128)(2,1)S(1)} collective-permute-done((bf16[1024,512]{1,0:T(8,128)(2,1)S(1)}, bf16[1024,512]{1,0:T(8,128)(2,1)S(1)}, u32[]{:S(2)}, u32[]{:S(2)}) %collective-permute-start.49) | collective-permute-done | bytes 1048608 | tf_op jit(solution)/shard_map/ppermute | solution.py:18
  384.9 12.2 %collective-permute-done.51 = bf16[256,1024]{1,0:T(8,128)(2,1)S(1)} collective-permute-done((bf16[256,1024]{1,0:T(8,128)(2,1)S(1)}, bf16[256,1024]{1,0:T(8,128)(2,1)S(1)}, u32[]{:S(2)}, u32[]{:S(2)}) %collective-permute-start.51) | collective-permute-done | bytes 524320 | tf_op jit(solution)/shard_map/ppermute | solution.py:18
  397.6 7.2 collective-permute-done.52
  404.9 3.6 collective-permute-done.53
  414.0 13.6 %collective-permute-done.55 = bf16[256,1024]{1,0:T(8,128)(2,1)S(1)} collective-permute-done((bf16[256,1024]{1,0:T(8,128)(2,1)S(1)}, bf16[256,1024]{1,0:T(8,128)(2,1)S(1)}, u32[]{:S(2)}, u32[]{:S(2)}) %collective-permute-start.55) | collective-permute-done | bytes 524320 | tf_op jit(solution)/shard_map/ppermute | solution.py:18
  429.6 5.8 collective-permute-done.56
  438.5 4.6 collective-permute-done.57
  446.7 8.0 collective-permute-done.59
  464.2 4.0 convolution_convert_fusion.5
  474.7 3.3 multiply_convert_fusion.1
  482.1 3.3 multiply_convert_fusion.3
  509.0 16.1 %collective-permute-done.65 = bf16[1024,512]{1,0:T(8,128)(2,1)} collective-permute-done((bf16[1024,512]{1,0:T(8,128)(2,1)}, bf16[1024,512]{1,0:T(8,128)(2,1)}, u32[]{:S(2)}, u32[]{:S(2)}) %collective-permute-start.65) | collective-permute-done | bytes 1048608 | tf_op jit(solution)/shard_map/ppermute | solution.py:18
  530.0 7.4 collective-permute-done.66
  554.8 11.4 %collective-permute-done.71 = bf16[512,512]{1,0:T(8,128)(2,1)S(1)} collective-permute-done((bf16[512,512]{1,0:T(8,128)(2,1)S(1)}, bf16[512,512]{1,0:T(8,128)(2,1)S(1)}, u32[]{:S(2)}, u32[]{:S(2)}) %collective-permute-start.71) | collective-permute-done | bytes 524320 | tf_op jit(solution)/shard_map/ppermute | solution.py:18
  577.2 7.3 collective-permute-done.74
  640.0 15.3 %collective-permute-done.81 = f32[2,1024]{1,0:T(2,128)S(1)} collective-permute-done((f32[2,1024]{1,0:T(2,128)S(1)}, f32[2,1024]{1,0:T(2,128)S(1)}, u32[]{:S(2)}, u32[]{:S(2)}) %collective-permute-start.81) | collective-permute-done | bytes 8224 | tf_op jit(solution)/shard_map/ppermute | solution.py:18
  670.8 10.1 %collective-permute-done.116 = bf16[1024,256]{1,0:T(8,128)(2,1)S(1)} collective-permute-done((bf16[1024,256]{1,0:T(8,128)(2,1)S(1)}, bf16[1024,256]{1,0:T(8,128)(2,1)S(1)}, u32[]{:S(2)}, u32[]{:S(2)}) %collective-permute-start.116) | collective-permute-done | bytes 524320 | tf_op jit(solution)/shard_map/ppermute | solution.py:18
  685.1 9.3 %collective-permute-done.117 = bf16[512,256]{1,0:T(8,128)(2,1)S(1)} collective-permute-done((bf16[512,256]{1,0:T(8,128)(2,1)S(1)}, bf16[512,256]{1,0:T(8,128)(2,1)S(1)}, u32[]{:S(2)}, u32[]{:S(2)}) %collective-permute-start.117) | collective-permute-done | bytes 262176 | tf_op jit(solution)/shard_map/ppermute | solution.py:18
  698.1 3.2 collective-permute-done.118
  709.3 11.3 %collective-permute-done.90 = bf16[512,512]{1,0:T(8,128)(2,1)S(1)} collective-permute-done((bf16[512,512]{1,0:T(8,128)(2,1)S(1)}, bf16[512,512]{1,0:T(8,128)(2,1)S(1)}, u32[]{:S(2)}, u32[]{:S(2)}) %collective-permute-start.90) | collective-permute-done | bytes 524320 | tf_op jit(solution)/shard_map/ppermute | solution.py:18
  727.0 15.8 %collective-permute-done.91 = bf16[256,1024]{1,0:T(8,128)(2,1)S(1)} collective-permute-done((bf16[256,1024]{1,0:T(8,128)(2,1)S(1)}, bf16[256,1024]{1,0:T(8,128)(2,1)S(1)}, u32[]{:S(2)}, u32[]{:S(2)}) %collective-permute-start.91) | collective-permute-done | bytes 524320 | tf_op jit(solution)/shard_map/ppermute | solution.py:18
  746.2 5.0 collective-permute-done.93
  755.5 3.2 collective-permute-done.97
  759.3 4.0 collective-permute-done.98
  763.8 3.3 collective-permute-done.99
  768.8 3.2 collective-permute-done.101
  778.4 8.0 collective-permute-done.108
  787.2 16.4 %collective-permute-done.114 = bf16[256,256]{1,0:T(8,128)(2,1)S(1)} collective-permute-done((bf16[256,256]{1,0:T(8,128)(2,1)S(1)}, bf16[256,256]{1,0:T(8,128)(2,1)S(1)}, u32[]{:S(2)}, u32[]{:S(2)}) %collective-permute-start.114) | collective-permute-done | bytes 131104 | tf_op jit(solution)/shard_map/ppermute | solution.py:18
  813.4 7.1 collective-permute-done.115
  820.7 10.5 %collective-permute-done.110 = bf16[512,256]{1,0:T(8,128)(2,1)S(1)} collective-permute-done((bf16[512,256]{1,0:T(8,128)(2,1)S(1)}, bf16[512,256]{1,0:T(8,128)(2,1)S(1)}, u32[]{:S(2)}, u32[]{:S(2)}) %collective-permute-start.110) | collective-permute-done | bytes 262176 | tf_op jit(solution)/shard_map/ppermute | solution.py:18
  (950 shorter events, 367.7 us)
Async XLA Ops:
  10.4 20.2 %collective-permute-start.2 = (bf16[128,6144]{1,0:T(8,128)(2,1)}, bf16[128,6144]{1,0:T(8,128)(2,1)}, u32[]{:S(2)}, u32[]{:S(2)}) collective-permute-start(bf16[128,6144]{1,0:T(8,128)(2,1)} %pad_maximum_fusion.7), channel_id=1, source_target_pairs={{0,2},{2,0},{1,3},{3,1},{4,6},{6,4},{5,7},{7,5},{8,10},{10,8},{9,1... | collective-permute-start | bytes 4718600 | tf_op jit(solution)/shard_map/ppermute | solution.py:18
  10.4 23.2 %collective-permute-start.3 = (bf16[128,1024]{1,0:T(8,128)(2,1)}, bf16[128,1024]{1,0:T(8,128)(2,1)S(1)}, u32[]{:S(2)}, u32[]{:S(2)}) collective-permute-start(bf16[128,1024]{1,0:T(8,128)(2,1)} %pad_maximum_fusion.64), channel_id=1, source_target_pairs={{0,1},{1,0},{2,3},{3,2},{4,5},{5,4},{6,7},{7,6},{8,9},{9,8},{10,11... | collective-permute-start | bytes 786440 | tf_op jit(solution)/shard_map/ppermute | solution.py:18
  56.8 26.6 %collective-permute-start.10 = (bf16[256,1024]{1,0:T(8,128)(2,1)}, bf16[256,1024]{1,0:T(8,128)(2,1)S(1)}, u32[]{:S(2)}, u32[]{:S(2)}) collective-permute-start(bf16[256,1024]{1,0:T(8,128)(2,1)} %broadcast_select_fusion.14), channel_id=1, source_target_pairs={{0,8},{8,0},{1,9},{9,1},{2,10},{10,2},{3,11},{11,3},{4,12},{12,4},... | collective-permute-start | bytes 1572872 | tf_op jit(solution)/shard_map/ppermute | solution.py:18
  57.5 58.9 %collective-permute-start.16 = (bf16[512,512]{1,0:T(8,128)(2,1)}, bf16[512,512]{1,0:T(8,128)(2,1)S(1)}, u32[]{:S(2)}, u32[]{:S(2)}) collective-permute-start(bf16[512,512]{1,0:T(8,128)(2,1)} %pad_maximum_fusion.40), channel_id=1, source_target_pairs={{0,16},{16,0},{1,17},{17,1},{2,18},{18,2},{3,19},{19,3},{4,20},{20... | collective-permute-start | bytes 1572872 | tf_op jit(solution)/shard_map/ppermute | solution.py:18
  60.2 85.1 %collective-permute-start.21 = (bf16[512,512]{1,0:T(8,128)(2,1)}, bf16[512,512]{1,0:T(8,128)(2,1)S(1)}, u32[]{:S(2)}, u32[]{:S(2)}) collective-permute-start(bf16[512,512]{1,0:T(8,128)(2,1)} %pad_maximum_fusion.41), channel_id=1, source_target_pairs={{0,16},{16,0},{1,17},{17,1},{2,18},{18,2},{3,19},{19,3},{4,20},{20... | collective-permute-start | bytes 1572872 | tf_op jit(solution)/shard_map/ppermute | solution.py:18
  84.0 38.6 %collective-permute-start.19 = (bf16[256,1024]{1,0:T(8,128)(2,1)S(1)}, bf16[256,1024]{1,0:T(8,128)(2,1)S(1)}, u32[]{:S(2)}, u32[]{:S(2)}) collective-permute-start(bf16[256,1024]{1,0:T(8,128)(2,1)S(1)} %broadcast_select_fusion.13), channel_id=1, source_target_pairs={{0,8},{8,0},{1,9},{9,1},{2,10},{10,2},{3,11},{11,3},{4,12},{12,4},... | collective-permute-start | bytes 1572872 | tf_op jit(solution)/shard_map/ppermute | solution.py:18
  89.8 18.0 %collective-permute-start.13 = (f32[4,256]{1,0:T(4,128)S(1)}, f32[4,256]{1,0:T(4,128)S(1)}, u32[]{:S(2)}, u32[]{:S(2)}) collective-permute-start(f32[4,256]{1,0:T(4,128)S(1)} %pad_maximum_fusion.85), channel_id=1, source_target_pairs={{0,8},{8,0},{1,9},{9,1},{2,10},{10,2},{3,11},{11,3},{4,12},{12,4},... | collective-permute-start | bytes 12296 | tf_op jit(solution)/shard_map/ppermute | solution.py:18
  117.0 29.4 %collective-permute-start.22 = (bf16[1024,512]{1,0:T(8,128)(2,1)S(1)}, bf16[1024,512]{1,0:T(8,128)(2,1)S(1)}, u32[]{:S(2)}, u32[]{:S(2)}) collective-permute-start(bf16[1024,512]{1,0:T(8,128)(2,1)S(1)} %pad_maximum_fusion.16), channel_id=1, source_target_pairs={{0,4},{4,0},{1,5},{5,1},{2,6},{6,2},{3,7},{7,3},{8,12},{12,8},{9,1... | collective-permute-start | bytes 3145736 | tf_op jit(solution)/shard_map/ppermute | solution.py:18
  118.4 41.4 %collective-permute-start.26 = (bf16[512,512]{1,0:T(8,128)(2,1)S(1)}, bf16[512,512]{1,0:T(8,128)(2,1)S(1)}, u32[]{:S(2)}, u32[]{:S(2)}) collective-permute-start(bf16[512,512]{1,0:T(8,128)(2,1)S(1)} %get-tuple-element.578), channel_id=1, source_target_pairs={{0,16},{16,0},{1,17},{17,1},{2,18},{18,2},{3,19},{19,3},{4,20},{20... | collective-permute-start | bytes 1572872 | tf_op jit(solution)/shard_map/ppermute | solution.py:18
  122.6 22.6 %collective-permute-start.20 = (bf16[256,1024]{1,0:T(8,128)(2,1)S(1)}, bf16[256,1024]{1,0:T(8,128)(2,1)S(1)}, u32[]{:S(2)}, u32[]{:S(2)}) collective-permute-start(bf16[256,1024]{1,0:T(8,128)(2,1)S(1)} %broadcast_select_fusion.9), channel_id=1, source_target_pairs={{0,8},{8,0},{1,9},{9,1},{2,10},{10,2},{3,11},{11,3},{4,12},{12,4},... | collective-permute-start | bytes 1572872 | tf_op jit(solution)/shard_map/ppermute | solution.py:18
  159.1 24.1 %collective-permute-start.27 = (bf16[1024,512]{1,0:T(8,128)(2,1)}, bf16[1024,512]{1,0:T(8,128)(2,1)}, u32[]{:S(2)}, u32[]{:S(2)}) collective-permute-start(bf16[1024,512]{1,0:T(8,128)(2,1)} %pad_maximum_fusion.17), channel_id=1, source_target_pairs={{0,4},{4,0},{1,5},{5,1},{2,6},{6,2},{3,7},{7,3},{8,12},{12,8},{9,1... | collective-permute-start | bytes 3145736 | tf_op jit(solution)/shard_map/ppermute | solution.py:18
  198.0 25.8 %collective-permute-start.30 = (bf16[512,512]{1,0:T(8,128)(2,1)S(1)}, bf16[512,512]{1,0:T(8,128)(2,1)S(1)}, u32[]{:S(2)}, u32[]{:S(2)}) collective-permute-start(bf16[512,512]{1,0:T(8,128)(2,1)S(1)} %copy-done.17), channel_id=1, source_target_pairs={{0,16},{16,0},{1,17},{17,1},{2,18},{18,2},{3,19},{19,3},{4,20},{20... | collective-permute-start | bytes 1572872 | tf_op jit(solution)/shard_map/ppermute | solution.py:18
  198.2 25.6 %collective-permute-start.31 = (bf16[1024,512]{1,0:T(8,128)(2,1)}, bf16[1024,512]{1,0:T(8,128)(2,1)S(1)}, u32[]{:S(2)}, u32[]{:S(2)}) collective-permute-start(bf16[1024,512]{1,0:T(8,128)(2,1)} %pad_maximum_fusion.18), channel_id=1, source_target_pairs={{0,4},{4,0},{1,5},{5,1},{2,6},{6,2},{3,7},{7,3},{8,12},{12,8},{9,1... | collective-permute-start | bytes 3145736 | tf_op jit(solution)/shard_map/ppermute | solution.py:18
  203.1 24.8 %collective-permute-start.32 = (bf16[256,1024]{1,0:T(8,128)(2,1)S(1)}, bf16[256,1024]{1,0:T(8,128)(2,1)S(1)}, u32[]{:S(2)}, u32[]{:S(2)}) collective-permute-start(bf16[256,1024]{1,0:T(8,128)(2,1)S(1)} %slice.2477), channel_id=1, source_target_pairs={{0,8},{8,0},{1,9},{9,1},{2,10},{10,2},{3,11},{11,3},{4,12},{12,4},... | collective-permute-start | bytes 1572872 | tf_op jit(solution)/shard_map/ppermute | solution.py:18
  205.0 22.9 %collective-permute-start.33 = (bf16[256,1024]{1,0:T(8,128)(2,1)S(1)}, bf16[256,1024]{1,0:T(8,128)(2,1)S(1)}, u32[]{:S(2)}, u32[]{:S(2)}) collective-permute-start(bf16[256,1024]{1,0:T(8,128)(2,1)S(1)} %pad_maximum_fusion.44), channel_id=1, source_target_pairs={{0,1},{1,0},{2,3},{3,2},{4,5},{5,4},{6,7},{7,6},{8,9},{9,8},{10,11... | collective-permute-start | bytes 1572872 | tf_op jit(solution)/shard_map/ppermute | solution.py:18
  258.1 38.6 %collective-permute-start.43 = (bf16[1024,512]{1,0:T(8,128)(2,1)S(1)}, bf16[1024,512]{1,0:T(8,128)(2,1)S(1)}, u32[]{:S(2)}, u32[]{:S(2)}) collective-permute-start(bf16[1024,512]{1,0:T(8,128)(2,1)S(1)} %pad_maximum_fusion.19), channel_id=1, source_target_pairs={{0,4},{4,0},{1,5},{5,1},{2,6},{6,2},{3,7},{7,3},{8,12},{12,8},{9,1... | collective-permute-start | bytes 3145736 | tf_op jit(solution)/shard_map/ppermute | solution.py:18
  259.0 37.6 %collective-permute-start.42 = (bf16[512,512]{1,0:T(8,128)(2,1)S(1)}, bf16[512,512]{1,0:T(8,128)(2,1)S(1)}, u32[]{:S(2)}, u32[]{:S(2)}) collective-permute-start(bf16[512,512]{1,0:T(8,128)(2,1)S(1)} %copy-done.19), channel_id=1, source_target_pairs={{0,16},{16,0},{1,17},{17,1},{2,18},{18,2},{3,19},{19,3},{4,20},{20... | collective-permute-start | bytes 1572872 | tf_op jit(solution)/shard_map/ppermute | solution.py:18
  260.7 46.6 %collective-permute-start.44 = (bf16[512,512]{1,0:T(8,128)(2,1)S(1)}, bf16[512,512]{1,0:T(8,128)(2,1)S(1)}, u32[]{:S(2)}, u32[]{:S(2)}) collective-permute-start(bf16[512,512]{1,0:T(8,128)(2,1)S(1)} %copy-done.21), channel_id=1, source_target_pairs={{0,16},{16,0},{1,17},{17,1},{2,18},{18,2},{3,19},{19,3},{4,20},{20... | collective-permute-start | bytes 1572872 | tf_op jit(solution)/shard_map/ppermute | solution.py:18
  307.3 24.6 %collective-permute-start.45 = (bf16[1024,512]{1,0:T(8,128)(2,1)S(1)}, bf16[1024,512]{1,0:T(8,128)(2,1)S(1)}, u32[]{:S(2)}, u32[]{:S(2)}) collective-permute-start(bf16[1024,512]{1,0:T(8,128)(2,1)S(1)} %pad_maximum_fusion.23), channel_id=1, source_target_pairs={{0,4},{4,0},{1,5},{5,1},{2,6},{6,2},{3,7},{7,3},{8,12},{12,8},{9,1... | collective-permute-start | bytes 3145736 | tf_op jit(solution)/shard_map/ppermute | solution.py:18
  308.4 35.2 %collective-permute-start.46 = (bf16[512,512]{1,0:T(8,128)(2,1)S(1)}, bf16[512,512]{1,0:T(8,128)(2,1)S(1)}, u32[]{:S(2)}, u32[]{:S(2)}) collective-permute-start(bf16[512,512]{1,0:T(8,128)(2,1)S(1)} %get-tuple-element.662), channel_id=1, source_target_pairs={{0,16},{16,0},{1,17},{17,1},{2,18},{18,2},{3,19},{19,3},{4,20},{20... | collective-permute-start | bytes 1572872 | tf_op jit(solution)/shard_map/ppermute | solution.py:18
  308.4 47.2 %collective-permute-start.48 = (bf16[512,512]{1,0:T(8,128)(2,1)S(1)}, bf16[512,512]{1,0:T(8,128)(2,1)S(1)}, u32[]{:S(2)}, u32[]{:S(2)}) collective-permute-start(bf16[512,512]{1,0:T(8,128)(2,1)S(1)} %get-tuple-element.670), channel_id=1, source_target_pairs={{0,16},{16,0},{1,17},{17,1},{2,18},{18,2},{3,19},{19,3},{4,20},{20... | collective-permute-start | bytes 1572872 | tf_op jit(solution)/shard_map/ppermute | solution.py:18
  331.8 23.7 %collective-permute-start.47 = (bf16[1024,512]{1,0:T(8,128)(2,1)S(1)}, bf16[1024,512]{1,0:T(8,128)(2,1)S(1)}, u32[]{:S(2)}, u32[]{:S(2)}) collective-permute-start(bf16[1024,512]{1,0:T(8,128)(2,1)S(1)} %pad_maximum_fusion.24), channel_id=1, source_target_pairs={{0,4},{4,0},{1,5},{5,1},{2,6},{6,2},{3,7},{7,3},{8,12},{12,8},{9,1... | collective-permute-start | bytes 3145736 | tf_op jit(solution)/shard_map/ppermute | solution.py:18
  355.5 24.3 %collective-permute-start.49 = (bf16[1024,512]{1,0:T(8,128)(2,1)S(1)}, bf16[1024,512]{1,0:T(8,128)(2,1)S(1)}, u32[]{:S(2)}, u32[]{:S(2)}) collective-permute-start(bf16[1024,512]{1,0:T(8,128)(2,1)S(1)} %pad_maximum_fusion.25), channel_id=1, source_target_pairs={{0,4},{4,0},{1,5},{5,1},{2,6},{6,2},{3,7},{7,3},{8,12},{12,8},{9,1... | collective-permute-start | bytes 3145736 | tf_op jit(solution)/shard_map/ppermute | solution.py:18
  383.2 25.3 %collective-permute-start.53 = (bf16[1024,512]{1,0:T(8,128)(2,1)S(1)}, bf16[1024,512]{1,0:T(8,128)(2,1)S(1)}, u32[]{:S(2)}, u32[]{:S(2)}) collective-permute-start(bf16[1024,512]{1,0:T(8,128)(2,1)S(1)} %pad_maximum_fusion.26), channel_id=1, source_target_pairs={{0,4},{4,0},{1,5},{5,1},{2,6},{6,2},{3,7},{7,3},{8,12},{12,8},{9,1... | collective-permute-start | bytes 3145736 | tf_op jit(solution)/shard_map/ppermute | solution.py:18
  498.8 26.4 %collective-permute-start.65 = (bf16[1024,512]{1,0:T(8,128)(2,1)}, bf16[1024,512]{1,0:T(8,128)(2,1)}, u32[]{:S(2)}, u32[]{:S(2)}) collective-permute-start(bf16[1024,512]{1,0:T(8,128)(2,1)} %convolution_convert_fusion.5), channel_id=1, source_target_pairs={{0,4},{4,0},{1,5},{5,1},{2,6},{6,2},{3,7},{7,3},{8,12},{12,8},{9,1... | collective-permute-start | bytes 3145736 | tf_op jit(solution)/shard_map/ppermute | solution.py:18
  500.4 47.5 %collective-permute-start.70 = (bf16[1024,512]{1,0:T(8,128)(2,1)}, bf16[1024,512]{1,0:T(8,128)(2,1)}, u32[]{:S(2)}, u32[]{:S(2)}) collective-permute-start(bf16[1024,512]{1,0:T(8,128)(2,1)} %convolution_convert_fusion.4), channel_id=1, source_target_pairs={{0,4},{4,0},{1,5},{5,1},{2,6},{6,2},{3,7},{7,3},{8,12},{12,8},{9,1... | collective-permute-start | bytes 3145736 | tf_op jit(solution)/shard_map/ppermute | solution.py:18
  543.4 22.8 %collective-permute-start.71 = (bf16[512,512]{1,0:T(8,128)(2,1)S(1)}, bf16[512,512]{1,0:T(8,128)(2,1)S(1)}, u32[]{:S(2)}, u32[]{:S(2)}) collective-permute-start(bf16[512,512]{1,0:T(8,128)(2,1)S(1)} %slice.2474), channel_id=1, source_target_pairs={{0,16},{16,0},{1,17},{17,1},{2,18},{18,2},{3,19},{19,3},{4,20},{20... | collective-permute-start | bytes 1572872 | tf_op jit(solution)/shard_map/ppermute | solution.py:18
  569.3 33.8 %collective-permute-start.78 = (bf16[1024,512]{1,0:T(8,128)(2,1)}, bf16[1024,512]{1,0:T(8,128)(2,1)}, u32[]{:S(2)}, u32[]{:S(2)}) collective-permute-start(bf16[1024,512]{1,0:T(8,128)(2,1)} %convolution_convert_fusion.3), channel_id=1, source_target_pairs={{0,4},{4,0},{1,5},{5,1},{2,6},{6,2},{3,7},{7,3},{8,12},{12,8},{9,1... | collective-permute-start | bytes 3145736 | tf_op jit(solution)/shard_map/ppermute | solution.py:18
  586.4 37.5 %collective-permute-start.79 = (bf16[512,512]{1,0:T(8,128)(2,1)}, bf16[512,512]{1,0:T(8,128)(2,1)}, u32[]{:S(2)}, u32[]{:S(2)}) collective-permute-start(bf16[512,512]{1,0:T(8,128)(2,1)} %slice.2473), channel_id=1, source_target_pairs={{0,16},{16,0},{1,17},{17,1},{2,18},{18,2},{3,19},{19,3},{4,20},{20... | collective-permute-start | bytes 1572872 | tf_op jit(solution)/shard_map/ppermute | solution.py:18
  588.6 74.5 %collective-permute-start.83 = (bf16[1024,512]{1,0:T(8,128)(2,1)}, bf16[1024,512]{1,0:T(8,128)(2,1)}, u32[]{:S(2)}, u32[]{:S(2)}) collective-permute-start(bf16[1024,512]{1,0:T(8,128)(2,1)} %convolution_convert_fusion.2), channel_id=1, source_target_pairs={{0,4},{4,0},{1,5},{5,1},{2,6},{6,2},{3,7},{7,3},{8,12},{12,8},{9,1... | collective-permute-start | bytes 3145736 | tf_op jit(solution)/shard_map/ppermute | solution.py:18
  630.1 40.7 %collective-permute-start.84 = (bf16[256,1024]{1,0:T(8,128)(2,1)}, bf16[256,1024]{1,0:T(8,128)(2,1)}, u32[]{:S(2)}, u32[]{:S(2)}) collective-permute-start(bf16[256,1024]{1,0:T(8,128)(2,1)} %select_convert_fusion.5), channel_id=1, source_target_pairs={{0,8},{8,0},{1,9},{9,1},{2,10},{10,2},{3,11},{11,3},{4,12},{12,4},... | collective-permute-start | bytes 1572872 | tf_op jit(solution)/shard_map/ppermute | solution.py:18
  630.7 54.3 %collective-permute-start.85 = (bf16[512,512]{1,0:T(8,128)(2,1)}, bf16[512,512]{1,0:T(8,128)(2,1)}, u32[]{:S(2)}, u32[]{:S(2)}) collective-permute-start(bf16[512,512]{1,0:T(8,128)(2,1)} %slice.2472), channel_id=1, source_target_pairs={{0,16},{16,0},{1,17},{17,1},{2,18},{18,2},{3,19},{19,3},{4,20},{20... | collective-permute-start | bytes 1572872 | tf_op jit(solution)/shard_map/ppermute | solution.py:18
  636.1 70.6 %collective-permute-start.88 = (bf16[1024,512]{1,0:T(8,128)(2,1)}, bf16[1024,512]{1,0:T(8,128)(2,1)S(1)}, u32[]{:S(2)}, u32[]{:S(2)}) collective-permute-start(bf16[1024,512]{1,0:T(8,128)(2,1)} %convolution_convert_fusion.1), channel_id=1, source_target_pairs={{0,4},{4,0},{1,5},{5,1},{2,6},{6,2},{3,7},{7,3},{8,12},{12,8},{9,1... | collective-permute-start | bytes 3145736 | tf_op jit(solution)/shard_map/ppermute | solution.py:18
  685.0 19.0 %collective-permute-start.86 = (bf16[512,1024]{1,0:T(8,128)(2,1)S(1)}, bf16[512,1024]{1,0:T(8,128)(2,1)S(1)}, u32[]{:S(2)}, u32[]{:S(2)}) collective-permute-start(bf16[512,1024]{1,0:T(8,128)(2,1)S(1)} %add_convert_fusion.1), channel_id=1, source_target_pairs={{0,2},{2,0},{1,3},{3,1},{4,6},{6,4},{5,7},{7,5},{8,10},{10,8},{9,1... | collective-permute-start | bytes 3145736 | tf_op jit(solution)/shard_map/ppermute | solution.py:18
  695.4 25.2 %collective-permute-start.90 = (bf16[512,512]{1,0:T(8,128)(2,1)S(1)}, bf16[512,512]{1,0:T(8,128)(2,1)S(1)}, u32[]{:S(2)}, u32[]{:S(2)}) collective-permute-start(bf16[512,512]{1,0:T(8,128)(2,1)S(1)} %slice.2471), channel_id=1, source_target_pairs={{0,16},{16,0},{1,17},{17,1},{2,18},{18,2},{3,19},{19,3},{4,20},{20... | collective-permute-start | bytes 1572872 | tf_op jit(solution)/shard_map/ppermute | solution.py:18
  702.9 50.0 %collective-permute-start.95 = (bf16[1024,512]{1,0:T(8,128)(2,1)S(1)}, bf16[1024,512]{1,0:T(8,128)(2,1)S(1)}, u32[]{:S(2)}, u32[]{:S(2)}) collective-permute-start(bf16[1024,512]{1,0:T(8,128)(2,1)S(1)} %copy-done.166), channel_id=1, source_target_pairs={{0,4},{4,0},{1,5},{5,1},{2,6},{6,2},{3,7},{7,3},{8,12},{12,8},{9,1... | collective-permute-start | bytes 3145736 | tf_op jit(solution)/shard_map/ppermute | solution.py:18
  720.6 22.2 %collective-permute-start.91 = (bf16[256,1024]{1,0:T(8,128)(2,1)S(1)}, bf16[256,1024]{1,0:T(8,128)(2,1)S(1)}, u32[]{:S(2)}, u32[]{:S(2)}) collective-permute-start(bf16[256,1024]{1,0:T(8,128)(2,1)S(1)} %slice.2470), channel_id=1, source_target_pairs={{0,8},{8,0},{1,9},{9,1},{2,10},{10,2},{3,11},{11,3},{4,12},{12,4},... | collective-permute-start | bytes 1572872 | tf_op jit(solution)/shard_map/ppermute | solution.py:18
  720.6 22.2 %collective-permute-start.92 = (bf16[256,1024]{1,0:T(8,128)(2,1)S(1)}, bf16[256,1024]{1,0:T(8,128)(2,1)S(1)}, u32[]{:S(2)}, u32[]{:S(2)}) collective-permute-start(bf16[256,1024]{1,0:T(8,128)(2,1)S(1)} %pad_maximum_fusion.53), channel_id=1, source_target_pairs={{0,1},{1,0},{2,3},{3,2},{4,5},{5,4},{6,7},{7,6},{8,9},{9,8},{10,11... | collective-permute-start | bytes 1572872 | tf_op jit(solution)/shard_map/ppermute | solution.py:18
  722.2 32.4 %collective-permute-start.96 = (bf16[512,512]{1,0:T(8,128)(2,1)S(1)}, bf16[512,512]{1,0:T(8,128)(2,1)S(1)}, u32[]{:S(2)}, u32[]{:S(2)}) collective-permute-start(bf16[512,512]{1,0:T(8,128)(2,1)S(1)} %slice.2469), channel_id=1, source_target_pairs={{0,16},{16,0},{1,17},{17,1},{2,18},{18,2},{3,19},{19,3},{4,20},{20... | collective-permute-start | bytes 1572872 | tf_op jit(solution)/shard_map/ppermute | solution.py:18
  725.1 46.8 %collective-permute-start.102 = (bf16[1024,256]{1,0:T(8,128)(2,1)S(1)}, bf16[1024,256]{1,0:T(8,128)(2,1)S(1)}, u32[]{:S(2)}, u32[]{:S(2)}) collective-permute-start(bf16[1024,256]{1,0:T(8,128)(2,1)S(1)} %convolution_convert_fusion.11), channel_id=1, source_target_pairs={{0,4},{4,0},{1,5},{5,1},{2,6},{6,2},{3,7},{7,3},{8,12},{12,8},{9,1... | collective-permute-start | bytes 1572872 | tf_op jit(solution)/shard_map/ppermute | solution.py:18
  773.6 30.2 %collective-permute-start.105 = (bf16[1024,256]{1,0:T(8,128)(2,1)S(1)}, bf16[1024,256]{1,0:T(8,128)(2,1)S(1)}, u32[]{:S(2)}, u32[]{:S(2)}) collective-permute-start(bf16[1024,256]{1,0:T(8,128)(2,1)S(1)} %convolution_convert_fusion.10), channel_id=1, source_target_pairs={{0,4},{4,0},{1,5},{5,1},{2,6},{6,2},{3,7},{7,3},{8,12},{12,8},{9,1... | collective-permute-start | bytes 1572872 | tf_op jit(solution)/shard_map/ppermute | solution.py:18
  773.8 33.8 %collective-permute-start.103 = (bf16[256,1024]{1,0:T(8,128)(2,1)S(1)}, bf16[256,1024]{1,0:T(8,128)(2,1)S(1)}, u32[]{:S(2)}, u32[]{:S(2)}) collective-permute-start(bf16[256,1024]{1,0:T(8,128)(2,1)S(1)} %select_convert_fusion.3), channel_id=1, source_target_pairs={{0,8},{8,0},{1,9},{9,1},{2,10},{10,2},{3,11},{11,3},{4,12},{12,4},... | collective-permute-start | bytes 1572872 | tf_op jit(solution)/shard_map/ppermute | solution.py:18
  775.8 33.0 %collective-permute-start.104 = (bf16[512,512]{1,0:T(8,128)(2,1)S(1)}, bf16[512,512]{1,0:T(8,128)(2,1)S(1)}, u32[]{:S(2)}, u32[]{:S(2)}) collective-permute-start(bf16[512,512]{1,0:T(8,128)(2,1)S(1)} %slice.2468), channel_id=1, source_target_pairs={{0,16},{16,0},{1,17},{17,1},{2,18},{18,2},{3,19},{19,3},{4,20},{20... | collective-permute-start | bytes 1572872 | tf_op jit(solution)/shard_map/ppermute | solution.py:18
  776.8 32.4 %collective-permute-start.109 = (bf16[1024,256]{1,0:T(8,128)(2,1)S(1)}, bf16[1024,256]{1,0:T(8,128)(2,1)S(1)}, u32[]{:S(2)}, u32[]{:S(2)}) collective-permute-start(bf16[1024,256]{1,0:T(8,128)(2,1)S(1)} %convolution_convert_fusion.9), channel_id=1, source_target_pairs={{0,4},{4,0},{1,5},{5,1},{2,6},{6,2},{3,7},{7,3},{8,12},{12,8},{9,1... | collective-permute-start | bytes 1572872 | tf_op jit(solution)/shard_map/ppermute | solution.py:18
  786.6 17.1 %collective-permute-start.114 = (bf16[256,256]{1,0:T(8,128)(2,1)S(1)}, bf16[256,256]{1,0:T(8,128)(2,1)S(1)}, u32[]{:S(2)}, u32[]{:S(2)}) collective-permute-start(bf16[256,256]{1,0:T(8,128)(2,1)S(1)} %select_convert_fusion.13), channel_id=1, source_target_pairs={{0,8},{8,0},{1,9},{9,1},{2,10},{10,2},{3,11},{11,3},{4,12},{12,4},... | collective-permute-start | bytes 393224 | tf_op jit(solution)/shard_map/ppermute | solution.py:18
  808.1 30.3 %collective-permute-start.106 = (bf16[128,2048]{1,0:T(8,128)(2,1)S(1)}, bf16[128,2048]{1,0:T(8,128)(2,1)S(1)}, u32[]{:S(2)}, u32[]{:S(2)}) collective-permute-start(bf16[128,2048]{1,0:T(8,128)(2,1)S(1)} %select_convert_fusion.2), channel_id=1, source_target_pairs={{0,2},{2,0},{1,3},{3,1},{4,6},{6,4},{5,7},{7,5},{8,10},{10,8},{9,1... | collective-permute-start | bytes 1572872 | tf_op jit(solution)/shard_map/ppermute | solution.py:18
  809.1 29.5 %collective-permute-start.107 = (bf16[256,1024]{1,0:T(8,128)(2,1)S(1)}, bf16[256,1024]{1,0:T(8,128)(2,1)S(1)}, u32[]{:S(2)}, u32[]{:S(2)}) collective-permute-start(bf16[256,1024]{1,0:T(8,128)(2,1)S(1)} %select_convert_fusion.1), channel_id=1, source_target_pairs={{0,8},{8,0},{1,9},{9,1},{2,10},{10,2},{3,11},{11,3},{4,12},{12,4},... | collective-permute-start | bytes 1572872 | tf_op jit(solution)/shard_map/ppermute | solution.py:18
  810.0 21.2 %collective-permute-start.110 = (bf16[512,256]{1,0:T(8,128)(2,1)S(1)}, bf16[512,256]{1,0:T(8,128)(2,1)S(1)}, u32[]{:S(2)}, u32[]{:S(2)}) collective-permute-start(bf16[512,256]{1,0:T(8,128)(2,1)S(1)} %slice.2481), channel_id=1, source_target_pairs={{0,16},{16,0},{1,17},{17,1},{2,18},{18,2},{3,19},{19,3},{4,20},{20... | collective-permute-start | bytes 786440 | tf_op jit(solution)/shard_map/ppermute | solution.py:18
  (250 other events, 3037.2 us)

commit v4 on v1

v4 whole, which is shorter than its diff:
```python
import math

import jax
import jax.numpy as jnp
from jax import lax
from jax.sharding import Mesh, PartitionSpec as P

HD = 128

EPSILON = 1e-06
NEGATIVE = -1e30
FLIP = [(0, 1), (1, 0)]
BF = jnp.bfloat16
F32 = jnp.float32


def swap(value, axis):
    return lax.ppermute(value, axis, FLIP)


def bit(axis):
    return lax.axis_index(axis)


def pick(axis, low, high):
    return jnp.where(bit(axis) == 0, low, high)


def ordered(axis, own, other, dim=0):
    return jnp.concatenate([pick(axis, own, other), pick(axis, other, own)], axis=dim)


def split(value, axis, dim):
    half = value.shape[dim] // 2
    low = lax.slice_in_dim(value, 0, half, axis=dim)
    high = lax.slice_in_dim(value, half, 2 * half, axis=dim)
    return pick(axis, low, high), pick(axis, high, low)


def dot(a, b):
    return jnp.dot(a, b, preferred_element_type=F32)


def dot_nt(a, b):
    return jnp.einsum("sc,rc->sr", a, b, preferred_element_type=F32)


def dot_tn(a, b):
    return jnp.einsum("sr,sc->rc", a, b, preferred_element_type=F32)


def rms_scale(values):
    return lax.rsqrt(jnp.mean(values * values, axis=1, keepdims=True) + EPSILON)


def build(high_bits):
    def to_relative(value):
        rows, width = value.shape
        count = 2 ** (len(high_bits) + 2)
        run = width // count
        pieces = [value[:, i * run : (i + 1) * run] for i in range(count)]
        names = list(high_bits) + ["zl", "x"]
        for position, name in enumerate(names):
            if name == "zl":
                continue
            mask = 1 << (len(names) - 1 - position)
            pieces = [pick(name, pieces[i], pieces[i ^ mask]) for i in range(count)]
        order = []
        for xr in range(2):
            for rest in range(count // 2):
                order.append(rest * 2 + xr)
        return jnp.concatenate([pieces[i] for i in order], axis=1)

    def to_natural(value):
        rows, width = value.shape
        count = 2 ** (len(high_bits) + 2)
        run = width // count
        moved = [value[:, i * run : (i + 1) * run] for i in range(count)]
        pieces = [None] * count
        place = 0
        for xr in range(2):
            for rest in range(count // 2):
                pieces[rest * 2 + xr] = moved[place]
                place += 1
        names = list(high_bits) + ["zl", "x"]
        for position, name in enumerate(names):
            if name == "zl":
                continue
            mask = 1 << (len(names) - 1 - position)
            pieces = [pick(name, pieces[i], pieces[i ^ mask]) for i in range(count)]
        return jnp.concatenate(pieces, axis=1)

    class Chain:
        def __init__(self, token):
            self.token = token
            self.zero = jnp.int32(0)

        def sync(self, *values):
            out = lax.optimization_barrier((self.token,) + values)
            self.token = out[0]
            return out[1] if len(values) == 1 else out[1:]

        def start(self, value, axis):
            return swap(self.sync(value), axis)

        def fence(self, *values):
            moved = self.sync(self.start(jnp.full((1, HD), bit("core"), jnp.int32), "core"))
            self.zero = self.zero + (moved[0, 0] + bit("core") - 1)
            return self.sync(*values)

    def gather_gains(c, gains):
        for name in ("tensor", "core", "zl"):
            sent = c.start(gains, name)
            yield
            gains = ordered(name, gains, c.sync(sent), dim=1)
        for name in list(high_bits)[::-1] + ["x"]:
            sent = c.start(gains, name)
            yield
            gains = jnp.concatenate([gains, c.sync(sent)], axis=1)
        return gains

    def pair_sum(c, values, between=None):
        count, width = values.shape
        for level, axis in ((1, "zl"), (2, "tensor"), (0, "core")):
            run = width >> (level + 1)
            other = c.sync(c.start(values, axis))
            blocks = [other[:, i * run : (i + 1) * run] for i in range(width // run)]
            values = values + jnp.concatenate([blocks[i ^ 1] for i in range(len(blocks))], axis=1)
            if between and axis == "zl":
                between()
        return values

    def scatter_gains(c, gains):
        for name in ["x"] + list(high_bits):
            half = gains.shape[1] // 2
            sent = c.start(gains[:, half:], name)
            yield
            gains = gains[:, :half] + c.sync(sent)
        for name in ("zl", "core", "tensor"):
            own, sent = split(gains, name, 1)
            sent = c.start(sent, name)
            yield
            gains = own + c.sync(sent)
        return gains

    class Steps:
        def __init__(self, stages):
            self.stages, self.done = stages, False
            self()

        def __call__(self):
            if not self.done:
                try:
                    next(self.stages)
                except StopIteration as end:
                    self.value, self.done = end.value, True

        def finish(self):
            while not self.done:
                self()
            return self.value

    def stack2(low, high):
        return jnp.concatenate([low, high], axis=0)

    def shards(
        tokens,
        segment_ids,
        w_query,
        w_key,
        w_value,
        w_output,
        w_gate,
        w_up,
        w_down,
        query_gain,
        key_gain,
        attn_gain,
        ffn_gain,
        cotangent,
    ):
        own_tokens, model_width = tokens.shape
        half_width = model_width // 2
        block_width = half_width // 2
        seq_length = own_tokens * 2
        core_tokens = seq_length * 2
        group_tokens = core_tokens * 2
        head_width = w_query.shape[1] // 4
        local_heads = head_width // HD
        score_scale = 1.0 / math.sqrt(HD)
        own, other = slice(0, core_tokens), slice(core_tokens, group_tokens)
        c = Chain(query_gain)

        def columns(parts):
            return parts[0] if len(parts) == 1 else jnp.concatenate(parts, axis=1)

        class Weight:
            def __init__(self, matrices, sent):
                width = sent.shape[1] // len(matrices)
                pairs = [
                    split(ordered("core", m, sent[:, i * width : (i + 1) * width]), "zl", 1)
                    for i, m in enumerate(matrices)
                ]
                self.own = columns([p[0] for p in pairs])
                self.sent = columns([p[1] for p in pairs])
                self.blocks = [[None, None], [None, None]]

            def start_line(self):
                self.line = c.start(self.sent, "zl")

            def end_line(self):
                rows = ordered("zl", self.own, c.sync(self.line))
                for name in high_bits[:0:-1]:
                    rows = stack2(rows, c.sync(c.start(rows, name)))
                self.blocks[0][0] = rows

            def start_high(self):
                self.high = c.start(self.blocks[0][0], high_bits[0])

            def end_high(self):
                self.blocks[0][1] = c.sync(self.high)

            def start_x(self, block):
                self.blocks[1][block] = c.start(self.blocks[0][block], "x")

            def end_x(self, block):
                self.blocks[1][block] = c.sync(self.blocks[1][block])

            def rows(self, side):
                return stack2(*self.blocks[side])

        attn_split = [split(w, "core", 1) for w in (w_query, w_key, w_value, w_output)]
        attn_sent = c.start(columns([s[1] for s in attn_split]), "core")
        gains = jnp.stack([query_gain, key_gain, attn_gain, ffn_gain])
        gain_steps = Steps(gather_gains(c, gains))
        tokens_rel = to_relative(tokens)
        left, right = tokens_rel[:, :half_width], tokens_rel[:, half_width:]
        left_sent = c.start(left, "tensor")
        ffn_split = [split(w, "core", 1) for w in (w_gate, w_up, w_down)]
        ffn_sent = c.start(columns([s[1] for s in ffn_split]), "core")
        gain_steps()

        attn_sent = c.sync(attn_sent)
        pair_width = 4 * head_width
        qk = Weight([s[0] for s in attn_split[:2]], attn_sent[:, :pair_width])
        vo = Weight([s[0] for s in attn_split[2:]], attn_sent[:, pair_width:])
        qk.start_line()
        gain_steps()
        ids = jnp.concatenate(
            [
                pick("tensor", segment_ids[:, :own_tokens], segment_ids[:, own_tokens:]),
                pick("tensor", segment_ids[:, own_tokens:], segment_ids[:, :own_tokens]),
            ],
            axis=1,
        )
        ids_sent = c.start(ids, "zl")
        right_sent = c.start(right, "zl")
        qk.end_line()
        gain_steps()
        qk.start_x(0)
        qk.start_high()
        vo.start_line()
        left = stack2(left, c.sync(left_sent))
        seq_ids = stack2(ids, c.sync(ids_sent))
        ids_sent = c.start(seq_ids, "core")
        right = stack2(right, c.sync(right_sent))

        def rows_second(left, right, between=None, last=None):
            left_sent = c.start(left, "zl")
            right_sent = c.start(right, "tensor")
            if between:
                between()
            left = stack2(left, c.sync(left_sent))
            right_sent = c.sync(right_sent)
            rows = own_tokens
            right = jnp.concatenate(
                [right[:rows], right_sent[:rows], right[rows:], right_sent[rows:]], axis=0
            )
            if last:
                last()
            left_sent = c.start(left, "core")
            right_sent = c.start(right, "core")
            return stack2(left, c.sync(left_sent)), stack2(right, c.sync(right_sent))

        def gather_rows(value, between=None):
            left, right = value[:, :half_width], value[:, half_width:]
            left_sent = c.start(left, "tensor")
            right_sent = c.start(right, "zl")
            left = stack2(left, c.sync(left_sent))
            right = stack2(right, c.sync(right_sent))
            return rows_second(left, right, between)

        ffn_sent = c.sync(ffn_sent)
        width = ffn_sent.shape[1] // 3
        gate_w, up_w, down_w = [
            Weight([s[0]], ffn_sent[:, i * width : (i + 1) * width])
            for i, s in enumerate(ffn_split)
        ]

        def tokens_between():
            vo.end_line()
            gate_w.start_line()
            gain_steps()
            qk.end_x(0)
            vo.start_x(0)

        def tokens_last():
            qk.end_high()
            qk.start_x(1)
            vo.start_high()

        in0, in1 = rows_second(left, right, tokens_between, tokens_last)
        seq_ids = stack2(seq_ids, c.sync(ids_sent))
        gate_w.end_line()
        gate_w.start_x(0)
        gains = gain_steps.finish()
        qk.end_x(1)

        attn_scale = gains[2]
        ffn_scale = gains[3]
        head_gains = to_natural(gains[:2])
        head_start = (bit("tensor") * 4 + bit("core") * 2 + bit("zl")) * head_width
        head_gains = lax.dynamic_slice_in_dim(head_gains, head_start, head_width, axis=1)
        query_scale, key_scale = head_gains[0], head_gains[1]
        tokens_f = tokens_rel.astype(F32)
        d_out = to_relative(cotangent).astype(F32)
        places = jnp.arange(own_tokens)
        positions = jnp.concatenate(
            [places + bit("tensor") * own_tokens, places + (1 - bit("tensor")) * own_tokens]
        )
        visible = (positions[:, None] >= positions[None, :])[None] & (
            seq_ids[:, :, None] == seq_ids[:, None, :]
        )
        visible = visible[:, None]

        wqk0, wqk1 = qk.rows(0), qk.rows(1)
        projected = dot(in0, wqk0) + dot(in1, wqk1)
        query, key_proj = projected[:, :head_width], projected[:, head_width:]
        squares = pair_sum(
            c,
            jnp.stack([jnp.sum(query * query, axis=1), jnp.sum(key_proj * key_proj, axis=1)]),
            up_w.start_line,
        )
        q_rms = lax.rsqrt(squares[0] / model_width + EPSILON)[:, None]
        k_rms = lax.rsqrt(squares[1] / model_width + EPSILON)[:, None]
        normed_query = (query * q_rms * query_scale).astype(BF)
        normed_key = (key_proj * k_rms * key_scale).astype(BF)
        vo.end_high()
        vo.end_x(0)
        vo.start_x(1)
        gate_w.start_high()
        up_w.end_line()
        down_w.start_line()
        gate_w.end_x(0)
        up_w.start_x(0)
        vo.end_x(1)
        normed_query, normed_key = c.sync(normed_query, normed_key)
        wvo0, wvo1 = vo.rows(0), vo.rows(1)
        wv0, wo0 = wvo0[:, :head_width], wvo0[:, head_width:]
        wv1, wo1 = wvo1[:, :head_width], wvo1[:, head_width:]
        value_bf = (dot(in0, wv0) + dot(in1, wv1)).astype(BF)
        heads = (4, seq_length, local_heads, HD)
        query_heads = normed_query.reshape(heads)
        key_heads = normed_key.reshape(heads)
        value_heads = value_bf.reshape(heads)
        scores = (
            jnp.einsum("bqhd,bkhd->bhqk", query_heads, key_heads, preferred_element_type=F32)
            * score_scale
        )
        scores = jnp.where(visible, scores, NEGATIVE)
        peak = jnp.max(scores, axis=-1, keepdims=True)
        expo = jnp.exp(scores - peak)
        total = jnp.sum(expo, axis=-1, keepdims=True)
        prob = expo / total
        prob_bf = prob.astype(BF)
        attn_heads = jnp.einsum(
            "bhqk,bkhd->bqhd", prob_bf, value_heads, preferred_element_type=F32
        ).astype(BF)
        attn = attn_heads.reshape(group_tokens, head_width)
        down_w.end_line()
        gate_w.end_high()
        gate_w.start_x(1)
        up_w.start_high()
        up_w.end_x(0)

        def halve(total, axis):
            half = total.shape[0] // 2
            return total[:half], c.start(total[half:].astype(BF), axis)

        def added(pair):
            return pair[0] + c.sync(pair[1]).astype(F32)

        def cross(total):
            rows = own_tokens
            own = stack2(total[:rows], total[2 * rows : 3 * rows])
            sent = stack2(total[rows : 2 * rows], total[3 * rows :])
            return own, c.start(sent.astype(BF), "tensor")

        def scatter_rows(left_of, right_of, first=None, second=None):
            left_sent = c.start(left_of(other).astype(BF), "core")
            right_sent = c.start(right_of(other).astype(BF), "core")
            left = halve(left_of(own) + c.sync(left_sent).astype(F32), "zl")
            right = cross(right_of(own) + c.sync(right_sent).astype(F32))
            if first:
                first()
            left, right = added(left), added(right)
            left, right = halve(left, "tensor"), halve(right, "zl")
            if second:
                second()
            return added(left), added(right)

        def first_down():
            down_w.start_x(0)

        proj = columns(
            scatter_rows(
                lambda rows: dot_nt(attn[rows], wo0), lambda rows: dot_nt(attn[rows], wo1), first_down
            )
        )
        attn_rms = rms_scale(proj)
        resid = tokens_f + proj * attn_rms * attn_scale

        def resid_between():
            gate_w.end_x(1)
            down_w.end_x(0)

        resid_bf = c.sync(resid.astype(BF))
        up_w.end_high()
        up_w.start_x(1)
        down_w.start_high()
        h0, h1 = gather_rows(resid_bf, resid_between)
        wg0, wg1 = gate_w.rows(0), gate_w.rows(1)
        gate = dot(h0, wg0) + dot(h1, wg1)
        gate = c.sync(gate)
        sigma = jax.nn.sigmoid(gate)
        down_w.end_high()
        down_w.start_x(1)
        up_w.end_x(1)
        wu0, wu1 = up_w.rows(0), up_w.rows(1)
        up = dot(h0, wu0) + dot(h1, wu1)
        act = (gate * sigma * up).astype(BF)

        wd0 = down_w.rows(0)
        first_rows = down_w.blocks[1][0]
        left, right = scatter_rows(
            lambda rows: dot_nt(act[rows], wd0), lambda rows: dot_nt(act[rows], first_rows)
        )
        down_w.end_x(1)
        last_rows = down_w.blocks[1][1]
        sent = c.start(dot_nt(act[other], last_rows).astype(BF), "core")
        last = cross(dot_nt(act[own], last_rows) + c.sync(sent).astype(F32))
        last = halve(added(last), "zl")
        ffn = columns([left, right, added(last)])
        wd1 = down_w.rows(1)

        ffn_rms = rms_scale(ffn)
        output = to_natural((resid + ffn * ffn_rms * ffn_scale).astype(BF))
        ffn_gain_term = jnp.sum(d_out * ffn * ffn_rms, axis=0)
        scaled_out = d_out * ffn_scale
        d_ffn = (
            ffn_rms
            * (
                scaled_out
                - ffn * ffn_rms * ffn_rms * jnp.mean(scaled_out * ffn, axis=1, keepdims=True)
            )
        ).astype(BF)
        f0, f1 = gather_rows(d_ffn)

        class Grad:
            def __init__(self, *terms):
                self.terms = terms
                self.x, self.total = [None, None], [None, None]

            def product(self, side, block):
                cols = slice(block * block_width, (block + 1) * block_width)
                return columns([dot_tn(halves[side][:, cols], r) for halves, r in self.terms])

            def start_x(self, block):
                self.x[block] = c.start(self.product(1, block).astype(BF), "x")

            def end_x(self, block):
                moved = c.sync(self.x[block])
                self.total[block] = self.product(0, block) + moved.astype(F32)

            def start_high(self):
                self.high = c.start(self.total[1].astype(BF), high_bits[0])

            def end_high(self):
                total = self.total[0] + c.sync(self.high).astype(F32)
                for name in high_bits[1:]:
                    total = added(halve(total, name))
                self.own, self.sent = split(total, "zl", 0)

            def start_line(self):
                self.line = c.start(self.sent.astype(BF), "zl")

            def joined(self, axis, moved):
                width = moved.shape[1] // len(self.terms)
                cols = [slice(i * width, (i + 1) * width) for i in range(len(self.terms))]
                return [ordered(axis, self.own[:, s], moved[:, s], dim=1) for s in cols]

            def end_line(self):
                moved = c.sync(self.line).astype(F32)
                self.own, sent = split(columns(self.joined("zl", moved)), "core", 0)
                self.core = c.start(sent.astype(BF), "core")

            def end(self):
                self.results = self.joined("core", c.sync(self.core).astype(F32))

        down_grad = Grad(((f0, f1), act))
        down_grad.start_x(1)
        down_grad.start_x(0)
        f0, f1 = c.fence(f0, f1)
        d_act = dot(f0, wd0) + dot(f1, wd1)
        d_gate = (d_act * up * sigma * (1.0 + gate * (1.0 - sigma))).astype(BF)
        d_up = (d_act * gate * sigma).astype(BF)
        gate_grad = Grad(((h0, h1), d_gate))
        up_grad = Grad(((h0, h1), d_up))
        down_grad.end_x(1)
        down_grad.start_high()
        gate_grad.start_x(1)

        def hidden_first():
            down_grad.end_x(0)
            gate_grad.start_x(0)

        d_resid = d_out + columns(
            scatter_rows(
                lambda rows: dot_nt(d_gate[rows], wg0) + dot_nt(d_up[rows], wu0),
                lambda rows: dot_nt(d_gate[rows], wg1) + dot_nt(d_up[rows], wu1),
                hidden_first,
            )
        )
        attn_gain_term = jnp.sum(d_resid * proj * attn_rms, axis=0)
        scaled_resid = d_resid * attn_scale
        d_proj = (
            attn_rms
            * (
                scaled_resid
                - proj * attn_rms * attn_rms * jnp.mean(scaled_resid * proj, axis=1, keepdims=True)
            )
        ).astype(BF)
        gate_grad.end_x(1)
        up_grad.start_x(1)

        d_proj = c.sync(d_proj)
        down_grad.end_high()
        gate_grad.start_high()

        def proj_between():
            down_grad.start_line()

        p0, p1 = gather_rows(d_proj, proj_between)
        gate_grad.end_x(0)
        up_grad.start_x(0)
        p0, p1 = c.fence(p0, p1)
        d_attn = (dot(p0, wo0) + dot(p1, wo1)).astype(BF)

        d_attn_heads = d_attn.reshape(heads)
        d_value = (
            jnp.einsum("bhqk,bqhd->bkhd", prob_bf, d_attn_heads, preferred_element_type=F32)
            .reshape(group_tokens, head_width)
            .astype(BF)
        )
        d_prob = jnp.einsum(
            "bqhd,bkhd->bhqk", d_attn_heads, value_heads, preferred_element_type=F32
        )
        delta = jnp.einsum(
            "bqhd,bqhd->bhq", d_attn_heads, attn.reshape(heads), preferred_element_type=F32
        )[..., None]
        d_score = (prob * (d_prob - delta)).astype(BF)
        d_nq = (
            jnp.einsum("bhqk,bkhd->bqhd", d_score, key_heads, preferred_element_type=F32).reshape(
                group_tokens, head_width
            )
            * score_scale
        )
        d_nk = (
            jnp.einsum("bhqk,bqhd->bkhd", d_score, query_heads, preferred_element_type=F32).reshape(
                group_tokens, head_width
            )
            * score_scale
        )
        query_gain_term = jnp.sum(d_nq * query * q_rms, axis=0)
        key_gain_term = jnp.sum(d_nk * key_proj * k_rms, axis=0)
        scaled_q = d_nq * query_scale
        scaled_k = d_nk * key_scale
        zero = jnp.zeros((2, model_width), F32)
        placed = lax.dynamic_update_slice_in_dim(
            zero, jnp.stack([query_gain_term, key_gain_term]), head_start + c.zero, 1
        )
        gain_parts = jnp.concatenate(
            [to_relative(placed), jnp.stack([attn_gain_term, ffn_gain_term])], axis=0
        )
        gain_steps = Steps(scatter_gains(c, gain_parts))
        up_grad.end_x(1)
        down_grad.end_line()
        inner = pair_sum(
            c, jnp.stack([jnp.sum(scaled_q * query, axis=1), jnp.sum(scaled_k * key_proj, axis=1)])
        )
        gain_steps()
        d_query = (
            q_rms * (scaled_q - query * q_rms * q_rms * (inner[0] / model_width)[:, None])
        ).astype(BF)
        d_key = (
            k_rms * (scaled_k - key_proj * k_rms * k_rms * (inner[1] / model_width)[:, None])
        ).astype(BF)
        d_qk = columns([d_query, d_key])
        ov_grad = Grad(((p0, p1), attn), ((in0, in1), d_value))
        qk_grad = Grad(((in0, in1), d_query), ((in0, in1), d_key))
        gate_grad.end_high()
        gain_steps()
        up_grad.start_high()
        ov_grad.start_x(1)
        down_grad.end()

        def tokens_first():
            up_grad.end_x(0)
            qk_grad.start_x(1)
            gate_grad.start_line()
            ov_grad.end_x(1)
            ov_grad.start_x(0)

        def tokens_second():
            gain_steps()
            qk_grad.end_x(1)
            qk_grad.start_x(0)

        d_tokens = columns(
            scatter_rows(
                lambda rows: dot_nt(d_qk[rows], wqk0) + dot_nt(d_value[rows], wv0),
                lambda rows: dot_nt(d_qk[rows], wqk1) + dot_nt(d_value[rows], wv1),
                tokens_first,
                tokens_second,
            )
        )
        grad_tokens = to_natural(d_resid + d_tokens)
        gate_grad.end_line()
        gain_steps()
        ov_grad.end_x(0)
        up_grad.end_high()
        ov_grad.start_high()
        up_grad.start_line()
        gate_grad.end()
        qk_grad.end_x(0)
        qk_grad.start_high()
        gain_parts = gain_steps.finish()
        up_grad.end_line()
        ov_grad.end_high()
        ov_grad.start_line()
        up_grad.end()
        ov_grad.end_line()
        qk_grad.end_high()
        qk_grad.start_line()
        ov_grad.end()
        qk_grad.end_line()
        qk_grad.end()
        grad_output, grad_value = ov_grad.results
        grad_query, grad_key = qk_grad.results
        return (
            output,
            grad_tokens,
            grad_query,
            grad_key,
            grad_value,
            grad_output,
            gate_grad.results[0],
            up_grad.results[0],
            down_grad.results[0],
            gain_parts[0],
            gain_parts[1],
            gain_parts[2],
            gain_parts[3],
        )

    return shards


def solution(mesh):
    dp = mesh.shape["dp"]
    high = max(dp.bit_length() - 4, 0)
    high_bits = tuple(f"z{i}" for i in range(high))
    names = high_bits + ("zl", "x", "core", "tensor")
    fine = Mesh(mesh.devices.reshape((2,) * len(names)), names)
    rows = names[:-1]
    both = names
    mapped = jax.shard_map(
        build(high_bits),
        mesh=fine,
        in_specs=(
            P(both, None),
            P(rows, None),
            P(rows, "tensor"),
            P(rows, "tensor"),
            P(rows, "tensor"),
            P(rows, "tensor"),
            P(rows, "tensor"),
            P(rows, "tensor"),
            P(rows, "tensor"),
            P(both),
            P(both),
            P(both),
            P(both),
            P(both, None),
        ),
        out_specs=(
            P(both, None),
            P(both, None),
            P(rows, "tensor"),
            P(rows, "tensor"),
            P(rows, "tensor"),
            P(rows, "tensor"),
            P(rows, "tensor"),
            P(rows, "tensor"),
            P(rows, "tensor"),
            P(both),
            P(both),
            P(both),
            P(both),
        ),
        check_vma=False,
    )
    return mapped
```

time: 949 us -> 782 us (0.82)
  waiting for transfers between devices: 605 us -> 401 us
  matrix products: 100 us -> 137 us
  local copies, waits for them, and re-layouts: 42.2 us -> 61.7 us
  other arithmetic: 82.8 us -> 63.4 us
    ppermute x101 -> x118, waiting for transfers between devices: 605 us -> 401 us  [swap(): return lax.ppermute(value, axis, FLIP)]
    dot_general x14 -> x28, matrix products: 30.2 us -> 48.5 us  [dot_tn(): return jnp.einsum('sr,sc->rc', a, b, preferred_element_type=F32)]
    dot_general x22 -> x26, matrix products: 26.5 us -> 44.3 us  [dot_nt(): return jnp.einsum('sc,rc->sr', a, b, preferred_element_type=F32)]
    concatenate x31 -> x41, other arithmetic: 35.1 us -> 18.9 us  [the longest x24 13.1 us: stack2(): return jnp.concatenate([low, high], axis=0)]
    unnamed x296 -> x498, local copies, waits for them, and re-layouts: 25 us -> 33.8 us
    select_n x50 -> x41, other arithmetic: 19.3 us -> 13.5 us  [pick(): return jnp.where(bit(axis) == 0, low, high)]
    dot_general x14 -> x12, matrix products: 34.8 us -> 31.1 us  [dot(): return jnp.dot(a, b, preferred_element_type=F32)]
    ppermute x101 -> x118, starting transfers between devices: 103 us -> 105 us  [swap(): return lax.ppermute(value, axis, FLIP)]
  transfers between devices with their start and end apart: 101 -> 118, of which waited for: 51 -> 53; matrix products, arithmetic and copies ran while one was open for 19% -> 27% of each run, Pallas kernels for 0% -> 0%
where the time goes in v4:
time: 782 us; the launch traced here: 774 us
  waiting for transfers between devices  401 us (51%)
  matrix products  137 us (18%)
  starting transfers between devices  105 us (13%)
  other arithmetic  63.4 us (8%)
  local copies, waits for them, and re-layouts  61.7 us (8%)
    ppermute x118, waiting for transfers between devices, swap(): return lax.ppermute(value, axis, FLIP)  401 us
    ppermute x118, starting transfers between devices, swap(): return lax.ppermute(value, axis, FLIP)  105 us
    dot_general x28, matrix products, dot_tn(): return jnp.einsum('sr,sc->rc', a, b, preferred_element_type=F32)  48.5 us
    dot_general x26, matrix products, dot_nt(): return jnp.einsum('sc,rc->sr', a, b, preferred_element_type=F32)  44.3 us
    unnamed x498, local copies, waits for them, and re-layouts  33.8 us
    dot_general x12, matrix products, dot(): return jnp.dot(a, b, preferred_element_type=F32)  31.1 us
  transfers between devices with their start and end apart: 118, of which 53 were waited for; matrix products, arithmetic and copies ran while one was open for 27% of the time, Pallas kernels for 0%

profile of v4, /device:TPU:0, one launch (start us, length us, event | category | flops | bytes accessed | tf_op | source)
XLA Modules:
  0.0 773.8 jit_solution(13303376133258587617)
XLA Ops:
  5.5 3.1 collective-permute-start
  20.0 4.9 collective-permute-done.3
  27.3 5.3 collective-permute-done.7
  44.7 4.0 collective-permute-done.11
  50.4 12.6 %collective-permute-done.12 = bf16[256,1024]{1,0:T(8,128)(2,1)S(1)} collective-permute-done((bf16[256,1024]{1,0:T(8,128)(2,1)S(1)}, bf16[256,1024]{1,0:T(8,128)(2,1)S(1)}, u32[]{:S(2)}, u32[]{:S(2)}) %collective-permute-start.12) | collective-permute-done | bytes 524320 | tf_op jit(solution)/shard_map/ppermute | solution.py:18
  78.7 9.8 %collective-permute-done.18 = bf16[256,1024]{1,0:T(8,128)(2,1)S(1)} collective-permute-done((bf16[256,1024]{1,0:T(8,128)(2,1)}, bf16[256,1024]{1,0:T(8,128)(2,1)S(1)}, u32[]{:S(2)}, u32[]{:S(2)}) %collective-permute-start.18) | collective-permute-done | bytes 524320 | tf_op jit(solution)/shard_map/ppermute | solution.py:18
  90.0 3.0 pad_maximum_fusion
  113.1 17.0 %collective-permute-done.26 = bf16[256,1024]{1,0:T(8,128)(2,1)S(1)} collective-permute-done((bf16[256,1024]{1,0:T(8,128)(2,1)S(1)}, bf16[256,1024]{1,0:T(8,128)(2,1)S(1)}, u32[]{:S(2)}, u32[]{:S(2)}) %collective-permute-start.26) | collective-permute-done | bytes 524320 | tf_op jit(solution)/shard_map/ppermute | solution.py:18
  131.8 3.3 collective-permute-done.28
  142.8 3.4 add_convert_fusion.8
  146.2 3.4 fusion.228
  169.4 10.0 %collective-permute-done.34 = bf16[256,1024]{1,0:T(8,128)(2,1)S(1)} collective-permute-done((bf16[256,1024]{1,0:T(8,128)(2,1)S(1)}, bf16[256,1024]{1,0:T(8,128)(2,1)S(1)}, u32[]{:S(2)}, u32[]{:S(2)}) %collective-permute-start.34) | collective-permute-done | bytes 524320 | tf_op jit(solution)/shard_map/ppermute | solution.py:18
  188.2 5.9 collective-permute-done.37
  195.2 34.6 %collective-permute-done.38 = bf16[512,1024]{1,0:T(8,128)(2,1)S(1)} collective-permute-done((bf16[512,1024]{1,0:T(8,128)(2,1)}, bf16[512,1024]{1,0:T(8,128)(2,1)S(1)}, u32[]{:S(2)}, u32[]{:S(2)}) %collective-permute-start.38) | collective-permute-done | bytes 1048608 | tf_op jit(solution)/shard_map/ppermute | solution.py:18
  230.9 5.3 collective-permute-done.39
  239.3 9.2 %collective-permute-done.43 = bf16[256,1024]{1,0:T(8,128)(2,1)S(1)} collective-permute-done((bf16[256,1024]{1,0:T(8,128)(2,1)S(1)}, bf16[256,1024]{1,0:T(8,128)(2,1)S(1)}, u32[]{:S(2)}, u32[]{:S(2)}) %collective-permute-start.43) | collective-permute-done | bytes 524320 | tf_op jit(solution)/shard_map/ppermute | solution.py:18
  258.9 3.6 fusion.202
  262.5 36.8 %collective-permute-done.47 = bf16[512,1024]{1,0:T(8,128)(2,1)S(1)} collective-permute-done((bf16[512,1024]{1,0:T(8,128)(2,1)S(1)}, bf16[512,1024]{1,0:T(8,128)(2,1)S(1)}, u32[]{:S(2)}, u32[]{:S(2)}) %collective-permute-start.47) | collective-permute-done | bytes 1048608 | tf_op jit(solution)/shard_map/ppermute | solution.py:18
  301.9 4.9 multiply_convert_fusion.2
  314.8 12.4 %collective-permute-done.51 = bf16[256,1024]{1,0:T(8,128)(2,1)S(1)} collective-permute-done((bf16[256,1024]{1,0:T(8,128)(2,1)S(1)}, bf16[256,1024]{1,0:T(8,128)(2,1)S(1)}, u32[]{:S(2)}, u32[]{:S(2)}) %collective-permute-start.51) | collective-permute-done | bytes 524320 | tf_op jit(solution)/shard_map/ppermute | solution.py:18
  328.9 5.7 collective-permute-done.53
  339.4 7.3 collective-permute-done.57
  347.3 4.5 collective-permute-done.58
  354.9 5.0 collective-permute-done.59
  362.8 9.3 %collective-permute-done.61 = bf16[256,1024]{1,0:T(8,128)(2,1)S(1)} collective-permute-done((bf16[256,1024]{1,0:T(8,128)(2,1)S(1)}, bf16[256,1024]{1,0:T(8,128)(2,1)S(1)}, u32[]{:S(2)}, u32[]{:S(2)}) %collective-permute-start.61) | collective-permute-done | bytes 524320 | tf_op jit(solution)/shard_map/ppermute | solution.py:18
  379.1 3.0 pad_maximum_fusion.1
  384.3 3.5 convolution_convert_fusion.5
  387.8 3.6 convolution_convert_fusion.4
  397.6 4.1 fusion.1
  402.3 4.3 multiply_convert_fusion
  414.6 4.0 fusion.59
  426.3 4.0 add_convert_fusion.4
  452.8 7.0 collective-permute-done.70
  472.0 5.0 collective-permute-done.74
  478.0 34.5 %collective-permute-done.75 = bf16[512,1024]{1,0:T(8,128)(2,1)S(1)} collective-permute-done((bf16[512,1024]{1,0:T(8,128)(2,1)S(1)}, bf16[512,1024]{1,0:T(8,128)(2,1)S(1)}, u32[]{:S(2)}, u32[]{:S(2)}) %collective-permute-start.75) | collective-permute-done | bytes 1048608 | tf_op jit(solution)/shard_map/ppermute | solution.py:18
  517.6 3.0 collective-permute-start.90
  522.4 4.8 collective-permute-done.77
  529.6 24.2 %collective-permute-done.78 = bf16[256,1024]{1,0:T(8,128)(2,1)S(1)} collective-permute-done((bf16[256,1024]{1,0:T(8,128)(2,1)S(1)}, bf16[256,1024]{1,0:T(8,128)(2,1)S(1)}, u32[]{:S(2)}, u32[]{:S(2)}) %collective-permute-start.78) | collective-permute-done | bytes 524320 | tf_op jit(solution)/shard_map/ppermute | solution.py:18
  573.9 2.9 fusion.9
  596.0 3.0 fusion.137
  608.1 3.5 add_convert_fusion.2
  644.3 8.5 %collective-permute-done.108 = bf16[512,512]{0,1:T(8,128)(2,1)S(1)} collective-permute-done((bf16[512,512]{0,1:T(8,128)(2,1)S(1)}, bf16[512,512]{0,1:T(8,128)(2,1)S(1)}, u32[]{:S(2)}, u32[]{:S(2)}) %collective-permute-start.108) | collective-permute-done | bytes 524320 | tf_op jit(solution)/shard_map/ppermute | solution.py:18
  654.0 30.3 %collective-permute-done.106 = bf16[512,1024]{1,0:T(8,128)(2,1)S(1)} collective-permute-done((bf16[512,1024]{1,0:T(8,128)(2,1)S(1)}, bf16[512,1024]{1,0:T(8,128)(2,1)S(1)}, u32[]{:S(2)}, u32[]{:S(2)}) %collective-permute-start.106) | collective-permute-done | bytes 1048608 | tf_op jit(solution)/shard_map/ppermute | solution.py:18
  692.8 16.5 %collective-permute-done.97 = bf16[256,1024]{1,0:T(8,128)(2,1)S(1)} collective-permute-done((bf16[256,1024]{1,0:T(8,128)(2,1)S(1)}, bf16[256,1024]{1,0:T(8,128)(2,1)S(1)}, u32[]{:S(2)}, u32[]{:S(2)}) %collective-permute-start.97) | collective-permute-done | bytes 524320 | tf_op jit(solution)/shard_map/ppermute | solution.py:18
  716.6 20.0 %collective-permute-done.103 = bf16[256,1024]{1,0:T(8,128)(2,1)S(1)} collective-permute-done((bf16[256,1024]{1,0:T(8,128)(2,1)S(1)}, bf16[256,1024]{1,0:T(8,128)(2,1)S(1)}, u32[]{:S(2)}, u32[]{:S(2)}) %collective-permute-start.103) | collective-permute-done | bytes 524320 | tf_op jit(solution)/shard_map/ppermute | solution.py:18
  737.0 10.8 %collective-permute-done.115 = bf16[256,1024]{1,0:T(8,128)(2,1)S(1)} collective-permute-done((bf16[256,1024]{1,0:T(8,128)(2,1)S(1)}, bf16[256,1024]{1,0:T(8,128)(2,1)S(1)}, u32[]{:S(2)}, u32[]{:S(2)}) %collective-permute-start.115) | collective-permute-done | bytes 524320 | tf_op jit(solution)/shard_map/ppermute | solution.py:18
  748.4 5.1 collective-permute-done.102
  754.2 4.4 collective-permute-done.113
  (1051 shorter events, 334.4 us)
Async XLA Ops:
  11.5 28.2 %collective-permute-start.8 = (bf16[128,6144]{1,0:T(8,128)(2,1)}, bf16[128,6144]{1,0:T(8,128)(2,1)}, u32[]{:S(2)}, u32[]{:S(2)}) collective-permute-start(bf16[128,6144]{1,0:T(8,128)(2,1)} %pad_maximum_fusion.10), channel_id=1, source_target_pairs={{0,2},{2,0},{1,3},{3,1},{4,6},{6,4},{5,7},{7,5},{8,10},{10,8},{9,1... | collective-permute-start | bytes 4718600 | tf_op jit(solution)/shard_map/ppermute | solution.py:18
  38.3 24.8 %collective-permute-start.14 = (bf16[512,512]{0,1:T(8,128)(2,1)S(1)}, bf16[512,512]{0,1:T(8,128)(2,1)S(1)}, u32[]{:S(2)}, u32[]{:S(2)}) collective-permute-start(bf16[512,512]{0,1:T(8,128)(2,1)S(1)} %pad_maximum_fusion.36), channel_id=1, source_target_pairs={{0,16},{16,0},{1,17},{17,1},{2,18},{18,2},{3,19},{19,3},{4,20},{20... | collective-permute-start | bytes 1572872 | tf_op jit(solution)/shard_map/ppermute | solution.py:18
  41.4 21.6 %collective-permute-start.12 = (bf16[256,1024]{1,0:T(8,128)(2,1)S(1)}, bf16[256,1024]{1,0:T(8,128)(2,1)S(1)}, u32[]{:S(2)}, u32[]{:S(2)}) collective-permute-start(bf16[256,1024]{1,0:T(8,128)(2,1)S(1)} %pad_maximum_fusion.37), channel_id=1, source_target_pairs={{0,8},{8,0},{1,9},{9,1},{2,10},{10,2},{3,11},{11,3},{4,12},{12,4},... | collective-permute-start | bytes 1572872 | tf_op jit(solution)/shard_map/ppermute | solution.py:18
  41.9 21.1 %collective-permute-start.13 = (bf16[256,1024]{1,0:T(8,128)(2,1)S(1)}, bf16[256,1024]{1,0:T(8,128)(2,1)S(1)}, u32[]{:S(2)}, u32[]{:S(2)}) collective-permute-start(bf16[256,1024]{1,0:T(8,128)(2,1)S(1)} %pad_maximum_fusion.38), channel_id=1, source_target_pairs={{0,1},{1,0},{2,3},{3,2},{4,5},{5,4},{6,7},{7,6},{8,9},{9,8},{10,11... | collective-permute-start | bytes 1572872 | tf_op jit(solution)/shard_map/ppermute | solution.py:18
  69.1 19.4 %collective-permute-start.18 = (bf16[256,1024]{1,0:T(8,128)(2,1)}, bf16[256,1024]{1,0:T(8,128)(2,1)S(1)}, u32[]{:S(2)}, u32[]{:S(2)}) collective-permute-start(bf16[256,1024]{1,0:T(8,128)(2,1)} %broadcast_select_fusion.11), channel_id=1, source_target_pairs={{0,8},{8,0},{1,9},{9,1},{2,10},{10,2},{3,11},{11,3},{4,12},{12,4},... | collective-permute-start | bytes 1572872 | tf_op jit(solution)/shard_map/ppermute | solution.py:18
  71.4 18.5 %collective-permute-start.20 = (bf16[512,512]{0,1:T(8,128)(2,1)S(1)}, bf16[512,512]{0,1:T(8,128)(2,1)S(1)}, u32[]{:S(2)}, u32[]{:S(2)}) collective-permute-start(bf16[512,512]{0,1:T(8,128)(2,1)S(1)} %copy-done.176), channel_id=1, source_target_pairs={{0,4},{4,0},{1,5},{5,1},{2,6},{6,2},{3,7},{7,3},{8,12},{12,8},{9,1... | collective-permute-start | bytes 1572872 | tf_op jit(solution)/shard_map/ppermute | solution.py:18
  74.6 33.4 %collective-permute-start.25 = (bf16[512,512]{0,1:T(8,128)(2,1)S(1)}, bf16[512,512]{0,1:T(8,128)(2,1)S(1)}, u32[]{:S(2)}, u32[]{:S(2)}) collective-permute-start(bf16[512,512]{0,1:T(8,128)(2,1)S(1)} %copy-done.165), channel_id=1, source_target_pairs={{0,4},{4,0},{1,5},{5,1},{2,6},{6,2},{3,7},{7,3},{8,12},{12,8},{9,1... | collective-permute-start | bytes 1572872 | tf_op jit(solution)/shard_map/ppermute | solution.py:18
  76.1 31.9 %collective-permute-start.24 = (bf16[512,512]{0,1:T(8,128)(2,1)S(1)}, bf16[512,512]{0,1:T(8,128)(2,1)S(1)}, u32[]{:S(2)}, u32[]{:S(2)}) collective-permute-start(bf16[512,512]{0,1:T(8,128)(2,1)S(1)} %copy-done.165), channel_id=1, source_target_pairs={{0,16},{16,0},{1,17},{17,1},{2,18},{18,2},{3,19},{19,3},{4,20},{20... | collective-permute-start | bytes 1572872 | tf_op jit(solution)/shard_map/ppermute | solution.py:18
  99.3 32.4 %collective-permute-start.27 = (bf16[512,1024]{1,0:T(8,128)(2,1)}, bf16[512,1024]{1,0:T(8,128)(2,1)S(1)}, u32[]{:S(2)}, u32[]{:S(2)}) collective-permute-start(bf16[512,1024]{1,0:T(8,128)(2,1)} %pad_maximum_fusion.16), channel_id=1, source_target_pairs={{0,4},{4,0},{1,5},{5,1},{2,6},{6,2},{3,7},{7,3},{8,12},{12,8},{9,1... | collective-permute-start | bytes 3145736 | tf_op jit(solution)/shard_map/ppermute | solution.py:18
  106.9 23.2 %collective-permute-start.26 = (bf16[256,1024]{1,0:T(8,128)(2,1)S(1)}, bf16[256,1024]{1,0:T(8,128)(2,1)S(1)}, u32[]{:S(2)}, u32[]{:S(2)}) collective-permute-start(bf16[256,1024]{1,0:T(8,128)(2,1)S(1)} %broadcast_select_fusion.7), channel_id=1, source_target_pairs={{0,8},{8,0},{1,9},{9,1},{2,10},{10,2},{3,11},{11,3},{4,12},{12,4},... | collective-permute-start | bytes 1572872 | tf_op jit(solution)/shard_map/ppermute | solution.py:18
  108.0 27.0 %collective-permute-start.28 = (bf16[512,512]{0,1:T(8,128)(2,1)S(1)}, bf16[512,512]{0,1:T(8,128)(2,1)S(1)}, u32[]{:S(2)}, u32[]{:S(2)}) collective-permute-start(bf16[512,512]{0,1:T(8,128)(2,1)S(1)} %collective-permute-done.24), channel_id=1, source_target_pairs={{0,4},{4,0},{1,5},{5,1},{2,6},{6,2},{3,7},{7,3},{8,12},{12,8},{9,1... | collective-permute-start | bytes 1572872 | tf_op jit(solution)/shard_map/ppermute | solution.py:18
  109.6 48.7 %collective-permute-start.30 = (bf16[512,1024]{1,0:T(8,128)(2,1)}, bf16[512,1024]{1,0:T(8,128)(2,1)}, u32[]{:S(2)}, u32[]{:S(2)}) collective-permute-start(bf16[512,1024]{1,0:T(8,128)(2,1)} %pad_maximum_fusion.16), channel_id=1, source_target_pairs={{0,16},{16,0},{1,17},{17,1},{2,18},{18,2},{3,19},{19,3},{4,20},{20... | collective-permute-start | bytes 3145736 | tf_op jit(solution)/shard_map/ppermute | solution.py:18
  130.1 27.8 %collective-permute-start.29 = (bf16[256,1024]{1,0:T(8,128)(2,1)}, bf16[256,1024]{1,0:T(8,128)(2,1)}, u32[]{:S(2)}, u32[]{:S(2)}) collective-permute-start(bf16[256,1024]{1,0:T(8,128)(2,1)} %broadcast_select_fusion.6), channel_id=1, source_target_pairs={{0,8},{8,0},{1,9},{9,1},{2,10},{10,2},{3,11},{11,3},{4,12},{12,4},... | collective-permute-start | bytes 1572872 | tf_op jit(solution)/shard_map/ppermute | solution.py:18
  135.1 23.8 %collective-permute-start.31 = (bf16[512,1024]{1,0:T(8,128)(2,1)}, bf16[512,1024]{1,0:T(8,128)(2,1)}, u32[]{:S(2)}, u32[]{:S(2)}) collective-permute-start(bf16[512,1024]{1,0:T(8,128)(2,1)} %pad_maximum_fusion.19), channel_id=1, source_target_pairs={{0,4},{4,0},{1,5},{5,1},{2,6},{6,2},{3,7},{7,3},{8,12},{12,8},{9,1... | collective-permute-start | bytes 3145736 | tf_op jit(solution)/shard_map/ppermute | solution.py:18
  182.6 47.2 %collective-permute-start.38 = (bf16[512,1024]{1,0:T(8,128)(2,1)}, bf16[512,1024]{1,0:T(8,128)(2,1)S(1)}, u32[]{:S(2)}, u32[]{:S(2)}) collective-permute-start(bf16[512,1024]{1,0:T(8,128)(2,1)} %pad_maximum_fusion.19), channel_id=1, source_target_pairs={{0,16},{16,0},{1,17},{17,1},{2,18},{18,2},{3,19},{19,3},{4,20},{20... | collective-permute-start | bytes 3145736 | tf_op jit(solution)/shard_map/ppermute | solution.py:18
  185.1 54.1 %collective-permute-start.41 = (bf16[512,1024]{1,0:T(8,128)(2,1)}, bf16[512,1024]{1,0:T(8,128)(2,1)S(1)}, u32[]{:S(2)}, u32[]{:S(2)}) collective-permute-start(bf16[512,1024]{1,0:T(8,128)(2,1)} %collective-permute-done.30), channel_id=1, source_target_pairs={{0,4},{4,0},{1,5},{5,1},{2,6},{6,2},{3,7},{7,3},{8,12},{12,8},{9,1... | collective-permute-start | bytes 3145736 | tf_op jit(solution)/shard_map/ppermute | solution.py:18
  186.6 52.7 %collective-permute-start.42 = (bf16[512,1024]{1,0:T(8,128)(2,1)S(1)}, bf16[512,1024]{1,0:T(8,128)(2,1)S(1)}, u32[]{:S(2)}, u32[]{:S(2)}) collective-permute-start(bf16[512,1024]{1,0:T(8,128)(2,1)S(1)} %pad_maximum_fusion.20), channel_id=1, source_target_pairs={{0,4},{4,0},{1,5},{5,1},{2,6},{6,2},{3,7},{7,3},{8,12},{12,8},{9,1... | collective-permute-start | bytes 3145736 | tf_op jit(solution)/shard_map/ppermute | solution.py:18
  251.3 48.0 %collective-permute-start.47 = (bf16[512,1024]{1,0:T(8,128)(2,1)S(1)}, bf16[512,1024]{1,0:T(8,128)(2,1)S(1)}, u32[]{:S(2)}, u32[]{:S(2)}) collective-permute-start(bf16[512,1024]{1,0:T(8,128)(2,1)S(1)} %pad_maximum_fusion.20), channel_id=1, source_target_pairs={{0,16},{16,0},{1,17},{17,1},{2,18},{18,2},{3,19},{19,3},{4,20},{20... | collective-permute-start | bytes 3145736 | tf_op jit(solution)/shard_map/ppermute | solution.py:18
  253.7 45.6 %collective-permute-start.48 = (bf16[512,1024]{1,0:T(8,128)(2,1)S(1)}, bf16[512,1024]{1,0:T(8,128)(2,1)S(1)}, u32[]{:S(2)}, u32[]{:S(2)}) collective-permute-start(bf16[512,1024]{1,0:T(8,128)(2,1)S(1)} %collective-permute-done.38), channel_id=1, source_target_pairs={{0,4},{4,0},{1,5},{5,1},{2,6},{6,2},{3,7},{7,3},{8,12},{12,8},{9,1... | collective-permute-start | bytes 3145736 | tf_op jit(solution)/shard_map/ppermute | solution.py:18
  309.6 25.2 %collective-permute-start.55 = (bf16[512,1024]{1,0:T(8,128)(2,1)S(1)}, bf16[512,1024]{1,0:T(8,128)(2,1)S(1)}, u32[]{:S(2)}, u32[]{:S(2)}) collective-permute-start(bf16[512,1024]{1,0:T(8,128)(2,1)S(1)} %collective-permute-done.47), channel_id=1, source_target_pairs={{0,4},{4,0},{1,5},{5,1},{2,6},{6,2},{3,7},{7,3},{8,12},{12,8},{9,1... | collective-permute-start | bytes 3145736 | tf_op jit(solution)/shard_map/ppermute | solution.py:18
  392.8 40.3 %collective-permute-start.66 = (bf16[512,1024]{1,0:T(8,128)(2,1)}, bf16[512,1024]{1,0:T(8,128)(2,1)}, u32[]{:S(2)}, u32[]{:S(2)}) collective-permute-start(bf16[512,1024]{1,0:T(8,128)(2,1)} %convolution_convert_fusion.5), channel_id=1, source_target_pairs={{0,4},{4,0},{1,5},{5,1},{2,6},{6,2},{3,7},{7,3},{8,12},{12,8},{9,1... | collective-permute-start | bytes 3145736 | tf_op jit(solution)/shard_map/ppermute | solution.py:18
  394.6 58.1 %collective-permute-start.69 = (bf16[512,1024]{1,0:T(8,128)(2,1)}, bf16[512,1024]{1,0:T(8,128)(2,1)}, u32[]{:S(2)}, u32[]{:S(2)}) collective-permute-start(bf16[512,1024]{1,0:T(8,128)(2,1)} %convolution_convert_fusion.4), channel_id=1, source_target_pairs={{0,4},{4,0},{1,5},{5,1},{2,6},{6,2},{3,7},{7,3},{8,12},{12,8},{9,1... | collective-permute-start | bytes 3145736 | tf_op jit(solution)/shard_map/ppermute | solution.py:18
  451.0 26.0 %collective-permute-start.74 = (bf16[512,1024]{1,0:T(8,128)(2,1)S(1)}, bf16[512,1024]{1,0:T(8,128)(2,1)S(1)}, u32[]{:S(2)}, u32[]{:S(2)}) collective-permute-start(bf16[512,1024]{1,0:T(8,128)(2,1)S(1)} %copy-done.157), channel_id=1, source_target_pairs={{0,4},{4,0},{1,5},{5,1},{2,6},{6,2},{3,7},{7,3},{8,12},{12,8},{9,1... | collective-permute-start | bytes 3145736 | tf_op jit(solution)/shard_map/ppermute | solution.py:18
  465.8 46.8 %collective-permute-start.75 = (bf16[512,1024]{1,0:T(8,128)(2,1)S(1)}, bf16[512,1024]{1,0:T(8,128)(2,1)S(1)}, u32[]{:S(2)}, u32[]{:S(2)}) collective-permute-start(bf16[512,1024]{1,0:T(8,128)(2,1)S(1)} %add_convert_fusion.6), channel_id=1, source_target_pairs={{0,16},{16,0},{1,17},{17,1},{2,18},{18,2},{3,19},{19,3},{4,20},{20... | collective-permute-start | bytes 3145736 | tf_op jit(solution)/shard_map/ppermute | solution.py:18
  468.2 91.1 %collective-permute-start.82 = (bf16[512,1024]{1,0:T(8,128)(2,1)S(1)}, bf16[512,1024]{1,0:T(8,128)(2,1)S(1)}, u32[]{:S(2)}, u32[]{:S(2)}) collective-permute-start(bf16[512,1024]{1,0:T(8,128)(2,1)S(1)} %copy-done.154), channel_id=1, source_target_pairs={{0,4},{4,0},{1,5},{5,1},{2,6},{6,2},{3,7},{7,3},{8,12},{12,8},{9,1... | collective-permute-start | bytes 3145736 | tf_op jit(solution)/shard_map/ppermute | solution.py:18
  515.9 78.9 %collective-permute-start.84 = (bf16[512,1024]{1,0:T(8,128)(2,1)}, bf16[512,1024]{1,0:T(8,128)(2,1)}, u32[]{:S(2)}, u32[]{:S(2)}) collective-permute-start(bf16[512,1024]{1,0:T(8,128)(2,1)} %convolution_convert_fusion.1), channel_id=1, source_target_pairs={{0,4},{4,0},{1,5},{5,1},{2,6},{6,2},{3,7},{7,3},{8,12},{12,8},{9,1... | collective-permute-start | bytes 3145736 | tf_op jit(solution)/shard_map/ppermute | solution.py:18
  517.6 110.2 %collective-permute-start.90 = (bf16[512,1024]{1,0:T(8,128)(2,1)}, bf16[512,1024]{1,0:T(8,128)(2,1)}, u32[]{:S(2)}, u32[]{:S(2)}) collective-permute-start(bf16[512,1024]{1,0:T(8,128)(2,1)} %add_convert_fusion.3), channel_id=1, source_target_pairs={{0,16},{16,0},{1,17},{17,1},{2,18},{18,2},{3,19},{19,3},{4,20},{20... | collective-permute-start | bytes 3145736 | tf_op jit(solution)/shard_map/ppermute | solution.py:18
  527.4 26.4 %collective-permute-start.78 = (bf16[256,1024]{1,0:T(8,128)(2,1)S(1)}, bf16[256,1024]{1,0:T(8,128)(2,1)S(1)}, u32[]{:S(2)}, u32[]{:S(2)}) collective-permute-start(bf16[256,1024]{1,0:T(8,128)(2,1)S(1)} %pad_maximum_fusion.46), channel_id=1, source_target_pairs={{0,8},{8,0},{1,9},{9,1},{2,10},{10,2},{3,11},{11,3},{4,12},{12,4},... | collective-permute-start | bytes 1572872 | tf_op jit(solution)/shard_map/ppermute | solution.py:18
  527.4 26.3 %collective-permute-start.79 = (bf16[256,1024]{1,0:T(8,128)(2,1)S(1)}, bf16[256,1024]{1,0:T(8,128)(2,1)S(1)}, u32[]{:S(2)}, u32[]{:S(2)}) collective-permute-start(bf16[256,1024]{1,0:T(8,128)(2,1)S(1)} %pad_maximum_fusion.47), channel_id=1, source_target_pairs={{0,1},{1,0},{2,3},{3,2},{4,5},{5,4},{6,7},{7,6},{8,9},{9,8},{10,11... | collective-permute-start | bytes 1572872 | tf_op jit(solution)/shard_map/ppermute | solution.py:18
  556.8 45.1 %collective-permute-start.85 = (bf16[256,1024]{1,0:T(8,128)(2,1)}, bf16[256,1024]{1,0:T(8,128)(2,1)}, u32[]{:S(2)}, u32[]{:S(2)}) collective-permute-start(bf16[256,1024]{1,0:T(8,128)(2,1)} %select_convert_fusion.5), channel_id=1, source_target_pairs={{0,8},{8,0},{1,9},{9,1},{2,10},{10,2},{3,11},{11,3},{4,12},{12,4},... | collective-permute-start | bytes 1572872 | tf_op jit(solution)/shard_map/ppermute | solution.py:18
  606.3 18.5 %collective-permute-start.89 = (f32[4,1024]{1,0:T(4,128)S(1)}, f32[4,1024]{1,0:T(4,128)S(1)}, u32[]{:S(2)}, u32[]{:S(2)}) collective-permute-start(f32[4,1024]{1,0:T(4,128)S(1)} %slice.1249), channel_id=1, source_target_pairs={{0,4},{4,0},{1,5},{5,1},{2,6},{6,2},{3,7},{7,3},{8,12},{12,8},{9,1... | collective-permute-start | bytes 49160 | tf_op jit(solution)/shard_map/ppermute | solution.py:18
  611.6 25.8 %collective-permute-start.92 = (bf16[128,2048]{1,0:T(8,128)(2,1)}, bf16[128,2048]{1,0:T(8,128)(2,1)}, u32[]{:S(2)}, u32[]{:S(2)}) collective-permute-start(bf16[128,2048]{1,0:T(8,128)(2,1)} %select_convert_fusion.4), channel_id=1, source_target_pairs={{0,2},{2,0},{1,3},{3,1},{4,6},{6,4},{5,7},{7,5},{8,10},{10,8},{9,1... | collective-permute-start | bytes 1572872 | tf_op jit(solution)/shard_map/ppermute | solution.py:18
  636.1 48.1 %collective-permute-start.106 = (bf16[512,1024]{1,0:T(8,128)(2,1)S(1)}, bf16[512,1024]{1,0:T(8,128)(2,1)S(1)}, u32[]{:S(2)}, u32[]{:S(2)}) collective-permute-start(bf16[512,1024]{1,0:T(8,128)(2,1)S(1)} %copy-done.220), channel_id=1, source_target_pairs={{0,16},{16,0},{1,17},{17,1},{2,18},{18,2},{3,19},{19,3},{4,20},{20... | collective-permute-start | bytes 3145736 | tf_op jit(solution)/shard_map/ppermute | solution.py:18
  637.4 46.8 %collective-permute-start.93 = (bf16[512,1024]{1,0:T(8,128)(2,1)S(1)}, bf16[512,1024]{1,0:T(8,128)(2,1)S(1)}, u32[]{:S(2)}, u32[]{:S(2)}) collective-permute-start(bf16[512,1024]{1,0:T(8,128)(2,1)S(1)} %add_convert_fusion.1), channel_id=1, source_target_pairs={{0,2},{2,0},{1,3},{3,1},{4,6},{6,4},{5,7},{7,5},{8,10},{10,8},{9,1... | collective-permute-start | bytes 3145736 | tf_op jit(solution)/shard_map/ppermute | solution.py:18
  639.2 45.9 %collective-permute-start.94 = (bf16[512,1024]{1,0:T(8,128)(2,1)S(1)}, bf16[512,1024]{1,0:T(8,128)(2,1)S(1)}, u32[]{:S(2)}, u32[]{:S(2)}) collective-permute-start(bf16[512,1024]{1,0:T(8,128)(2,1)S(1)} %add_convert_fusion), channel_id=1, source_target_pairs={{0,2},{2,0},{1,3},{3,1},{4,6},{6,4},{5,7},{7,5},{8,10},{10,8},{9,1... | collective-permute-start | bytes 3145736 | tf_op jit(solution)/shard_map/ppermute | solution.py:18
  642.8 43.9 %collective-permute-start.95 = (bf16[512,1024]{1,0:T(8,128)(2,1)S(1)}, bf16[512,1024]{1,0:T(8,128)(2,1)S(1)}, u32[]{:S(2)}, u32[]{:S(2)}) collective-permute-start(bf16[512,1024]{1,0:T(8,128)(2,1)S(1)} %copy-done.148), channel_id=1, source_target_pairs={{0,4},{4,0},{1,5},{5,1},{2,6},{6,2},{3,7},{7,3},{8,12},{12,8},{9,1... | collective-permute-start | bytes 3145736 | tf_op jit(solution)/shard_map/ppermute | solution.py:18
  652.8 33.9 %collective-permute-start.96 = (bf16[512,512]{0,1:T(8,128)(2,1)S(1)}, bf16[512,512]{0,1:T(8,128)(2,1)S(1)}, u32[]{:S(2)}, u32[]{:S(2)}) collective-permute-start(bf16[512,512]{0,1:T(8,128)(2,1)S(1)} %pad_maximum_fusion.48), channel_id=1, source_target_pairs={{0,4},{4,0},{1,5},{5,1},{2,6},{6,2},{3,7},{7,3},{8,12},{12,8},{9,1... | collective-permute-start | bytes 1572872 | tf_op jit(solution)/shard_map/ppermute | solution.py:18
  686.8 22.5 %collective-permute-start.97 = (bf16[256,1024]{1,0:T(8,128)(2,1)S(1)}, bf16[256,1024]{1,0:T(8,128)(2,1)S(1)}, u32[]{:S(2)}, u32[]{:S(2)}) collective-permute-start(bf16[256,1024]{1,0:T(8,128)(2,1)S(1)} %slice.2335), channel_id=1, source_target_pairs={{0,8},{8,0},{1,9},{9,1},{2,10},{10,2},{3,11},{11,3},{4,12},{12,4},... | collective-permute-start | bytes 1572872 | tf_op jit(solution)/shard_map/ppermute | solution.py:18
  687.1 22.2 %collective-permute-start.98 = (bf16[256,1024]{1,0:T(8,128)(2,1)S(1)}, bf16[256,1024]{1,0:T(8,128)(2,1)S(1)}, u32[]{:S(2)}, u32[]{:S(2)}) collective-permute-start(bf16[256,1024]{1,0:T(8,128)(2,1)S(1)} %pad_maximum_fusion.49), channel_id=1, source_target_pairs={{0,1},{1,0},{2,3},{3,2},{4,5},{5,4},{6,7},{7,6},{8,9},{9,8},{10,11... | collective-permute-start | bytes 1572872 | tf_op jit(solution)/shard_map/ppermute | solution.py:18
  688.2 23.4 %collective-permute-start.100 = (bf16[512,512]{0,1:T(8,128)(2,1)S(1)}, bf16[512,512]{0,1:T(8,128)(2,1)S(1)}, u32[]{:S(2)}, u32[]{:S(2)}) collective-permute-start(bf16[512,512]{0,1:T(8,128)(2,1)S(1)} %pad_maximum_fusion.50), channel_id=1, source_target_pairs={{0,4},{4,0},{1,5},{5,1},{2,6},{6,2},{3,7},{7,3},{8,12},{12,8},{9,1... | collective-permute-start | bytes 1572872 | tf_op jit(solution)/shard_map/ppermute | solution.py:18
  688.8 25.4 %collective-permute-start.112 = (bf16[512,512]{0,1:T(8,128)(2,1)S(1)}, bf16[512,512]{0,1:T(8,128)(2,1)S(1)}, u32[]{:S(2)}, u32[]{:S(2)}) collective-permute-start(bf16[512,512]{0,1:T(8,128)(2,1)S(1)} %fusion.29), channel_id=1, source_target_pairs={{0,16},{16,0},{1,17},{17,1},{2,18},{18,2},{3,19},{19,3},{4,20},{20... | collective-permute-start | bytes 1572872 | tf_op jit(solution)/shard_map/ppermute | solution.py:18
  690.5 22.2 %collective-permute-start.105 = (bf16[512,512]{0,1:T(8,128)(2,1)S(1)}, bf16[512,512]{0,1:T(8,128)(2,1)S(1)}, u32[]{:S(2)}, u32[]{:S(2)}) collective-permute-start(bf16[512,512]{0,1:T(8,128)(2,1)S(1)} %pad_maximum_fusion.51), channel_id=1, source_target_pairs={{0,4},{4,0},{1,5},{5,1},{2,6},{6,2},{3,7},{7,3},{8,12},{12,8},{9,1... | collective-permute-start | bytes 1572872 | tf_op jit(solution)/shard_map/ppermute | solution.py:18
  709.3 27.3 %collective-permute-start.103 = (bf16[256,1024]{1,0:T(8,128)(2,1)S(1)}, bf16[256,1024]{1,0:T(8,128)(2,1)S(1)}, u32[]{:S(2)}, u32[]{:S(2)}) collective-permute-start(bf16[256,1024]{1,0:T(8,128)(2,1)S(1)} %select_convert_fusion.3), channel_id=1, source_target_pairs={{0,8},{8,0},{1,9},{9,1},{2,10},{10,2},{3,11},{11,3},{4,12},{12,4},... | collective-permute-start | bytes 1572872 | tf_op jit(solution)/shard_map/ppermute | solution.py:18
  709.3 38.6 %collective-permute-start.115 = (bf16[256,1024]{1,0:T(8,128)(2,1)S(1)}, bf16[256,1024]{1,0:T(8,128)(2,1)S(1)}, u32[]{:S(2)}, u32[]{:S(2)}) collective-permute-start(bf16[256,1024]{1,0:T(8,128)(2,1)S(1)} %select_convert_fusion.1), channel_id=1, source_target_pairs={{0,8},{8,0},{1,9},{9,1},{2,10},{10,2},{3,11},{11,3},{4,12},{12,4},... | collective-permute-start | bytes 1572872 | tf_op jit(solution)/shard_map/ppermute | solution.py:18
  711.6 41.9 %collective-permute-start.102 = (bf16[128,1024]{1,0:T(8,128)(2,1)S(1)}, bf16[128,1024]{1,0:T(8,128)(2,1)S(1)}, u32[]{:S(2)}, u32[]{:S(2)}) collective-permute-start(bf16[128,1024]{1,0:T(8,128)(2,1)S(1)} %slice.2339), channel_id=1, source_target_pairs={{0,8},{8,0},{1,9},{9,1},{2,10},{10,2},{3,11},{11,3},{4,12},{12,4},... | collective-permute-start | bytes 786440 | tf_op jit(solution)/shard_map/ppermute | solution.py:18
  712.8 40.7 %collective-permute-start.101 = (bf16[128,1024]{1,0:T(8,128)(2,1)S(1)}, bf16[128,1024]{1,0:T(8,128)(2,1)S(1)}, u32[]{:S(2)}, u32[]{:S(2)}) collective-permute-start(bf16[128,1024]{1,0:T(8,128)(2,1)S(1)} %slice.2340), channel_id=1, source_target_pairs={{0,1},{1,0},{2,3},{3,2},{4,5},{5,4},{6,7},{7,6},{8,9},{9,8},{10,11... | collective-permute-start | bytes 786440 | tf_op jit(solution)/shard_map/ppermute | solution.py:18
  714.2 45.0 %collective-permute-start.109 = (bf16[512,512]{0,1:T(8,128)(2,1)S(1)}, bf16[512,512]{0,1:T(8,128)(2,1)S(1)}, u32[]{:S(2)}, u32[]{:S(2)}) collective-permute-start(bf16[512,512]{0,1:T(8,128)(2,1)S(1)} %fusion.27), channel_id=1, source_target_pairs={{0,16},{16,0},{1,17},{17,1},{2,18},{18,2},{3,19},{19,3},{4,20},{20... | collective-permute-start | bytes 1572872 | tf_op jit(solution)/shard_map/ppermute | solution.py:18
  736.6 22.0 %collective-permute-start.113 = (bf16[256,512]{0,1:T(8,128)(2,1)S(1)}, bf16[256,512]{0,1:T(8,128)(2,1)S(1)}, u32[]{:S(2)}, u32[]{:S(2)}) collective-permute-start(bf16[256,512]{0,1:T(8,128)(2,1)S(1)} %select_convert_fusion.7), channel_id=1, source_target_pairs={{0,8},{8,0},{1,9},{9,1},{2,10},{10,2},{3,11},{11,3},{4,12},{12,4},... | collective-permute-start | bytes 786440 | tf_op jit(solution)/shard_map/ppermute | solution.py:18
  (295 other events, 2765.1 us)

commit v5 on v4

--- a/solution.py
+++ b/solution.py
@@ -189,7 +189,7 @@
         local_heads = head_width // HD
         score_scale = 1.0 / math.sqrt(HD)
         own, other = slice(0, core_tokens), slice(core_tokens, group_tokens)
-        c = Chain(query_gain)
+        c = Chain(jnp.full((1, HD), bit("core"), jnp.int32))
 
         def columns(parts):
             return parts[0] if len(parts) == 1 else jnp.concatenate(parts, axis=1)
@@ -282,13 +282,13 @@
             right_sent = c.start(right, "core")
             return stack2(left, c.sync(left_sent)), stack2(right, c.sync(right_sent))
 
-        def gather_rows(value, between=None):
+        def gather_rows(value, between=None, last=None):
             left, right = value[:, :half_width], value[:, half_width:]
             left_sent = c.start(left, "tensor")
             right_sent = c.start(right, "zl")
             left = stack2(left, c.sync(left_sent))
             right = stack2(right, c.sync(right_sent))
-            return rows_second(left, right, between)
+            return rows_second(left, right, between, last)
 
         ffn_sent = c.sync(ffn_sent)
         width = ffn_sent.shape[1] // 3
@@ -312,7 +312,6 @@
         in0, in1 = rows_second(left, right, tokens_between, tokens_last)
         seq_ids = stack2(seq_ids, c.sync(ids_sent))
         gate_w.end_line()
-        gate_w.start_x(0)
         gains = gain_steps.finish()
         qk.end_x(1)
 
@@ -336,23 +335,25 @@
         wqk0, wqk1 = qk.rows(0), qk.rows(1)
         projected = dot(in0, wqk0) + dot(in1, wqk1)
         query, key_proj = projected[:, :head_width], projected[:, head_width:]
+
+        def squares_between():
+            vo.end_high()
+            vo.end_x(0)
+            vo.start_x(1)
+            gate_w.start_high()
+            up_w.start_line()
+
         squares = pair_sum(
             c,
             jnp.stack([jnp.sum(query * query, axis=1), jnp.sum(key_proj * key_proj, axis=1)]),
-            up_w.start_line,
+            squares_between,
         )
         q_rms = lax.rsqrt(squares[0] / model_width + EPSILON)[:, None]
         k_rms = lax.rsqrt(squares[1] / model_width + EPSILON)[:, None]
         normed_query = (query * q_rms * query_scale).astype(BF)
         normed_key = (key_proj * k_rms * key_scale).astype(BF)
-        vo.end_high()
-        vo.end_x(0)
-        vo.start_x(1)
-        gate_w.start_high()
-        up_w.end_line()
+        gate_w.start_x(0)
         down_w.start_line()
-        gate_w.end_x(0)
-        up_w.start_x(0)
         vo.end_x(1)
         normed_query, normed_key = c.sync(normed_query, normed_key)
         wvo0, wvo1 = vo.rows(0), vo.rows(1)
@@ -377,11 +378,13 @@
             "bhqk,bkhd->bqhd", prob_bf, value_heads, preferred_element_type=F32
         ).astype(BF)
         attn = attn_heads.reshape(group_tokens, head_width)
+        up_w.end_line()
+        gate_w.end_x(0)
+        up_w.start_x(0)
         down_w.end_line()
         gate_w.end_high()
         gate_w.start_x(1)
         up_w.start_high()
-        up_w.end_x(0)
 
         def halve(total, axis):
             half = total.shape[0] // 2
@@ -409,33 +412,32 @@
                 second()
             return added(left), added(right)
 
-        def first_down():
+        def proj_second():
+            up_w.end_x(0)
+            up_w.end_high()
+            gate_w.end_x(1)
+            up_w.start_x(1)
+            down_w.start_high()
             down_w.start_x(0)
 
         proj = columns(
             scatter_rows(
-                lambda rows: dot_nt(attn[rows], wo0), lambda rows: dot_nt(attn[rows], wo1), first_down
+                lambda rows: dot_nt(attn[rows], wo0), lambda rows: dot_nt(attn[rows], wo1), None, proj_second
             )
         )
         attn_rms = rms_scale(proj)
         resid = tokens_f + proj * attn_rms * attn_scale
 
-        def resid_between():
-            gate_w.end_x(1)
+        def resid_last():
+            up_w.end_x(1)
+            down_w.end_high()
             down_w.end_x(0)
-
-        resid_bf = c.sync(resid.astype(BF))
-        up_w.end_high()
-        up_w.start_x(1)
-        down_w.start_high()
-        h0, h1 = gather_rows(resid_bf, resid_between)
+            down_w.start_x(1)
+
+        h0, h1 = gather_rows(resid.astype(BF), None, resid_last)
         wg0, wg1 = gate_w.rows(0), gate_w.rows(1)
         gate = dot(h0, wg0) + dot(h1, wg1)
-        gate = c.sync(gate)
         sigma = jax.nn.sigmoid(gate)
-        down_w.end_high()
-        down_w.start_x(1)
-        up_w.end_x(1)
         wu0, wu1 = up_w.rows(0), up_w.rows(1)
         up = dot(h0, wu0) + dot(h1, wu1)
         act = (gate * sigma * up).astype(BF)
@@ -494,10 +496,13 @@
             def start_line(self):
                 self.line = c.start(self.sent.astype(BF), "zl")
 
-            def joined(self, axis, moved):
+            def joined(self, axis, moved, low=None):
                 width = moved.shape[1] // len(self.terms)
                 cols = [slice(i * width, (i + 1) * width) for i in range(len(self.terms))]
-                return [ordered(axis, self.own[:, s], moved[:, s], dim=1) for s in cols]
+                if low is None:
+                    return [ordered(axis, self.own[:, s], moved[:, s], dim=1) for s in cols]
+                pairs = [(self.own[:, s], moved[:, s]) for s in cols]
+                return [columns([jnp.where(low, a, b), jnp.where(low, b, a)]) for a, b in pairs]
 
             def end_line(self):
                 moved = c.sync(self.line).astype(F32)
@@ -505,7 +510,8 @@
                 self.core = c.start(sent.astype(BF), "core")
 
             def end(self):
-                self.results = self.joined("core", c.sync(self.core).astype(F32))
+                moved = c.sync(self.core).astype(F32)
+                self.results = self.joined("core", moved, c.token[0, 0] == 0)
 
         down_grad = Grad(((f0, f1), act))
         down_grad.start_x(1)
@@ -519,16 +525,24 @@
         down_grad.end_x(1)
         down_grad.start_high()
         gate_grad.start_x(1)
+        d_gate, d_up = c.fence(d_gate, d_up)
 
         def hidden_first():
             down_grad.end_x(0)
             gate_grad.start_x(0)
+
+        def hidden_second():
+            gate_grad.end_x(1)
+            up_grad.start_x(1)
+            down_grad.end_high()
+            gate_grad.start_high()
 
         d_resid = d_out + columns(
             scatter_rows(
                 lambda rows: dot_nt(d_gate[rows], wg0) + dot_nt(d_up[rows], wu0),
                 lambda rows: dot_nt(d_gate[rows], wg1) + dot_nt(d_up[rows], wu1),
                 hidden_first,
+                hidden_second,
             )
         )
         attn_gain_term = jnp.sum(d_resid * proj * attn_rms, axis=0)
@@ -540,19 +554,21 @@
                 - proj * attn_rms * attn_rms * jnp.mean(scaled_resid * proj, axis=1, keepdims=True)
             )
         ).astype(BF)
-        gate_grad.end_x(1)
-        up_grad.start_x(1)
-
-        d_proj = c.sync(d_proj)
-        down_grad.end_high()
-        gate_grad.start_high()
 
         def proj_between():
             down_grad.start_line()
-
-        p0, p1 = gather_rows(d_proj, proj_between)
-        gate_grad.end_x(0)
-        up_grad.start_x(0)
+            gate_grad.end_x(0)
+            up_grad.start_x(0)
+
+        def proj_last():
+            up_grad.end_x(1)
+            gate_grad.end_high()
+            up_grad.start_high()
+            gate_grad.start_line()
+
+        p0, p1 = gather_rows(d_proj, proj_between, proj_last)
+        up_grad.end_x(0)
+        down_grad.end_line()
         p0, p1 = c.fence(p0, p1)
         d_attn = (dot(p0, wo0) + dot(p1, wo1)).astype(BF)
 
@@ -593,8 +609,11 @@
             [to_relative(placed), jnp.stack([attn_gain_term, ffn_gain_term])], axis=0
         )
         gain_steps = Steps(scatter_gains(c, gain_parts))
-        up_grad.end_x(1)
-        down_grad.end_line()
+        gate_grad.end_line()
+        ov_grad = Grad(((p0, p1), attn), ((in0, in1), d_value))
+        ov_grad.start_x(1)
+        up_grad.end_high()
+        down_grad.end()
         inner = pair_sum(
             c, jnp.stack([jnp.sum(scaled_q * query, axis=1), jnp.sum(scaled_k * key_proj, axis=1)])
         )
@@ -606,25 +625,23 @@
             k_rms * (scaled_k - key_proj * k_rms * k_rms * (inner[1] / model_width)[:, None])
         ).astype(BF)
         d_qk = columns([d_query, d_key])
-        ov_grad = Grad(((p0, p1), attn), ((in0, in1), d_value))
         qk_grad = Grad(((in0, in1), d_query), ((in0, in1), d_key))
-        gate_grad.end_high()
-        gain_steps()
-        up_grad.start_high()
-        ov_grad.start_x(1)
-        down_grad.end()
+        ov_grad.end_x(1)
+        ov_grad.start_high()
+        qk_grad.start_x(1)
+        ov_grad.start_x(0)
+        gate_grad.end()
 
         def tokens_first():
-            up_grad.end_x(0)
-            qk_grad.start_x(1)
-            gate_grad.start_line()
-            ov_grad.end_x(1)
-            ov_grad.start_x(0)
+            up_grad.start_line()
+            qk_grad.end_x(1)
+            qk_grad.start_x(0)
 
         def tokens_second():
             gain_steps()
-            qk_grad.end_x(1)
-            qk_grad.start_x(0)
+            ov_grad.end_x(0)
+            ov_grad.end_high()
+            qk_grad.start_high()
 
         d_tokens = columns(
             scatter_rows(
@@ -635,20 +652,13 @@
             )
         )
         grad_tokens = to_natural(d_resid + d_tokens)
-        gate_grad.end_line()
         gain_steps()
-        ov_grad.end_x(0)
-        up_grad.end_high()
-        ov_grad.start_high()
-        up_grad.start_line()
-        gate_grad.end()
+        up_grad.end_line()
+        ov_grad.start_line()
         qk_grad.end_x(0)
-        qk_grad.start_high()
+        gain_steps()
+        up_grad.end()
         gain_parts = gain_steps.finish()
-        up_grad.end_line()
-        ov_grad.end_high()
-        ov_grad.start_line()
-        up_grad.end()
         ov_grad.end_line()
         qk_grad.end_high()
         qk_grad.start_line()

time: 782 us -> 745 us (0.953)
  waiting for transfers between devices: 401 us -> 365 us
  other arithmetic: 63.4 us -> 81.4 us
  starting transfers between devices: 105 us -> 94.6 us
  matrix products: 137 us -> 128 us
    ppermute x118 -> x119, waiting for transfers between devices: 401 us -> 365 us  [swap(): return lax.ppermute(value, axis, FLIP)]
    dot_general x26, matrix products: 44.3 us -> 34.3 us  [dot_nt(): return jnp.einsum('sc,rc->sr', a, b, preferred_element_type=F32)]
    ppermute x118 -> x119, starting transfers between devices: 105 us -> 94.6 us  [swap(): return lax.ppermute(value, axis, FLIP)]
    select_n x41 -> x34, other arithmetic: 13.5 us -> 16.1 us  [pick(): return jnp.where(bit(axis) == 0, low, high)]
    unnamed x498 -> x452, local copies, waits for them, and re-layouts: 33.8 us -> 34.1 us
  transfers between devices with their start and end apart: 118 -> 119, of which waited for: 53 -> 47; matrix products, arithmetic and copies ran while one was open for 27% -> 28% of each run, Pallas kernels for 0% -> 0%
where the time goes in v5:
time: 745 us; the launch traced here: 737 us
  waiting for transfers between devices  365 us (49%)
  matrix products  128 us (17%)
  starting transfers between devices  94.6 us (13%)
  other arithmetic  81.4 us (11%)
  local copies, waits for them, and re-layouts  62.8 us (8%)
    ppermute x119, waiting for transfers between devices, swap(): return lax.ppermute(value, axis, FLIP)  365 us
    ppermute x119, starting transfers between devices, swap(): return lax.ppermute(value, axis, FLIP)  94.6 us
    dot_general x28, matrix products, dot_tn(): return jnp.einsum('sr,sc->rc', a, b, preferred_element_type=F32)  48.5 us
    dot_general x26, matrix products, dot_nt(): return jnp.einsum('sc,rc->sr', a, b, preferred_element_type=F32)  34.3 us
    unnamed x452, local copies, waits for them, and re-layouts  34.1 us
    dot_general x12, matrix products, dot(): return jnp.dot(a, b, preferred_element_type=F32)  32.6 us
    select_n x34, other arithmetic, pick(): return jnp.where(bit(axis) == 0, low, high)  16.1 us
  transfers between devices with their start and end apart: 119, of which 47 were waited for; matrix products, arithmetic and copies ran while one was open for 28% of the time, Pallas kernels for 0%

profile of v5, /device:TPU:0, one launch (start us, length us, event | category | flops | bytes accessed | tf_op | source)
XLA Modules:
  0.0 737.2 jit_solution(9133935461516129633)
XLA Ops:
  6.0 3.1 collective-permute-start
  25.9 4.5 collective-permute-done.3
  33.0 5.2 collective-permute-done.7
  50.6 3.4 collective-permute-done.11
  55.1 13.3 %collective-permute-done.12 = bf16[256,1024]{1,0:T(8,128)(2,1)S(1)} collective-permute-done((bf16[256,1024]{1,0:T(8,128)(2,1)S(1)}, bf16[256,1024]{1,0:T(8,128)(2,1)S(1)}, u32[]{:S(2)}, u32[]{:S(2)}) %collective-permute-start.12) | collective-permute-done | bytes 524320 | tf_op jit(solution)/shard_map/ppermute | solution.py:18
  84.0 9.5 %collective-permute-done.18 = bf16[256,1024]{1,0:T(8,128)(2,1)S(1)} collective-permute-done((bf16[256,1024]{1,0:T(8,128)(2,1)}, bf16[256,1024]{1,0:T(8,128)(2,1)S(1)}, u32[]{:S(2)}, u32[]{:S(2)}) %collective-permute-start.18) | collective-permute-done | bytes 524320 | tf_op jit(solution)/shard_map/ppermute | solution.py:18
  93.5 2.8 pad_maximum_fusion
  110.1 2.8 collective-permute-start.30
  117.0 7.1 collective-permute-done.26
  124.1 10.0 %collective-permute-done.27 = bf16[256,1024]{1,0:T(8,128)(2,1)S(1)} collective-permute-done((bf16[256,1024]{1,0:T(8,128)(2,1)S(1)}, bf16[256,1024]{1,0:T(8,128)(2,1)S(1)}, u32[]{:S(2)}, u32[]{:S(2)}) %collective-permute-start.27) | collective-permute-done | bytes 524320 | tf_op jit(solution)/shard_map/ppermute | solution.py:18
  141.1 3.4 add_convert_fusion.8
  144.5 3.4 fusion.228
  147.9 3.0 broadcast_select_fusion.4
  172.8 16.8 %collective-permute-done.33 = bf16[256,1024]{1,0:T(8,128)(2,1)S(1)} collective-permute-done((bf16[256,1024]{1,0:T(8,128)(2,1)S(1)}, bf16[256,1024]{1,0:T(8,128)(2,1)S(1)}, u32[]{:S(2)}, u32[]{:S(2)}) %collective-permute-start.33) | collective-permute-done | bytes 524320 | tf_op jit(solution)/shard_map/ppermute | solution.py:18
  195.2 23.8 %collective-permute-done.36 = bf16[512,1024]{1,0:T(8,128)(2,1)S(1)} collective-permute-done((bf16[512,1024]{1,0:T(8,128)(2,1)S(1)}, bf16[512,1024]{1,0:T(8,128)(2,1)S(1)}, u32[]{:S(2)}, u32[]{:S(2)}) %collective-permute-start.36) | collective-permute-done | bytes 1048608 | tf_op jit(solution)/shard_map/ppermute | solution.py:18
  225.7 3.8 collective-permute-done.40
  229.5 17.3 %collective-permute-done.41 = bf16[128,1024]{1,0:T(8,128)(2,1)S(1)} collective-permute-done((bf16[128,1024]{1,0:T(8,128)(2,1)S(1)}, bf16[128,1024]{1,0:T(8,128)(2,1)S(1)}, u32[]{:S(2)}, u32[]{:S(2)}) %collective-permute-start.41) | collective-permute-done | bytes 262176 | tf_op jit(solution)/shard_map/ppermute | solution.py:18
  250.1 26.8 %collective-permute-done.42 = bf16[256,1024]{1,0:T(8,128)(2,1)S(1)} collective-permute-done((bf16[256,1024]{1,0:T(8,128)(2,1)S(1)}, bf16[256,1024]{1,0:T(8,128)(2,1)S(1)}, u32[]{:S(2)}, u32[]{:S(2)}) %collective-permute-start.42) | collective-permute-done | bytes 524320 | tf_op jit(solution)/shard_map/ppermute | solution.py:18
  286.3 3.7 fusion.202
  290.0 4.9 multiply_convert_fusion.2
  303.1 12.3 %collective-permute-done.51 = bf16[256,1024]{1,0:T(8,128)(2,1)S(1)} collective-permute-done((bf16[256,1024]{1,0:T(8,128)(2,1)S(1)}, bf16[256,1024]{1,0:T(8,128)(2,1)S(1)}, u32[]{:S(2)}, u32[]{:S(2)}) %collective-permute-start.51) | collective-permute-done | bytes 524320 | tf_op jit(solution)/shard_map/ppermute | solution.py:18
  317.6 5.5 collective-permute-done.53
  328.3 6.7 collective-permute-done.57
  335.8 4.4 collective-permute-done.58
  344.0 4.3 collective-permute-done.59
  351.3 9.8 %collective-permute-done.61 = bf16[256,1024]{1,0:T(8,128)(2,1)S(1)} collective-permute-done((bf16[256,1024]{1,0:T(8,128)(2,1)S(1)}, bf16[256,1024]{1,0:T(8,128)(2,1)S(1)}, u32[]{:S(2)}, u32[]{:S(2)}) %collective-permute-start.61) | collective-permute-done | bytes 524320 | tf_op jit(solution)/shard_map/ppermute | solution.py:18
  369.7 3.0 constant_dynamic-update-slice_fusion.58
  375.2 3.6 convolution_convert_fusion.4
  382.3 2.7 fusion.18
  385.0 4.1 fusion.1
  389.2 6.0 multiply_convert_fusion
  411.9 3.1 fusion.57
  419.4 2.7 add_convert_fusion.5
  440.7 29.1 %collective-permute-done.71 = bf16[256,1024]{1,0:T(8,128)(2,1)} collective-permute-done((bf16[256,1024]{1,0:T(8,128)(2,1)}, bf16[256,1024]{1,0:T(8,128)(2,1)}, u32[]{:S(2)}, u32[]{:S(2)}) %collective-permute-start.71) | collective-permute-done | bytes 524320 | tf_op jit(solution)/shard_map/ppermute | solution.py:18
  473.0 2.7 add_convert_fusion.3
  484.0 4.7 collective-permute-done.76
  492.6 6.8 collective-permute-done.77
  499.4 11.7 %collective-permute-done.78 = bf16[128,1024]{1,0:T(8,128)(2,1)S(1)} collective-permute-done((bf16[128,1024]{1,0:T(8,128)(2,1)S(1)}, bf16[128,1024]{1,0:T(8,128)(2,1)S(1)}, u32[]{:S(2)}, u32[]{:S(2)}) %collective-permute-start.78) | collective-permute-done | bytes 262176 | tf_op jit(solution)/shard_map/ppermute | solution.py:18
  514.6 22.1 %collective-permute-done.80 = bf16[256,1024]{1,0:T(8,128)(2,1)S(1)} collective-permute-done((bf16[256,1024]{1,0:T(8,128)(2,1)S(1)}, bf16[256,1024]{1,0:T(8,128)(2,1)S(1)}, u32[]{:S(2)}, u32[]{:S(2)}) %collective-permute-start.80) | collective-permute-done | bytes 524320 | tf_op jit(solution)/shard_map/ppermute | solution.py:18
  545.7 30.5 %collective-permute-done.87 = bf16[256,1024]{1,0:T(8,128)(2,1)S(1)} collective-permute-done((bf16[256,1024]{1,0:T(8,128)(2,1)S(1)}, bf16[256,1024]{1,0:T(8,128)(2,1)S(1)}, u32[]{:S(2)}, u32[]{:S(2)}) %collective-permute-start.87) | collective-permute-done | bytes 524320 | tf_op jit(solution)/shard_map/ppermute | solution.py:18
  593.2 2.7 convolution_convert_fusion.19
  623.9 2.7 convert_add_fusion
  627.7 3.3 collective-permute-done.92
  663.8 17.3 %collective-permute-done.101 = bf16[256,1024]{1,0:T(8,128)(2,1)S(1)} collective-permute-done((bf16[256,1024]{1,0:T(8,128)(2,1)S(1)}, bf16[256,1024]{1,0:T(8,128)(2,1)S(1)}, u32[]{:S(2)}, u32[]{:S(2)}) %collective-permute-start.101) | collective-permute-done | bytes 524320 | tf_op jit(solution)/shard_map/ppermute | solution.py:18
  683.2 4.7 collective-permute-done.105
  694.3 15.5 %collective-permute-done.107 = bf16[128,1024]{1,0:T(8,128)(2,1)S(1)} collective-permute-done((bf16[128,1024]{1,0:T(8,128)(2,1)S(1)}, bf16[128,1024]{1,0:T(8,128)(2,1)S(1)}, u32[]{:S(2)}, u32[]{:S(2)}) %collective-permute-start.107) | collective-permute-done | bytes 262176 | tf_op jit(solution)/shard_map/ppermute | solution.py:18
  715.8 6.8 collective-permute-done.114
  725.9 6.2 collective-permute-done.117
  (1006 shorter events, 328.3 us)
Async XLA Ops:
  14.1 31.1 %collective-permute-start.8 = (bf16[128,6144]{1,0:T(8,128)(2,1)S(1)}, bf16[128,6144]{1,0:T(8,128)(2,1)}, u32[]{:S(2)}, u32[]{:S(2)}) collective-permute-start(bf16[128,6144]{1,0:T(8,128)(2,1)S(1)} %pad_maximum_fusion.10), channel_id=1, source_target_pairs={{0,2},{2,0},{1,3},{3,1},{4,6},{6,4},{5,7},{7,5},{8,10},{10,8},{9,1... | collective-permute-start | bytes 4718600 | tf_op jit(solution)/shard_map/ppermute | solution.py:18
  43.7 24.6 %collective-permute-start.14 = (bf16[512,512]{0,1:T(8,128)(2,1)S(1)}, bf16[512,512]{0,1:T(8,128)(2,1)S(1)}, u32[]{:S(2)}, u32[]{:S(2)}) collective-permute-start(bf16[512,512]{0,1:T(8,128)(2,1)S(1)} %pad_maximum_fusion.36), channel_id=1, source_target_pairs={{0,16},{16,0},{1,17},{17,1},{2,18},{18,2},{3,19},{19,3},{4,20},{20... | collective-permute-start | bytes 1572872 | tf_op jit(solution)/shard_map/ppermute | solution.py:18
  46.9 21.4 %collective-permute-start.12 = (bf16[256,1024]{1,0:T(8,128)(2,1)S(1)}, bf16[256,1024]{1,0:T(8,128)(2,1)S(1)}, u32[]{:S(2)}, u32[]{:S(2)}) collective-permute-start(bf16[256,1024]{1,0:T(8,128)(2,1)S(1)} %pad_maximum_fusion.37), channel_id=1, source_target_pairs={{0,8},{8,0},{1,9},{9,1},{2,10},{10,2},{3,11},{11,3},{4,12},{12,4},... | collective-permute-start | bytes 1572872 | tf_op jit(solution)/shard_map/ppermute | solution.py:18
  47.4 20.9 %collective-permute-start.13 = (bf16[256,1024]{1,0:T(8,128)(2,1)S(1)}, bf16[256,1024]{1,0:T(8,128)(2,1)S(1)}, u32[]{:S(2)}, u32[]{:S(2)}) collective-permute-start(bf16[256,1024]{1,0:T(8,128)(2,1)S(1)} %pad_maximum_fusion.38), channel_id=1, source_target_pairs={{0,1},{1,0},{2,3},{3,2},{4,5},{5,4},{6,7},{7,6},{8,9},{9,8},{10,11... | collective-permute-start | bytes 1572872 | tf_op jit(solution)/shard_map/ppermute | solution.py:18
  79.9 27.6 %collective-permute-start.23 = (bf16[512,512]{0,1:T(8,128)(2,1)S(1)}, bf16[512,512]{0,1:T(8,128)(2,1)S(1)}, u32[]{:S(2)}, u32[]{:S(2)}) collective-permute-start(bf16[512,512]{0,1:T(8,128)(2,1)S(1)} %copy-done.150), channel_id=1, source_target_pairs={{0,4},{4,0},{1,5},{5,1},{2,6},{6,2},{3,7},{7,3},{8,12},{12,8},{9,1... | collective-permute-start | bytes 1572872 | tf_op jit(solution)/shard_map/ppermute | solution.py:18
  81.4 26.0 %collective-permute-start.22 = (bf16[512,512]{0,1:T(8,128)(2,1)S(1)}, bf16[512,512]{0,1:T(8,128)(2,1)S(1)}, u32[]{:S(2)}, u32[]{:S(2)}) collective-permute-start(bf16[512,512]{0,1:T(8,128)(2,1)S(1)} %copy-done.150), channel_id=1, source_target_pairs={{0,16},{16,0},{1,17},{17,1},{2,18},{18,2},{3,19},{19,3},{4,20},{20... | collective-permute-start | bytes 1572872 | tf_op jit(solution)/shard_map/ppermute | solution.py:18
  109.9 24.3 %collective-permute-start.27 = (bf16[256,1024]{1,0:T(8,128)(2,1)S(1)}, bf16[256,1024]{1,0:T(8,128)(2,1)S(1)}, u32[]{:S(2)}, u32[]{:S(2)}) collective-permute-start(bf16[256,1024]{1,0:T(8,128)(2,1)S(1)} %broadcast_select_fusion.7), channel_id=1, source_target_pairs={{0,8},{8,0},{1,9},{9,1},{2,10},{10,2},{3,11},{11,3},{4,12},{12,4},... | collective-permute-start | bytes 1572872 | tf_op jit(solution)/shard_map/ppermute | solution.py:18
  110.1 51.3 %collective-permute-start.30 = (bf16[512,1024]{1,0:T(8,128)(2,1)}, bf16[512,1024]{1,0:T(8,128)(2,1)}, u32[]{:S(2)}, u32[]{:S(2)}) collective-permute-start(bf16[512,1024]{1,0:T(8,128)(2,1)} %pad_maximum_fusion.18), channel_id=1, source_target_pairs={{0,16},{16,0},{1,17},{17,1},{2,18},{18,2},{3,19},{19,3},{4,20},{20... | collective-permute-start | bytes 3145736 | tf_op jit(solution)/shard_map/ppermute | solution.py:18
  114.3 47.1 %collective-permute-start.28 = (bf16[512,1024]{1,0:T(8,128)(2,1)}, bf16[512,1024]{1,0:T(8,128)(2,1)}, u32[]{:S(2)}, u32[]{:S(2)}) collective-permute-start(bf16[512,1024]{1,0:T(8,128)(2,1)} %pad_maximum_fusion.18), channel_id=1, source_target_pairs={{0,4},{4,0},{1,5},{5,1},{2,6},{6,2},{3,7},{7,3},{8,12},{12,8},{9,1... | collective-permute-start | bytes 3145736 | tf_op jit(solution)/shard_map/ppermute | solution.py:18
  115.7 45.6 %collective-permute-start.29 = (bf16[256,1024]{1,0:T(8,128)(2,1)}, bf16[256,1024]{1,0:T(8,128)(2,1)}, u32[]{:S(2)}, u32[]{:S(2)}) collective-permute-start(bf16[256,1024]{1,0:T(8,128)(2,1)} %broadcast_select_fusion.6), channel_id=1, source_target_pairs={{0,8},{8,0},{1,9},{9,1},{2,10},{10,2},{3,11},{11,3},{4,12},{12,4},... | collective-permute-start | bytes 1572872 | tf_op jit(solution)/shard_map/ppermute | solution.py:18
  168.0 21.6 %collective-permute-start.33 = (bf16[256,1024]{1,0:T(8,128)(2,1)S(1)}, bf16[256,1024]{1,0:T(8,128)(2,1)S(1)}, u32[]{:S(2)}, u32[]{:S(2)}) collective-permute-start(bf16[256,1024]{1,0:T(8,128)(2,1)S(1)} %slice.2362), channel_id=1, source_target_pairs={{0,8},{8,0},{1,9},{9,1},{2,10},{10,2},{3,11},{11,3},{4,12},{12,4},... | collective-permute-start | bytes 1572872 | tf_op jit(solution)/shard_map/ppermute | solution.py:18
  168.1 21.5 %collective-permute-start.34 = (bf16[256,1024]{1,0:T(8,128)(2,1)S(1)}, bf16[256,1024]{1,0:T(8,128)(2,1)S(1)}, u32[]{:S(2)}, u32[]{:S(2)}) collective-permute-start(bf16[256,1024]{1,0:T(8,128)(2,1)S(1)} %pad_maximum_fusion.40), channel_id=1, source_target_pairs={{0,1},{1,0},{2,3},{3,2},{4,5},{5,4},{6,7},{7,6},{8,9},{9,8},{10,11... | collective-permute-start | bytes 1572872 | tf_op jit(solution)/shard_map/ppermute | solution.py:18
  169.2 26.0 %collective-permute-start.35 = (bf16[512,1024]{1,0:T(8,128)(2,1)S(1)}, bf16[512,1024]{1,0:T(8,128)(2,1)S(1)}, u32[]{:S(2)}, u32[]{:S(2)}) collective-permute-start(bf16[512,1024]{1,0:T(8,128)(2,1)S(1)} %copy-done.132), channel_id=1, source_target_pairs={{0,4},{4,0},{1,5},{5,1},{2,6},{6,2},{3,7},{7,3},{8,12},{12,8},{9,1... | collective-permute-start | bytes 3145736 | tf_op jit(solution)/shard_map/ppermute | solution.py:18
  170.7 48.3 %collective-permute-start.36 = (bf16[512,1024]{1,0:T(8,128)(2,1)S(1)}, bf16[512,1024]{1,0:T(8,128)(2,1)S(1)}, u32[]{:S(2)}, u32[]{:S(2)}) collective-permute-start(bf16[512,1024]{1,0:T(8,128)(2,1)S(1)} %copy-done.132), channel_id=1, source_target_pairs={{0,16},{16,0},{1,17},{17,1},{2,18},{18,2},{3,19},{19,3},{4,20},{20... | collective-permute-start | bytes 3145736 | tf_op jit(solution)/shard_map/ppermute | solution.py:18
  172.2 46.8 %collective-permute-start.37 = (bf16[512,1024]{1,0:T(8,128)(2,1)}, bf16[512,1024]{1,0:T(8,128)(2,1)S(1)}, u32[]{:S(2)}, u32[]{:S(2)}) collective-permute-start(bf16[512,1024]{1,0:T(8,128)(2,1)} %collective-permute-done.30), channel_id=1, source_target_pairs={{0,4},{4,0},{1,5},{5,1},{2,6},{6,2},{3,7},{7,3},{8,12},{12,8},{9,1... | collective-permute-start | bytes 3145736 | tf_op jit(solution)/shard_map/ppermute | solution.py:18
  190.0 31.0 %collective-permute-start.38 = (bf16[128,1024]{1,0:T(8,128)(2,1)S(1)}, bf16[128,1024]{1,0:T(8,128)(2,1)S(1)}, u32[]{:S(2)}, u32[]{:S(2)}) collective-permute-start(bf16[128,1024]{1,0:T(8,128)(2,1)S(1)} %slice.2369), channel_id=1, source_target_pairs={{0,1},{1,0},{2,3},{3,2},{4,5},{5,4},{6,7},{7,6},{8,9},{9,8},{10,11... | collective-permute-start | bytes 786440 | tf_op jit(solution)/shard_map/ppermute | solution.py:18
  190.3 30.8 %collective-permute-start.39 = (bf16[128,1024]{1,0:T(8,128)(2,1)S(1)}, bf16[128,1024]{1,0:T(8,128)(2,1)S(1)}, u32[]{:S(2)}, u32[]{:S(2)}) collective-permute-start(bf16[128,1024]{1,0:T(8,128)(2,1)S(1)} %slice.2368), channel_id=1, source_target_pairs={{0,8},{8,0},{1,9},{9,1},{2,10},{10,2},{3,11},{11,3},{4,12},{12,4},... | collective-permute-start | bytes 786440 | tf_op jit(solution)/shard_map/ppermute | solution.py:18
  219.0 57.9 %collective-permute-start.44 = (bf16[512,1024]{1,0:T(8,128)(2,1)S(1)}, bf16[512,1024]{1,0:T(8,128)(2,1)S(1)}, u32[]{:S(2)}, u32[]{:S(2)}) collective-permute-start(bf16[512,1024]{1,0:T(8,128)(2,1)S(1)} %collective-permute-done.36), channel_id=1, source_target_pairs={{0,4},{4,0},{1,5},{5,1},{2,6},{6,2},{3,7},{7,3},{8,12},{12,8},{9,1... | collective-permute-start | bytes 3145736 | tf_op jit(solution)/shard_map/ppermute | solution.py:18
  219.5 57.4 %collective-permute-start.45 = (bf16[512,1024]{1,0:T(8,128)(2,1)S(1)}, bf16[512,1024]{1,0:T(8,128)(2,1)S(1)}, u32[]{:S(2)}, u32[]{:S(2)}) collective-permute-start(bf16[512,1024]{1,0:T(8,128)(2,1)S(1)} %pad_maximum_fusion.20), channel_id=1, source_target_pairs={{0,16},{16,0},{1,17},{17,1},{2,18},{18,2},{3,19},{19,3},{4,20},{20... | collective-permute-start | bytes 3145736 | tf_op jit(solution)/shard_map/ppermute | solution.py:18
  219.5 57.4 %collective-permute-start.46 = (bf16[512,1024]{1,0:T(8,128)(2,1)S(1)}, bf16[512,1024]{1,0:T(8,128)(2,1)S(1)}, u32[]{:S(2)}, u32[]{:S(2)}) collective-permute-start(bf16[512,1024]{1,0:T(8,128)(2,1)S(1)} %pad_maximum_fusion.20), channel_id=1, source_target_pairs={{0,4},{4,0},{1,5},{5,1},{2,6},{6,2},{3,7},{7,3},{8,12},{12,8},{9,1... | collective-permute-start | bytes 3145736 | tf_op jit(solution)/shard_map/ppermute | solution.py:18
  223.7 23.1 %collective-permute-start.41 = (bf16[128,1024]{1,0:T(8,128)(2,1)S(1)}, bf16[128,1024]{1,0:T(8,128)(2,1)S(1)}, u32[]{:S(2)}, u32[]{:S(2)}) collective-permute-start(bf16[128,1024]{1,0:T(8,128)(2,1)S(1)} %get-tuple-element.664), channel_id=1, source_target_pairs={{0,8},{8,0},{1,9},{9,1},{2,10},{10,2},{3,11},{11,3},{4,12},{12,4},... | collective-permute-start | bytes 786440 | tf_op jit(solution)/shard_map/ppermute | solution.py:18
  246.8 30.1 %collective-permute-start.42 = (bf16[256,1024]{1,0:T(8,128)(2,1)S(1)}, bf16[256,1024]{1,0:T(8,128)(2,1)S(1)}, u32[]{:S(2)}, u32[]{:S(2)}) collective-permute-start(bf16[256,1024]{1,0:T(8,128)(2,1)S(1)} %pad_maximum_fusion.41), channel_id=1, source_target_pairs={{0,8},{8,0},{1,9},{9,1},{2,10},{10,2},{3,11},{11,3},{4,12},{12,4},... | collective-permute-start | bytes 1572872 | tf_op jit(solution)/shard_map/ppermute | solution.py:18
  249.4 27.5 %collective-permute-start.43 = (bf16[256,1024]{1,0:T(8,128)(2,1)S(1)}, bf16[256,1024]{1,0:T(8,128)(2,1)S(1)}, u32[]{:S(2)}, u32[]{:S(2)}) collective-permute-start(bf16[256,1024]{1,0:T(8,128)(2,1)S(1)} %pad_maximum_fusion.42), channel_id=1, source_target_pairs={{0,1},{1,0},{2,3},{3,2},{4,5},{5,4},{6,7},{7,6},{8,9},{9,8},{10,11... | collective-permute-start | bytes 1572872 | tf_op jit(solution)/shard_map/ppermute | solution.py:18
  297.6 25.5 %collective-permute-start.55 = (bf16[512,1024]{1,0:T(8,128)(2,1)S(1)}, bf16[512,1024]{1,0:T(8,128)(2,1)S(1)}, u32[]{:S(2)}, u32[]{:S(2)}) collective-permute-start(bf16[512,1024]{1,0:T(8,128)(2,1)S(1)} %collective-permute-done.45), channel_id=1, source_target_pairs={{0,4},{4,0},{1,5},{5,1},{2,6},{6,2},{3,7},{7,3},{8,12},{12,8},{9,1... | collective-permute-start | bytes 3145736 | tf_op jit(solution)/shard_map/ppermute | solution.py:18
  380.2 26.6 %collective-permute-start.66 = (bf16[512,1024]{1,0:T(8,128)(2,1)S(1)}, bf16[512,1024]{1,0:T(8,128)(2,1)S(1)}, u32[]{:S(2)}, u32[]{:S(2)}) collective-permute-start(bf16[512,1024]{1,0:T(8,128)(2,1)S(1)} %convolution_convert_fusion.5), channel_id=1, source_target_pairs={{0,4},{4,0},{1,5},{5,1},{2,6},{6,2},{3,7},{7,3},{8,12},{12,8},{9,1... | collective-permute-start | bytes 3145736 | tf_op jit(solution)/shard_map/ppermute | solution.py:18
  380.6 58.3 %collective-permute-start.70 = (bf16[512,1024]{1,0:T(8,128)(2,1)}, bf16[512,1024]{1,0:T(8,128)(2,1)}, u32[]{:S(2)}, u32[]{:S(2)}) collective-permute-start(bf16[512,1024]{1,0:T(8,128)(2,1)} %convolution_convert_fusion.4), channel_id=1, source_target_pairs={{0,4},{4,0},{1,5},{5,1},{2,6},{6,2},{3,7},{7,3},{8,12},{12,8},{9,1... | collective-permute-start | bytes 3145736 | tf_op jit(solution)/shard_map/ppermute | solution.py:18
  409.2 63.4 %collective-permute-start.73 = (bf16[512,1024]{1,0:T(8,128)(2,1)}, bf16[512,1024]{1,0:T(8,128)(2,1)}, u32[]{:S(2)}, u32[]{:S(2)}) collective-permute-start(bf16[512,1024]{1,0:T(8,128)(2,1)} %convolution_convert_fusion.3), channel_id=1, source_target_pairs={{0,4},{4,0},{1,5},{5,1},{2,6},{6,2},{3,7},{7,3},{8,12},{12,8},{9,1... | collective-permute-start | bytes 3145736 | tf_op jit(solution)/shard_map/ppermute | solution.py:18
  409.5 63.1 %collective-permute-start.74 = (bf16[512,1024]{1,0:T(8,128)(2,1)}, bf16[512,1024]{1,0:T(8,128)(2,1)}, u32[]{:S(2)}, u32[]{:S(2)}) collective-permute-start(bf16[512,1024]{1,0:T(8,128)(2,1)} %add_convert_fusion.6), channel_id=1, source_target_pairs={{0,16},{16,0},{1,17},{17,1},{2,18},{18,2},{3,19},{19,3},{4,20},{20... | collective-permute-start | bytes 3145736 | tf_op jit(solution)/shard_map/ppermute | solution.py:18
  434.1 35.7 %collective-permute-start.71 = (bf16[256,1024]{1,0:T(8,128)(2,1)}, bf16[256,1024]{1,0:T(8,128)(2,1)}, u32[]{:S(2)}, u32[]{:S(2)}) collective-permute-start(bf16[256,1024]{1,0:T(8,128)(2,1)} %slice.2360), channel_id=1, source_target_pairs={{0,8},{8,0},{1,9},{9,1},{2,10},{10,2},{3,11},{11,3},{4,12},{12,4},... | collective-permute-start | bytes 1572872 | tf_op jit(solution)/shard_map/ppermute | solution.py:18
  434.8 35.1 %collective-permute-start.72 = (bf16[256,1024]{1,0:T(8,128)(2,1)}, bf16[256,1024]{1,0:T(8,128)(2,1)}, u32[]{:S(2)}, u32[]{:S(2)}) collective-permute-start(bf16[256,1024]{1,0:T(8,128)(2,1)} %pad_maximum_fusion.45), channel_id=1, source_target_pairs={{0,1},{1,0},{2,3},{3,2},{4,5},{5,4},{6,7},{7,6},{8,9},{9,8},{10,11... | collective-permute-start | bytes 1572872 | tf_op jit(solution)/shard_map/ppermute | solution.py:18
  438.9 75.6 %collective-permute-start.79 = (bf16[512,1024]{1,0:T(8,128)(2,1)}, bf16[512,1024]{1,0:T(8,128)(2,1)S(1)}, u32[]{:S(2)}, u32[]{:S(2)}) collective-permute-start(bf16[512,1024]{1,0:T(8,128)(2,1)} %convolution_convert_fusion.2), channel_id=1, source_target_pairs={{0,4},{4,0},{1,5},{5,1},{2,6},{6,2},{3,7},{7,3},{8,12},{12,8},{9,1... | collective-permute-start | bytes 3145736 | tf_op jit(solution)/shard_map/ppermute | solution.py:18
  477.2 59.5 %collective-permute-start.82 = (bf16[512,1024]{1,0:T(8,128)(2,1)S(1)}, bf16[512,1024]{1,0:T(8,128)(2,1)S(1)}, u32[]{:S(2)}, u32[]{:S(2)}) collective-permute-start(bf16[512,1024]{1,0:T(8,128)(2,1)S(1)} %copy-done.143), channel_id=1, source_target_pairs={{0,4},{4,0},{1,5},{5,1},{2,6},{6,2},{3,7},{7,3},{8,12},{12,8},{9,1... | collective-permute-start | bytes 3145736 | tf_op jit(solution)/shard_map/ppermute | solution.py:18
  477.6 59.1 %collective-permute-start.83 = (bf16[512,1024]{1,0:T(8,128)(2,1)S(1)}, bf16[512,1024]{1,0:T(8,128)(2,1)S(1)}, u32[]{:S(2)}, u32[]{:S(2)}) collective-permute-start(bf16[512,1024]{1,0:T(8,128)(2,1)S(1)} %add_convert_fusion.3), channel_id=1, source_target_pairs={{0,16},{16,0},{1,17},{17,1},{2,18},{18,2},{3,19},{19,3},{4,20},{20... | collective-permute-start | bytes 3145736 | tf_op jit(solution)/shard_map/ppermute | solution.py:18
  511.1 25.6 %collective-permute-start.80 = (bf16[256,1024]{1,0:T(8,128)(2,1)S(1)}, bf16[256,1024]{1,0:T(8,128)(2,1)S(1)}, u32[]{:S(2)}, u32[]{:S(2)}) collective-permute-start(bf16[256,1024]{1,0:T(8,128)(2,1)S(1)} %pad_maximum_fusion.46), channel_id=1, source_target_pairs={{0,8},{8,0},{1,9},{9,1},{2,10},{10,2},{3,11},{11,3},{4,12},{12,4},... | collective-permute-start | bytes 1572872 | tf_op jit(solution)/shard_map/ppermute | solution.py:18
  513.7 23.0 %collective-permute-start.81 = (bf16[256,1024]{1,0:T(8,128)(2,1)S(1)}, bf16[256,1024]{1,0:T(8,128)(2,1)S(1)}, u32[]{:S(2)}, u32[]{:S(2)}) collective-permute-start(bf16[256,1024]{1,0:T(8,128)(2,1)S(1)} %pad_maximum_fusion.47), channel_id=1, source_target_pairs={{0,1},{1,0},{2,3},{3,2},{4,5},{5,4},{6,7},{7,6},{8,9},{9,8},{10,11... | collective-permute-start | bytes 1572872 | tf_op jit(solution)/shard_map/ppermute | solution.py:18
  514.5 31.1 %collective-permute-start.86 = (bf16[512,1024]{1,0:T(8,128)(2,1)S(1)}, bf16[512,1024]{1,0:T(8,128)(2,1)S(1)}, u32[]{:S(2)}, u32[]{:S(2)}) collective-permute-start(bf16[512,1024]{1,0:T(8,128)(2,1)S(1)} %copy-done.138), channel_id=1, source_target_pairs={{0,4},{4,0},{1,5},{5,1},{2,6},{6,2},{3,7},{7,3},{8,12},{12,8},{9,1... | collective-permute-start | bytes 3145736 | tf_op jit(solution)/shard_map/ppermute | solution.py:18
  542.1 34.1 %collective-permute-start.87 = (bf16[256,1024]{1,0:T(8,128)(2,1)S(1)}, bf16[256,1024]{1,0:T(8,128)(2,1)S(1)}, u32[]{:S(2)}, u32[]{:S(2)}) collective-permute-start(bf16[256,1024]{1,0:T(8,128)(2,1)S(1)} %select_convert_fusion.5), channel_id=1, source_target_pairs={{0,8},{8,0},{1,9},{9,1},{2,10},{10,2},{3,11},{11,3},{4,12},{12,4},... | collective-permute-start | bytes 1572872 | tf_op jit(solution)/shard_map/ppermute | solution.py:18
  542.3 66.9 %collective-permute-start.89 = (bf16[256,1024]{1,0:T(8,128)(2,1)}, bf16[256,1024]{1,0:T(8,128)(2,1)}, u32[]{:S(2)}, u32[]{:S(2)}) collective-permute-start(bf16[256,1024]{1,0:T(8,128)(2,1)} %select_convert_fusion.4), channel_id=1, source_target_pairs={{0,8},{8,0},{1,9},{9,1},{2,10},{10,2},{3,11},{11,3},{4,12},{12,4},... | collective-permute-start | bytes 1572872 | tf_op jit(solution)/shard_map/ppermute | solution.py:18
  544.4 77.3 %collective-permute-start.90 = (bf16[512,1024]{1,0:T(8,128)(2,1)}, bf16[512,1024]{1,0:T(8,128)(2,1)}, u32[]{:S(2)}, u32[]{:S(2)}) collective-permute-start(bf16[512,1024]{1,0:T(8,128)(2,1)} %add_convert_fusion.2), channel_id=1, source_target_pairs={{0,16},{16,0},{1,17},{17,1},{2,18},{18,2},{3,19},{19,3},{4,20},{20... | collective-permute-start | bytes 3145736 | tf_op jit(solution)/shard_map/ppermute | solution.py:18
  578.6 48.6 %collective-permute-start.91 = (bf16[128,2048]{1,0:T(8,128)(2,1)}, bf16[128,2048]{1,0:T(8,128)(2,1)}, u32[]{:S(2)}, u32[]{:S(2)}) collective-permute-start(bf16[128,2048]{1,0:T(8,128)(2,1)} %select_convert_fusion.3), channel_id=1, source_target_pairs={{0,2},{2,0},{1,3},{3,1},{4,6},{6,4},{5,7},{7,5},{8,10},{10,8},{9,1... | collective-permute-start | bytes 1572872 | tf_op jit(solution)/shard_map/ppermute | solution.py:18
  623.7 21.6 %collective-permute-start.97 = (bf16[128,2048]{1,0:T(8,128)(2,1)}, bf16[128,2048]{1,0:T(8,128)(2,1)}, u32[]{:S(2)}, u32[]{:S(2)}) collective-permute-start(bf16[128,2048]{1,0:T(8,128)(2,1)} %select_convert_fusion.2), channel_id=1, source_target_pairs={{0,2},{2,0},{1,3},{3,1},{4,6},{6,4},{5,7},{7,5},{8,10},{10,8},{9,1... | collective-permute-start | bytes 1572872 | tf_op jit(solution)/shard_map/ppermute | solution.py:18
  649.5 33.7 %collective-permute-start.103 = (f32[4,512]{1,0:T(4,128)S(1)}, f32[4,512]{1,0:T(4,128)S(1)}, u32[]{:S(2)}, u32[]{:S(2)}) collective-permute-start(f32[4,512]{1,0:T(4,128)S(1)} %slice.1296), channel_id=1, source_target_pairs={{0,16},{16,0},{1,17},{17,1},{2,18},{18,2},{3,19},{19,3},{4,20},{20... | collective-permute-start | bytes 24584 | tf_op jit(solution)/shard_map/ppermute | solution.py:18
  650.4 32.8 %collective-permute-start.104 = (bf16[512,512]{0,1:T(8,128)(2,1)S(1)}, bf16[512,512]{0,1:T(8,128)(2,1)S(1)}, u32[]{:S(2)}, u32[]{:S(2)}) collective-permute-start(bf16[512,512]{0,1:T(8,128)(2,1)S(1)} %pad_maximum_fusion.50), channel_id=1, source_target_pairs={{0,4},{4,0},{1,5},{5,1},{2,6},{6,2},{3,7},{7,3},{8,12},{12,8},{9,1... | collective-permute-start | bytes 1572872 | tf_op jit(solution)/shard_map/ppermute | solution.py:18
  658.7 22.3 %collective-permute-start.101 = (bf16[256,1024]{1,0:T(8,128)(2,1)S(1)}, bf16[256,1024]{1,0:T(8,128)(2,1)S(1)}, u32[]{:S(2)}, u32[]{:S(2)}) collective-permute-start(bf16[256,1024]{1,0:T(8,128)(2,1)S(1)} %slice.2359), channel_id=1, source_target_pairs={{0,8},{8,0},{1,9},{9,1},{2,10},{10,2},{3,11},{11,3},{4,12},{12,4},... | collective-permute-start | bytes 1572872 | tf_op jit(solution)/shard_map/ppermute | solution.py:18
  662.8 25.1 %collective-permute-start.105 = (bf16[512,512]{0,1:T(8,128)(2,1)S(1)}, bf16[512,512]{0,1:T(8,128)(2,1)S(1)}, u32[]{:S(2)}, u32[]{:S(2)}) collective-permute-start(bf16[512,512]{0,1:T(8,128)(2,1)S(1)} %fusion.26), channel_id=1, source_target_pairs={{0,16},{16,0},{1,17},{17,1},{2,18},{18,2},{3,19},{19,3},{4,20},{20... | collective-permute-start | bytes 1572872 | tf_op jit(solution)/shard_map/ppermute | solution.py:18
  681.1 29.5 %collective-permute-start.109 = (bf16[256,1024]{1,0:T(8,128)(2,1)S(1)}, bf16[256,1024]{1,0:T(8,128)(2,1)S(1)}, u32[]{:S(2)}, u32[]{:S(2)}) collective-permute-start(bf16[256,1024]{1,0:T(8,128)(2,1)S(1)} %select_convert_fusion.1), channel_id=1, source_target_pairs={{0,8},{8,0},{1,9},{9,1},{2,10},{10,2},{3,11},{11,3},{4,12},{12,4},... | collective-permute-start | bytes 1572872 | tf_op jit(solution)/shard_map/ppermute | solution.py:18
  681.1 30.1 %collective-permute-start.110 = (bf16[512,512]{0,1:T(8,128)(2,1)S(1)}, bf16[512,512]{0,1:T(8,128)(2,1)S(1)}, u32[]{:S(2)}, u32[]{:S(2)}) collective-permute-start(bf16[512,512]{0,1:T(8,128)(2,1)S(1)} %pad_maximum_fusion.52), channel_id=1, source_target_pairs={{0,4},{4,0},{1,5},{5,1},{2,6},{6,2},{3,7},{7,3},{8,12},{12,8},{9,1... | collective-permute-start | bytes 1572872 | tf_op jit(solution)/shard_map/ppermute | solution.py:18
  694.3 28.6 %collective-permute-start.115 = (bf16[512,512]{0,1:T(8,128)(2,1)S(1)}, bf16[512,512]{0,1:T(8,128)(2,1)S(1)}, u32[]{:S(2)}, u32[]{:S(2)}) collective-permute-start(bf16[512,512]{0,1:T(8,128)(2,1)S(1)} %fusion.27), channel_id=1, source_target_pairs={{0,16},{16,0},{1,17},{17,1},{2,18},{18,2},{3,19},{19,3},{4,20},{20... | collective-permute-start | bytes 1572872 | tf_op jit(solution)/shard_map/ppermute | solution.py:18
  (273 other events, 2520.6 us)

commit v6 on v5

--- a/solution.py
+++ b/solution.py
@@ -254,11 +254,11 @@
             axis=1,
         )
         ids_sent = c.start(ids, "zl")
-        right_sent = c.start(right, "zl")
         qk.end_line()
         gain_steps()
         qk.start_x(0)
         qk.start_high()
+        right_sent = c.start(right, "zl")
         vo.start_line()
         left = stack2(left, c.sync(left_sent))
         seq_ids = stack2(ids, c.sync(ids_sent))
@@ -303,13 +303,11 @@
             gain_steps()
             qk.end_x(0)
             vo.start_x(0)
-
-        def tokens_last():
             qk.end_high()
             qk.start_x(1)
             vo.start_high()
 
-        in0, in1 = rows_second(left, right, tokens_between, tokens_last)
+        in0, in1 = rows_second(left, right, tokens_between)
         seq_ids = stack2(seq_ids, c.sync(ids_sent))
         gate_w.end_line()
         gains = gain_steps.finish()
@@ -378,6 +376,7 @@
             "bhqk,bkhd->bqhd", prob_bf, value_heads, preferred_element_type=F32
         ).astype(BF)
         attn = attn_heads.reshape(group_tokens, head_width)
+        attn = c.sync(attn)
         up_w.end_line()
         gate_w.end_x(0)
         up_w.start_x(0)
@@ -568,8 +567,6 @@
 
         p0, p1 = gather_rows(d_proj, proj_between, proj_last)
         up_grad.end_x(0)
-        down_grad.end_line()
-        p0, p1 = c.fence(p0, p1)
         d_attn = (dot(p0, wo0) + dot(p1, wo1)).astype(BF)
 
         d_attn_heads = d_attn.reshape(heads)
@@ -578,6 +575,10 @@
             .reshape(group_tokens, head_width)
             .astype(BF)
         )
+        ov_grad = Grad(((p0, p1), attn), ((in0, in1), d_value))
+        ov_grad.start_x(1)
+        d_attn = c.fence(d_attn)
+        d_attn_heads = d_attn.reshape(heads)
         d_prob = jnp.einsum(
             "bqhd,bkhd->bhqk", d_attn_heads, value_heads, preferred_element_type=F32
         )
@@ -609,14 +610,14 @@
             [to_relative(placed), jnp.stack([attn_gain_term, ffn_gain_term])], axis=0
         )
         gain_steps = Steps(scatter_gains(c, gain_parts))
-        gate_grad.end_line()
-        ov_grad = Grad(((p0, p1), attn), ((in0, in1), d_value))
-        ov_grad.start_x(1)
+        inner = c.sync(
+            jnp.stack([jnp.sum(scaled_q * query, axis=1), jnp.sum(scaled_k * key_proj, axis=1)])
+        )
         up_grad.end_high()
-        down_grad.end()
-        inner = pair_sum(
-            c, jnp.stack([jnp.sum(scaled_q * query, axis=1), jnp.sum(scaled_k * key_proj, axis=1)])
-        )
+        ov_grad.end_x(1)
+        ov_grad.start_high()
+        down_grad.end_line()
+        inner = pair_sum(c, inner)
         gain_steps()
         d_query = (
             q_rms * (scaled_q - query * q_rms * q_rms * (inner[0] / model_width)[:, None])
@@ -626,22 +627,22 @@
         ).astype(BF)
         d_qk = columns([d_query, d_key])
         qk_grad = Grad(((in0, in1), d_query), ((in0, in1), d_key))
-        ov_grad.end_x(1)
-        ov_grad.start_high()
         qk_grad.start_x(1)
+        gate_grad.end_line()
+        down_grad.end()
         ov_grad.start_x(0)
-        gate_grad.end()
 
         def tokens_first():
-            up_grad.start_line()
+            ov_grad.end_x(0)
+            ov_grad.end_high()
             qk_grad.end_x(1)
+            qk_grad.start_high()
             qk_grad.start_x(0)
 
         def tokens_second():
             gain_steps()
-            ov_grad.end_x(0)
-            ov_grad.end_high()
-            qk_grad.start_high()
+            up_grad.start_line()
+            gate_grad.end()
 
         d_tokens = columns(
             scatter_rows(
@@ -653,15 +654,15 @@
         )
         grad_tokens = to_natural(d_resid + d_tokens)
         gain_steps()
+        ov_grad.start_line()
         up_grad.end_line()
-        ov_grad.start_line()
+        gain_steps()
         qk_grad.end_x(0)
-        gain_steps()
-        up_grad.end()
+        ov_grad.end_line()
         gain_parts = gain_steps.finish()
-        ov_grad.end_line()
         qk_grad.end_high()
         qk_grad.start_line()
+        up_grad.end()
         ov_grad.end()
         qk_grad.end_line()
         qk_grad.end()

time: 745 us -> 714 us (0.958)
  waiting for transfers between devices: 365 us -> 328 us
  starting transfers between devices: 94.6 us -> 110 us
    ppermute x119, waiting for transfers between devices: 365 us -> 328 us  [swap(): return lax.ppermute(value, axis, FLIP)]
    ppermute x119, starting transfers between devices: 94.6 us -> 110 us  [swap(): return lax.ppermute(value, axis, FLIP)]
    unnamed x452 -> x442, local copies, waits for them, and re-layouts: 34.1 us -> 30.7 us
  transfers between devices with their start and end apart: 119 -> 119, of which waited for: 47 -> 48; matrix products, arithmetic and copies ran while one was open for 28% -> 28% of each run, Pallas kernels for 0% -> 0%
where the time goes in v6:
time: 714 us; the launch traced here: 707 us
  waiting for transfers between devices  328 us (46%)
  matrix products  124 us (17%)
  starting transfers between devices  110 us (15%)
  other arithmetic  77.3 us (11%)
  local copies, waits for them, and re-layouts  61.4 us (9%)
    ppermute x119, waiting for transfers between devices, swap(): return lax.ppermute(value, axis, FLIP)  328 us
    ppermute x119, starting transfers between devices, swap(): return lax.ppermute(value, axis, FLIP)  110 us
    dot_general x28, matrix products, dot_tn(): return jnp.einsum('sr,sc->rc', a, b, preferred_element_type=F32)  46.8 us
    dot_general x12, matrix products, dot(): return jnp.dot(a, b, preferred_element_type=F32)  33.1 us
    dot_general x26, matrix products, dot_nt(): return jnp.einsum('sc,rc->sr', a, b, preferred_element_type=F32)  31 us
    unnamed x442, local copies, waits for them, and re-layouts  30.7 us
    select_n x34, other arithmetic, pick(): return jnp.where(bit(axis) == 0, low, high)  16.7 us
  transfers between devices with their start and end apart: 119, of which 48 were waited for; matrix products, arithmetic and copies ran while one was open for 28% of the time, Pallas kernels for 0%

profile of v6, /device:TPU:0, one launch (start us, length us, event | category | flops | bytes accessed | tf_op | source)
XLA Modules:
  0.0 707.1 jit_solution(13689752368539070107)
XLA Ops:
  6.0 3.1 collective-permute-start
  25.8 4.5 collective-permute-done.3
  33.4 2.8 collective-permute-start.10
  46.3 4.7 collective-permute-done.9
  55.7 7.9 %collective-permute-done.12 = bf16[512,512]{0,1:T(8,128)(2,1)S(1)} collective-permute-done((bf16[512,512]{0,1:T(8,128)(2,1)S(1)}, bf16[512,512]{0,1:T(8,128)(2,1)S(1)}, u32[]{:S(2)}, u32[]{:S(2)}) %collective-permute-start.12) | collective-permute-done | bytes 524320 | tf_op jit(solution)/shard_map/ppermute | solution.py:18
  63.6 3.2 collective-permute-done.13
  84.0 8.3 %collective-permute-done.18 = bf16[256,1024]{1,0:T(8,128)(2,1)S(1)} collective-permute-done((bf16[256,1024]{1,0:T(8,128)(2,1)}, bf16[256,1024]{1,0:T(8,128)(2,1)S(1)}, u32[]{:S(2)}, u32[]{:S(2)}) %collective-permute-start.18) | collective-permute-done | bytes 524320 | tf_op jit(solution)/shard_map/ppermute | solution.py:18
  92.3 2.8 pad_maximum_fusion
  110.3 3.0 collective-permute-start.30
  116.2 6.7 collective-permute-done.26
  129.2 3.4 add_convert_fusion.9
  132.6 3.4 fusion.221
  138.0 2.9 fusion.8
  147.2 9.4 %collective-permute-done.29 = bf16[256,1024]{1,0:T(8,128)(2,1)} collective-permute-done((bf16[256,1024]{1,0:T(8,128)(2,1)}, bf16[256,1024]{1,0:T(8,128)(2,1)}, u32[]{:S(2)}, u32[]{:S(2)}) %collective-permute-start.29) | collective-permute-done | bytes 524320 | tf_op jit(solution)/shard_map/ppermute | solution.py:18
  156.5 3.2 collective-permute-done.30
  167.7 3.0 collective-permute-start.36
  171.3 15.5 %collective-permute-done.33 = bf16[256,1024]{1,0:T(8,128)(2,1)S(1)} collective-permute-done((bf16[256,1024]{1,0:T(8,128)(2,1)S(1)}, bf16[256,1024]{1,0:T(8,128)(2,1)S(1)}, u32[]{:S(2)}, u32[]{:S(2)}) %collective-permute-start.33) | collective-permute-done | bytes 524320 | tf_op jit(solution)/shard_map/ppermute | solution.py:18
  192.2 23.6 %collective-permute-done.36 = bf16[512,1024]{1,0:T(8,128)(2,1)S(1)} collective-permute-done((bf16[512,1024]{1,0:T(8,128)(2,1)S(1)}, bf16[512,1024]{1,0:T(8,128)(2,1)S(1)}, u32[]{:S(2)}, u32[]{:S(2)}) %collective-permute-start.36) | collective-permute-done | bytes 1048608 | tf_op jit(solution)/shard_map/ppermute | solution.py:18
  223.1 3.4 collective-permute-done.40
  226.5 18.0 %collective-permute-done.41 = bf16[128,1024]{1,0:T(8,128)(2,1)S(1)} collective-permute-done((bf16[128,1024]{1,0:T(8,128)(2,1)S(1)}, bf16[128,1024]{1,0:T(8,128)(2,1)S(1)}, u32[]{:S(2)}, u32[]{:S(2)}) %collective-permute-start.41) | collective-permute-done | bytes 262176 | tf_op jit(solution)/shard_map/ppermute | solution.py:18
  247.7 26.7 %collective-permute-done.42 = bf16[256,1024]{1,0:T(8,128)(2,1)S(1)} collective-permute-done((bf16[256,1024]{1,0:T(8,128)(2,1)S(1)}, bf16[256,1024]{1,0:T(8,128)(2,1)S(1)}, u32[]{:S(2)}, u32[]{:S(2)}) %collective-permute-start.42) | collective-permute-done | bytes 524320 | tf_op jit(solution)/shard_map/ppermute | solution.py:18
  283.7 3.6 fusion.196
  287.4 5.1 multiply_convert_fusion.2
  299.5 13.2 %collective-permute-done.51 = bf16[256,1024]{1,0:T(8,128)(2,1)S(1)} collective-permute-done((bf16[256,1024]{1,0:T(8,128)(2,1)S(1)}, bf16[256,1024]{1,0:T(8,128)(2,1)S(1)}, u32[]{:S(2)}, u32[]{:S(2)}) %collective-permute-start.51) | collective-permute-done | bytes 524320 | tf_op jit(solution)/shard_map/ppermute | solution.py:18
  313.9 6.4 collective-permute-done.53
  324.6 7.7 %collective-permute-done.57 = bf16[256,512]{1,0:T(8,128)(2,1)S(1)} collective-permute-done((bf16[256,512]{1,0:T(8,128)(2,1)S(1)}, bf16[256,512]{1,0:T(8,128)(2,1)S(1)}, u32[]{:S(2)}, u32[]{:S(2)}) %collective-permute-start.57) | collective-permute-done | bytes 262176 | tf_op jit(solution)/shard_map/ppermute | solution.py:18
  333.1 4.4 collective-permute-done.58
  340.3 5.3 collective-permute-done.59
  348.6 8.8 %collective-permute-done.61 = bf16[256,1024]{1,0:T(8,128)(2,1)S(1)} collective-permute-done((bf16[256,1024]{1,0:T(8,128)(2,1)S(1)}, bf16[256,1024]{1,0:T(8,128)(2,1)S(1)}, u32[]{:S(2)}, u32[]{:S(2)}) %collective-permute-start.61) | collective-permute-done | bytes 524320 | tf_op jit(solution)/shard_map/ppermute | solution.py:18
  365.9 3.0 constant_dynamic-update-slice_fusion.58
  371.4 3.5 convolution_convert_fusion.4
  381.7 4.1 fusion.1
  385.8 5.6 multiply_convert_fusion
  408.5 3.1 fusion.58
  438.5 28.0 %collective-permute-done.71 = bf16[256,1024]{1,0:T(8,128)(2,1)} collective-permute-done((bf16[256,1024]{1,0:T(8,128)(2,1)}, bf16[256,1024]{1,0:T(8,128)(2,1)}, u32[]{:S(2)}, u32[]{:S(2)}) %collective-permute-start.71) | collective-permute-done | bytes 524320 | tf_op jit(solution)/shard_map/ppermute | solution.py:18
  469.7 2.7 add_convert_fusion.3
  480.0 5.5 collective-permute-done.76
  490.2 5.0 collective-permute-done.77
  495.2 11.9 %collective-permute-done.78 = bf16[128,1024]{1,0:T(8,128)(2,1)S(1)} collective-permute-done((bf16[128,1024]{1,0:T(8,128)(2,1)S(1)}, bf16[128,1024]{1,0:T(8,128)(2,1)S(1)}, u32[]{:S(2)}, u32[]{:S(2)}) %collective-permute-start.78) | collective-permute-done | bytes 262176 | tf_op jit(solution)/shard_map/ppermute | solution.py:18
  510.4 24.1 %collective-permute-done.80 = bf16[256,1024]{1,0:T(8,128)(2,1)S(1)} collective-permute-done((bf16[256,1024]{1,0:T(8,128)(2,1)S(1)}, bf16[256,1024]{1,0:T(8,128)(2,1)S(1)}, u32[]{:S(2)}, u32[]{:S(2)}) %collective-permute-start.80) | collective-permute-done | bytes 524320 | tf_op jit(solution)/shard_map/ppermute | solution.py:18
  541.1 2.9 collective-permute-start.88
  550.3 3.1 fusion.9
  555.4 2.7 convolution_convert_fusion.19
  625.5 15.1 %collective-permute-done.99 = bf16[512,512]{0,1:T(8,128)(2,1)S(1)} collective-permute-done((bf16[512,512]{0,1:T(8,128)(2,1)S(1)}, bf16[512,512]{0,1:T(8,128)(2,1)S(1)}, u32[]{:S(2)}, u32[]{:S(2)}) %collective-permute-start.99) | collective-permute-done | bytes 524320 | tf_op jit(solution)/shard_map/ppermute | solution.py:18
  643.5 9.9 %collective-permute-done.102 = bf16[256,1024]{1,0:T(8,128)(2,1)S(1)} collective-permute-done((bf16[256,1024]{1,0:T(8,128)(2,1)S(1)}, bf16[256,1024]{1,0:T(8,128)(2,1)S(1)}, u32[]{:S(2)}, u32[]{:S(2)}) %collective-permute-start.102) | collective-permute-done | bytes 524320 | tf_op jit(solution)/shard_map/ppermute | solution.py:18
  663.3 9.2 %collective-permute-done.107 = bf16[128,1024]{1,0:T(8,128)(2,1)S(1)} collective-permute-done((bf16[128,1024]{1,0:T(8,128)(2,1)S(1)}, bf16[128,1024]{1,0:T(8,128)(2,1)S(1)}, u32[]{:S(2)}, u32[]{:S(2)}) %collective-permute-start.107) | collective-permute-done | bytes 262176 | tf_op jit(solution)/shard_map/ppermute | solution.py:18
  677.0 9.3 %collective-permute-done.109 = bf16[256,1024]{1,0:T(8,128)(2,1)S(1)} collective-permute-done((bf16[256,1024]{1,0:T(8,128)(2,1)S(1)}, bf16[256,1024]{1,0:T(8,128)(2,1)S(1)}, u32[]{:S(2)}, u32[]{:S(2)}) %collective-permute-start.109) | collective-permute-done | bytes 524320 | tf_op jit(solution)/shard_map/ppermute | solution.py:18
  694.1 6.1 collective-permute-done.117
  (994 shorter events, 332.4 us)
Async XLA Ops:
  12.5 20.0 %collective-permute-start.5 = (bf16[128,1024]{1,0:T(8,128)(2,1)}, bf16[128,1024]{1,0:T(8,128)(2,1)}, u32[]{:S(2)}, u32[]{:S(2)}) collective-permute-start(bf16[128,1024]{1,0:T(8,128)(2,1)} %pad_maximum_fusion.57), channel_id=1, source_target_pairs={{0,1},{1,0},{2,3},{3,2},{4,5},{5,4},{6,7},{7,6},{8,9},{9,8},{10,11... | collective-permute-start | bytes 786440 | tf_op jit(solution)/shard_map/ppermute | solution.py:18
  14.1 28.6 %collective-permute-start.8 = (bf16[128,6144]{1,0:T(8,128)(2,1)S(1)}, bf16[128,6144]{1,0:T(8,128)(2,1)}, u32[]{:S(2)}, u32[]{:S(2)}) collective-permute-start(bf16[128,6144]{1,0:T(8,128)(2,1)S(1)} %pad_maximum_fusion.10), channel_id=1, source_target_pairs={{0,2},{2,0},{1,3},{3,1},{4,6},{6,4},{5,7},{7,5},{8,10},{10,8},{9,1... | collective-permute-start | bytes 4718600 | tf_op jit(solution)/shard_map/ppermute | solution.py:18
  33.4 20.6 %collective-permute-start.10 = (f32[4,512]{1,0:T(4,128)S(1)}, f32[4,512]{1,0:T(4,128)S(1)}, u32[]{:S(2)}, u32[]{:S(2)}) collective-permute-start(f32[4,512]{1,0:T(4,128)S(1)} %pad_maximum_fusion.77), channel_id=1, source_target_pairs={{0,16},{16,0},{1,17},{17,1},{2,18},{18,2},{3,19},{19,3},{4,20},{20... | collective-permute-start | bytes 24584 | tf_op jit(solution)/shard_map/ppermute | solution.py:18
  40.1 23.6 %collective-permute-start.12 = (bf16[512,512]{0,1:T(8,128)(2,1)S(1)}, bf16[512,512]{0,1:T(8,128)(2,1)S(1)}, u32[]{:S(2)}, u32[]{:S(2)}) collective-permute-start(bf16[512,512]{0,1:T(8,128)(2,1)S(1)} %pad_maximum_fusion.36), channel_id=1, source_target_pairs={{0,16},{16,0},{1,17},{17,1},{2,18},{18,2},{3,19},{19,3},{4,20},{20... | collective-permute-start | bytes 1572872 | tf_op jit(solution)/shard_map/ppermute | solution.py:18
  44.4 22.3 %collective-permute-start.13 = (bf16[256,1024]{1,0:T(8,128)(2,1)S(1)}, bf16[256,1024]{1,0:T(8,128)(2,1)S(1)}, u32[]{:S(2)}, u32[]{:S(2)}) collective-permute-start(bf16[256,1024]{1,0:T(8,128)(2,1)S(1)} %pad_maximum_fusion.37), channel_id=1, source_target_pairs={{0,8},{8,0},{1,9},{9,1},{2,10},{10,2},{3,11},{11,3},{4,12},{12,4},... | collective-permute-start | bytes 1572872 | tf_op jit(solution)/shard_map/ppermute | solution.py:18
  72.8 19.5 %collective-permute-start.18 = (bf16[256,1024]{1,0:T(8,128)(2,1)}, bf16[256,1024]{1,0:T(8,128)(2,1)S(1)}, u32[]{:S(2)}, u32[]{:S(2)}) collective-permute-start(bf16[256,1024]{1,0:T(8,128)(2,1)} %broadcast_select_fusion.11), channel_id=1, source_target_pairs={{0,8},{8,0},{1,9},{9,1},{2,10},{10,2},{3,11},{11,3},{4,12},{12,4},... | collective-permute-start | bytes 1572872 | tf_op jit(solution)/shard_map/ppermute | solution.py:18
  79.9 26.4 %collective-permute-start.22 = (bf16[512,512]{0,1:T(8,128)(2,1)S(1)}, bf16[512,512]{0,1:T(8,128)(2,1)S(1)}, u32[]{:S(2)}, u32[]{:S(2)}) collective-permute-start(bf16[512,512]{0,1:T(8,128)(2,1)S(1)} %copy-done.146), channel_id=1, source_target_pairs={{0,16},{16,0},{1,17},{17,1},{2,18},{18,2},{3,19},{19,3},{4,20},{20... | collective-permute-start | bytes 1572872 | tf_op jit(solution)/shard_map/ppermute | solution.py:18
  82.5 23.8 %collective-permute-start.23 = (bf16[512,512]{0,1:T(8,128)(2,1)S(1)}, bf16[512,512]{0,1:T(8,128)(2,1)S(1)}, u32[]{:S(2)}, u32[]{:S(2)}) collective-permute-start(bf16[512,512]{0,1:T(8,128)(2,1)S(1)} %copy-done.146), channel_id=1, source_target_pairs={{0,4},{4,0},{1,5},{5,1},{2,6},{6,2},{3,7},{7,3},{8,12},{12,8},{9,1... | collective-permute-start | bytes 1572872 | tf_op jit(solution)/shard_map/ppermute | solution.py:18
  110.3 34.2 %collective-permute-start.27 = (bf16[256,1024]{1,0:T(8,128)(2,1)}, bf16[256,1024]{1,0:T(8,128)(2,1)}, u32[]{:S(2)}, u32[]{:S(2)}) collective-permute-start(bf16[256,1024]{1,0:T(8,128)(2,1)} %broadcast_select_fusion.7), channel_id=1, source_target_pairs={{0,8},{8,0},{1,9},{9,1},{2,10},{10,2},{3,11},{11,3},{4,12},{12,4},... | collective-permute-start | bytes 1572872 | tf_op jit(solution)/shard_map/ppermute | solution.py:18
  110.3 49.4 %collective-permute-start.30 = (bf16[512,1024]{1,0:T(8,128)(2,1)}, bf16[512,1024]{1,0:T(8,128)(2,1)}, u32[]{:S(2)}, u32[]{:S(2)}) collective-permute-start(bf16[512,1024]{1,0:T(8,128)(2,1)} %pad_maximum_fusion.17), channel_id=1, source_target_pairs={{0,16},{16,0},{1,17},{17,1},{2,18},{18,2},{3,19},{19,3},{4,20},{20... | collective-permute-start | bytes 3145736 | tf_op jit(solution)/shard_map/ppermute | solution.py:18
  113.4 33.8 %collective-permute-start.28 = (bf16[512,1024]{1,0:T(8,128)(2,1)}, bf16[512,1024]{1,0:T(8,128)(2,1)}, u32[]{:S(2)}, u32[]{:S(2)}) collective-permute-start(bf16[512,1024]{1,0:T(8,128)(2,1)} %pad_maximum_fusion.17), channel_id=1, source_target_pairs={{0,4},{4,0},{1,5},{5,1},{2,6},{6,2},{3,7},{7,3},{8,12},{12,8},{9,1... | collective-permute-start | bytes 3145736 | tf_op jit(solution)/shard_map/ppermute | solution.py:18
  114.9 41.7 %collective-permute-start.29 = (bf16[256,1024]{1,0:T(8,128)(2,1)}, bf16[256,1024]{1,0:T(8,128)(2,1)}, u32[]{:S(2)}, u32[]{:S(2)}) collective-permute-start(bf16[256,1024]{1,0:T(8,128)(2,1)} %broadcast_select_fusion.6), channel_id=1, source_target_pairs={{0,8},{8,0},{1,9},{9,1},{2,10},{10,2},{3,11},{11,3},{4,12},{12,4},... | collective-permute-start | bytes 1572872 | tf_op jit(solution)/shard_map/ppermute | solution.py:18
  164.4 22.4 %collective-permute-start.33 = (bf16[256,1024]{1,0:T(8,128)(2,1)S(1)}, bf16[256,1024]{1,0:T(8,128)(2,1)S(1)}, u32[]{:S(2)}, u32[]{:S(2)}) collective-permute-start(bf16[256,1024]{1,0:T(8,128)(2,1)S(1)} %slice.2366), channel_id=1, source_target_pairs={{0,8},{8,0},{1,9},{9,1},{2,10},{10,2},{3,11},{11,3},{4,12},{12,4},... | collective-permute-start | bytes 1572872 | tf_op jit(solution)/shard_map/ppermute | solution.py:18
  164.5 22.3 %collective-permute-start.34 = (bf16[256,1024]{1,0:T(8,128)(2,1)S(1)}, bf16[256,1024]{1,0:T(8,128)(2,1)S(1)}, u32[]{:S(2)}, u32[]{:S(2)}) collective-permute-start(bf16[256,1024]{1,0:T(8,128)(2,1)S(1)} %pad_maximum_fusion.40), channel_id=1, source_target_pairs={{0,1},{1,0},{2,3},{3,2},{4,5},{5,4},{6,7},{7,6},{8,9},{9,8},{10,11... | collective-permute-start | bytes 1572872 | tf_op jit(solution)/shard_map/ppermute | solution.py:18
  166.1 26.1 %collective-permute-start.35 = (bf16[512,1024]{1,0:T(8,128)(2,1)S(1)}, bf16[512,1024]{1,0:T(8,128)(2,1)S(1)}, u32[]{:S(2)}, u32[]{:S(2)}) collective-permute-start(bf16[512,1024]{1,0:T(8,128)(2,1)S(1)} %pad_maximum_fusion.19), channel_id=1, source_target_pairs={{0,4},{4,0},{1,5},{5,1},{2,6},{6,2},{3,7},{7,3},{8,12},{12,8},{9,1... | collective-permute-start | bytes 3145736 | tf_op jit(solution)/shard_map/ppermute | solution.py:18
  167.7 48.1 %collective-permute-start.36 = (bf16[512,1024]{1,0:T(8,128)(2,1)S(1)}, bf16[512,1024]{1,0:T(8,128)(2,1)S(1)}, u32[]{:S(2)}, u32[]{:S(2)}) collective-permute-start(bf16[512,1024]{1,0:T(8,128)(2,1)S(1)} %pad_maximum_fusion.19), channel_id=1, source_target_pairs={{0,16},{16,0},{1,17},{17,1},{2,18},{18,2},{3,19},{19,3},{4,20},{20... | collective-permute-start | bytes 3145736 | tf_op jit(solution)/shard_map/ppermute | solution.py:18
  170.7 45.1 %collective-permute-start.37 = (bf16[512,1024]{1,0:T(8,128)(2,1)}, bf16[512,1024]{1,0:T(8,128)(2,1)S(1)}, u32[]{:S(2)}, u32[]{:S(2)}) collective-permute-start(bf16[512,1024]{1,0:T(8,128)(2,1)} %collective-permute-done.30), channel_id=1, source_target_pairs={{0,4},{4,0},{1,5},{5,1},{2,6},{6,2},{3,7},{7,3},{8,12},{12,8},{9,1... | collective-permute-start | bytes 3145736 | tf_op jit(solution)/shard_map/ppermute | solution.py:18
  187.2 31.1 %collective-permute-start.38 = (bf16[128,1024]{1,0:T(8,128)(2,1)S(1)}, bf16[128,1024]{1,0:T(8,128)(2,1)S(1)}, u32[]{:S(2)}, u32[]{:S(2)}) collective-permute-start(bf16[128,1024]{1,0:T(8,128)(2,1)S(1)} %slice.2373), channel_id=1, source_target_pairs={{0,1},{1,0},{2,3},{3,2},{4,5},{5,4},{6,7},{7,6},{8,9},{9,8},{10,11... | collective-permute-start | bytes 786440 | tf_op jit(solution)/shard_map/ppermute | solution.py:18
  189.8 28.6 %collective-permute-start.39 = (bf16[128,1024]{1,0:T(8,128)(2,1)S(1)}, bf16[128,1024]{1,0:T(8,128)(2,1)S(1)}, u32[]{:S(2)}, u32[]{:S(2)}) collective-permute-start(bf16[128,1024]{1,0:T(8,128)(2,1)S(1)} %slice.2372), channel_id=1, source_target_pairs={{0,8},{8,0},{1,9},{9,1},{2,10},{10,2},{3,11},{11,3},{4,12},{12,4},... | collective-permute-start | bytes 786440 | tf_op jit(solution)/shard_map/ppermute | solution.py:18
  215.8 58.5 %collective-permute-start.44 = (bf16[512,1024]{1,0:T(8,128)(2,1)S(1)}, bf16[512,1024]{1,0:T(8,128)(2,1)S(1)}, u32[]{:S(2)}, u32[]{:S(2)}) collective-permute-start(bf16[512,1024]{1,0:T(8,128)(2,1)S(1)} %collective-permute-done.36), channel_id=1, source_target_pairs={{0,4},{4,0},{1,5},{5,1},{2,6},{6,2},{3,7},{7,3},{8,12},{12,8},{9,1... | collective-permute-start | bytes 3145736 | tf_op jit(solution)/shard_map/ppermute | solution.py:18
  216.4 58.0 %collective-permute-start.45 = (bf16[512,1024]{1,0:T(8,128)(2,1)S(1)}, bf16[512,1024]{1,0:T(8,128)(2,1)S(1)}, u32[]{:S(2)}, u32[]{:S(2)}) collective-permute-start(bf16[512,1024]{1,0:T(8,128)(2,1)S(1)} %pad_maximum_fusion.20), channel_id=1, source_target_pairs={{0,16},{16,0},{1,17},{17,1},{2,18},{18,2},{3,19},{19,3},{4,20},{20... | collective-permute-start | bytes 3145736 | tf_op jit(solution)/shard_map/ppermute | solution.py:18
  217.8 56.6 %collective-permute-start.46 = (bf16[512,1024]{1,0:T(8,128)(2,1)S(1)}, bf16[512,1024]{1,0:T(8,128)(2,1)S(1)}, u32[]{:S(2)}, u32[]{:S(2)}) collective-permute-start(bf16[512,1024]{1,0:T(8,128)(2,1)S(1)} %pad_maximum_fusion.20), channel_id=1, source_target_pairs={{0,4},{4,0},{1,5},{5,1},{2,6},{6,2},{3,7},{7,3},{8,12},{12,8},{9,1... | collective-permute-start | bytes 3145736 | tf_op jit(solution)/shard_map/ppermute | solution.py:18
  220.6 23.8 %collective-permute-start.41 = (bf16[128,1024]{1,0:T(8,128)(2,1)S(1)}, bf16[128,1024]{1,0:T(8,128)(2,1)S(1)}, u32[]{:S(2)}, u32[]{:S(2)}) collective-permute-start(bf16[128,1024]{1,0:T(8,128)(2,1)S(1)} %get-tuple-element.669), channel_id=1, source_target_pairs={{0,8},{8,0},{1,9},{9,1},{2,10},{10,2},{3,11},{11,3},{4,12},{12,4},... | collective-permute-start | bytes 786440 | tf_op jit(solution)/shard_map/ppermute | solution.py:18
  244.5 29.8 %collective-permute-start.42 = (bf16[256,1024]{1,0:T(8,128)(2,1)S(1)}, bf16[256,1024]{1,0:T(8,128)(2,1)S(1)}, u32[]{:S(2)}, u32[]{:S(2)}) collective-permute-start(bf16[256,1024]{1,0:T(8,128)(2,1)S(1)} %pad_maximum_fusion.41), channel_id=1, source_target_pairs={{0,8},{8,0},{1,9},{9,1},{2,10},{10,2},{3,11},{11,3},{4,12},{12,4},... | collective-permute-start | bytes 1572872 | tf_op jit(solution)/shard_map/ppermute | solution.py:18
  247.1 27.2 %collective-permute-start.43 = (bf16[256,1024]{1,0:T(8,128)(2,1)S(1)}, bf16[256,1024]{1,0:T(8,128)(2,1)S(1)}, u32[]{:S(2)}, u32[]{:S(2)}) collective-permute-start(bf16[256,1024]{1,0:T(8,128)(2,1)S(1)} %pad_maximum_fusion.42), channel_id=1, source_target_pairs={{0,1},{1,0},{2,3},{3,2},{4,5},{5,4},{6,7},{7,6},{8,9},{9,8},{10,11... | collective-permute-start | bytes 1572872 | tf_op jit(solution)/shard_map/ppermute | solution.py:18
  295.2 25.2 %collective-permute-start.55 = (bf16[512,1024]{1,0:T(8,128)(2,1)S(1)}, bf16[512,1024]{1,0:T(8,128)(2,1)S(1)}, u32[]{:S(2)}, u32[]{:S(2)}) collective-permute-start(bf16[512,1024]{1,0:T(8,128)(2,1)S(1)} %collective-permute-done.45), channel_id=1, source_target_pairs={{0,4},{4,0},{1,5},{5,1},{2,6},{6,2},{3,7},{7,3},{8,12},{12,8},{9,1... | collective-permute-start | bytes 3145736 | tf_op jit(solution)/shard_map/ppermute | solution.py:18
  376.9 26.4 %collective-permute-start.66 = (bf16[512,1024]{1,0:T(8,128)(2,1)S(1)}, bf16[512,1024]{1,0:T(8,128)(2,1)S(1)}, u32[]{:S(2)}, u32[]{:S(2)}) collective-permute-start(bf16[512,1024]{1,0:T(8,128)(2,1)S(1)} %convolution_convert_fusion.5), channel_id=1, source_target_pairs={{0,4},{4,0},{1,5},{5,1},{2,6},{6,2},{3,7},{7,3},{8,12},{12,8},{9,1... | collective-permute-start | bytes 3145736 | tf_op jit(solution)/shard_map/ppermute | solution.py:18
  378.4 57.2 %collective-permute-start.70 = (bf16[512,1024]{1,0:T(8,128)(2,1)}, bf16[512,1024]{1,0:T(8,128)(2,1)}, u32[]{:S(2)}, u32[]{:S(2)}) collective-permute-start(bf16[512,1024]{1,0:T(8,128)(2,1)} %convolution_convert_fusion.4), channel_id=1, source_target_pairs={{0,4},{4,0},{1,5},{5,1},{2,6},{6,2},{3,7},{7,3},{8,12},{12,8},{9,1... | collective-permute-start | bytes 3145736 | tf_op jit(solution)/shard_map/ppermute | solution.py:18
  405.5 63.8 %collective-permute-start.73 = (bf16[512,1024]{1,0:T(8,128)(2,1)}, bf16[512,1024]{1,0:T(8,128)(2,1)}, u32[]{:S(2)}, u32[]{:S(2)}) collective-permute-start(bf16[512,1024]{1,0:T(8,128)(2,1)} %convolution_convert_fusion.3), channel_id=1, source_target_pairs={{0,4},{4,0},{1,5},{5,1},{2,6},{6,2},{3,7},{7,3},{8,12},{12,8},{9,1... | collective-permute-start | bytes 3145736 | tf_op jit(solution)/shard_map/ppermute | solution.py:18
  407.1 62.3 %collective-permute-start.74 = (bf16[512,1024]{1,0:T(8,128)(2,1)}, bf16[512,1024]{1,0:T(8,128)(2,1)}, u32[]{:S(2)}, u32[]{:S(2)}) collective-permute-start(bf16[512,1024]{1,0:T(8,128)(2,1)} %add_convert_fusion.6), channel_id=1, source_target_pairs={{0,16},{16,0},{1,17},{17,1},{2,18},{18,2},{3,19},{19,3},{4,20},{20... | collective-permute-start | bytes 3145736 | tf_op jit(solution)/shard_map/ppermute | solution.py:18
  430.8 35.8 %collective-permute-start.71 = (bf16[256,1024]{1,0:T(8,128)(2,1)}, bf16[256,1024]{1,0:T(8,128)(2,1)}, u32[]{:S(2)}, u32[]{:S(2)}) collective-permute-start(bf16[256,1024]{1,0:T(8,128)(2,1)} %slice.2364), channel_id=1, source_target_pairs={{0,8},{8,0},{1,9},{9,1},{2,10},{10,2},{3,11},{11,3},{4,12},{12,4},... | collective-permute-start | bytes 1572872 | tf_op jit(solution)/shard_map/ppermute | solution.py:18
  431.4 35.1 %collective-permute-start.72 = (bf16[256,1024]{1,0:T(8,128)(2,1)}, bf16[256,1024]{1,0:T(8,128)(2,1)}, u32[]{:S(2)}, u32[]{:S(2)}) collective-permute-start(bf16[256,1024]{1,0:T(8,128)(2,1)} %pad_maximum_fusion.45), channel_id=1, source_target_pairs={{0,1},{1,0},{2,3},{3,2},{4,5},{5,4},{6,7},{7,6},{8,9},{9,8},{10,11... | collective-permute-start | bytes 1572872 | tf_op jit(solution)/shard_map/ppermute | solution.py:18
  435.6 74.8 %collective-permute-start.79 = (bf16[512,1024]{1,0:T(8,128)(2,1)}, bf16[512,1024]{1,0:T(8,128)(2,1)S(1)}, u32[]{:S(2)}, u32[]{:S(2)}) collective-permute-start(bf16[512,1024]{1,0:T(8,128)(2,1)} %convolution_convert_fusion.2), channel_id=1, source_target_pairs={{0,4},{4,0},{1,5},{5,1},{2,6},{6,2},{3,7},{7,3},{8,12},{12,8},{9,1... | collective-permute-start | bytes 3145736 | tf_op jit(solution)/shard_map/ppermute | solution.py:18
  474.0 60.5 %collective-permute-start.82 = (bf16[512,1024]{1,0:T(8,128)(2,1)S(1)}, bf16[512,1024]{1,0:T(8,128)(2,1)S(1)}, u32[]{:S(2)}, u32[]{:S(2)}) collective-permute-start(bf16[512,1024]{1,0:T(8,128)(2,1)S(1)} %copy-done.139), channel_id=1, source_target_pairs={{0,4},{4,0},{1,5},{5,1},{2,6},{6,2},{3,7},{7,3},{8,12},{12,8},{9,1... | collective-permute-start | bytes 3145736 | tf_op jit(solution)/shard_map/ppermute | solution.py:18
  475.3 59.2 %collective-permute-start.83 = (bf16[512,1024]{1,0:T(8,128)(2,1)S(1)}, bf16[512,1024]{1,0:T(8,128)(2,1)S(1)}, u32[]{:S(2)}, u32[]{:S(2)}) collective-permute-start(bf16[512,1024]{1,0:T(8,128)(2,1)S(1)} %add_convert_fusion.3), channel_id=1, source_target_pairs={{0,16},{16,0},{1,17},{17,1},{2,18},{18,2},{3,19},{19,3},{4,20},{20... | collective-permute-start | bytes 3145736 | tf_op jit(solution)/shard_map/ppermute | solution.py:18
  507.3 27.2 %collective-permute-start.80 = (bf16[256,1024]{1,0:T(8,128)(2,1)S(1)}, bf16[256,1024]{1,0:T(8,128)(2,1)S(1)}, u32[]{:S(2)}, u32[]{:S(2)}) collective-permute-start(bf16[256,1024]{1,0:T(8,128)(2,1)S(1)} %pad_maximum_fusion.46), channel_id=1, source_target_pairs={{0,8},{8,0},{1,9},{9,1},{2,10},{10,2},{3,11},{11,3},{4,12},{12,4},... | collective-permute-start | bytes 1572872 | tf_op jit(solution)/shard_map/ppermute | solution.py:18
  509.8 24.7 %collective-permute-start.81 = (bf16[256,1024]{1,0:T(8,128)(2,1)S(1)}, bf16[256,1024]{1,0:T(8,128)(2,1)S(1)}, u32[]{:S(2)}, u32[]{:S(2)}) collective-permute-start(bf16[256,1024]{1,0:T(8,128)(2,1)S(1)} %pad_maximum_fusion.47), channel_id=1, source_target_pairs={{0,1},{1,0},{2,3},{3,2},{4,5},{5,4},{6,7},{7,6},{8,9},{9,8},{10,11... | collective-permute-start | bytes 1572872 | tf_op jit(solution)/shard_map/ppermute | solution.py:18
  540.4 32.2 %collective-permute-start.86 = (bf16[512,1024]{1,0:T(8,128)(2,1)}, bf16[512,1024]{1,0:T(8,128)(2,1)}, u32[]{:S(2)}, u32[]{:S(2)}) collective-permute-start(bf16[512,1024]{1,0:T(8,128)(2,1)} %convolution_convert_fusion), channel_id=1, source_target_pairs={{0,4},{4,0},{1,5},{5,1},{2,6},{6,2},{3,7},{7,3},{8,12},{12,8},{9,1... | collective-permute-start | bytes 3145736 | tf_op jit(solution)/shard_map/ppermute | solution.py:18
  541.1 51.8 %collective-permute-start.90 = (bf16[256,1024]{1,0:T(8,128)(2,1)}, bf16[256,1024]{1,0:T(8,128)(2,1)}, u32[]{:S(2)}, u32[]{:S(2)}) collective-permute-start(bf16[256,1024]{1,0:T(8,128)(2,1)} %select_convert_fusion.5), channel_id=1, source_target_pairs={{0,8},{8,0},{1,9},{9,1},{2,10},{10,2},{3,11},{11,3},{4,12},{12,4},... | collective-permute-start | bytes 1572872 | tf_op jit(solution)/shard_map/ppermute | solution.py:18
  541.1 48.6 %collective-permute-start.88 = (bf16[512,1024]{1,0:T(8,128)(2,1)}, bf16[512,1024]{1,0:T(8,128)(2,1)}, u32[]{:S(2)}, u32[]{:S(2)}) collective-permute-start(bf16[512,1024]{1,0:T(8,128)(2,1)} %add_convert_fusion.2), channel_id=1, source_target_pairs={{0,16},{16,0},{1,17},{17,1},{2,18},{18,2},{3,19},{19,3},{4,20},{20... | collective-permute-start | bytes 3145736 | tf_op jit(solution)/shard_map/ppermute | solution.py:18
  544.0 68.8 %collective-permute-start.95 = (bf16[256,1024]{1,0:T(8,128)(2,1)}, bf16[256,1024]{1,0:T(8,128)(2,1)}, u32[]{:S(2)}, u32[]{:S(2)}) collective-permute-start(bf16[256,1024]{1,0:T(8,128)(2,1)} %select_convert_fusion.4), channel_id=1, source_target_pairs={{0,8},{8,0},{1,9},{9,1},{2,10},{10,2},{3,11},{11,3},{4,12},{12,4},... | collective-permute-start | bytes 1572872 | tf_op jit(solution)/shard_map/ppermute | solution.py:18
  602.7 38.0 %collective-permute-start.100 = (bf16[512,512]{0,1:T(8,128)(2,1)S(1)}, bf16[512,512]{0,1:T(8,128)(2,1)S(1)}, u32[]{:S(2)}, u32[]{:S(2)}) collective-permute-start(bf16[512,512]{0,1:T(8,128)(2,1)S(1)} %fusion.32), channel_id=1, source_target_pairs={{0,16},{16,0},{1,17},{17,1},{2,18},{18,2},{3,19},{19,3},{4,20},{20... | collective-permute-start | bytes 1572872 | tf_op jit(solution)/shard_map/ppermute | solution.py:18
  615.7 24.9 %collective-permute-start.101 = (bf16[512,512]{0,1:T(8,128)(2,1)S(1)}, bf16[512,512]{0,1:T(8,128)(2,1)S(1)}, u32[]{:S(2)}, u32[]{:S(2)}) collective-permute-start(bf16[512,512]{0,1:T(8,128)(2,1)S(1)} %pad_maximum_fusion.49), channel_id=1, source_target_pairs={{0,4},{4,0},{1,5},{5,1},{2,6},{6,2},{3,7},{7,3},{8,12},{12,8},{9,1... | collective-permute-start | bytes 1572872 | tf_op jit(solution)/shard_map/ppermute | solution.py:18
  617.2 37.9 %collective-permute-start.104 = (f32[4,512]{1,0:T(4,128)S(1)}, f32[4,512]{1,0:T(4,128)S(1)}, u32[]{:S(2)}, u32[]{:S(2)}) collective-permute-start(f32[4,512]{1,0:T(4,128)S(1)} %slice.1287), channel_id=1, source_target_pairs={{0,16},{16,0},{1,17},{17,1},{2,18},{18,2},{3,19},{19,3},{4,20},{20... | collective-permute-start | bytes 24584 | tf_op jit(solution)/shard_map/ppermute | solution.py:18
  621.9 33.2 %collective-permute-start.105 = (bf16[128,2048]{1,0:T(8,128)(2,1)S(1)}, bf16[128,2048]{1,0:T(8,128)(2,1)S(1)}, u32[]{:S(2)}, u32[]{:S(2)}) collective-permute-start(bf16[128,2048]{1,0:T(8,128)(2,1)S(1)} %select_convert_fusion.2), channel_id=1, source_target_pairs={{0,2},{2,0},{1,3},{3,1},{4,6},{6,4},{5,7},{7,5},{8,10},{10,8},{9,1... | collective-permute-start | bytes 1572872 | tf_op jit(solution)/shard_map/ppermute | solution.py:18
  642.6 44.3 %collective-permute-start.111 = (bf16[512,512]{0,1:T(8,128)(2,1)S(1)}, bf16[512,512]{0,1:T(8,128)(2,1)S(1)}, u32[]{:S(2)}, u32[]{:S(2)}) collective-permute-start(bf16[512,512]{0,1:T(8,128)(2,1)S(1)} %pad_maximum_fusion.52), channel_id=1, source_target_pairs={{0,4},{4,0},{1,5},{5,1},{2,6},{6,2},{3,7},{7,3},{8,12},{12,8},{9,1... | collective-permute-start | bytes 1572872 | tf_op jit(solution)/shard_map/ppermute | solution.py:18
  653.4 39.4 %collective-permute-start.114 = (bf16[512,512]{0,1:T(8,128)(2,1)S(1)}, bf16[512,512]{0,1:T(8,128)(2,1)S(1)}, u32[]{:S(2)}, u32[]{:S(2)}) collective-permute-start(bf16[512,512]{0,1:T(8,128)(2,1)S(1)} %fusion.33), channel_id=1, source_target_pairs={{0,16},{16,0},{1,17},{17,1},{2,18},{18,2},{3,19},{19,3},{4,20},{20... | collective-permute-start | bytes 1572872 | tf_op jit(solution)/shard_map/ppermute | solution.py:18
  661.5 24.8 %collective-permute-start.109 = (bf16[256,1024]{1,0:T(8,128)(2,1)S(1)}, bf16[256,1024]{1,0:T(8,128)(2,1)S(1)}, u32[]{:S(2)}, u32[]{:S(2)}) collective-permute-start(bf16[256,1024]{1,0:T(8,128)(2,1)S(1)} %select_convert_fusion.1), channel_id=1, source_target_pairs={{0,8},{8,0},{1,9},{9,1},{2,10},{10,2},{3,11},{11,3},{4,12},{12,4},... | collective-permute-start | bytes 1572872 | tf_op jit(solution)/shard_map/ppermute | solution.py:18
  (268 other events, 2815.2 us)

commit v7 on v6

--- a/solution.py
+++ b/solution.py
@@ -236,8 +236,6 @@
         tokens_rel = to_relative(tokens)
         left, right = tokens_rel[:, :half_width], tokens_rel[:, half_width:]
         left_sent = c.start(left, "tensor")
-        ffn_split = [split(w, "core", 1) for w in (w_gate, w_up, w_down)]
-        ffn_sent = c.start(columns([s[1] for s in ffn_split]), "core")
         gain_steps()
 
         attn_sent = c.sync(attn_sent)
@@ -254,6 +252,8 @@
             axis=1,
         )
         ids_sent = c.start(ids, "zl")
+        ffn_split = [split(w, "core", 1) for w in (w_gate, w_up, w_down)]
+        ffn_sent = c.start(columns([s[1] for s in ffn_split]), "core")
         qk.end_line()
         gain_steps()
         qk.start_x(0)
@@ -265,30 +265,32 @@
         ids_sent = c.start(seq_ids, "core")
         right = stack2(right, c.sync(right_sent))
 
-        def rows_second(left, right, between=None, last=None):
-            left_sent = c.start(left, "zl")
+        def rows_second(left, right, between=None, last=None, busy=False):
+            left_sent = c.start(left, "tensor" if busy else "zl")
             right_sent = c.start(right, "tensor")
             if between:
                 between()
-            left = stack2(left, c.sync(left_sent))
-            right_sent = c.sync(right_sent)
-            rows = own_tokens
-            right = jnp.concatenate(
-                [right[:rows], right_sent[:rows], right[rows:], right_sent[rows:]], axis=0
-            )
+
+            def woven(rows, sent):
+                half = own_tokens
+                return jnp.concatenate([rows[:half], sent[:half], rows[half:], sent[half:]], axis=0)
+
+            left_sent = c.sync(left_sent)
+            left = woven(left, left_sent) if busy else stack2(left, left_sent)
+            right = woven(right, c.sync(right_sent))
             if last:
                 last()
             left_sent = c.start(left, "core")
             right_sent = c.start(right, "core")
             return stack2(left, c.sync(left_sent)), stack2(right, c.sync(right_sent))
 
-        def gather_rows(value, between=None, last=None):
+        def gather_rows(value, between=None, last=None, busy=False):
             left, right = value[:, :half_width], value[:, half_width:]
-            left_sent = c.start(left, "tensor")
+            left_sent = c.start(left, "zl" if busy else "tensor")
             right_sent = c.start(right, "zl")
             left = stack2(left, c.sync(left_sent))
             right = stack2(right, c.sync(right_sent))
-            return rows_second(left, right, between, last)
+            return rows_second(left, right, between, last, busy)
 
         ffn_sent = c.sync(ffn_sent)
         width = ffn_sent.shape[1] // 3
@@ -398,15 +400,16 @@
             sent = stack2(total[rows : 2 * rows], total[3 * rows :])
             return own, c.start(sent.astype(BF), "tensor")
 
-        def scatter_rows(left_of, right_of, first=None, second=None):
+        def scatter_rows(left_of, right_of, first=None, second=None, busy=False):
             left_sent = c.start(left_of(other).astype(BF), "core")
             right_sent = c.start(right_of(other).astype(BF), "core")
-            left = halve(left_of(own) + c.sync(left_sent).astype(F32), "zl")
+            left = left_of(own) + c.sync(left_sent).astype(F32)
+            left = cross(left) if busy else halve(left, "zl")
             right = cross(right_of(own) + c.sync(right_sent).astype(F32))
             if first:
                 first()
             left, right = added(left), added(right)
-            left, right = halve(left, "tensor"), halve(right, "zl")
+            left, right = halve(left, "zl" if busy else "tensor"), halve(right, "zl")
             if second:
                 second()
             return added(left), added(right)
@@ -421,7 +424,7 @@
 
         proj = columns(
             scatter_rows(
-                lambda rows: dot_nt(attn[rows], wo0), lambda rows: dot_nt(attn[rows], wo1), None, proj_second
+                lambda rows: dot_nt(attn[rows], wo0), lambda rows: dot_nt(attn[rows], wo1), None, proj_second, True
             )
         )
         attn_rms = rms_scale(proj)
@@ -433,7 +436,7 @@
             down_w.end_x(0)
             down_w.start_x(1)
 
-        h0, h1 = gather_rows(resid.astype(BF), None, resid_last)
+        h0, h1 = gather_rows(resid.astype(BF), None, resid_last, True)
         wg0, wg1 = gate_w.rows(0), gate_w.rows(1)
         gate = dot(h0, wg0) + dot(h1, wg1)
         sigma = jax.nn.sigmoid(gate)
@@ -514,8 +517,9 @@
 
         down_grad = Grad(((f0, f1), act))
         down_grad.start_x(1)
+        f0, f1 = c.fence(f0, f1)
+        down_grad.terms = (((f0, f1), act),)
         down_grad.start_x(0)
-        f0, f1 = c.fence(f0, f1)
         d_act = dot(f0, wd0) + dot(f1, wd1)
         d_gate = (d_act * up * sigma * (1.0 + gate * (1.0 - sigma))).astype(BF)
         d_up = (d_act * gate * sigma).astype(BF)
@@ -542,6 +546,7 @@
                 lambda rows: dot_nt(d_gate[rows], wg1) + dot_nt(d_up[rows], wu1),
                 hidden_first,
                 hidden_second,
+                True,
             )
         )
         attn_gain_term = jnp.sum(d_resid * proj * attn_rms, axis=0)
@@ -565,7 +570,7 @@
             up_grad.start_high()
             gate_grad.start_line()
 
-        p0, p1 = gather_rows(d_proj, proj_between, proj_last)
+        p0, p1 = gather_rows(d_proj, proj_between, proj_last, True)
         up_grad.end_x(0)
         d_attn = (dot(p0, wo0) + dot(p1, wo1)).astype(BF)
 
@@ -617,7 +622,7 @@
         ov_grad.end_x(1)
         ov_grad.start_high()
         down_grad.end_line()
-        inner = pair_sum(c, inner)
+        inner = pair_sum(c, inner, up_grad.start_line)
         gain_steps()
         d_query = (
             q_rms * (scaled_q - query * q_rms * q_rms * (inner[0] / model_width)[:, None])
@@ -630,18 +635,17 @@
         qk_grad.start_x(1)
         gate_grad.end_line()
         down_grad.end()
-        ov_grad.start_x(0)
 
         def tokens_first():
-            ov_grad.end_x(0)
-            ov_grad.end_high()
+            ov_grad.high = c.sync(ov_grad.high)
             qk_grad.end_x(1)
             qk_grad.start_high()
+            ov_grad.start_x(0)
             qk_grad.start_x(0)
 
         def tokens_second():
             gain_steps()
-            up_grad.start_line()
+            up_grad.end_line()
             gate_grad.end()
 
         d_tokens = columns(
@@ -650,12 +654,14 @@
                 lambda rows: dot_nt(d_qk[rows], wqk1) + dot_nt(d_value[rows], wv1),
                 tokens_first,
                 tokens_second,
+                True,
             )
         )
         grad_tokens = to_natural(d_resid + d_tokens)
         gain_steps()
+        ov_grad.end_x(0)
+        ov_grad.end_high()
         ov_grad.start_line()
-        up_grad.end_line()
         gain_steps()
         qk_grad.end_x(0)
         ov_grad.end_line()

time: 714 us -> 720 us (level)
  waiting for transfers between devices: 328 us -> 360 us
  other arithmetic: 77.3 us -> 64.5 us
  starting transfers between devices: 110 us -> 101 us
    ppermute x119, waiting for transfers between devices: 328 us -> 360 us  [swap(): return lax.ppermute(value, axis, FLIP)]
    ppermute x119, starting transfers between devices: 110 us -> 101 us  [swap(): return lax.ppermute(value, axis, FLIP)]
    unnamed x442 -> x440, local copies, waits for them, and re-layouts: 30.7 us -> 35.5 us
  transfers between devices with their start and end apart: 119 -> 119, of which waited for: 48 -> 56; matrix products, arithmetic and copies ran while one was open for 28% -> 26% of each run, Pallas kernels for 0% -> 0%
where the time goes in v7:
time: 720 us; the launch traced here: 713 us
  waiting for transfers between devices  360 us (50%)
  matrix products  124 us (17%)
  starting transfers between devices  101 us (14%)
  other arithmetic  64.5 us (9%)
  local copies, waits for them, and re-layouts  58.4 us (8%)
    ppermute x119, waiting for transfers between devices, swap(): return lax.ppermute(value, axis, FLIP)  360 us
    ppermute x119, starting transfers between devices, swap(): return lax.ppermute(value, axis, FLIP)  101 us
    dot_general x28, matrix products, dot_tn(): return jnp.einsum('sr,sc->rc', a, b, preferred_element_type=F32)  44.4 us
    dot_general x26, matrix products, dot_nt(): return jnp.einsum('sc,rc->sr', a, b, preferred_element_type=F32)  36 us
    unnamed x440, local copies, waits for them, and re-layouts  35.5 us
    dot_general x12, matrix products, dot(): return jnp.dot(a, b, preferred_element_type=F32)  32.3 us
  transfers between devices with their start and end apart: 119, of which 56 were waited for; matrix products, arithmetic and copies ran while one was open for 26% of the time, Pallas kernels for 0%

profile of v7, /device:TPU:0, one launch (start us, length us, event | category | flops | bytes accessed | tf_op | source)
XLA Modules:
  0.0 713.4 jit_solution(1196978344284925001)
XLA Ops:
  20.7 4.5 collective-permute-done.3
  39.8 6.0 collective-permute-done.9
  50.5 8.0 %collective-permute-done.12 = bf16[512,512]{0,1:T(8,128)(2,1)S(1)} collective-permute-done((bf16[512,512]{0,1:T(8,128)(2,1)S(1)}, bf16[512,512]{0,1:T(8,128)(2,1)S(1)}, u32[]{:S(2)}, u32[]{:S(2)}) %collective-permute-start.12) | collective-permute-done | bytes 524320 | tf_op jit(solution)/shard_map/ppermute | solution.py:18
  58.6 3.1 collective-permute-done.13
  76.9 9.3 %collective-permute-done.18 = bf16[256,1024]{1,0:T(8,128)(2,1)S(1)} collective-permute-done((bf16[256,1024]{1,0:T(8,128)(2,1)}, bf16[256,1024]{1,0:T(8,128)(2,1)S(1)}, u32[]{:S(2)}, u32[]{:S(2)}) %collective-permute-start.18) | collective-permute-done | bytes 524320 | tf_op jit(solution)/shard_map/ppermute | solution.py:18
  109.1 6.7 collective-permute-done.26
  125.9 3.4 fusion.221
  136.3 13.2 %collective-permute-done.29 = bf16[256,1024]{1,0:T(8,128)(2,1)} collective-permute-done((bf16[256,1024]{1,0:T(8,128)(2,1)}, bf16[256,1024]{1,0:T(8,128)(2,1)}, u32[]{:S(2)}, u32[]{:S(2)}) %collective-permute-start.29) | collective-permute-done | bytes 524320 | tf_op jit(solution)/shard_map/ppermute | solution.py:18
  149.4 3.2 collective-permute-done.30
  159.7 12.5 %collective-permute-done.33 = bf16[256,1024]{1,0:T(8,128)(2,1)S(1)} collective-permute-done((bf16[256,1024]{1,0:T(8,128)(2,1)S(1)}, bf16[256,1024]{1,0:T(8,128)(2,1)S(1)}, u32[]{:S(2)}, u32[]{:S(2)}) %collective-permute-start.33) | collective-permute-done | bytes 524320 | tf_op jit(solution)/shard_map/ppermute | solution.py:18
  172.2 10.4 %collective-permute-done.34 = bf16[256,1024]{1,0:T(8,128)(2,1)S(1)} collective-permute-done((bf16[256,1024]{1,0:T(8,128)(2,1)S(1)}, bf16[256,1024]{1,0:T(8,128)(2,1)S(1)}, u32[]{:S(2)}, u32[]{:S(2)}) %collective-permute-start.34) | collective-permute-done | bytes 524320 | tf_op jit(solution)/shard_map/ppermute | solution.py:18
  186.6 16.7 %collective-permute-done.36 = bf16[512,1024]{1,0:T(8,128)(2,1)S(1)} collective-permute-done((bf16[512,1024]{1,0:T(8,128)(2,1)S(1)}, bf16[512,1024]{1,0:T(8,128)(2,1)S(1)}, u32[]{:S(2)}, u32[]{:S(2)}) %collective-permute-start.36) | collective-permute-done | bytes 1048608 | tf_op jit(solution)/shard_map/ppermute | solution.py:18
  205.3 3.7 collective-permute-done.38
  209.0 5.5 collective-permute-done.39
  217.6 15.5 %collective-permute-done.40 = bf16[128,1024]{1,0:T(8,128)(2,1)S(1)} collective-permute-done((bf16[128,1024]{1,0:T(8,128)(2,1)S(1)}, bf16[128,1024]{1,0:T(8,128)(2,1)S(1)}, u32[]{:S(2)}, u32[]{:S(2)}) %collective-permute-start.40) | collective-permute-done | bytes 262176 | tf_op jit(solution)/shard_map/ppermute | solution.py:18
  233.1 18.7 %collective-permute-done.41 = bf16[128,1024]{1,0:T(8,128)(2,1)S(1)} collective-permute-done((bf16[128,1024]{1,0:T(8,128)(2,1)S(1)}, bf16[128,1024]{1,0:T(8,128)(2,1)S(1)}, u32[]{:S(2)}, u32[]{:S(2)}) %collective-permute-start.41) | collective-permute-done | bytes 262176 | tf_op jit(solution)/shard_map/ppermute | solution.py:18
  254.0 12.7 %collective-permute-done.42 = bf16[256,1024]{1,0:T(8,128)(2,1)S(1)} collective-permute-done((bf16[256,1024]{1,0:T(8,128)(2,1)S(1)}, bf16[256,1024]{1,0:T(8,128)(2,1)S(1)}, u32[]{:S(2)}, u32[]{:S(2)}) %collective-permute-start.42) | collective-permute-done | bytes 524320 | tf_op jit(solution)/shard_map/ppermute | solution.py:18
  266.7 9.4 %collective-permute-done.43 = bf16[256,1024]{1,0:T(8,128)(2,1)S(1)} collective-permute-done((bf16[256,1024]{1,0:T(8,128)(2,1)S(1)}, bf16[256,1024]{1,0:T(8,128)(2,1)S(1)}, u32[]{:S(2)}, u32[]{:S(2)}) %collective-permute-start.43) | collective-permute-done | bytes 524320 | tf_op jit(solution)/shard_map/ppermute | solution.py:18
  286.7 4.3 convolution_add_fusion.2
  291.1 4.6 multiply_convert_fusion.2
  303.7 12.3 %collective-permute-done.51 = bf16[256,1024]{1,0:T(8,128)(2,1)S(1)} collective-permute-done((bf16[256,1024]{1,0:T(8,128)(2,1)S(1)}, bf16[256,1024]{1,0:T(8,128)(2,1)S(1)}, u32[]{:S(2)}, u32[]{:S(2)}) %collective-permute-start.51) | collective-permute-done | bytes 524320 | tf_op jit(solution)/shard_map/ppermute | solution.py:18
  318.2 5.5 collective-permute-done.53
  329.0 6.7 collective-permute-done.57
  336.5 4.4 collective-permute-done.58
  344.6 4.3 collective-permute-done.59
  351.9 9.8 %collective-permute-done.61 = bf16[256,1024]{1,0:T(8,128)(2,1)S(1)} collective-permute-done((bf16[256,1024]{1,0:T(8,128)(2,1)S(1)}, bf16[256,1024]{1,0:T(8,128)(2,1)S(1)}, u32[]{:S(2)}, u32[]{:S(2)}) %collective-permute-start.61) | collective-permute-done | bytes 524320 | tf_op jit(solution)/shard_map/ppermute | solution.py:18
  376.3 3.6 convolution_convert_fusion.4
  379.9 4.5 fusion.1
  385.9 5.6 multiply_convert_fusion
  417.6 3.8 fusion.67
  421.5 3.7 add_convert_fusion.5
  428.2 3.3 fusion.65
  442.3 11.6 %collective-permute-done.71 = bf16[256,1024]{1,0:T(8,128)(2,1)S(1)} collective-permute-done((bf16[256,1024]{1,0:T(8,128)(2,1)S(1)}, bf16[256,1024]{1,0:T(8,128)(2,1)S(1)}, u32[]{:S(2)}, u32[]{:S(2)}) %collective-permute-start.71) | collective-permute-done | bytes 524320 | tf_op jit(solution)/shard_map/ppermute | solution.py:18
  453.8 10.4 %collective-permute-done.72 = bf16[256,1024]{1,0:T(8,128)(2,1)S(1)} collective-permute-done((bf16[256,1024]{1,0:T(8,128)(2,1)S(1)}, bf16[256,1024]{1,0:T(8,128)(2,1)S(1)}, u32[]{:S(2)}, u32[]{:S(2)}) %collective-permute-start.72) | collective-permute-done | bytes 524320 | tf_op jit(solution)/shard_map/ppermute | solution.py:18
  477.0 10.7 %collective-permute-done.75 = bf16[128,1024]{1,0:T(8,128)(2,1)S(1)} collective-permute-done((bf16[128,1024]{1,0:T(8,128)(2,1)S(1)}, bf16[128,1024]{1,0:T(8,128)(2,1)S(1)}, u32[]{:S(2)}, u32[]{:S(2)}) %collective-permute-start.75) | collective-permute-done | bytes 262176 | tf_op jit(solution)/shard_map/ppermute | solution.py:18
  487.8 4.0 collective-permute-done.76
  497.2 13.8 %collective-permute-done.77 = bf16[128,1024]{1,0:T(8,128)(2,1)S(1)} collective-permute-done((bf16[128,1024]{1,0:T(8,128)(2,1)S(1)}, bf16[128,1024]{1,0:T(8,128)(2,1)S(1)}, u32[]{:S(2)}, u32[]{:S(2)}) %collective-permute-start.77) | collective-permute-done | bytes 262176 | tf_op jit(solution)/shard_map/ppermute | solution.py:18
  510.9 8.6 %collective-permute-done.78 = bf16[128,1024]{1,0:T(8,128)(2,1)S(1)} collective-permute-done((bf16[128,1024]{1,0:T(8,128)(2,1)S(1)}, bf16[128,1024]{1,0:T(8,128)(2,1)S(1)}, u32[]{:S(2)}, u32[]{:S(2)}) %collective-permute-start.78) | collective-permute-done | bytes 262176 | tf_op jit(solution)/shard_map/ppermute | solution.py:18
  521.9 11.1 %collective-permute-done.80 = bf16[256,1024]{1,0:T(8,128)(2,1)S(1)} collective-permute-done((bf16[256,1024]{1,0:T(8,128)(2,1)S(1)}, bf16[256,1024]{1,0:T(8,128)(2,1)S(1)}, u32[]{:S(2)}, u32[]{:S(2)}) %collective-permute-start.80) | collective-permute-done | bytes 524320 | tf_op jit(solution)/shard_map/ppermute | solution.py:18
  533.0 5.6 collective-permute-done.81
  590.2 5.9 collective-permute-done.88
  602.2 3.5 collective-permute-done.91
  640.3 12.6 %collective-permute-done.101 = bf16[256,1024]{1,0:T(8,128)(2,1)S(1)} collective-permute-done((bf16[256,1024]{1,0:T(8,128)(2,1)S(1)}, bf16[256,1024]{1,0:T(8,128)(2,1)S(1)}, u32[]{:S(2)}, u32[]{:S(2)}) %collective-permute-start.101) | collective-permute-done | bytes 524320 | tf_op jit(solution)/shard_map/ppermute | solution.py:18
  654.5 7.5 %collective-permute-done.102 = bf16[256,1024]{1,0:T(8,128)(2,1)S(1)} collective-permute-done((bf16[256,1024]{1,0:T(8,128)(2,1)S(1)}, bf16[256,1024]{1,0:T(8,128)(2,1)S(1)}, u32[]{:S(2)}, u32[]{:S(2)}) %collective-permute-start.102) | collective-permute-done | bytes 524320 | tf_op jit(solution)/shard_map/ppermute | solution.py:18
  669.3 8.5 %collective-permute-done.106 = bf16[128,1024]{1,0:T(8,128)(2,1)S(1)} collective-permute-done((bf16[128,1024]{1,0:T(8,128)(2,1)S(1)}, bf16[128,1024]{1,0:T(8,128)(2,1)S(1)}, u32[]{:S(2)}, u32[]{:S(2)}) %collective-permute-start.106) | collective-permute-done | bytes 262176 | tf_op jit(solution)/shard_map/ppermute | solution.py:18
  678.0 3.6 collective-permute-done.107
  685.9 12.9 %collective-permute-done.112 = bf16[256,512]{0,1:T(8,128)(2,1)S(1)} collective-permute-done((bf16[256,512]{0,1:T(8,128)(2,1)S(1)}, bf16[256,512]{0,1:T(8,128)(2,1)S(1)}, u32[]{:S(2)}, u32[]{:S(2)}) %collective-permute-start.112) | collective-permute-done | bytes 262176 | tf_op jit(solution)/shard_map/ppermute | solution.py:18
  702.1 6.2 collective-permute-done.117
  (999 shorter events, 331.9 us)
Async XLA Ops:
  16.1 21.5 %collective-permute-start.8 = (bf16[128,6144]{1,0:T(8,128)(2,1)S(1)}, bf16[128,6144]{1,0:T(8,128)(2,1)S(1)}, u32[]{:S(2)}, u32[]{:S(2)}) collective-permute-start(bf16[128,6144]{1,0:T(8,128)(2,1)S(1)} %copy-done.117), channel_id=1, source_target_pairs={{0,2},{2,0},{1,3},{3,1},{4,6},{6,4},{5,7},{7,5},{8,10},{10,8},{9,1... | collective-permute-start | bytes 4718600 | tf_op jit(solution)/shard_map/ppermute | solution.py:18
  27.7 21.1 %collective-permute-start.10 = (f32[4,512]{1,0:T(4,128)S(1)}, f32[4,512]{1,0:T(4,128)S(1)}, u32[]{:S(2)}, u32[]{:S(2)}) collective-permute-start(f32[4,512]{1,0:T(4,128)S(1)} %pad_maximum_fusion.78), channel_id=1, source_target_pairs={{0,16},{16,0},{1,17},{17,1},{2,18},{18,2},{3,19},{19,3},{4,20},{20... | collective-permute-start | bytes 24584 | tf_op jit(solution)/shard_map/ppermute | solution.py:18
  34.9 23.6 %collective-permute-start.12 = (bf16[512,512]{0,1:T(8,128)(2,1)S(1)}, bf16[512,512]{0,1:T(8,128)(2,1)S(1)}, u32[]{:S(2)}, u32[]{:S(2)}) collective-permute-start(bf16[512,512]{0,1:T(8,128)(2,1)S(1)} %pad_maximum_fusion.34), channel_id=1, source_target_pairs={{0,16},{16,0},{1,17},{17,1},{2,18},{18,2},{3,19},{19,3},{4,20},{20... | collective-permute-start | bytes 1572872 | tf_op jit(solution)/shard_map/ppermute | solution.py:18
  38.0 23.7 %collective-permute-start.13 = (bf16[256,1024]{1,0:T(8,128)(2,1)S(1)}, bf16[256,1024]{1,0:T(8,128)(2,1)S(1)}, u32[]{:S(2)}, u32[]{:S(2)}) collective-permute-start(bf16[256,1024]{1,0:T(8,128)(2,1)S(1)} %pad_maximum_fusion.35), channel_id=1, source_target_pairs={{0,8},{8,0},{1,9},{9,1},{2,10},{10,2},{3,11},{11,3},{4,12},{12,4},... | collective-permute-start | bytes 1572872 | tf_op jit(solution)/shard_map/ppermute | solution.py:18
  65.7 20.5 %collective-permute-start.18 = (bf16[256,1024]{1,0:T(8,128)(2,1)}, bf16[256,1024]{1,0:T(8,128)(2,1)S(1)}, u32[]{:S(2)}, u32[]{:S(2)}) collective-permute-start(bf16[256,1024]{1,0:T(8,128)(2,1)} %broadcast_select_fusion.11), channel_id=1, source_target_pairs={{0,8},{8,0},{1,9},{9,1},{2,10},{10,2},{3,11},{11,3},{4,12},{12,4},... | collective-permute-start | bytes 1572872 | tf_op jit(solution)/shard_map/ppermute | solution.py:18
  67.3 18.9 %collective-permute-start.20 = (bf16[512,512]{0,1:T(8,128)(2,1)S(1)}, bf16[512,512]{0,1:T(8,128)(2,1)S(1)}, u32[]{:S(2)}, u32[]{:S(2)}) collective-permute-start(bf16[512,512]{0,1:T(8,128)(2,1)S(1)} %copy-done.160), channel_id=1, source_target_pairs={{0,4},{4,0},{1,5},{5,1},{2,6},{6,2},{3,7},{7,3},{8,12},{12,8},{9,1... | collective-permute-start | bytes 1572872 | tf_op jit(solution)/shard_map/ppermute | solution.py:18
  72.8 26.4 %collective-permute-start.22 = (bf16[512,512]{0,1:T(8,128)(2,1)S(1)}, bf16[512,512]{0,1:T(8,128)(2,1)S(1)}, u32[]{:S(2)}, u32[]{:S(2)}) collective-permute-start(bf16[512,512]{0,1:T(8,128)(2,1)S(1)} %copy-done.151), channel_id=1, source_target_pairs={{0,16},{16,0},{1,17},{17,1},{2,18},{18,2},{3,19},{19,3},{4,20},{20... | collective-permute-start | bytes 1572872 | tf_op jit(solution)/shard_map/ppermute | solution.py:18
  75.4 23.8 %collective-permute-start.23 = (bf16[512,512]{0,1:T(8,128)(2,1)S(1)}, bf16[512,512]{0,1:T(8,128)(2,1)S(1)}, u32[]{:S(2)}, u32[]{:S(2)}) collective-permute-start(bf16[512,512]{0,1:T(8,128)(2,1)S(1)} %copy-done.151), channel_id=1, source_target_pairs={{0,4},{4,0},{1,5},{5,1},{2,6},{6,2},{3,7},{7,3},{8,12},{12,8},{9,1... | collective-permute-start | bytes 1572872 | tf_op jit(solution)/shard_map/ppermute | solution.py:18
  103.2 30.0 %collective-permute-start.27 = (bf16[256,1024]{1,0:T(8,128)(2,1)}, bf16[256,1024]{1,0:T(8,128)(2,1)}, u32[]{:S(2)}, u32[]{:S(2)}) collective-permute-start(bf16[256,1024]{1,0:T(8,128)(2,1)} %broadcast_select_fusion.7), channel_id=1, source_target_pairs={{0,8},{8,0},{1,9},{9,1},{2,10},{10,2},{3,11},{11,3},{4,12},{12,4},... | collective-permute-start | bytes 1572872 | tf_op jit(solution)/shard_map/ppermute | solution.py:18
  103.2 49.4 %collective-permute-start.30 = (bf16[512,1024]{1,0:T(8,128)(2,1)}, bf16[512,1024]{1,0:T(8,128)(2,1)}, u32[]{:S(2)}, u32[]{:S(2)}) collective-permute-start(bf16[512,1024]{1,0:T(8,128)(2,1)} %pad_maximum_fusion.15), channel_id=1, source_target_pairs={{0,16},{16,0},{1,17},{17,1},{2,18},{18,2},{3,19},{19,3},{4,20},{20... | collective-permute-start | bytes 3145736 | tf_op jit(solution)/shard_map/ppermute | solution.py:18
  106.3 30.0 %collective-permute-start.28 = (bf16[512,1024]{1,0:T(8,128)(2,1)}, bf16[512,1024]{1,0:T(8,128)(2,1)}, u32[]{:S(2)}, u32[]{:S(2)}) collective-permute-start(bf16[512,1024]{1,0:T(8,128)(2,1)} %pad_maximum_fusion.15), channel_id=1, source_target_pairs={{0,4},{4,0},{1,5},{5,1},{2,6},{6,2},{3,7},{7,3},{8,12},{12,8},{9,1... | collective-permute-start | bytes 3145736 | tf_op jit(solution)/shard_map/ppermute | solution.py:18
  107.8 41.7 %collective-permute-start.29 = (bf16[256,1024]{1,0:T(8,128)(2,1)}, bf16[256,1024]{1,0:T(8,128)(2,1)}, u32[]{:S(2)}, u32[]{:S(2)}) collective-permute-start(bf16[256,1024]{1,0:T(8,128)(2,1)} %broadcast_select_fusion.6), channel_id=1, source_target_pairs={{0,8},{8,0},{1,9},{9,1},{2,10},{10,2},{3,11},{11,3},{4,12},{12,4},... | collective-permute-start | bytes 1572872 | tf_op jit(solution)/shard_map/ppermute | solution.py:18
  153.7 32.9 %collective-permute-start.35 = (bf16[512,1024]{1,0:T(8,128)(2,1)S(1)}, bf16[512,1024]{1,0:T(8,128)(2,1)S(1)}, u32[]{:S(2)}, u32[]{:S(2)}) collective-permute-start(bf16[512,1024]{1,0:T(8,128)(2,1)S(1)} %pad_maximum_fusion.17), channel_id=1, source_target_pairs={{0,4},{4,0},{1,5},{5,1},{2,6},{6,2},{3,7},{7,3},{8,12},{12,8},{9,1... | collective-permute-start | bytes 3145736 | tf_op jit(solution)/shard_map/ppermute | solution.py:18
  155.2 48.1 %collective-permute-start.36 = (bf16[512,1024]{1,0:T(8,128)(2,1)S(1)}, bf16[512,1024]{1,0:T(8,128)(2,1)S(1)}, u32[]{:S(2)}, u32[]{:S(2)}) collective-permute-start(bf16[512,1024]{1,0:T(8,128)(2,1)S(1)} %pad_maximum_fusion.17), channel_id=1, source_target_pairs={{0,16},{16,0},{1,17},{17,1},{2,18},{18,2},{3,19},{19,3},{4,20},{20... | collective-permute-start | bytes 3145736 | tf_op jit(solution)/shard_map/ppermute | solution.py:18
  155.5 47.8 %collective-permute-start.37 = (bf16[512,1024]{1,0:T(8,128)(2,1)}, bf16[512,1024]{1,0:T(8,128)(2,1)S(1)}, u32[]{:S(2)}, u32[]{:S(2)}) collective-permute-start(bf16[512,1024]{1,0:T(8,128)(2,1)} %collective-permute-done.30), channel_id=1, source_target_pairs={{0,4},{4,0},{1,5},{5,1},{2,6},{6,2},{3,7},{7,3},{8,12},{12,8},{9,1... | collective-permute-start | bytes 3145736 | tf_op jit(solution)/shard_map/ppermute | solution.py:18
  158.9 23.7 %collective-permute-start.34 = (bf16[256,1024]{1,0:T(8,128)(2,1)S(1)}, bf16[256,1024]{1,0:T(8,128)(2,1)S(1)}, u32[]{:S(2)}, u32[]{:S(2)}) collective-permute-start(bf16[256,1024]{1,0:T(8,128)(2,1)S(1)} %pad_maximum_fusion.39), channel_id=1, source_target_pairs={{0,1},{1,0},{2,3},{3,2},{4,5},{5,4},{6,7},{7,6},{8,9},{9,8},{10,11... | collective-permute-start | bytes 1572872 | tf_op jit(solution)/shard_map/ppermute | solution.py:18
  183.0 26.0 %collective-permute-start.38 = (bf16[128,1024]{1,0:T(8,128)(2,1)S(1)}, bf16[128,1024]{1,0:T(8,128)(2,1)S(1)}, u32[]{:S(2)}, u32[]{:S(2)}) collective-permute-start(bf16[128,1024]{1,0:T(8,128)(2,1)S(1)} %slice.2412), channel_id=1, source_target_pairs={{0,8},{8,0},{1,9},{9,1},{2,10},{10,2},{3,11},{11,3},{4,12},{12,4},... | collective-permute-start | bytes 786440 | tf_op jit(solution)/shard_map/ppermute | solution.py:18
  184.7 29.9 %collective-permute-start.39 = (bf16[128,1024]{1,0:T(8,128)(2,1)S(1)}, bf16[128,1024]{1,0:T(8,128)(2,1)S(1)}, u32[]{:S(2)}, u32[]{:S(2)}) collective-permute-start(bf16[128,1024]{1,0:T(8,128)(2,1)S(1)} %slice.2411), channel_id=1, source_target_pairs={{0,8},{8,0},{1,9},{9,1},{2,10},{10,2},{3,11},{11,3},{4,12},{12,4},... | collective-permute-start | bytes 786440 | tf_op jit(solution)/shard_map/ppermute | solution.py:18
  203.3 72.8 %collective-permute-start.44 = (bf16[512,1024]{1,0:T(8,128)(2,1)S(1)}, bf16[512,1024]{1,0:T(8,128)(2,1)S(1)}, u32[]{:S(2)}, u32[]{:S(2)}) collective-permute-start(bf16[512,1024]{1,0:T(8,128)(2,1)S(1)} %collective-permute-done.36), channel_id=1, source_target_pairs={{0,4},{4,0},{1,5},{5,1},{2,6},{6,2},{3,7},{7,3},{8,12},{12,8},{9,1... | collective-permute-start | bytes 3145736 | tf_op jit(solution)/shard_map/ppermute | solution.py:18
  203.9 72.3 %collective-permute-start.45 = (bf16[512,1024]{1,0:T(8,128)(2,1)S(1)}, bf16[512,1024]{1,0:T(8,128)(2,1)S(1)}, u32[]{:S(2)}, u32[]{:S(2)}) collective-permute-start(bf16[512,1024]{1,0:T(8,128)(2,1)S(1)} %pad_maximum_fusion.18), channel_id=1, source_target_pairs={{0,16},{16,0},{1,17},{17,1},{2,18},{18,2},{3,19},{19,3},{4,20},{20... | collective-permute-start | bytes 3145736 | tf_op jit(solution)/shard_map/ppermute | solution.py:18
  203.9 72.3 %collective-permute-start.46 = (bf16[512,1024]{1,0:T(8,128)(2,1)S(1)}, bf16[512,1024]{1,0:T(8,128)(2,1)S(1)}, u32[]{:S(2)}, u32[]{:S(2)}) collective-permute-start(bf16[512,1024]{1,0:T(8,128)(2,1)S(1)} %pad_maximum_fusion.18), channel_id=1, source_target_pairs={{0,4},{4,0},{1,5},{5,1},{2,6},{6,2},{3,7},{7,3},{8,12},{12,8},{9,1... | collective-permute-start | bytes 3145736 | tf_op jit(solution)/shard_map/ppermute | solution.py:18
  215.6 36.2 %collective-permute-start.41 = (bf16[128,1024]{1,0:T(8,128)(2,1)S(1)}, bf16[128,1024]{1,0:T(8,128)(2,1)S(1)}, u32[]{:S(2)}, u32[]{:S(2)}) collective-permute-start(bf16[128,1024]{1,0:T(8,128)(2,1)S(1)} %get-tuple-element.670), channel_id=1, source_target_pairs={{0,8},{8,0},{1,9},{9,1},{2,10},{10,2},{3,11},{11,3},{4,12},{12,4},... | collective-permute-start | bytes 786440 | tf_op jit(solution)/shard_map/ppermute | solution.py:18
  253.5 22.7 %collective-permute-start.43 = (bf16[256,1024]{1,0:T(8,128)(2,1)S(1)}, bf16[256,1024]{1,0:T(8,128)(2,1)S(1)}, u32[]{:S(2)}, u32[]{:S(2)}) collective-permute-start(bf16[256,1024]{1,0:T(8,128)(2,1)S(1)} %pad_maximum_fusion.41), channel_id=1, source_target_pairs={{0,1},{1,0},{2,3},{3,2},{4,5},{5,4},{6,7},{7,6},{8,9},{9,8},{10,11... | collective-permute-start | bytes 1572872 | tf_op jit(solution)/shard_map/ppermute | solution.py:18
  298.4 25.3 %collective-permute-start.55 = (bf16[512,1024]{1,0:T(8,128)(2,1)S(1)}, bf16[512,1024]{1,0:T(8,128)(2,1)S(1)}, u32[]{:S(2)}, u32[]{:S(2)}) collective-permute-start(bf16[512,1024]{1,0:T(8,128)(2,1)S(1)} %collective-permute-done.45), channel_id=1, source_target_pairs={{0,4},{4,0},{1,5},{5,1},{2,6},{6,2},{3,7},{7,3},{8,12},{12,8},{9,1... | collective-permute-start | bytes 3145736 | tf_op jit(solution)/shard_map/ppermute | solution.py:18
  376.1 34.4 %collective-permute-start.66 = (bf16[512,1024]{1,0:T(8,128)(2,1)S(1)}, bf16[512,1024]{1,0:T(8,128)(2,1)S(1)}, u32[]{:S(2)}, u32[]{:S(2)}) collective-permute-start(bf16[512,1024]{1,0:T(8,128)(2,1)S(1)} %convolution_convert_fusion.5), channel_id=1, source_target_pairs={{0,4},{4,0},{1,5},{5,1},{2,6},{6,2},{3,7},{7,3},{8,12},{12,8},{9,1... | collective-permute-start | bytes 3145736 | tf_op jit(solution)/shard_map/ppermute | solution.py:18
  398.8 40.2 %collective-permute-start.70 = (bf16[512,1024]{1,0:T(8,128)(2,1)}, bf16[512,1024]{1,0:T(8,128)(2,1)}, u32[]{:S(2)}, u32[]{:S(2)}) collective-permute-start(bf16[512,1024]{1,0:T(8,128)(2,1)} %convolution_convert_fusion.4), channel_id=1, source_target_pairs={{0,4},{4,0},{1,5},{5,1},{2,6},{6,2},{3,7},{7,3},{8,12},{12,8},{9,1... | collective-permute-start | bytes 3145736 | tf_op jit(solution)/shard_map/ppermute | solution.py:18
  411.9 52.9 %collective-permute-start.73 = (bf16[512,1024]{1,0:T(8,128)(2,1)}, bf16[512,1024]{1,0:T(8,128)(2,1)}, u32[]{:S(2)}, u32[]{:S(2)}) collective-permute-start(bf16[512,1024]{1,0:T(8,128)(2,1)} %convolution_convert_fusion.3), channel_id=1, source_target_pairs={{0,4},{4,0},{1,5},{5,1},{2,6},{6,2},{3,7},{7,3},{8,12},{12,8},{9,1... | collective-permute-start | bytes 3145736 | tf_op jit(solution)/shard_map/ppermute | solution.py:18
  412.2 52.6 %collective-permute-start.74 = (bf16[512,1024]{1,0:T(8,128)(2,1)}, bf16[512,1024]{1,0:T(8,128)(2,1)}, u32[]{:S(2)}, u32[]{:S(2)}) collective-permute-start(bf16[512,1024]{1,0:T(8,128)(2,1)} %add_convert_fusion.6), channel_id=1, source_target_pairs={{0,16},{16,0},{1,17},{17,1},{2,18},{18,2},{3,19},{19,3},{4,20},{20... | collective-permute-start | bytes 3145736 | tf_op jit(solution)/shard_map/ppermute | solution.py:18
  439.5 24.7 %collective-permute-start.72 = (bf16[256,1024]{1,0:T(8,128)(2,1)S(1)}, bf16[256,1024]{1,0:T(8,128)(2,1)S(1)}, u32[]{:S(2)}, u32[]{:S(2)}) collective-permute-start(bf16[256,1024]{1,0:T(8,128)(2,1)S(1)} %pad_maximum_fusion.45), channel_id=1, source_target_pairs={{0,1},{1,0},{2,3},{3,2},{4,5},{5,4},{6,7},{7,6},{8,9},{9,8},{10,11... | collective-permute-start | bytes 1572872 | tf_op jit(solution)/shard_map/ppermute | solution.py:18
  441.1 80.8 %collective-permute-start.79 = (bf16[512,1024]{1,0:T(8,128)(2,1)S(1)}, bf16[512,1024]{1,0:T(8,128)(2,1)S(1)}, u32[]{:S(2)}, u32[]{:S(2)}) collective-permute-start(bf16[512,1024]{1,0:T(8,128)(2,1)S(1)} %copy-done.141), channel_id=1, source_target_pairs={{0,4},{4,0},{1,5},{5,1},{2,6},{6,2},{3,7},{7,3},{8,12},{12,8},{9,1... | collective-permute-start | bytes 3145736 | tf_op jit(solution)/shard_map/ppermute | solution.py:18
  469.1 18.7 %collective-permute-start.75 = (bf16[128,1024]{1,0:T(8,128)(2,1)S(1)}, bf16[128,1024]{1,0:T(8,128)(2,1)S(1)}, u32[]{:S(2)}, u32[]{:S(2)}) collective-permute-start(bf16[128,1024]{1,0:T(8,128)(2,1)S(1)} %slice.2409), channel_id=1, source_target_pairs={{0,8},{8,0},{1,9},{9,1},{2,10},{10,2},{3,11},{11,3},{4,12},{12,4},... | collective-permute-start | bytes 786440 | tf_op jit(solution)/shard_map/ppermute | solution.py:18
  470.5 21.2 %collective-permute-start.76 = (bf16[128,1024]{1,0:T(8,128)(2,1)S(1)}, bf16[128,1024]{1,0:T(8,128)(2,1)S(1)}, u32[]{:S(2)}, u32[]{:S(2)}) collective-permute-start(bf16[128,1024]{1,0:T(8,128)(2,1)S(1)} %slice.2408), channel_id=1, source_target_pairs={{0,8},{8,0},{1,9},{9,1},{2,10},{10,2},{3,11},{11,3},{4,12},{12,4},... | collective-permute-start | bytes 786440 | tf_op jit(solution)/shard_map/ppermute | solution.py:18
  471.2 67.4 %collective-permute-start.82 = (bf16[512,1024]{1,0:T(8,128)(2,1)S(1)}, bf16[512,1024]{1,0:T(8,128)(2,1)S(1)}, u32[]{:S(2)}, u32[]{:S(2)}) collective-permute-start(bf16[512,1024]{1,0:T(8,128)(2,1)S(1)} %copy-done.140), channel_id=1, source_target_pairs={{0,4},{4,0},{1,5},{5,1},{2,6},{6,2},{3,7},{7,3},{8,12},{12,8},{9,1... | collective-permute-start | bytes 3145736 | tf_op jit(solution)/shard_map/ppermute | solution.py:18
  472.2 66.4 %collective-permute-start.83 = (bf16[512,1024]{1,0:T(8,128)(2,1)S(1)}, bf16[512,1024]{1,0:T(8,128)(2,1)S(1)}, u32[]{:S(2)}, u32[]{:S(2)}) collective-permute-start(bf16[512,1024]{1,0:T(8,128)(2,1)S(1)} %add_convert_fusion.3), channel_id=1, source_target_pairs={{0,16},{16,0},{1,17},{17,1},{2,18},{18,2},{3,19},{19,3},{4,20},{20... | collective-permute-start | bytes 3145736 | tf_op jit(solution)/shard_map/ppermute | solution.py:18
  494.3 25.3 %collective-permute-start.78 = (bf16[128,1024]{1,0:T(8,128)(2,1)S(1)}, bf16[128,1024]{1,0:T(8,128)(2,1)S(1)}, u32[]{:S(2)}, u32[]{:S(2)}) collective-permute-start(bf16[128,1024]{1,0:T(8,128)(2,1)S(1)} %get-tuple-element.824), channel_id=1, source_target_pairs={{0,8},{8,0},{1,9},{9,1},{2,10},{10,2},{3,11},{11,3},{4,12},{12,4},... | collective-permute-start | bytes 786440 | tf_op jit(solution)/shard_map/ppermute | solution.py:18
  544.1 29.8 %collective-permute-start.86 = (bf16[512,1024]{1,0:T(8,128)(2,1)}, bf16[512,1024]{1,0:T(8,128)(2,1)}, u32[]{:S(2)}, u32[]{:S(2)}) collective-permute-start(bf16[512,1024]{1,0:T(8,128)(2,1)} %convolution_convert_fusion), channel_id=1, source_target_pairs={{0,4},{4,0},{1,5},{5,1},{2,6},{6,2},{3,7},{7,3},{8,12},{12,8},{9,1... | collective-permute-start | bytes 3145736 | tf_op jit(solution)/shard_map/ppermute | solution.py:18
  545.4 54.8 %collective-permute-start.90 = (bf16[256,1024]{1,0:T(8,128)(2,1)}, bf16[256,1024]{1,0:T(8,128)(2,1)}, u32[]{:S(2)}, u32[]{:S(2)}) collective-permute-start(bf16[256,1024]{1,0:T(8,128)(2,1)} %select_convert_fusion.5), channel_id=1, source_target_pairs={{0,8},{8,0},{1,9},{9,1},{2,10},{10,2},{3,11},{11,3},{4,12},{12,4},... | collective-permute-start | bytes 1572872 | tf_op jit(solution)/shard_map/ppermute | solution.py:18
  547.8 48.3 %collective-permute-start.88 = (bf16[512,1024]{1,0:T(8,128)(2,1)}, bf16[512,1024]{1,0:T(8,128)(2,1)}, u32[]{:S(2)}, u32[]{:S(2)}) collective-permute-start(bf16[512,1024]{1,0:T(8,128)(2,1)} %add_convert_fusion.2), channel_id=1, source_target_pairs={{0,16},{16,0},{1,17},{17,1},{2,18},{18,2},{3,19},{19,3},{4,20},{20... | collective-permute-start | bytes 3145736 | tf_op jit(solution)/shard_map/ppermute | solution.py:18
  548.7 72.7 %collective-permute-start.95 = (bf16[256,1024]{1,0:T(8,128)(2,1)}, bf16[256,1024]{1,0:T(8,128)(2,1)}, u32[]{:S(2)}, u32[]{:S(2)}) collective-permute-start(bf16[256,1024]{1,0:T(8,128)(2,1)} %select_convert_fusion.4), channel_id=1, source_target_pairs={{0,8},{8,0},{1,9},{9,1},{2,10},{10,2},{3,11},{11,3},{4,12},{12,4},... | collective-permute-start | bytes 1572872 | tf_op jit(solution)/shard_map/ppermute | solution.py:18
  578.8 20.0 %collective-permute-start.89 = (bf16[512,512]{0,1:T(8,128)(2,1)}, bf16[512,512]{0,1:T(8,128)(2,1)}, u32[]{:S(2)}, u32[]{:S(2)}) collective-permute-start(bf16[512,512]{0,1:T(8,128)(2,1)} %pad_maximum_fusion.48), channel_id=1, source_target_pairs={{0,4},{4,0},{1,5},{5,1},{2,6},{6,2},{3,7},{7,3},{8,12},{12,8},{9,1... | collective-permute-start | bytes 1572872 | tf_op jit(solution)/shard_map/ppermute | solution.py:18
  610.8 25.9 %collective-permute-start.99 = (bf16[512,512]{0,1:T(8,128)(2,1)S(1)}, bf16[512,512]{0,1:T(8,128)(2,1)S(1)}, u32[]{:S(2)}, u32[]{:S(2)}) collective-permute-start(bf16[512,512]{0,1:T(8,128)(2,1)S(1)} %fusion.26), channel_id=1, source_target_pairs={{0,16},{16,0},{1,17},{17,1},{2,18},{18,2},{3,19},{19,3},{4,20},{20... | collective-permute-start | bytes 1572872 | tf_op jit(solution)/shard_map/ppermute | solution.py:18
  611.3 52.9 %collective-permute-start.104 = (bf16[256,1024]{1,0:T(8,128)(2,1)S(1)}, bf16[256,1024]{1,0:T(8,128)(2,1)S(1)}, u32[]{:S(2)}, u32[]{:S(2)}) collective-permute-start(bf16[256,1024]{1,0:T(8,128)(2,1)S(1)} %select_convert_fusion.2), channel_id=1, source_target_pairs={{0,8},{8,0},{1,9},{9,1},{2,10},{10,2},{3,11},{11,3},{4,12},{12,4},... | collective-permute-start | bytes 1572872 | tf_op jit(solution)/shard_map/ppermute | solution.py:18
  630.2 33.9 %collective-permute-start.103 = (f32[4,512]{1,0:T(4,128)S(1)}, f32[4,512]{1,0:T(4,128)S(1)}, u32[]{:S(2)}, u32[]{:S(2)}) collective-permute-start(f32[4,512]{1,0:T(4,128)S(1)} %slice.1333), channel_id=1, source_target_pairs={{0,16},{16,0},{1,17},{17,1},{2,18},{18,2},{3,19},{19,3},{4,20},{20... | collective-permute-start | bytes 24584 | tf_op jit(solution)/shard_map/ppermute | solution.py:18
  631.7 32.9 %collective-permute-start.105 = (bf16[128,2048]{1,0:T(8,128)(2,1)S(1)}, bf16[128,2048]{1,0:T(8,128)(2,1)S(1)}, u32[]{:S(2)}, u32[]{:S(2)}) collective-permute-start(bf16[128,2048]{1,0:T(8,128)(2,1)S(1)} %select_convert_fusion.1), channel_id=1, source_target_pairs={{0,2},{2,0},{1,3},{3,1},{4,6},{6,4},{5,7},{7,5},{8,10},{10,8},{9,1... | collective-permute-start | bytes 1572872 | tf_op jit(solution)/shard_map/ppermute | solution.py:18
  638.6 23.5 %collective-permute-start.102 = (bf16[256,1024]{1,0:T(8,128)(2,1)S(1)}, bf16[256,1024]{1,0:T(8,128)(2,1)S(1)}, u32[]{:S(2)}, u32[]{:S(2)}) collective-permute-start(bf16[256,1024]{1,0:T(8,128)(2,1)S(1)} %pad_maximum_fusion.51), channel_id=1, source_target_pairs={{0,1},{1,0},{2,3},{3,2},{4,5},{5,4},{6,7},{7,6},{8,9},{9,8},{10,11... | collective-permute-start | bytes 1572872 | tf_op jit(solution)/shard_map/ppermute | solution.py:18
  652.9 28.7 %collective-permute-start.109 = (bf16[512,512]{0,1:T(8,128)(2,1)S(1)}, bf16[512,512]{0,1:T(8,128)(2,1)S(1)}, u32[]{:S(2)}, u32[]{:S(2)}) collective-permute-start(bf16[512,512]{0,1:T(8,128)(2,1)S(1)} %pad_maximum_fusion.52), channel_id=1, source_target_pairs={{0,4},{4,0},{1,5},{5,1},{2,6},{6,2},{3,7},{7,3},{8,12},{12,8},{9,1... | collective-permute-start | bytes 1572872 | tf_op jit(solution)/shard_map/ppermute | solution.py:18
  662.1 23.4 %collective-permute-start.111 = (bf16[512,512]{0,1:T(8,128)(2,1)S(1)}, bf16[512,512]{0,1:T(8,128)(2,1)S(1)}, u32[]{:S(2)}, u32[]{:S(2)}) collective-permute-start(bf16[512,512]{0,1:T(8,128)(2,1)S(1)} %pad_maximum_fusion.53), channel_id=1, source_target_pairs={{0,4},{4,0},{1,5},{5,1},{2,6},{6,2},{3,7},{7,3},{8,12},{12,8},{9,1... | collective-permute-start | bytes 1572872 | tf_op jit(solution)/shard_map/ppermute | solution.py:18
  677.8 21.3 %collective-permute-start.114 = (bf16[512,512]{0,1:T(8,128)(2,1)S(1)}, bf16[512,512]{0,1:T(8,128)(2,1)S(1)}, u32[]{:S(2)}, u32[]{:S(2)}) collective-permute-start(bf16[512,512]{0,1:T(8,128)(2,1)S(1)} %fusion.27), channel_id=1, source_target_pairs={{0,16},{16,0},{1,17},{17,1},{2,18},{18,2},{3,19},{19,3},{4,20},{20... | collective-permute-start | bytes 1572872 | tf_op jit(solution)/shard_map/ppermute | solution.py:18
  (264 other events, 2540.7 us)

commit v8 on v6

--- a/solution.py
+++ b/solution.py
@@ -236,8 +236,6 @@
         tokens_rel = to_relative(tokens)
         left, right = tokens_rel[:, :half_width], tokens_rel[:, half_width:]
         left_sent = c.start(left, "tensor")
-        ffn_split = [split(w, "core", 1) for w in (w_gate, w_up, w_down)]
-        ffn_sent = c.start(columns([s[1] for s in ffn_split]), "core")
         gain_steps()
 
         attn_sent = c.sync(attn_sent)
@@ -254,6 +252,8 @@
             axis=1,
         )
         ids_sent = c.start(ids, "zl")
+        ffn_split = [split(w, "core", 1) for w in (w_gate, w_up, w_down)]
+        ffn_sent = c.start(columns([s[1] for s in ffn_split]), "core")
         qk.end_line()
         gain_steps()
         qk.start_x(0)
@@ -442,17 +442,11 @@
         act = (gate * sigma * up).astype(BF)
 
         wd0 = down_w.rows(0)
-        first_rows = down_w.blocks[1][0]
-        left, right = scatter_rows(
-            lambda rows: dot_nt(act[rows], wd0), lambda rows: dot_nt(act[rows], first_rows)
-        )
         down_w.end_x(1)
-        last_rows = down_w.blocks[1][1]
-        sent = c.start(dot_nt(act[other], last_rows).astype(BF), "core")
-        last = cross(dot_nt(act[own], last_rows) + c.sync(sent).astype(F32))
-        last = halve(added(last), "zl")
-        ffn = columns([left, right, added(last)])
         wd1 = down_w.rows(1)
+        ffn = columns(
+            scatter_rows(lambda rows: dot_nt(act[rows], wd0), lambda rows: dot_nt(act[rows], wd1))
+        )
 
         ffn_rms = rms_scale(ffn)
         output = to_natural((resid + ffn * ffn_rms * ffn_scale).astype(BF))
@@ -617,7 +611,7 @@
         ov_grad.end_x(1)
         ov_grad.start_high()
         down_grad.end_line()
-        inner = pair_sum(c, inner)
+        inner = pair_sum(c, inner, up_grad.start_line)
         gain_steps()
         d_query = (
             q_rms * (scaled_q - query * q_rms * q_rms * (inner[0] / model_width)[:, None])
@@ -630,19 +624,19 @@
         qk_grad.start_x(1)
         gate_grad.end_line()
         down_grad.end()
-        ov_grad.start_x(0)
 
         def tokens_first():
-            ov_grad.end_x(0)
-            ov_grad.end_high()
+            ov_grad.high = c.sync(ov_grad.high)
             qk_grad.end_x(1)
             qk_grad.start_high()
+            ov_grad.start_x(0)
             qk_grad.start_x(0)
 
         def tokens_second():
+            qk_grad.end_x(0)
+            qk_grad.end_high()
+            qk_grad.start_line()
             gain_steps()
-            up_grad.start_line()
-            gate_grad.end()
 
         d_tokens = columns(
             scatter_rows(
@@ -653,19 +647,19 @@
             )
         )
         grad_tokens = to_natural(d_resid + d_tokens)
+        ov_grad.end_x(0)
+        ov_grad.end_high()
+        ov_grad.start_line()
         gain_steps()
-        ov_grad.start_line()
         up_grad.end_line()
+        gate_grad.end()
         gain_steps()
-        qk_grad.end_x(0)
+        qk_grad.end_line()
         ov_grad.end_line()
         gain_parts = gain_steps.finish()
-        qk_grad.end_high()
-        qk_grad.start_line()
         up_grad.end()
+        qk_grad.end()
         ov_grad.end()
-        qk_grad.end_line()
-        qk_grad.end()
         grad_output, grad_value = ov_grad.results
         grad_query, grad_key = qk_grad.results
         return (

time: 714 us -> 710 us (level)
    dot_general x26 -> x24, matrix products: 31 us -> 35.8 us  [dot_nt(): return jnp.einsum('sc,rc->sr', a, b, preferred_element_type=F32)]
    ppermute x119 -> x116, starting transfers between devices: 110 us -> 114 us  [swap(): return lax.ppermute(value, axis, FLIP)]
    unnamed x442 -> x425, local copies, waits for them, and re-layouts: 30.7 us -> 27 us
    ppermute x119 -> x116, waiting for transfers between devices: 328 us -> 325 us  [swap(): return lax.ppermute(value, axis, FLIP)]
  transfers between devices with their start and end apart: 119 -> 116, of which waited for: 48 -> 49; matrix products, arithmetic and copies ran while one was open for 28% -> 28% of each run, Pallas kernels for 0% -> 0%
where the time goes in v8:
time: 710 us; the launch traced here: 703 us
  waiting for transfers between devices  325 us (46%)
  matrix products  127 us (18%)
  starting transfers between devices  114 us (16%)
  other arithmetic  73.2 us (10%)
  local copies, waits for them, and re-layouts  58.6 us (8%)
    ppermute x116, waiting for transfers between devices, swap(): return lax.ppermute(value, axis, FLIP)  325 us
    ppermute x116, starting transfers between devices, swap(): return lax.ppermute(value, axis, FLIP)  114 us
    dot_general x28, matrix products, dot_tn(): return jnp.einsum('sr,sc->rc', a, b, preferred_element_type=F32)  45.4 us
    dot_general x24, matrix products, dot_nt(): return jnp.einsum('sc,rc->sr', a, b, preferred_element_type=F32)  35.8 us
    dot_general x12, matrix products, dot(): return jnp.dot(a, b, preferred_element_type=F32)  32.4 us
    unnamed x425, local copies, waits for them, and re-layouts  27 us
  transfers between devices with their start and end apart: 116, of which 49 were waited for; matrix products, arithmetic and copies ran while one was open for 28% of the time, Pallas kernels for 0%

profile of v8, /device:TPU:0, one launch (start us, length us, event | category | flops | bytes accessed | tf_op | source)
XLA Modules:
  0.0 703.2 jit_solution(15296633558968167332)
XLA Ops:
  6.0 3.1 collective-permute-start
  22.6 4.4 collective-permute-done.3
  41.6 6.0 collective-permute-done.9
  52.5 7.9 %collective-permute-done.12 = bf16[512,512]{0,1:T(8,128)(2,1)S(1)} collective-permute-done((bf16[512,512]{0,1:T(8,128)(2,1)S(1)}, bf16[512,512]{0,1:T(8,128)(2,1)S(1)}, u32[]{:S(2)}, u32[]{:S(2)}) %collective-permute-start.12) | collective-permute-done | bytes 524320 | tf_op jit(solution)/shard_map/ppermute | solution.py:18
  60.4 3.1 collective-permute-done.13
  78.7 8.6 %collective-permute-done.18 = bf16[256,1024]{1,0:T(8,128)(2,1)S(1)} collective-permute-done((bf16[256,1024]{1,0:T(8,128)(2,1)}, bf16[256,1024]{1,0:T(8,128)(2,1)S(1)}, u32[]{:S(2)}, u32[]{:S(2)}) %collective-permute-start.18) | collective-permute-done | bytes 524320 | tf_op jit(solution)/shard_map/ppermute | solution.py:18
  87.5 2.9 pad_maximum_fusion
  104.8 3.0 collective-permute-start.30
  110.7 6.8 collective-permute-done.26
  123.1 2.8 fusion.130
  127.5 3.4 fusion.213
  132.8 2.9 fusion.4
  141.8 9.2 %collective-permute-done.29 = bf16[256,1024]{1,0:T(8,128)(2,1)} collective-permute-done((bf16[256,1024]{1,0:T(8,128)(2,1)}, bf16[256,1024]{1,0:T(8,128)(2,1)}, u32[]{:S(2)}, u32[]{:S(2)}) %collective-permute-start.29) | collective-permute-done | bytes 524320 | tf_op jit(solution)/shard_map/ppermute | solution.py:18
  151.0 3.2 collective-permute-done.30
  160.1 2.8 collective-permute-start.33
  164.6 26.1 %collective-permute-done.33 = bf16[256,1024]{1,0:T(8,128)(2,1)S(1)} collective-permute-done((bf16[256,1024]{1,0:T(8,128)(2,1)S(1)}, bf16[256,1024]{1,0:T(8,128)(2,1)S(1)}, u32[]{:S(2)}, u32[]{:S(2)}) %collective-permute-start.33) | collective-permute-done | bytes 524320 | tf_op jit(solution)/shard_map/ppermute | solution.py:18
  195.3 9.6 %collective-permute-done.36 = bf16[512,1024]{1,0:T(8,128)(2,1)S(1)} collective-permute-done((bf16[512,1024]{1,0:T(8,128)(2,1)S(1)}, bf16[512,1024]{1,0:T(8,128)(2,1)S(1)}, u32[]{:S(2)}, u32[]{:S(2)}) %collective-permute-start.36) | collective-permute-done | bytes 1048608 | tf_op jit(solution)/shard_map/ppermute | solution.py:18
  205.5 5.0 collective-permute-done.39
  212.9 6.7 collective-permute-done.40
  219.6 14.0 %collective-permute-done.41 = bf16[128,1024]{1,0:T(8,128)(2,1)S(1)} collective-permute-done((bf16[128,1024]{1,0:T(8,128)(2,1)S(1)}, bf16[128,1024]{1,0:T(8,128)(2,1)S(1)}, u32[]{:S(2)}, u32[]{:S(2)}) %collective-permute-start.41) | collective-permute-done | bytes 262176 | tf_op jit(solution)/shard_map/ppermute | solution.py:18
  239.3 24.2 %collective-permute-done.42 = bf16[256,1024]{1,0:T(8,128)(2,1)S(1)} collective-permute-done((bf16[256,1024]{1,0:T(8,128)(2,1)S(1)}, bf16[256,1024]{1,0:T(8,128)(2,1)S(1)}, u32[]{:S(2)}, u32[]{:S(2)}) %collective-permute-start.42) | collective-permute-done | bytes 524320 | tf_op jit(solution)/shard_map/ppermute | solution.py:18
  268.0 21.6 %collective-permute-done.49 = bf16[512,1024]{1,0:T(8,128)(2,1)S(1)} collective-permute-done((bf16[512,1024]{1,0:T(8,128)(2,1)S(1)}, bf16[512,1024]{1,0:T(8,128)(2,1)S(1)}, u32[]{:S(2)}, u32[]{:S(2)}) %collective-permute-start.49) | collective-permute-done | bytes 1048608 | tf_op jit(solution)/shard_map/ppermute | solution.py:18
  294.5 3.6 fusion.190
  298.2 5.4 multiply_convert_fusion.2
  312.3 12.5 %collective-permute-done.52 = bf16[256,1024]{1,0:T(8,128)(2,1)S(1)} collective-permute-done((bf16[256,1024]{1,0:T(8,128)(2,1)S(1)}, bf16[256,1024]{1,0:T(8,128)(2,1)S(1)}, u32[]{:S(2)}, u32[]{:S(2)}) %collective-permute-start.52) | collective-permute-done | bytes 524320 | tf_op jit(solution)/shard_map/ppermute | solution.py:18
  328.7 4.2 collective-permute-done.54
  338.1 4.6 collective-permute-done.56
  346.5 7.7 %collective-permute-done.58 = bf16[256,1024]{1,0:T(8,128)(2,1)S(1)} collective-permute-done((bf16[256,1024]{1,0:T(8,128)(2,1)S(1)}, bf16[256,1024]{1,0:T(8,128)(2,1)S(1)}, u32[]{:S(2)}, u32[]{:S(2)}) %collective-permute-start.58) | collective-permute-done | bytes 524320 | tf_op jit(solution)/shard_map/ppermute | solution.py:18
  363.5 3.0 constant_dynamic-update-slice_fusion.60
  366.6 3.5 convolution_convert_fusion.4
  374.2 2.9 fusion.20
  379.2 3.9 fusion.223
  383.2 5.6 multiply_convert_fusion
  409.2 4.2 fusion.67
  419.5 4.0 add_convert_fusion.5
  424.1 3.0 fusion.65
  438.7 28.5 %collective-permute-done.68 = bf16[256,1024]{1,0:T(8,128)(2,1)S(1)} collective-permute-done((bf16[256,1024]{1,0:T(8,128)(2,1)S(1)}, bf16[256,1024]{1,0:T(8,128)(2,1)S(1)}, u32[]{:S(2)}, u32[]{:S(2)}) %collective-permute-start.68) | collective-permute-done | bytes 524320 | tf_op jit(solution)/shard_map/ppermute | solution.py:18
  476.6 3.0 collective-permute-start.80
  479.9 3.2 collective-permute-done.73
  485.1 5.7 collective-permute-done.74
  490.8 16.2 %collective-permute-done.75 = bf16[128,1024]{1,0:T(8,128)(2,1)S(1)} collective-permute-done((bf16[128,1024]{1,0:T(8,128)(2,1)S(1)}, bf16[128,1024]{1,0:T(8,128)(2,1)S(1)}, u32[]{:S(2)}, u32[]{:S(2)}) %collective-permute-start.75) | collective-permute-done | bytes 262176 | tf_op jit(solution)/shard_map/ppermute | solution.py:18
  510.4 25.5 %collective-permute-done.77 = bf16[256,1024]{1,0:T(8,128)(2,1)S(1)} collective-permute-done((bf16[256,1024]{1,0:T(8,128)(2,1)S(1)}, bf16[256,1024]{1,0:T(8,128)(2,1)S(1)}, u32[]{:S(2)}, u32[]{:S(2)}) %collective-permute-start.77) | collective-permute-done | bytes 524320 | tf_op jit(solution)/shard_map/ppermute | solution.py:18
  542.4 2.9 collective-permute-start.85
  554.4 3.1 fusion.5
  635.7 7.8 %collective-permute-done.98 = bf16[256,1024]{1,0:T(8,128)(2,1)S(1)} collective-permute-done((bf16[256,1024]{1,0:T(8,128)(2,1)S(1)}, bf16[256,1024]{1,0:T(8,128)(2,1)S(1)}, u32[]{:S(2)}, u32[]{:S(2)}) %collective-permute-start.98) | collective-permute-done | bytes 524320 | tf_op jit(solution)/shard_map/ppermute | solution.py:18
  648.1 21.4 %collective-permute-done.101 = bf16[512,512]{0,1:T(8,128)(2,1)S(1)} collective-permute-done((bf16[512,512]{0,1:T(8,128)(2,1)S(1)}, bf16[512,512]{0,1:T(8,128)(2,1)S(1)}, u32[]{:S(2)}, u32[]{:S(2)}) %collective-permute-start.101) | collective-permute-done | bytes 524320 | tf_op jit(solution)/shard_map/ppermute | solution.py:18
  670.7 7.3 %collective-permute-done.103 = bf16[128,1024]{1,0:T(8,128)(2,1)S(1)} collective-permute-done((bf16[128,1024]{1,0:T(8,128)(2,1)S(1)}, bf16[128,1024]{1,0:T(8,128)(2,1)S(1)}, u32[]{:S(2)}, u32[]{:S(2)}) %collective-permute-start.103) | collective-permute-done | bytes 262176 | tf_op jit(solution)/shard_map/ppermute | solution.py:18
  688.1 3.1 collective-permute-done.111
  (964 shorter events, 323.9 us)
Async XLA Ops:
  10.0 19.2 %collective-permute-start.5 = (bf16[128,1024]{1,0:T(8,128)(2,1)}, bf16[128,1024]{1,0:T(8,128)(2,1)}, u32[]{:S(2)}, u32[]{:S(2)}) collective-permute-start(bf16[128,1024]{1,0:T(8,128)(2,1)} %pad_maximum_fusion.58), channel_id=1, source_target_pairs={{0,1},{1,0},{2,3},{3,2},{4,5},{5,4},{6,7},{7,6},{8,9},{9,8},{10,11... | collective-permute-start | bytes 786440 | tf_op jit(solution)/shard_map/ppermute | solution.py:18
  17.9 21.5 %collective-permute-start.8 = (bf16[128,6144]{1,0:T(8,128)(2,1)S(1)}, bf16[128,6144]{1,0:T(8,128)(2,1)S(1)}, u32[]{:S(2)}, u32[]{:S(2)}) collective-permute-start(bf16[128,6144]{1,0:T(8,128)(2,1)S(1)} %copy-done.109), channel_id=1, source_target_pairs={{0,2},{2,0},{1,3},{3,1},{4,6},{6,4},{5,7},{7,5},{8,10},{10,8},{9,1... | collective-permute-start | bytes 4718600 | tf_op jit(solution)/shard_map/ppermute | solution.py:18
  30.1 20.6 %collective-permute-start.10 = (f32[4,512]{1,0:T(4,128)S(1)}, f32[4,512]{1,0:T(4,128)S(1)}, u32[]{:S(2)}, u32[]{:S(2)}) collective-permute-start(f32[4,512]{1,0:T(4,128)S(1)} %pad_maximum_fusion.76), channel_id=1, source_target_pairs={{0,16},{16,0},{1,17},{17,1},{2,18},{18,2},{3,19},{19,3},{4,20},{20... | collective-permute-start | bytes 24584 | tf_op jit(solution)/shard_map/ppermute | solution.py:18
  32.9 18.4 %collective-permute-start.11 = (bf16[512,512]{0,1:T(8,128)(2,1)S(1)}, bf16[512,512]{0,1:T(8,128)(2,1)S(1)}, u32[]{:S(2)}, u32[]{:S(2)}) collective-permute-start(bf16[512,512]{0,1:T(8,128)(2,1)S(1)} %pad_maximum_fusion.36), channel_id=1, source_target_pairs={{0,4},{4,0},{1,5},{5,1},{2,6},{6,2},{3,7},{7,3},{8,12},{12,8},{9,1... | collective-permute-start | bytes 1572872 | tf_op jit(solution)/shard_map/ppermute | solution.py:18
  36.8 23.6 %collective-permute-start.12 = (bf16[512,512]{0,1:T(8,128)(2,1)S(1)}, bf16[512,512]{0,1:T(8,128)(2,1)S(1)}, u32[]{:S(2)}, u32[]{:S(2)}) collective-permute-start(bf16[512,512]{0,1:T(8,128)(2,1)S(1)} %pad_maximum_fusion.36), channel_id=1, source_target_pairs={{0,16},{16,0},{1,17},{17,1},{2,18},{18,2},{3,19},{19,3},{4,20},{20... | collective-permute-start | bytes 1572872 | tf_op jit(solution)/shard_map/ppermute | solution.py:18
  39.8 23.7 %collective-permute-start.13 = (bf16[256,1024]{1,0:T(8,128)(2,1)S(1)}, bf16[256,1024]{1,0:T(8,128)(2,1)S(1)}, u32[]{:S(2)}, u32[]{:S(2)}) collective-permute-start(bf16[256,1024]{1,0:T(8,128)(2,1)S(1)} %pad_maximum_fusion.37), channel_id=1, source_target_pairs={{0,8},{8,0},{1,9},{9,1},{2,10},{10,2},{3,11},{11,3},{4,12},{12,4},... | collective-permute-start | bytes 1572872 | tf_op jit(solution)/shard_map/ppermute | solution.py:18
  67.6 19.8 %collective-permute-start.18 = (bf16[256,1024]{1,0:T(8,128)(2,1)}, bf16[256,1024]{1,0:T(8,128)(2,1)S(1)}, u32[]{:S(2)}, u32[]{:S(2)}) collective-permute-start(bf16[256,1024]{1,0:T(8,128)(2,1)} %broadcast_select_fusion.11), channel_id=1, source_target_pairs={{0,8},{8,0},{1,9},{9,1},{2,10},{10,2},{3,11},{11,3},{4,12},{12,4},... | collective-permute-start | bytes 1572872 | tf_op jit(solution)/shard_map/ppermute | solution.py:18
  69.4 18.0 %collective-permute-start.19 = (f32[4,1024]{1,0:T(4,128)}, f32[4,1024]{1,0:T(4,128)S(1)}, u32[]{:S(2)}, u32[]{:S(2)}) collective-permute-start(f32[4,1024]{1,0:T(4,128)} %pad_maximum_fusion.71), channel_id=1, source_target_pairs={{0,4},{4,0},{1,5},{5,1},{2,6},{6,2},{3,7},{7,3},{8,12},{12,8},{9,1... | collective-permute-start | bytes 49160 | tf_op jit(solution)/shard_map/ppermute | solution.py:18
  74.7 26.1 %collective-permute-start.22 = (bf16[512,512]{0,1:T(8,128)(2,1)S(1)}, bf16[512,512]{0,1:T(8,128)(2,1)S(1)}, u32[]{:S(2)}, u32[]{:S(2)}) collective-permute-start(bf16[512,512]{0,1:T(8,128)(2,1)S(1)} %copy-done.133), channel_id=1, source_target_pairs={{0,16},{16,0},{1,17},{17,1},{2,18},{18,2},{3,19},{19,3},{4,20},{20... | collective-permute-start | bytes 1572872 | tf_op jit(solution)/shard_map/ppermute | solution.py:18
  77.2 23.5 %collective-permute-start.23 = (bf16[512,512]{0,1:T(8,128)(2,1)S(1)}, bf16[512,512]{0,1:T(8,128)(2,1)S(1)}, u32[]{:S(2)}, u32[]{:S(2)}) collective-permute-start(bf16[512,512]{0,1:T(8,128)(2,1)S(1)} %copy-done.133), channel_id=1, source_target_pairs={{0,4},{4,0},{1,5},{5,1},{2,6},{6,2},{3,7},{7,3},{8,12},{12,8},{9,1... | collective-permute-start | bytes 1572872 | tf_op jit(solution)/shard_map/ppermute | solution.py:18
  104.7 34.3 %collective-permute-start.27 = (bf16[256,1024]{1,0:T(8,128)(2,1)}, bf16[256,1024]{1,0:T(8,128)(2,1)}, u32[]{:S(2)}, u32[]{:S(2)}) collective-permute-start(bf16[256,1024]{1,0:T(8,128)(2,1)} %broadcast_select_fusion.7), channel_id=1, source_target_pairs={{0,8},{8,0},{1,9},{9,1},{2,10},{10,2},{3,11},{11,3},{4,12},{12,4},... | collective-permute-start | bytes 1572872 | tf_op jit(solution)/shard_map/ppermute | solution.py:18
  104.8 49.4 %collective-permute-start.30 = (bf16[512,1024]{1,0:T(8,128)(2,1)}, bf16[512,1024]{1,0:T(8,128)(2,1)}, u32[]{:S(2)}, u32[]{:S(2)}) collective-permute-start(bf16[512,1024]{1,0:T(8,128)(2,1)} %pad_maximum_fusion.17), channel_id=1, source_target_pairs={{0,16},{16,0},{1,17},{17,1},{2,18},{18,2},{3,19},{19,3},{4,20},{20... | collective-permute-start | bytes 3145736 | tf_op jit(solution)/shard_map/ppermute | solution.py:18
  107.9 33.9 %collective-permute-start.28 = (bf16[512,1024]{1,0:T(8,128)(2,1)}, bf16[512,1024]{1,0:T(8,128)(2,1)}, u32[]{:S(2)}, u32[]{:S(2)}) collective-permute-start(bf16[512,1024]{1,0:T(8,128)(2,1)} %pad_maximum_fusion.17), channel_id=1, source_target_pairs={{0,4},{4,0},{1,5},{5,1},{2,6},{6,2},{3,7},{7,3},{8,12},{12,8},{9,1... | collective-permute-start | bytes 3145736 | tf_op jit(solution)/shard_map/ppermute | solution.py:18
  109.3 41.7 %collective-permute-start.29 = (bf16[256,1024]{1,0:T(8,128)(2,1)}, bf16[256,1024]{1,0:T(8,128)(2,1)}, u32[]{:S(2)}, u32[]{:S(2)}) collective-permute-start(bf16[256,1024]{1,0:T(8,128)(2,1)} %broadcast_select_fusion.6), channel_id=1, source_target_pairs={{0,8},{8,0},{1,9},{9,1},{2,10},{10,2},{3,11},{11,3},{4,12},{12,4},... | collective-permute-start | bytes 1572872 | tf_op jit(solution)/shard_map/ppermute | solution.py:18
  155.3 40.0 %collective-permute-start.35 = (bf16[512,1024]{1,0:T(8,128)(2,1)S(1)}, bf16[512,1024]{1,0:T(8,128)(2,1)S(1)}, u32[]{:S(2)}, u32[]{:S(2)}) collective-permute-start(bf16[512,1024]{1,0:T(8,128)(2,1)S(1)} %pad_maximum_fusion.19), channel_id=1, source_target_pairs={{0,4},{4,0},{1,5},{5,1},{2,6},{6,2},{3,7},{7,3},{8,12},{12,8},{9,1... | collective-permute-start | bytes 3145736 | tf_op jit(solution)/shard_map/ppermute | solution.py:18
  156.8 48.1 %collective-permute-start.36 = (bf16[512,1024]{1,0:T(8,128)(2,1)S(1)}, bf16[512,1024]{1,0:T(8,128)(2,1)S(1)}, u32[]{:S(2)}, u32[]{:S(2)}) collective-permute-start(bf16[512,1024]{1,0:T(8,128)(2,1)S(1)} %pad_maximum_fusion.19), channel_id=1, source_target_pairs={{0,16},{16,0},{1,17},{17,1},{2,18},{18,2},{3,19},{19,3},{4,20},{20... | collective-permute-start | bytes 3145736 | tf_op jit(solution)/shard_map/ppermute | solution.py:18
  157.1 47.8 %collective-permute-start.37 = (bf16[512,1024]{1,0:T(8,128)(2,1)}, bf16[512,1024]{1,0:T(8,128)(2,1)S(1)}, u32[]{:S(2)}, u32[]{:S(2)}) collective-permute-start(bf16[512,1024]{1,0:T(8,128)(2,1)} %collective-permute-done.30), channel_id=1, source_target_pairs={{0,4},{4,0},{1,5},{5,1},{2,6},{6,2},{3,7},{7,3},{8,12},{12,8},{9,1... | collective-permute-start | bytes 3145736 | tf_op jit(solution)/shard_map/ppermute | solution.py:18
  160.1 30.6 %collective-permute-start.33 = (bf16[256,1024]{1,0:T(8,128)(2,1)S(1)}, bf16[256,1024]{1,0:T(8,128)(2,1)S(1)}, u32[]{:S(2)}, u32[]{:S(2)}) collective-permute-start(bf16[256,1024]{1,0:T(8,128)(2,1)S(1)} %slice.2325), channel_id=1, source_target_pairs={{0,8},{8,0},{1,9},{9,1},{2,10},{10,2},{3,11},{11,3},{4,12},{12,4},... | collective-permute-start | bytes 1572872 | tf_op jit(solution)/shard_map/ppermute | solution.py:18
  162.9 28.0 %collective-permute-start.34 = (bf16[256,1024]{1,0:T(8,128)(2,1)S(1)}, bf16[256,1024]{1,0:T(8,128)(2,1)S(1)}, u32[]{:S(2)}, u32[]{:S(2)}) collective-permute-start(bf16[256,1024]{1,0:T(8,128)(2,1)S(1)} %pad_maximum_fusion.40), channel_id=1, source_target_pairs={{0,1},{1,0},{2,3},{3,2},{4,5},{5,4},{6,7},{7,6},{8,9},{9,8},{10,11... | collective-permute-start | bytes 1572872 | tf_op jit(solution)/shard_map/ppermute | solution.py:18
  204.9 58.6 %collective-permute-start.44 = (bf16[512,1024]{1,0:T(8,128)(2,1)S(1)}, bf16[512,1024]{1,0:T(8,128)(2,1)S(1)}, u32[]{:S(2)}, u32[]{:S(2)}) collective-permute-start(bf16[512,1024]{1,0:T(8,128)(2,1)S(1)} %collective-permute-done.36), channel_id=1, source_target_pairs={{0,4},{4,0},{1,5},{5,1},{2,6},{6,2},{3,7},{7,3},{8,12},{12,8},{9,1... | collective-permute-start | bytes 3145736 | tf_op jit(solution)/shard_map/ppermute | solution.py:18
  205.4 58.1 %collective-permute-start.45 = (bf16[512,1024]{1,0:T(8,128)(2,1)S(1)}, bf16[512,1024]{1,0:T(8,128)(2,1)S(1)}, u32[]{:S(2)}, u32[]{:S(2)}) collective-permute-start(bf16[512,1024]{1,0:T(8,128)(2,1)S(1)} %pad_maximum_fusion.20), channel_id=1, source_target_pairs={{0,16},{16,0},{1,17},{17,1},{2,18},{18,2},{3,19},{19,3},{4,20},{20... | collective-permute-start | bytes 3145736 | tf_op jit(solution)/shard_map/ppermute | solution.py:18
  212.9 20.8 %collective-permute-start.41 = (bf16[128,1024]{1,0:T(8,128)(2,1)S(1)}, bf16[128,1024]{1,0:T(8,128)(2,1)S(1)}, u32[]{:S(2)}, u32[]{:S(2)}) collective-permute-start(bf16[128,1024]{1,0:T(8,128)(2,1)S(1)} %get-tuple-element.659), channel_id=1, source_target_pairs={{0,8},{8,0},{1,9},{9,1},{2,10},{10,2},{3,11},{11,3},{4,12},{12,4},... | collective-permute-start | bytes 786440 | tf_op jit(solution)/shard_map/ppermute | solution.py:18
  233.7 29.9 %collective-permute-start.42 = (bf16[256,1024]{1,0:T(8,128)(2,1)S(1)}, bf16[256,1024]{1,0:T(8,128)(2,1)S(1)}, u32[]{:S(2)}, u32[]{:S(2)}) collective-permute-start(bf16[256,1024]{1,0:T(8,128)(2,1)S(1)} %pad_maximum_fusion.41), channel_id=1, source_target_pairs={{0,8},{8,0},{1,9},{9,1},{2,10},{10,2},{3,11},{11,3},{4,12},{12,4},... | collective-permute-start | bytes 1572872 | tf_op jit(solution)/shard_map/ppermute | solution.py:18
  236.3 27.3 %collective-permute-start.43 = (bf16[256,1024]{1,0:T(8,128)(2,1)S(1)}, bf16[256,1024]{1,0:T(8,128)(2,1)S(1)}, u32[]{:S(2)}, u32[]{:S(2)}) collective-permute-start(bf16[256,1024]{1,0:T(8,128)(2,1)S(1)} %pad_maximum_fusion.42), channel_id=1, source_target_pairs={{0,1},{1,0},{2,3},{3,2},{4,5},{5,4},{6,7},{7,6},{8,9},{9,8},{10,11... | collective-permute-start | bytes 1572872 | tf_op jit(solution)/shard_map/ppermute | solution.py:18
  237.8 25.9 %collective-permute-start.46 = (bf16[512,1024]{1,0:T(8,128)(2,1)S(1)}, bf16[512,1024]{1,0:T(8,128)(2,1)S(1)}, u32[]{:S(2)}, u32[]{:S(2)}) collective-permute-start(bf16[512,1024]{1,0:T(8,128)(2,1)S(1)} %pad_maximum_fusion.20), channel_id=1, source_target_pairs={{0,4},{4,0},{1,5},{5,1},{2,6},{6,2},{3,7},{7,3},{8,12},{12,8},{9,1... | collective-permute-start | bytes 3145736 | tf_op jit(solution)/shard_map/ppermute | solution.py:18
  264.5 25.1 %collective-permute-start.49 = (bf16[512,1024]{1,0:T(8,128)(2,1)S(1)}, bf16[512,1024]{1,0:T(8,128)(2,1)S(1)}, u32[]{:S(2)}, u32[]{:S(2)}) collective-permute-start(bf16[512,1024]{1,0:T(8,128)(2,1)S(1)} %collective-permute-done.45), channel_id=1, source_target_pairs={{0,4},{4,0},{1,5},{5,1},{2,6},{6,2},{3,7},{7,3},{8,12},{12,8},{9,1... | collective-permute-start | bytes 3145736 | tf_op jit(solution)/shard_map/ppermute | solution.py:18
  377.1 26.1 %collective-permute-start.63 = (bf16[512,1024]{1,0:T(8,128)(2,1)S(1)}, bf16[512,1024]{1,0:T(8,128)(2,1)S(1)}, u32[]{:S(2)}, u32[]{:S(2)}) collective-permute-start(bf16[512,1024]{1,0:T(8,128)(2,1)S(1)} %convolution_convert_fusion.5), channel_id=1, source_target_pairs={{0,4},{4,0},{1,5},{5,1},{2,6},{6,2},{3,7},{7,3},{8,12},{12,8},{9,1... | collective-permute-start | bytes 3145736 | tf_op jit(solution)/shard_map/ppermute | solution.py:18
  378.7 57.8 %collective-permute-start.67 = (bf16[512,1024]{1,0:T(8,128)(2,1)}, bf16[512,1024]{1,0:T(8,128)(2,1)}, u32[]{:S(2)}, u32[]{:S(2)}) collective-permute-start(bf16[512,1024]{1,0:T(8,128)(2,1)} %convolution_convert_fusion.4), channel_id=1, source_target_pairs={{0,4},{4,0},{1,5},{5,1},{2,6},{6,2},{3,7},{7,3},{8,12},{12,8},{9,1... | collective-permute-start | bytes 3145736 | tf_op jit(solution)/shard_map/ppermute | solution.py:18
  405.7 61.9 %collective-permute-start.70 = (bf16[512,1024]{1,0:T(8,128)(2,1)}, bf16[512,1024]{1,0:T(8,128)(2,1)}, u32[]{:S(2)}, u32[]{:S(2)}) collective-permute-start(bf16[512,1024]{1,0:T(8,128)(2,1)} %convolution_convert_fusion.3), channel_id=1, source_target_pairs={{0,4},{4,0},{1,5},{5,1},{2,6},{6,2},{3,7},{7,3},{8,12},{12,8},{9,1... | collective-permute-start | bytes 3145736 | tf_op jit(solution)/shard_map/ppermute | solution.py:18
  407.3 60.4 %collective-permute-start.71 = (bf16[512,1024]{1,0:T(8,128)(2,1)}, bf16[512,1024]{1,0:T(8,128)(2,1)}, u32[]{:S(2)}, u32[]{:S(2)}) collective-permute-start(bf16[512,1024]{1,0:T(8,128)(2,1)} %add_convert_fusion.6), channel_id=1, source_target_pairs={{0,16},{16,0},{1,17},{17,1},{2,18},{18,2},{3,19},{19,3},{4,20},{20... | collective-permute-start | bytes 3145736 | tf_op jit(solution)/shard_map/ppermute | solution.py:18
  433.2 34.0 %collective-permute-start.68 = (bf16[256,1024]{1,0:T(8,128)(2,1)S(1)}, bf16[256,1024]{1,0:T(8,128)(2,1)S(1)}, u32[]{:S(2)}, u32[]{:S(2)}) collective-permute-start(bf16[256,1024]{1,0:T(8,128)(2,1)S(1)} %slice.2323), channel_id=1, source_target_pairs={{0,8},{8,0},{1,9},{9,1},{2,10},{10,2},{3,11},{11,3},{4,12},{12,4},... | collective-permute-start | bytes 1572872 | tf_op jit(solution)/shard_map/ppermute | solution.py:18
  436.5 30.9 %collective-permute-start.69 = (bf16[256,1024]{1,0:T(8,128)(2,1)S(1)}, bf16[256,1024]{1,0:T(8,128)(2,1)S(1)}, u32[]{:S(2)}, u32[]{:S(2)}) collective-permute-start(bf16[256,1024]{1,0:T(8,128)(2,1)S(1)} %pad_maximum_fusion.46), channel_id=1, source_target_pairs={{0,1},{1,0},{2,3},{3,2},{4,5},{5,4},{6,7},{7,6},{8,9},{9,8},{10,11... | collective-permute-start | bytes 1572872 | tf_op jit(solution)/shard_map/ppermute | solution.py:18
  438.1 72.3 %collective-permute-start.76 = (bf16[512,1024]{1,0:T(8,128)(2,1)S(1)}, bf16[512,1024]{1,0:T(8,128)(2,1)S(1)}, u32[]{:S(2)}, u32[]{:S(2)}) collective-permute-start(bf16[512,1024]{1,0:T(8,128)(2,1)S(1)} %copy-done.122), channel_id=1, source_target_pairs={{0,4},{4,0},{1,5},{5,1},{2,6},{6,2},{3,7},{7,3},{8,12},{12,8},{9,1... | collective-permute-start | bytes 3145736 | tf_op jit(solution)/shard_map/ppermute | solution.py:18
  476.1 59.8 %collective-permute-start.79 = (bf16[512,1024]{1,0:T(8,128)(2,1)S(1)}, bf16[512,1024]{1,0:T(8,128)(2,1)S(1)}, u32[]{:S(2)}, u32[]{:S(2)}) collective-permute-start(bf16[512,1024]{1,0:T(8,128)(2,1)S(1)} %copy-done.121), channel_id=1, source_target_pairs={{0,4},{4,0},{1,5},{5,1},{2,6},{6,2},{3,7},{7,3},{8,12},{12,8},{9,1... | collective-permute-start | bytes 3145736 | tf_op jit(solution)/shard_map/ppermute | solution.py:18
  476.6 59.3 %collective-permute-start.80 = (bf16[512,1024]{1,0:T(8,128)(2,1)S(1)}, bf16[512,1024]{1,0:T(8,128)(2,1)S(1)}, u32[]{:S(2)}, u32[]{:S(2)}) collective-permute-start(bf16[512,1024]{1,0:T(8,128)(2,1)S(1)} %add_convert_fusion.3), channel_id=1, source_target_pairs={{0,16},{16,0},{1,17},{17,1},{2,18},{18,2},{3,19},{19,3},{4,20},{20... | collective-permute-start | bytes 3145736 | tf_op jit(solution)/shard_map/ppermute | solution.py:18
  485.0 22.1 %collective-permute-start.75 = (bf16[128,1024]{1,0:T(8,128)(2,1)S(1)}, bf16[128,1024]{1,0:T(8,128)(2,1)S(1)}, u32[]{:S(2)}, u32[]{:S(2)}) collective-permute-start(bf16[128,1024]{1,0:T(8,128)(2,1)S(1)} %get-tuple-element.800), channel_id=1, source_target_pairs={{0,8},{8,0},{1,9},{9,1},{2,10},{10,2},{3,11},{11,3},{4,12},{12,4},... | collective-permute-start | bytes 786440 | tf_op jit(solution)/shard_map/ppermute | solution.py:18
  507.2 28.7 %collective-permute-start.77 = (bf16[256,1024]{1,0:T(8,128)(2,1)S(1)}, bf16[256,1024]{1,0:T(8,128)(2,1)S(1)}, u32[]{:S(2)}, u32[]{:S(2)}) collective-permute-start(bf16[256,1024]{1,0:T(8,128)(2,1)S(1)} %pad_maximum_fusion.47), channel_id=1, source_target_pairs={{0,8},{8,0},{1,9},{9,1},{2,10},{10,2},{3,11},{11,3},{4,12},{12,4},... | collective-permute-start | bytes 1572872 | tf_op jit(solution)/shard_map/ppermute | solution.py:18
  509.7 26.2 %collective-permute-start.78 = (bf16[256,1024]{1,0:T(8,128)(2,1)S(1)}, bf16[256,1024]{1,0:T(8,128)(2,1)S(1)}, u32[]{:S(2)}, u32[]{:S(2)}) collective-permute-start(bf16[256,1024]{1,0:T(8,128)(2,1)S(1)} %pad_maximum_fusion.48), channel_id=1, source_target_pairs={{0,1},{1,0},{2,3},{3,2},{4,5},{5,4},{6,7},{7,6},{8,9},{9,8},{10,11... | collective-permute-start | bytes 1572872 | tf_op jit(solution)/shard_map/ppermute | solution.py:18
  540.9 31.2 %collective-permute-start.83 = (bf16[512,1024]{1,0:T(8,128)(2,1)}, bf16[512,1024]{1,0:T(8,128)(2,1)}, u32[]{:S(2)}, u32[]{:S(2)}) collective-permute-start(bf16[512,1024]{1,0:T(8,128)(2,1)} %convolution_convert_fusion), channel_id=1, source_target_pairs={{0,4},{4,0},{1,5},{5,1},{2,6},{6,2},{3,7},{7,3},{8,12},{12,8},{9,1... | collective-permute-start | bytes 3145736 | tf_op jit(solution)/shard_map/ppermute | solution.py:18
  542.4 52.6 %collective-permute-start.87 = (bf16[256,1024]{1,0:T(8,128)(2,1)}, bf16[256,1024]{1,0:T(8,128)(2,1)}, u32[]{:S(2)}, u32[]{:S(2)}) collective-permute-start(bf16[256,1024]{1,0:T(8,128)(2,1)} %select_convert_fusion.5), channel_id=1, source_target_pairs={{0,8},{8,0},{1,9},{9,1},{2,10},{10,2},{3,11},{11,3},{4,12},{12,4},... | collective-permute-start | bytes 1572872 | tf_op jit(solution)/shard_map/ppermute | solution.py:18
  542.4 48.5 %collective-permute-start.85 = (bf16[512,1024]{1,0:T(8,128)(2,1)}, bf16[512,1024]{1,0:T(8,128)(2,1)}, u32[]{:S(2)}, u32[]{:S(2)}) collective-permute-start(bf16[512,1024]{1,0:T(8,128)(2,1)} %add_convert_fusion.2), channel_id=1, source_target_pairs={{0,16},{16,0},{1,17},{17,1},{2,18},{18,2},{3,19},{19,3},{4,20},{20... | collective-permute-start | bytes 3145736 | tf_op jit(solution)/shard_map/ppermute | solution.py:18
  545.4 71.7 %collective-permute-start.92 = (bf16[256,1024]{1,0:T(8,128)(2,1)}, bf16[256,1024]{1,0:T(8,128)(2,1)}, u32[]{:S(2)}, u32[]{:S(2)}) collective-permute-start(bf16[256,1024]{1,0:T(8,128)(2,1)} %select_convert_fusion.4), channel_id=1, source_target_pairs={{0,8},{8,0},{1,9},{9,1},{2,10},{10,2},{3,11},{11,3},{4,12},{12,4},... | collective-permute-start | bytes 1572872 | tf_op jit(solution)/shard_map/ppermute | solution.py:18
  605.8 26.5 %collective-permute-start.96 = (bf16[512,512]{0,1:T(8,128)(2,1)S(1)}, bf16[512,512]{0,1:T(8,128)(2,1)S(1)}, u32[]{:S(2)}, u32[]{:S(2)}) collective-permute-start(bf16[512,512]{0,1:T(8,128)(2,1)S(1)} %fusion.28), channel_id=1, source_target_pairs={{0,16},{16,0},{1,17},{17,1},{2,18},{18,2},{3,19},{19,3},{4,20},{20... | collective-permute-start | bytes 1572872 | tf_op jit(solution)/shard_map/ppermute | solution.py:18
  607.9 73.8 %collective-permute-start.107 = (bf16[256,1024]{1,0:T(8,128)(2,1)S(1)}, bf16[256,1024]{1,0:T(8,128)(2,1)S(1)}, u32[]{:S(2)}, u32[]{:S(2)}) collective-permute-start(bf16[256,1024]{1,0:T(8,128)(2,1)S(1)} %select_convert_fusion.2), channel_id=1, source_target_pairs={{0,8},{8,0},{1,9},{9,1},{2,10},{10,2},{3,11},{11,3},{4,12},{12,4},... | collective-permute-start | bytes 1572872 | tf_op jit(solution)/shard_map/ppermute | solution.py:18
  625.5 44.3 %collective-permute-start.102 = (f32[4,512]{1,0:T(4,128)S(1)}, f32[4,512]{1,0:T(4,128)S(1)}, u32[]{:S(2)}, u32[]{:S(2)}) collective-permute-start(f32[4,512]{1,0:T(4,128)S(1)} %slice.1254), channel_id=1, source_target_pairs={{0,16},{16,0},{1,17},{17,1},{2,18},{18,2},{3,19},{19,3},{4,20},{20... | collective-permute-start | bytes 24584 | tf_op jit(solution)/shard_map/ppermute | solution.py:18
  643.5 26.0 %collective-permute-start.101 = (bf16[512,512]{0,1:T(8,128)(2,1)S(1)}, bf16[512,512]{0,1:T(8,128)(2,1)S(1)}, u32[]{:S(2)}, u32[]{:S(2)}) collective-permute-start(bf16[512,512]{0,1:T(8,128)(2,1)S(1)} %fusion.29), channel_id=1, source_target_pairs={{0,16},{16,0},{1,17},{17,1},{2,18},{18,2},{3,19},{19,3},{4,20},{20... | collective-permute-start | bytes 1572872 | tf_op jit(solution)/shard_map/ppermute | solution.py:18
  646.3 36.1 %collective-permute-start.108 = (bf16[128,2048]{1,0:T(8,128)(2,1)S(1)}, bf16[128,2048]{1,0:T(8,128)(2,1)S(1)}, u32[]{:S(2)}, u32[]{:S(2)}) collective-permute-start(bf16[128,2048]{1,0:T(8,128)(2,1)S(1)} %select_convert_fusion.1), channel_id=1, source_target_pairs={{0,2},{2,0},{1,3},{3,1},{4,6},{6,4},{5,7},{7,5},{8,10},{10,8},{9,1... | collective-permute-start | bytes 1572872 | tf_op jit(solution)/shard_map/ppermute | solution.py:18
  646.5 33.5 %collective-permute-start.105 = (bf16[512,512]{0,1:T(8,128)(2,1)S(1)}, bf16[512,512]{0,1:T(8,128)(2,1)S(1)}, u32[]{:S(2)}, u32[]{:S(2)}) collective-permute-start(bf16[512,512]{0,1:T(8,128)(2,1)S(1)} %pad_maximum_fusion.52), channel_id=1, source_target_pairs={{0,4},{4,0},{1,5},{5,1},{2,6},{6,2},{3,7},{7,3},{8,12},{12,8},{9,1... | collective-permute-start | bytes 1572872 | tf_op jit(solution)/shard_map/ppermute | solution.py:18
  (256 other events, 2858.7 us)

commit v9 on v8

--- a/solution.py
+++ b/solution.py
@@ -439,7 +439,7 @@
         sigma = jax.nn.sigmoid(gate)
         wu0, wu1 = up_w.rows(0), up_w.rows(1)
         up = dot(h0, wu0) + dot(h1, wu1)
-        act = (gate * sigma * up).astype(BF)
+        act = c.sync((gate * sigma * up).astype(BF))
 
         wd0 = down_w.rows(0)
         down_w.end_x(1)
@@ -633,10 +633,8 @@
             qk_grad.start_x(0)
 
         def tokens_second():
-            qk_grad.end_x(0)
-            qk_grad.end_high()
-            qk_grad.start_line()
             gain_steps()
+            up_grad.end_line()
 
         d_tokens = columns(
             scatter_rows(
@@ -647,11 +645,13 @@
             )
         )
         grad_tokens = to_natural(d_resid + d_tokens)
+        qk_grad.end_x(0)
+        qk_grad.end_high()
+        qk_grad.start_line()
         ov_grad.end_x(0)
         ov_grad.end_high()
         ov_grad.start_line()
         gain_steps()
-        up_grad.end_line()
         gate_grad.end()
         gain_steps()
         qk_grad.end_line()

time: 710 us -> 688 us (0.969)
  waiting for transfers between devices: 325 us -> 304 us
    ppermute x116, waiting for transfers between devices: 325 us -> 304 us  [swap(): return lax.ppermute(value, axis, FLIP)]
    unnamed x425 -> x421, local copies, waits for them, and re-layouts: 27 us -> 26.2 us
  transfers between devices with their start and end apart: 116 -> 116, of which waited for: 49 -> 49; matrix products, arithmetic and copies ran while one was open for 28% -> 31% of each run, Pallas kernels for 0% -> 0%
where the time goes in v9:
time: 688 us; the launch traced here: 681 us
  waiting for transfers between devices  304 us (44%)
  matrix products  127 us (18%)
  starting transfers between devices  117 us (17%)
  other arithmetic  69.2 us (10%)
  local copies, waits for them, and re-layouts  57.8 us (8%)
    ppermute x116, waiting for transfers between devices, swap(): return lax.ppermute(value, axis, FLIP)  304 us
    ppermute x116, starting transfers between devices, swap(): return lax.ppermute(value, axis, FLIP)  117 us
    dot_general x28, matrix products, dot_tn(): return jnp.einsum('sr,sc->rc', a, b, preferred_element_type=F32)  45.3 us
    dot_general x24, matrix products, dot_nt(): return jnp.einsum('sc,rc->sr', a, b, preferred_element_type=F32)  35.8 us
    dot_general x12, matrix products, dot(): return jnp.dot(a, b, preferred_element_type=F32)  32.4 us
    unnamed x421, local copies, waits for them, and re-layouts  26.2 us
  transfers between devices with their start and end apart: 116, of which 49 were waited for; matrix products, arithmetic and copies ran while one was open for 31% of the time, Pallas kernels for 0%

profile of v9, /device:TPU:0, one launch (start us, length us, event | category | flops | bytes accessed | tf_op | source)
XLA Modules:
  0.0 680.5 jit_solution(11139143429260094350)
XLA Ops:
  6.0 3.1 collective-permute-start
  22.6 4.4 collective-permute-done.3
  41.6 6.0 collective-permute-done.9
  52.4 7.9 %collective-permute-done.12 = bf16[512,512]{0,1:T(8,128)(2,1)S(1)} collective-permute-done((bf16[512,512]{0,1:T(8,128)(2,1)S(1)}, bf16[512,512]{0,1:T(8,128)(2,1)S(1)}, u32[]{:S(2)}, u32[]{:S(2)}) %collective-permute-start.12) | collective-permute-done | bytes 524320 | tf_op jit(solution)/shard_map/ppermute | solution.py:18
  60.4 3.1 collective-permute-done.13
  78.7 8.7 %collective-permute-done.18 = bf16[256,1024]{1,0:T(8,128)(2,1)S(1)} collective-permute-done((bf16[256,1024]{1,0:T(8,128)(2,1)}, bf16[256,1024]{1,0:T(8,128)(2,1)S(1)}, u32[]{:S(2)}, u32[]{:S(2)}) %collective-permute-start.18) | collective-permute-done | bytes 524320 | tf_op jit(solution)/shard_map/ppermute | solution.py:18
  87.4 2.9 pad_maximum_fusion
  104.8 3.0 collective-permute-start.30
  110.7 6.8 collective-permute-done.26
  127.4 3.4 fusion.213
  132.8 2.9 fusion.4
  141.8 9.2 %collective-permute-done.29 = bf16[256,1024]{1,0:T(8,128)(2,1)} collective-permute-done((bf16[256,1024]{1,0:T(8,128)(2,1)}, bf16[256,1024]{1,0:T(8,128)(2,1)}, u32[]{:S(2)}, u32[]{:S(2)}) %collective-permute-start.29) | collective-permute-done | bytes 524320 | tf_op jit(solution)/shard_map/ppermute | solution.py:18
  151.0 3.2 collective-permute-done.30
  164.6 26.1 %collective-permute-done.33 = bf16[256,1024]{1,0:T(8,128)(2,1)S(1)} collective-permute-done((bf16[256,1024]{1,0:T(8,128)(2,1)S(1)}, bf16[256,1024]{1,0:T(8,128)(2,1)S(1)}, u32[]{:S(2)}, u32[]{:S(2)}) %collective-permute-start.33) | collective-permute-done | bytes 524320 | tf_op jit(solution)/shard_map/ppermute | solution.py:18
  195.3 9.6 %collective-permute-done.36 = bf16[512,1024]{1,0:T(8,128)(2,1)S(1)} collective-permute-done((bf16[512,1024]{1,0:T(8,128)(2,1)S(1)}, bf16[512,1024]{1,0:T(8,128)(2,1)S(1)}, u32[]{:S(2)}, u32[]{:S(2)}) %collective-permute-start.36) | collective-permute-done | bytes 1048608 | tf_op jit(solution)/shard_map/ppermute | solution.py:18
  205.5 5.0 collective-permute-done.39
  212.9 6.7 collective-permute-done.40
  219.6 14.0 %collective-permute-done.41 = bf16[128,1024]{1,0:T(8,128)(2,1)S(1)} collective-permute-done((bf16[128,1024]{1,0:T(8,128)(2,1)S(1)}, bf16[128,1024]{1,0:T(8,128)(2,1)S(1)}, u32[]{:S(2)}, u32[]{:S(2)}) %collective-permute-start.41) | collective-permute-done | bytes 262176 | tf_op jit(solution)/shard_map/ppermute | solution.py:18
  239.3 24.2 %collective-permute-done.42 = bf16[256,1024]{1,0:T(8,128)(2,1)S(1)} collective-permute-done((bf16[256,1024]{1,0:T(8,128)(2,1)S(1)}, bf16[256,1024]{1,0:T(8,128)(2,1)S(1)}, u32[]{:S(2)}, u32[]{:S(2)}) %collective-permute-start.42) | collective-permute-done | bytes 524320 | tf_op jit(solution)/shard_map/ppermute | solution.py:18
  272.8 3.6 fusion.190
  276.5 5.4 multiply_convert_fusion.2
  281.9 9.2 %collective-permute-done.49 = bf16[512,1024]{1,0:T(8,128)(2,1)S(1)} collective-permute-done((bf16[512,1024]{1,0:T(8,128)(2,1)S(1)}, bf16[512,1024]{1,0:T(8,128)(2,1)S(1)}, u32[]{:S(2)}, u32[]{:S(2)}) %collective-permute-start.49) | collective-permute-done | bytes 1048608 | tf_op jit(solution)/shard_map/ppermute | solution.py:18
  299.9 12.5 %collective-permute-done.52 = bf16[256,1024]{1,0:T(8,128)(2,1)S(1)} collective-permute-done((bf16[256,1024]{1,0:T(8,128)(2,1)S(1)}, bf16[256,1024]{1,0:T(8,128)(2,1)S(1)}, u32[]{:S(2)}, u32[]{:S(2)}) %collective-permute-start.52) | collective-permute-done | bytes 524320 | tf_op jit(solution)/shard_map/ppermute | solution.py:18
  316.2 4.2 collective-permute-done.54
  325.6 4.6 collective-permute-done.56
  334.1 7.7 %collective-permute-done.58 = bf16[256,1024]{1,0:T(8,128)(2,1)S(1)} collective-permute-done((bf16[256,1024]{1,0:T(8,128)(2,1)S(1)}, bf16[256,1024]{1,0:T(8,128)(2,1)S(1)}, u32[]{:S(2)}, u32[]{:S(2)}) %collective-permute-start.58) | collective-permute-done | bytes 524320 | tf_op jit(solution)/shard_map/ppermute | solution.py:18
  351.1 3.0 constant_dynamic-update-slice_fusion.60
  354.1 3.5 convolution_convert_fusion.4
  361.7 2.9 fusion.20
  366.7 3.9 fusion.223
  370.7 5.6 multiply_convert_fusion
  396.7 4.3 fusion.60
  407.0 4.0 add_convert_fusion.5
  411.5 3.0 fusion.58
  426.2 28.6 %collective-permute-done.68 = bf16[256,1024]{1,0:T(8,128)(2,1)S(1)} collective-permute-done((bf16[256,1024]{1,0:T(8,128)(2,1)S(1)}, bf16[256,1024]{1,0:T(8,128)(2,1)S(1)}, u32[]{:S(2)}, u32[]{:S(2)}) %collective-permute-start.68) | collective-permute-done | bytes 524320 | tf_op jit(solution)/shard_map/ppermute | solution.py:18
  464.2 3.0 collective-permute-start.80
  467.4 3.2 collective-permute-done.73
  472.6 5.7 collective-permute-done.74
  478.3 16.2 %collective-permute-done.75 = bf16[128,1024]{1,0:T(8,128)(2,1)S(1)} collective-permute-done((bf16[128,1024]{1,0:T(8,128)(2,1)S(1)}, bf16[128,1024]{1,0:T(8,128)(2,1)S(1)}, u32[]{:S(2)}, u32[]{:S(2)}) %collective-permute-start.75) | collective-permute-done | bytes 262176 | tf_op jit(solution)/shard_map/ppermute | solution.py:18
  497.9 25.5 %collective-permute-done.77 = bf16[256,1024]{1,0:T(8,128)(2,1)S(1)} collective-permute-done((bf16[256,1024]{1,0:T(8,128)(2,1)S(1)}, bf16[256,1024]{1,0:T(8,128)(2,1)S(1)}, u32[]{:S(2)}, u32[]{:S(2)}) %collective-permute-start.77) | collective-permute-done | bytes 524320 | tf_op jit(solution)/shard_map/ppermute | solution.py:18
  530.0 2.9 collective-permute-start.85
  541.9 3.1 fusion.5
  623.2 7.8 %collective-permute-done.98 = bf16[256,1024]{1,0:T(8,128)(2,1)S(1)} collective-permute-done((bf16[256,1024]{1,0:T(8,128)(2,1)S(1)}, bf16[256,1024]{1,0:T(8,128)(2,1)S(1)}, u32[]{:S(2)}, u32[]{:S(2)}) %collective-permute-start.98) | collective-permute-done | bytes 524320 | tf_op jit(solution)/shard_map/ppermute | solution.py:18
  637.4 4.7 collective-permute-done.102
  642.3 7.3 %collective-permute-done.103 = bf16[128,1024]{1,0:T(8,128)(2,1)S(1)} collective-permute-done((bf16[128,1024]{1,0:T(8,128)(2,1)S(1)}, bf16[128,1024]{1,0:T(8,128)(2,1)S(1)}, u32[]{:S(2)}, u32[]{:S(2)}) %collective-permute-start.103) | collective-permute-done | bytes 262176 | tf_op jit(solution)/shard_map/ppermute | solution.py:18
  652.1 5.0 collective-permute-done.105
  663.4 3.9 collective-permute-done.110
  667.6 4.8 collective-permute-done.111
  (960 shorter events, 325.3 us)
Async XLA Ops:
  10.0 19.2 %collective-permute-start.5 = (bf16[128,1024]{1,0:T(8,128)(2,1)}, bf16[128,1024]{1,0:T(8,128)(2,1)}, u32[]{:S(2)}, u32[]{:S(2)}) collective-permute-start(bf16[128,1024]{1,0:T(8,128)(2,1)} %pad_maximum_fusion.58), channel_id=1, source_target_pairs={{0,1},{1,0},{2,3},{3,2},{4,5},{5,4},{6,7},{7,6},{8,9},{9,8},{10,11... | collective-permute-start | bytes 786440 | tf_op jit(solution)/shard_map/ppermute | solution.py:18
  17.9 21.5 %collective-permute-start.8 = (bf16[128,6144]{1,0:T(8,128)(2,1)S(1)}, bf16[128,6144]{1,0:T(8,128)(2,1)S(1)}, u32[]{:S(2)}, u32[]{:S(2)}) collective-permute-start(bf16[128,6144]{1,0:T(8,128)(2,1)S(1)} %copy-done.109), channel_id=1, source_target_pairs={{0,2},{2,0},{1,3},{3,1},{4,6},{6,4},{5,7},{7,5},{8,10},{10,8},{9,1... | collective-permute-start | bytes 4718600 | tf_op jit(solution)/shard_map/ppermute | solution.py:18
  30.1 20.6 %collective-permute-start.10 = (f32[4,512]{1,0:T(4,128)S(1)}, f32[4,512]{1,0:T(4,128)S(1)}, u32[]{:S(2)}, u32[]{:S(2)}) collective-permute-start(f32[4,512]{1,0:T(4,128)S(1)} %pad_maximum_fusion.76), channel_id=1, source_target_pairs={{0,16},{16,0},{1,17},{17,1},{2,18},{18,2},{3,19},{19,3},{4,20},{20... | collective-permute-start | bytes 24584 | tf_op jit(solution)/shard_map/ppermute | solution.py:18
  32.9 18.4 %collective-permute-start.11 = (bf16[512,512]{0,1:T(8,128)(2,1)S(1)}, bf16[512,512]{0,1:T(8,128)(2,1)S(1)}, u32[]{:S(2)}, u32[]{:S(2)}) collective-permute-start(bf16[512,512]{0,1:T(8,128)(2,1)S(1)} %pad_maximum_fusion.36), channel_id=1, source_target_pairs={{0,4},{4,0},{1,5},{5,1},{2,6},{6,2},{3,7},{7,3},{8,12},{12,8},{9,1... | collective-permute-start | bytes 1572872 | tf_op jit(solution)/shard_map/ppermute | solution.py:18
  36.8 23.6 %collective-permute-start.12 = (bf16[512,512]{0,1:T(8,128)(2,1)S(1)}, bf16[512,512]{0,1:T(8,128)(2,1)S(1)}, u32[]{:S(2)}, u32[]{:S(2)}) collective-permute-start(bf16[512,512]{0,1:T(8,128)(2,1)S(1)} %pad_maximum_fusion.36), channel_id=1, source_target_pairs={{0,16},{16,0},{1,17},{17,1},{2,18},{18,2},{3,19},{19,3},{4,20},{20... | collective-permute-start | bytes 1572872 | tf_op jit(solution)/shard_map/ppermute | solution.py:18
  39.8 23.7 %collective-permute-start.13 = (bf16[256,1024]{1,0:T(8,128)(2,1)S(1)}, bf16[256,1024]{1,0:T(8,128)(2,1)S(1)}, u32[]{:S(2)}, u32[]{:S(2)}) collective-permute-start(bf16[256,1024]{1,0:T(8,128)(2,1)S(1)} %pad_maximum_fusion.37), channel_id=1, source_target_pairs={{0,8},{8,0},{1,9},{9,1},{2,10},{10,2},{3,11},{11,3},{4,12},{12,4},... | collective-permute-start | bytes 1572872 | tf_op jit(solution)/shard_map/ppermute | solution.py:18
  67.6 19.8 %collective-permute-start.18 = (bf16[256,1024]{1,0:T(8,128)(2,1)}, bf16[256,1024]{1,0:T(8,128)(2,1)S(1)}, u32[]{:S(2)}, u32[]{:S(2)}) collective-permute-start(bf16[256,1024]{1,0:T(8,128)(2,1)} %broadcast_select_fusion.11), channel_id=1, source_target_pairs={{0,8},{8,0},{1,9},{9,1},{2,10},{10,2},{3,11},{11,3},{4,12},{12,4},... | collective-permute-start | bytes 1572872 | tf_op jit(solution)/shard_map/ppermute | solution.py:18
  74.7 26.1 %collective-permute-start.22 = (bf16[512,512]{0,1:T(8,128)(2,1)S(1)}, bf16[512,512]{0,1:T(8,128)(2,1)S(1)}, u32[]{:S(2)}, u32[]{:S(2)}) collective-permute-start(bf16[512,512]{0,1:T(8,128)(2,1)S(1)} %copy-done.132), channel_id=1, source_target_pairs={{0,16},{16,0},{1,17},{17,1},{2,18},{18,2},{3,19},{19,3},{4,20},{20... | collective-permute-start | bytes 1572872 | tf_op jit(solution)/shard_map/ppermute | solution.py:18
  77.2 23.5 %collective-permute-start.23 = (bf16[512,512]{0,1:T(8,128)(2,1)S(1)}, bf16[512,512]{0,1:T(8,128)(2,1)S(1)}, u32[]{:S(2)}, u32[]{:S(2)}) collective-permute-start(bf16[512,512]{0,1:T(8,128)(2,1)S(1)} %copy-done.132), channel_id=1, source_target_pairs={{0,4},{4,0},{1,5},{5,1},{2,6},{6,2},{3,7},{7,3},{8,12},{12,8},{9,1... | collective-permute-start | bytes 1572872 | tf_op jit(solution)/shard_map/ppermute | solution.py:18
  104.7 34.3 %collective-permute-start.27 = (bf16[256,1024]{1,0:T(8,128)(2,1)}, bf16[256,1024]{1,0:T(8,128)(2,1)}, u32[]{:S(2)}, u32[]{:S(2)}) collective-permute-start(bf16[256,1024]{1,0:T(8,128)(2,1)} %broadcast_select_fusion.7), channel_id=1, source_target_pairs={{0,8},{8,0},{1,9},{9,1},{2,10},{10,2},{3,11},{11,3},{4,12},{12,4},... | collective-permute-start | bytes 1572872 | tf_op jit(solution)/shard_map/ppermute | solution.py:18
  104.8 49.4 %collective-permute-start.30 = (bf16[512,1024]{1,0:T(8,128)(2,1)}, bf16[512,1024]{1,0:T(8,128)(2,1)}, u32[]{:S(2)}, u32[]{:S(2)}) collective-permute-start(bf16[512,1024]{1,0:T(8,128)(2,1)} %pad_maximum_fusion.17), channel_id=1, source_target_pairs={{0,16},{16,0},{1,17},{17,1},{2,18},{18,2},{3,19},{19,3},{4,20},{20... | collective-permute-start | bytes 3145736 | tf_op jit(solution)/shard_map/ppermute | solution.py:18
  107.8 34.0 %collective-permute-start.28 = (bf16[512,1024]{1,0:T(8,128)(2,1)}, bf16[512,1024]{1,0:T(8,128)(2,1)}, u32[]{:S(2)}, u32[]{:S(2)}) collective-permute-start(bf16[512,1024]{1,0:T(8,128)(2,1)} %pad_maximum_fusion.17), channel_id=1, source_target_pairs={{0,4},{4,0},{1,5},{5,1},{2,6},{6,2},{3,7},{7,3},{8,12},{12,8},{9,1... | collective-permute-start | bytes 3145736 | tf_op jit(solution)/shard_map/ppermute | solution.py:18
  109.3 41.7 %collective-permute-start.29 = (bf16[256,1024]{1,0:T(8,128)(2,1)}, bf16[256,1024]{1,0:T(8,128)(2,1)}, u32[]{:S(2)}, u32[]{:S(2)}) collective-permute-start(bf16[256,1024]{1,0:T(8,128)(2,1)} %broadcast_select_fusion.6), channel_id=1, source_target_pairs={{0,8},{8,0},{1,9},{9,1},{2,10},{10,2},{3,11},{11,3},{4,12},{12,4},... | collective-permute-start | bytes 1572872 | tf_op jit(solution)/shard_map/ppermute | solution.py:18
  155.2 40.0 %collective-permute-start.35 = (bf16[512,1024]{1,0:T(8,128)(2,1)S(1)}, bf16[512,1024]{1,0:T(8,128)(2,1)S(1)}, u32[]{:S(2)}, u32[]{:S(2)}) collective-permute-start(bf16[512,1024]{1,0:T(8,128)(2,1)S(1)} %pad_maximum_fusion.19), channel_id=1, source_target_pairs={{0,4},{4,0},{1,5},{5,1},{2,6},{6,2},{3,7},{7,3},{8,12},{12,8},{9,1... | collective-permute-start | bytes 3145736 | tf_op jit(solution)/shard_map/ppermute | solution.py:18
  156.8 48.1 %collective-permute-start.36 = (bf16[512,1024]{1,0:T(8,128)(2,1)S(1)}, bf16[512,1024]{1,0:T(8,128)(2,1)S(1)}, u32[]{:S(2)}, u32[]{:S(2)}) collective-permute-start(bf16[512,1024]{1,0:T(8,128)(2,1)S(1)} %pad_maximum_fusion.19), channel_id=1, source_target_pairs={{0,16},{16,0},{1,17},{17,1},{2,18},{18,2},{3,19},{19,3},{4,20},{20... | collective-permute-start | bytes 3145736 | tf_op jit(solution)/shard_map/ppermute | solution.py:18
  157.1 47.8 %collective-permute-start.37 = (bf16[512,1024]{1,0:T(8,128)(2,1)}, bf16[512,1024]{1,0:T(8,128)(2,1)S(1)}, u32[]{:S(2)}, u32[]{:S(2)}) collective-permute-start(bf16[512,1024]{1,0:T(8,128)(2,1)} %collective-permute-done.30), channel_id=1, source_target_pairs={{0,4},{4,0},{1,5},{5,1},{2,6},{6,2},{3,7},{7,3},{8,12},{12,8},{9,1... | collective-permute-start | bytes 3145736 | tf_op jit(solution)/shard_map/ppermute | solution.py:18
  160.0 30.6 %collective-permute-start.33 = (bf16[256,1024]{1,0:T(8,128)(2,1)S(1)}, bf16[256,1024]{1,0:T(8,128)(2,1)S(1)}, u32[]{:S(2)}, u32[]{:S(2)}) collective-permute-start(bf16[256,1024]{1,0:T(8,128)(2,1)S(1)} %slice.2323), channel_id=1, source_target_pairs={{0,8},{8,0},{1,9},{9,1},{2,10},{10,2},{3,11},{11,3},{4,12},{12,4},... | collective-permute-start | bytes 1572872 | tf_op jit(solution)/shard_map/ppermute | solution.py:18
  162.9 28.0 %collective-permute-start.34 = (bf16[256,1024]{1,0:T(8,128)(2,1)S(1)}, bf16[256,1024]{1,0:T(8,128)(2,1)S(1)}, u32[]{:S(2)}, u32[]{:S(2)}) collective-permute-start(bf16[256,1024]{1,0:T(8,128)(2,1)S(1)} %pad_maximum_fusion.40), channel_id=1, source_target_pairs={{0,1},{1,0},{2,3},{3,2},{4,5},{5,4},{6,7},{7,6},{8,9},{9,8},{10,11... | collective-permute-start | bytes 1572872 | tf_op jit(solution)/shard_map/ppermute | solution.py:18
  204.9 58.6 %collective-permute-start.44 = (bf16[512,1024]{1,0:T(8,128)(2,1)S(1)}, bf16[512,1024]{1,0:T(8,128)(2,1)S(1)}, u32[]{:S(2)}, u32[]{:S(2)}) collective-permute-start(bf16[512,1024]{1,0:T(8,128)(2,1)S(1)} %collective-permute-done.36), channel_id=1, source_target_pairs={{0,4},{4,0},{1,5},{5,1},{2,6},{6,2},{3,7},{7,3},{8,12},{12,8},{9,1... | collective-permute-start | bytes 3145736 | tf_op jit(solution)/shard_map/ppermute | solution.py:18
  205.4 58.1 %collective-permute-start.45 = (bf16[512,1024]{1,0:T(8,128)(2,1)S(1)}, bf16[512,1024]{1,0:T(8,128)(2,1)S(1)}, u32[]{:S(2)}, u32[]{:S(2)}) collective-permute-start(bf16[512,1024]{1,0:T(8,128)(2,1)S(1)} %pad_maximum_fusion.20), channel_id=1, source_target_pairs={{0,16},{16,0},{1,17},{17,1},{2,18},{18,2},{3,19},{19,3},{4,20},{20... | collective-permute-start | bytes 3145736 | tf_op jit(solution)/shard_map/ppermute | solution.py:18
  212.9 20.8 %collective-permute-start.41 = (bf16[128,1024]{1,0:T(8,128)(2,1)S(1)}, bf16[128,1024]{1,0:T(8,128)(2,1)S(1)}, u32[]{:S(2)}, u32[]{:S(2)}) collective-permute-start(bf16[128,1024]{1,0:T(8,128)(2,1)S(1)} %get-tuple-element.660), channel_id=1, source_target_pairs={{0,8},{8,0},{1,9},{9,1},{2,10},{10,2},{3,11},{11,3},{4,12},{12,4},... | collective-permute-start | bytes 786440 | tf_op jit(solution)/shard_map/ppermute | solution.py:18
  233.7 29.9 %collective-permute-start.42 = (bf16[256,1024]{1,0:T(8,128)(2,1)S(1)}, bf16[256,1024]{1,0:T(8,128)(2,1)S(1)}, u32[]{:S(2)}, u32[]{:S(2)}) collective-permute-start(bf16[256,1024]{1,0:T(8,128)(2,1)S(1)} %pad_maximum_fusion.41), channel_id=1, source_target_pairs={{0,8},{8,0},{1,9},{9,1},{2,10},{10,2},{3,11},{11,3},{4,12},{12,4},... | collective-permute-start | bytes 1572872 | tf_op jit(solution)/shard_map/ppermute | solution.py:18
  236.2 27.3 %collective-permute-start.43 = (bf16[256,1024]{1,0:T(8,128)(2,1)S(1)}, bf16[256,1024]{1,0:T(8,128)(2,1)S(1)}, u32[]{:S(2)}, u32[]{:S(2)}) collective-permute-start(bf16[256,1024]{1,0:T(8,128)(2,1)S(1)} %pad_maximum_fusion.42), channel_id=1, source_target_pairs={{0,1},{1,0},{2,3},{3,2},{4,5},{5,4},{6,7},{7,6},{8,9},{9,8},{10,11... | collective-permute-start | bytes 1572872 | tf_op jit(solution)/shard_map/ppermute | solution.py:18
  237.8 25.9 %collective-permute-start.46 = (bf16[512,1024]{1,0:T(8,128)(2,1)S(1)}, bf16[512,1024]{1,0:T(8,128)(2,1)S(1)}, u32[]{:S(2)}, u32[]{:S(2)}) collective-permute-start(bf16[512,1024]{1,0:T(8,128)(2,1)S(1)} %pad_maximum_fusion.20), channel_id=1, source_target_pairs={{0,4},{4,0},{1,5},{5,1},{2,6},{6,2},{3,7},{7,3},{8,12},{12,8},{9,1... | collective-permute-start | bytes 3145736 | tf_op jit(solution)/shard_map/ppermute | solution.py:18
  265.9 25.1 %collective-permute-start.49 = (bf16[512,1024]{1,0:T(8,128)(2,1)S(1)}, bf16[512,1024]{1,0:T(8,128)(2,1)S(1)}, u32[]{:S(2)}, u32[]{:S(2)}) collective-permute-start(bf16[512,1024]{1,0:T(8,128)(2,1)S(1)} %collective-permute-done.45), channel_id=1, source_target_pairs={{0,4},{4,0},{1,5},{5,1},{2,6},{6,2},{3,7},{7,3},{8,12},{12,8},{9,1... | collective-permute-start | bytes 3145736 | tf_op jit(solution)/shard_map/ppermute | solution.py:18
  364.6 26.1 %collective-permute-start.63 = (bf16[512,1024]{1,0:T(8,128)(2,1)S(1)}, bf16[512,1024]{1,0:T(8,128)(2,1)S(1)}, u32[]{:S(2)}, u32[]{:S(2)}) collective-permute-start(bf16[512,1024]{1,0:T(8,128)(2,1)S(1)} %convolution_convert_fusion.5), channel_id=1, source_target_pairs={{0,4},{4,0},{1,5},{5,1},{2,6},{6,2},{3,7},{7,3},{8,12},{12,8},{9,1... | collective-permute-start | bytes 3145736 | tf_op jit(solution)/shard_map/ppermute | solution.py:18
  366.2 57.8 %collective-permute-start.67 = (bf16[512,1024]{1,0:T(8,128)(2,1)}, bf16[512,1024]{1,0:T(8,128)(2,1)}, u32[]{:S(2)}, u32[]{:S(2)}) collective-permute-start(bf16[512,1024]{1,0:T(8,128)(2,1)} %convolution_convert_fusion.4), channel_id=1, source_target_pairs={{0,4},{4,0},{1,5},{5,1},{2,6},{6,2},{3,7},{7,3},{8,12},{12,8},{9,1... | collective-permute-start | bytes 3145736 | tf_op jit(solution)/shard_map/ppermute | solution.py:18
  393.2 62.0 %collective-permute-start.70 = (bf16[512,1024]{1,0:T(8,128)(2,1)}, bf16[512,1024]{1,0:T(8,128)(2,1)}, u32[]{:S(2)}, u32[]{:S(2)}) collective-permute-start(bf16[512,1024]{1,0:T(8,128)(2,1)} %convolution_convert_fusion.3), channel_id=1, source_target_pairs={{0,4},{4,0},{1,5},{5,1},{2,6},{6,2},{3,7},{7,3},{8,12},{12,8},{9,1... | collective-permute-start | bytes 3145736 | tf_op jit(solution)/shard_map/ppermute | solution.py:18
  394.8 60.4 %collective-permute-start.71 = (bf16[512,1024]{1,0:T(8,128)(2,1)}, bf16[512,1024]{1,0:T(8,128)(2,1)}, u32[]{:S(2)}, u32[]{:S(2)}) collective-permute-start(bf16[512,1024]{1,0:T(8,128)(2,1)} %add_convert_fusion.6), channel_id=1, source_target_pairs={{0,16},{16,0},{1,17},{17,1},{2,18},{18,2},{3,19},{19,3},{4,20},{20... | collective-permute-start | bytes 3145736 | tf_op jit(solution)/shard_map/ppermute | solution.py:18
  420.7 34.0 %collective-permute-start.68 = (bf16[256,1024]{1,0:T(8,128)(2,1)S(1)}, bf16[256,1024]{1,0:T(8,128)(2,1)S(1)}, u32[]{:S(2)}, u32[]{:S(2)}) collective-permute-start(bf16[256,1024]{1,0:T(8,128)(2,1)S(1)} %slice.2321), channel_id=1, source_target_pairs={{0,8},{8,0},{1,9},{9,1},{2,10},{10,2},{3,11},{11,3},{4,12},{12,4},... | collective-permute-start | bytes 1572872 | tf_op jit(solution)/shard_map/ppermute | solution.py:18
  424.0 31.0 %collective-permute-start.69 = (bf16[256,1024]{1,0:T(8,128)(2,1)S(1)}, bf16[256,1024]{1,0:T(8,128)(2,1)S(1)}, u32[]{:S(2)}, u32[]{:S(2)}) collective-permute-start(bf16[256,1024]{1,0:T(8,128)(2,1)S(1)} %pad_maximum_fusion.46), channel_id=1, source_target_pairs={{0,1},{1,0},{2,3},{3,2},{4,5},{5,4},{6,7},{7,6},{8,9},{9,8},{10,11... | collective-permute-start | bytes 1572872 | tf_op jit(solution)/shard_map/ppermute | solution.py:18
  425.5 72.3 %collective-permute-start.76 = (bf16[512,1024]{1,0:T(8,128)(2,1)S(1)}, bf16[512,1024]{1,0:T(8,128)(2,1)S(1)}, u32[]{:S(2)}, u32[]{:S(2)}) collective-permute-start(bf16[512,1024]{1,0:T(8,128)(2,1)S(1)} %copy-done.122), channel_id=1, source_target_pairs={{0,4},{4,0},{1,5},{5,1},{2,6},{6,2},{3,7},{7,3},{8,12},{12,8},{9,1... | collective-permute-start | bytes 3145736 | tf_op jit(solution)/shard_map/ppermute | solution.py:18
  463.6 59.8 %collective-permute-start.79 = (bf16[512,1024]{1,0:T(8,128)(2,1)S(1)}, bf16[512,1024]{1,0:T(8,128)(2,1)S(1)}, u32[]{:S(2)}, u32[]{:S(2)}) collective-permute-start(bf16[512,1024]{1,0:T(8,128)(2,1)S(1)} %copy-done.121), channel_id=1, source_target_pairs={{0,4},{4,0},{1,5},{5,1},{2,6},{6,2},{3,7},{7,3},{8,12},{12,8},{9,1... | collective-permute-start | bytes 3145736 | tf_op jit(solution)/shard_map/ppermute | solution.py:18
  464.2 59.3 %collective-permute-start.80 = (bf16[512,1024]{1,0:T(8,128)(2,1)S(1)}, bf16[512,1024]{1,0:T(8,128)(2,1)S(1)}, u32[]{:S(2)}, u32[]{:S(2)}) collective-permute-start(bf16[512,1024]{1,0:T(8,128)(2,1)S(1)} %add_convert_fusion.3), channel_id=1, source_target_pairs={{0,16},{16,0},{1,17},{17,1},{2,18},{18,2},{3,19},{19,3},{4,20},{20... | collective-permute-start | bytes 3145736 | tf_op jit(solution)/shard_map/ppermute | solution.py:18
  472.5 22.1 %collective-permute-start.75 = (bf16[128,1024]{1,0:T(8,128)(2,1)S(1)}, bf16[128,1024]{1,0:T(8,128)(2,1)S(1)}, u32[]{:S(2)}, u32[]{:S(2)}) collective-permute-start(bf16[128,1024]{1,0:T(8,128)(2,1)S(1)} %get-tuple-element.804), channel_id=1, source_target_pairs={{0,8},{8,0},{1,9},{9,1},{2,10},{10,2},{3,11},{11,3},{4,12},{12,4},... | collective-permute-start | bytes 786440 | tf_op jit(solution)/shard_map/ppermute | solution.py:18
  494.7 28.7 %collective-permute-start.77 = (bf16[256,1024]{1,0:T(8,128)(2,1)S(1)}, bf16[256,1024]{1,0:T(8,128)(2,1)S(1)}, u32[]{:S(2)}, u32[]{:S(2)}) collective-permute-start(bf16[256,1024]{1,0:T(8,128)(2,1)S(1)} %pad_maximum_fusion.47), channel_id=1, source_target_pairs={{0,8},{8,0},{1,9},{9,1},{2,10},{10,2},{3,11},{11,3},{4,12},{12,4},... | collective-permute-start | bytes 1572872 | tf_op jit(solution)/shard_map/ppermute | solution.py:18
  497.2 26.2 %collective-permute-start.78 = (bf16[256,1024]{1,0:T(8,128)(2,1)S(1)}, bf16[256,1024]{1,0:T(8,128)(2,1)S(1)}, u32[]{:S(2)}, u32[]{:S(2)}) collective-permute-start(bf16[256,1024]{1,0:T(8,128)(2,1)S(1)} %pad_maximum_fusion.48), channel_id=1, source_target_pairs={{0,1},{1,0},{2,3},{3,2},{4,5},{5,4},{6,7},{7,6},{8,9},{9,8},{10,11... | collective-permute-start | bytes 1572872 | tf_op jit(solution)/shard_map/ppermute | solution.py:18
  528.4 31.3 %collective-permute-start.83 = (bf16[512,1024]{1,0:T(8,128)(2,1)}, bf16[512,1024]{1,0:T(8,128)(2,1)}, u32[]{:S(2)}, u32[]{:S(2)}) collective-permute-start(bf16[512,1024]{1,0:T(8,128)(2,1)} %convolution_convert_fusion), channel_id=1, source_target_pairs={{0,4},{4,0},{1,5},{5,1},{2,6},{6,2},{3,7},{7,3},{8,12},{12,8},{9,1... | collective-permute-start | bytes 3145736 | tf_op jit(solution)/shard_map/ppermute | solution.py:18
  529.9 52.6 %collective-permute-start.87 = (bf16[256,1024]{1,0:T(8,128)(2,1)}, bf16[256,1024]{1,0:T(8,128)(2,1)}, u32[]{:S(2)}, u32[]{:S(2)}) collective-permute-start(bf16[256,1024]{1,0:T(8,128)(2,1)} %select_convert_fusion.5), channel_id=1, source_target_pairs={{0,8},{8,0},{1,9},{9,1},{2,10},{10,2},{3,11},{11,3},{4,12},{12,4},... | collective-permute-start | bytes 1572872 | tf_op jit(solution)/shard_map/ppermute | solution.py:18
  530.0 48.5 %collective-permute-start.85 = (bf16[512,1024]{1,0:T(8,128)(2,1)}, bf16[512,1024]{1,0:T(8,128)(2,1)}, u32[]{:S(2)}, u32[]{:S(2)}) collective-permute-start(bf16[512,1024]{1,0:T(8,128)(2,1)} %add_convert_fusion.2), channel_id=1, source_target_pairs={{0,16},{16,0},{1,17},{17,1},{2,18},{18,2},{3,19},{19,3},{4,20},{20... | collective-permute-start | bytes 3145736 | tf_op jit(solution)/shard_map/ppermute | solution.py:18
  532.9 71.7 %collective-permute-start.92 = (bf16[256,1024]{1,0:T(8,128)(2,1)}, bf16[256,1024]{1,0:T(8,128)(2,1)}, u32[]{:S(2)}, u32[]{:S(2)}) collective-permute-start(bf16[256,1024]{1,0:T(8,128)(2,1)} %select_convert_fusion.4), channel_id=1, source_target_pairs={{0,8},{8,0},{1,9},{9,1},{2,10},{10,2},{3,11},{11,3},{4,12},{12,4},... | collective-permute-start | bytes 1572872 | tf_op jit(solution)/shard_map/ppermute | solution.py:18
  593.4 26.5 %collective-permute-start.96 = (bf16[512,512]{0,1:T(8,128)(2,1)S(1)}, bf16[512,512]{0,1:T(8,128)(2,1)S(1)}, u32[]{:S(2)}, u32[]{:S(2)}) collective-permute-start(bf16[512,512]{0,1:T(8,128)(2,1)S(1)} %fusion.28), channel_id=1, source_target_pairs={{0,16},{16,0},{1,17},{17,1},{2,18},{18,2},{3,19},{19,3},{4,20},{20... | collective-permute-start | bytes 1572872 | tf_op jit(solution)/shard_map/ppermute | solution.py:18
  595.4 40.1 %collective-permute-start.101 = (bf16[256,1024]{1,0:T(8,128)(2,1)S(1)}, bf16[256,1024]{1,0:T(8,128)(2,1)S(1)}, u32[]{:S(2)}, u32[]{:S(2)}) collective-permute-start(bf16[256,1024]{1,0:T(8,128)(2,1)S(1)} %select_convert_fusion.2), channel_id=1, source_target_pairs={{0,8},{8,0},{1,9},{9,1},{2,10},{10,2},{3,11},{11,3},{4,12},{12,4},... | collective-permute-start | bytes 1572872 | tf_op jit(solution)/shard_map/ppermute | solution.py:18
  613.1 22.5 %collective-permute-start.100 = (f32[4,512]{1,0:T(4,128)S(1)}, f32[4,512]{1,0:T(4,128)S(1)}, u32[]{:S(2)}, u32[]{:S(2)}) collective-permute-start(f32[4,512]{1,0:T(4,128)S(1)} %slice.1252), channel_id=1, source_target_pairs={{0,16},{16,0},{1,17},{17,1},{2,18},{18,2},{3,19},{19,3},{4,20},{20... | collective-permute-start | bytes 24584 | tf_op jit(solution)/shard_map/ppermute | solution.py:18
  621.6 30.5 %collective-permute-start.104 = (bf16[512,512]{0,1:T(8,128)(2,1)S(1)}, bf16[512,512]{0,1:T(8,128)(2,1)S(1)}, u32[]{:S(2)}, u32[]{:S(2)}) collective-permute-start(bf16[512,512]{0,1:T(8,128)(2,1)S(1)} %pad_maximum_fusion.53), channel_id=1, source_target_pairs={{0,4},{4,0},{1,5},{5,1},{2,6},{6,2},{3,7},{7,3},{8,12},{12,8},{9,1... | collective-permute-start | bytes 1572872 | tf_op jit(solution)/shard_map/ppermute | solution.py:18
  631.1 26.1 %collective-permute-start.105 = (bf16[512,512]{0,1:T(8,128)(2,1)S(1)}, bf16[512,512]{0,1:T(8,128)(2,1)S(1)}, u32[]{:S(2)}, u32[]{:S(2)}) collective-permute-start(bf16[512,512]{0,1:T(8,128)(2,1)S(1)} %fusion.29), channel_id=1, source_target_pairs={{0,16},{16,0},{1,17},{17,1},{2,18},{18,2},{3,19},{19,3},{4,20},{20... | collective-permute-start | bytes 1572872 | tf_op jit(solution)/shard_map/ppermute | solution.py:18
  633.8 23.6 %collective-permute-start.106 = (bf16[512,512]{0,1:T(8,128)(2,1)S(1)}, bf16[512,512]{0,1:T(8,128)(2,1)S(1)}, u32[]{:S(2)}, u32[]{:S(2)}) collective-permute-start(bf16[512,512]{0,1:T(8,128)(2,1)S(1)} %pad_maximum_fusion.52), channel_id=1, source_target_pairs={{0,4},{4,0},{1,5},{5,1},{2,6},{6,2},{3,7},{7,3},{8,12},{12,8},{9,1... | collective-permute-start | bytes 1572872 | tf_op jit(solution)/shard_map/ppermute | solution.py:18
  652.1 20.7 %collective-permute-start.113 = (bf16[128,2048]{1,0:T(8,128)(2,1)S(1)}, bf16[128,2048]{1,0:T(8,128)(2,1)S(1)}, u32[]{:S(2)}, u32[]{:S(2)}) collective-permute-start(bf16[128,2048]{1,0:T(8,128)(2,1)S(1)} %select_convert_fusion), channel_id=1, source_target_pairs={{0,2},{2,0},{1,3},{3,1},{4,6},{6,4},{5,7},{7,5},{8,10},{10,8},{9,1... | collective-permute-start | bytes 1572872 | tf_op jit(solution)/shard_map/ppermute | solution.py:18
  (254 other events, 2668.1 us)

commit v10 on v9

--- a/solution.py
+++ b/solution.py
@@ -645,21 +645,21 @@
             )
         )
         grad_tokens = to_natural(d_resid + d_tokens)
+        ov_grad.end_x(0)
+        ov_grad.end_high()
+        ov_grad.start_line()
         qk_grad.end_x(0)
         qk_grad.end_high()
         qk_grad.start_line()
-        ov_grad.end_x(0)
-        ov_grad.end_high()
-        ov_grad.start_line()
         gain_steps()
         gate_grad.end()
+        ov_grad.end_line()
         gain_steps()
+        up_grad.end()
+        ov_grad.end()
         qk_grad.end_line()
-        ov_grad.end_line()
         gain_parts = gain_steps.finish()
-        up_grad.end()
         qk_grad.end()
-        ov_grad.end()
         grad_output, grad_value = ov_grad.results
         grad_query, grad_key = qk_grad.results
         return (

time: 688 us -> 684 us (level)
  transfers between devices with their start and end apart: 116 -> 116, of which waited for: 49 -> 50; matrix products, arithmetic and copies ran while one was open for 31% -> 31% of each run, Pallas kernels for 0% -> 0%
where the time goes in v10:
time: 684 us; the launch traced here: 677 us
  waiting for transfers between devices  301 us (44%)
  matrix products  127 us (19%)
  starting transfers between devices  116 us (17%)
  other arithmetic  69.2 us (10%)
  local copies, waits for them, and re-layouts  57.8 us (8%)
    ppermute x116, waiting for transfers between devices, swap(): return lax.ppermute(value, axis, FLIP)  301 us
    ppermute x116, starting transfers between devices, swap(): return lax.ppermute(value, axis, FLIP)  116 us
    dot_general x28, matrix products, dot_tn(): return jnp.einsum('sr,sc->rc', a, b, preferred_element_type=F32)  45.3 us
    dot_general x24, matrix products, dot_nt(): return jnp.einsum('sc,rc->sr', a, b, preferred_element_type=F32)  35.8 us
    dot_general x12, matrix products, dot(): return jnp.dot(a, b, preferred_element_type=F32)  32.4 us
    unnamed x421, local copies, waits for them, and re-layouts  26.2 us
  transfers between devices with their start and end apart: 116, of which 50 were waited for; matrix products, arithmetic and copies ran while one was open for 31% of the time, Pallas kernels for 0%

profile of v10, /device:TPU:0, one launch (start us, length us, event | category | flops | bytes accessed | tf_op | source)
XLA Modules:
  0.0 677.3 jit_solution(5784326020445299730)
XLA Ops:
  6.0 3.1 collective-permute-start
  22.6 4.4 collective-permute-done.3
  41.6 6.0 collective-permute-done.9
  52.4 7.9 %collective-permute-done.12 = bf16[512,512]{0,1:T(8,128)(2,1)S(1)} collective-permute-done((bf16[512,512]{0,1:T(8,128)(2,1)S(1)}, bf16[512,512]{0,1:T(8,128)(2,1)S(1)}, u32[]{:S(2)}, u32[]{:S(2)}) %collective-permute-start.12) | collective-permute-done | bytes 524320 | tf_op jit(solution)/shard_map/ppermute | solution.py:18
  60.4 3.1 collective-permute-done.13
  78.7 8.7 %collective-permute-done.18 = bf16[256,1024]{1,0:T(8,128)(2,1)S(1)} collective-permute-done((bf16[256,1024]{1,0:T(8,128)(2,1)}, bf16[256,1024]{1,0:T(8,128)(2,1)S(1)}, u32[]{:S(2)}, u32[]{:S(2)}) %collective-permute-start.18) | collective-permute-done | bytes 524320 | tf_op jit(solution)/shard_map/ppermute | solution.py:18
  87.4 2.9 pad_maximum_fusion
  104.8 3.0 collective-permute-start.30
  110.7 6.8 %collective-permute-done.26 = bf16[512,512]{0,1:T(8,128)(2,1)} collective-permute-done((bf16[512,512]{0,1:T(8,128)(2,1)S(1)}, bf16[512,512]{0,1:T(8,128)(2,1)}, u32[]{:S(2)}, u32[]{:S(2)}) %collective-permute-start.26) | collective-permute-done | bytes 524320 | tf_op jit(solution)/shard_map/ppermute | solution.py:18
  127.4 3.4 fusion.213
  132.8 2.9 fusion.4
  141.8 9.2 %collective-permute-done.29 = bf16[256,1024]{1,0:T(8,128)(2,1)} collective-permute-done((bf16[256,1024]{1,0:T(8,128)(2,1)}, bf16[256,1024]{1,0:T(8,128)(2,1)}, u32[]{:S(2)}, u32[]{:S(2)}) %collective-permute-start.29) | collective-permute-done | bytes 524320 | tf_op jit(solution)/shard_map/ppermute | solution.py:18
  151.0 3.2 collective-permute-done.30
  160.0 2.8 collective-permute-start.33
  164.6 26.1 %collective-permute-done.33 = bf16[256,1024]{1,0:T(8,128)(2,1)S(1)} collective-permute-done((bf16[256,1024]{1,0:T(8,128)(2,1)S(1)}, bf16[256,1024]{1,0:T(8,128)(2,1)S(1)}, u32[]{:S(2)}, u32[]{:S(2)}) %collective-permute-start.33) | collective-permute-done | bytes 524320 | tf_op jit(solution)/shard_map/ppermute | solution.py:18
  195.3 9.6 %collective-permute-done.36 = bf16[512,1024]{1,0:T(8,128)(2,1)S(1)} collective-permute-done((bf16[512,1024]{1,0:T(8,128)(2,1)S(1)}, bf16[512,1024]{1,0:T(8,128)(2,1)S(1)}, u32[]{:S(2)}, u32[]{:S(2)}) %collective-permute-start.36) | collective-permute-done | bytes 1048608 | tf_op jit(solution)/shard_map/ppermute | solution.py:18
  205.5 5.0 collective-permute-done.39
  212.9 6.7 collective-permute-done.40
  219.6 14.0 %collective-permute-done.41 = bf16[128,1024]{1,0:T(8,128)(2,1)S(1)} collective-permute-done((bf16[128,1024]{1,0:T(8,128)(2,1)S(1)}, bf16[128,1024]{1,0:T(8,128)(2,1)S(1)}, u32[]{:S(2)}, u32[]{:S(2)}) %collective-permute-start.41) | collective-permute-done | bytes 262176 | tf_op jit(solution)/shard_map/ppermute | solution.py:18
  239.3 24.2 %collective-permute-done.42 = bf16[256,1024]{1,0:T(8,128)(2,1)S(1)} collective-permute-done((bf16[256,1024]{1,0:T(8,128)(2,1)S(1)}, bf16[256,1024]{1,0:T(8,128)(2,1)S(1)}, u32[]{:S(2)}, u32[]{:S(2)}) %collective-permute-start.42) | collective-permute-done | bytes 524320 | tf_op jit(solution)/shard_map/ppermute | solution.py:18
  272.8 3.6 fusion.190
  276.5 5.4 multiply_convert_fusion.2
  281.9 9.2 %collective-permute-done.49 = bf16[512,1024]{1,0:T(8,128)(2,1)S(1)} collective-permute-done((bf16[512,1024]{1,0:T(8,128)(2,1)S(1)}, bf16[512,1024]{1,0:T(8,128)(2,1)S(1)}, u32[]{:S(2)}, u32[]{:S(2)}) %collective-permute-start.49) | collective-permute-done | bytes 1048608 | tf_op jit(solution)/shard_map/ppermute | solution.py:18
  299.9 12.5 %collective-permute-done.52 = bf16[256,1024]{1,0:T(8,128)(2,1)S(1)} collective-permute-done((bf16[256,1024]{1,0:T(8,128)(2,1)S(1)}, bf16[256,1024]{1,0:T(8,128)(2,1)S(1)}, u32[]{:S(2)}, u32[]{:S(2)}) %collective-permute-start.52) | collective-permute-done | bytes 524320 | tf_op jit(solution)/shard_map/ppermute | solution.py:18
  316.2 4.2 collective-permute-done.54
  325.6 4.6 collective-permute-done.56
  334.1 7.7 %collective-permute-done.58 = bf16[256,1024]{1,0:T(8,128)(2,1)S(1)} collective-permute-done((bf16[256,1024]{1,0:T(8,128)(2,1)S(1)}, bf16[256,1024]{1,0:T(8,128)(2,1)S(1)}, u32[]{:S(2)}, u32[]{:S(2)}) %collective-permute-start.58) | collective-permute-done | bytes 524320 | tf_op jit(solution)/shard_map/ppermute | solution.py:18
  351.1 3.0 constant_dynamic-update-slice_fusion.60
  354.1 3.5 convolution_convert_fusion.4
  361.7 2.9 fusion.20
  366.7 3.9 fusion.223
  370.7 5.6 multiply_convert_fusion
  396.7 4.3 fusion.60
  407.0 4.0 add_convert_fusion.5
  411.5 3.0 fusion.58
  426.2 28.6 %collective-permute-done.68 = bf16[256,1024]{1,0:T(8,128)(2,1)S(1)} collective-permute-done((bf16[256,1024]{1,0:T(8,128)(2,1)S(1)}, bf16[256,1024]{1,0:T(8,128)(2,1)S(1)}, u32[]{:S(2)}, u32[]{:S(2)}) %collective-permute-start.68) | collective-permute-done | bytes 524320 | tf_op jit(solution)/shard_map/ppermute | solution.py:18
  464.2 3.0 collective-permute-start.80
  467.4 3.2 collective-permute-done.73
  472.6 5.7 collective-permute-done.74
  478.3 16.2 %collective-permute-done.75 = bf16[128,1024]{1,0:T(8,128)(2,1)S(1)} collective-permute-done((bf16[128,1024]{1,0:T(8,128)(2,1)S(1)}, bf16[128,1024]{1,0:T(8,128)(2,1)S(1)}, u32[]{:S(2)}, u32[]{:S(2)}) %collective-permute-start.75) | collective-permute-done | bytes 262176 | tf_op jit(solution)/shard_map/ppermute | solution.py:18
  497.9 25.5 %collective-permute-done.77 = bf16[256,1024]{1,0:T(8,128)(2,1)S(1)} collective-permute-done((bf16[256,1024]{1,0:T(8,128)(2,1)S(1)}, bf16[256,1024]{1,0:T(8,128)(2,1)S(1)}, u32[]{:S(2)}, u32[]{:S(2)}) %collective-permute-start.77) | collective-permute-done | bytes 524320 | tf_op jit(solution)/shard_map/ppermute | solution.py:18
  530.0 2.9 collective-permute-start.85
  541.9 3.1 fusion.5
  623.2 7.8 %collective-permute-done.98 = bf16[256,1024]{1,0:T(8,128)(2,1)S(1)} collective-permute-done((bf16[256,1024]{1,0:T(8,128)(2,1)S(1)}, bf16[256,1024]{1,0:T(8,128)(2,1)S(1)}, u32[]{:S(2)}, u32[]{:S(2)}) %collective-permute-start.98) | collective-permute-done | bytes 524320 | tf_op jit(solution)/shard_map/ppermute | solution.py:18
  638.3 4.8 collective-permute-done.102
  643.4 8.1 %collective-permute-done.103 = bf16[128,1024]{1,0:T(8,128)(2,1)S(1)} collective-permute-done((bf16[128,1024]{1,0:T(8,128)(2,1)S(1)}, bf16[128,1024]{1,0:T(8,128)(2,1)S(1)}, u32[]{:S(2)}, u32[]{:S(2)}) %collective-permute-start.103) | collective-permute-done | bytes 262176 | tf_op jit(solution)/shard_map/ppermute | solution.py:18
  654.3 3.8 collective-permute-done.106
  663.3 4.5 collective-permute-done.109
  (960 shorter events, 323.8 us)
Async XLA Ops:
  10.0 19.2 %collective-permute-start.5 = (bf16[128,1024]{1,0:T(8,128)(2,1)}, bf16[128,1024]{1,0:T(8,128)(2,1)}, u32[]{:S(2)}, u32[]{:S(2)}) collective-permute-start(bf16[128,1024]{1,0:T(8,128)(2,1)} %pad_maximum_fusion.58), channel_id=1, source_target_pairs={{0,1},{1,0},{2,3},{3,2},{4,5},{5,4},{6,7},{7,6},{8,9},{9,8},{10,11... | collective-permute-start | bytes 786440 | tf_op jit(solution)/shard_map/ppermute | solution.py:18
  17.9 21.5 %collective-permute-start.8 = (bf16[128,6144]{1,0:T(8,128)(2,1)S(1)}, bf16[128,6144]{1,0:T(8,128)(2,1)S(1)}, u32[]{:S(2)}, u32[]{:S(2)}) collective-permute-start(bf16[128,6144]{1,0:T(8,128)(2,1)S(1)} %copy-done.109), channel_id=1, source_target_pairs={{0,2},{2,0},{1,3},{3,1},{4,6},{6,4},{5,7},{7,5},{8,10},{10,8},{9,1... | collective-permute-start | bytes 4718600 | tf_op jit(solution)/shard_map/ppermute | solution.py:18
  30.1 20.6 %collective-permute-start.10 = (f32[4,512]{1,0:T(4,128)S(1)}, f32[4,512]{1,0:T(4,128)S(1)}, u32[]{:S(2)}, u32[]{:S(2)}) collective-permute-start(f32[4,512]{1,0:T(4,128)S(1)} %pad_maximum_fusion.76), channel_id=1, source_target_pairs={{0,16},{16,0},{1,17},{17,1},{2,18},{18,2},{3,19},{19,3},{4,20},{20... | collective-permute-start | bytes 24584 | tf_op jit(solution)/shard_map/ppermute | solution.py:18
  32.9 18.4 %collective-permute-start.11 = (bf16[512,512]{0,1:T(8,128)(2,1)S(1)}, bf16[512,512]{0,1:T(8,128)(2,1)S(1)}, u32[]{:S(2)}, u32[]{:S(2)}) collective-permute-start(bf16[512,512]{0,1:T(8,128)(2,1)S(1)} %pad_maximum_fusion.36), channel_id=1, source_target_pairs={{0,4},{4,0},{1,5},{5,1},{2,6},{6,2},{3,7},{7,3},{8,12},{12,8},{9,1... | collective-permute-start | bytes 1572872 | tf_op jit(solution)/shard_map/ppermute | solution.py:18
  36.8 23.6 %collective-permute-start.12 = (bf16[512,512]{0,1:T(8,128)(2,1)S(1)}, bf16[512,512]{0,1:T(8,128)(2,1)S(1)}, u32[]{:S(2)}, u32[]{:S(2)}) collective-permute-start(bf16[512,512]{0,1:T(8,128)(2,1)S(1)} %pad_maximum_fusion.36), channel_id=1, source_target_pairs={{0,16},{16,0},{1,17},{17,1},{2,18},{18,2},{3,19},{19,3},{4,20},{20... | collective-permute-start | bytes 1572872 | tf_op jit(solution)/shard_map/ppermute | solution.py:18
  39.8 23.7 %collective-permute-start.13 = (bf16[256,1024]{1,0:T(8,128)(2,1)S(1)}, bf16[256,1024]{1,0:T(8,128)(2,1)S(1)}, u32[]{:S(2)}, u32[]{:S(2)}) collective-permute-start(bf16[256,1024]{1,0:T(8,128)(2,1)S(1)} %pad_maximum_fusion.37), channel_id=1, source_target_pairs={{0,8},{8,0},{1,9},{9,1},{2,10},{10,2},{3,11},{11,3},{4,12},{12,4},... | collective-permute-start | bytes 1572872 | tf_op jit(solution)/shard_map/ppermute | solution.py:18
  67.6 19.8 %collective-permute-start.18 = (bf16[256,1024]{1,0:T(8,128)(2,1)}, bf16[256,1024]{1,0:T(8,128)(2,1)S(1)}, u32[]{:S(2)}, u32[]{:S(2)}) collective-permute-start(bf16[256,1024]{1,0:T(8,128)(2,1)} %broadcast_select_fusion.11), channel_id=1, source_target_pairs={{0,8},{8,0},{1,9},{9,1},{2,10},{10,2},{3,11},{11,3},{4,12},{12,4},... | collective-permute-start | bytes 1572872 | tf_op jit(solution)/shard_map/ppermute | solution.py:18
  69.4 18.0 %collective-permute-start.19 = (f32[4,1024]{1,0:T(4,128)}, f32[4,1024]{1,0:T(4,128)S(1)}, u32[]{:S(2)}, u32[]{:S(2)}) collective-permute-start(f32[4,1024]{1,0:T(4,128)} %pad_maximum_fusion.71), channel_id=1, source_target_pairs={{0,4},{4,0},{1,5},{5,1},{2,6},{6,2},{3,7},{7,3},{8,12},{12,8},{9,1... | collective-permute-start | bytes 49160 | tf_op jit(solution)/shard_map/ppermute | solution.py:18
  74.7 26.1 %collective-permute-start.22 = (bf16[512,512]{0,1:T(8,128)(2,1)S(1)}, bf16[512,512]{0,1:T(8,128)(2,1)S(1)}, u32[]{:S(2)}, u32[]{:S(2)}) collective-permute-start(bf16[512,512]{0,1:T(8,128)(2,1)S(1)} %copy-done.132), channel_id=1, source_target_pairs={{0,16},{16,0},{1,17},{17,1},{2,18},{18,2},{3,19},{19,3},{4,20},{20... | collective-permute-start | bytes 1572872 | tf_op jit(solution)/shard_map/ppermute | solution.py:18
  77.2 23.5 %collective-permute-start.23 = (bf16[512,512]{0,1:T(8,128)(2,1)S(1)}, bf16[512,512]{0,1:T(8,128)(2,1)S(1)}, u32[]{:S(2)}, u32[]{:S(2)}) collective-permute-start(bf16[512,512]{0,1:T(8,128)(2,1)S(1)} %copy-done.132), channel_id=1, source_target_pairs={{0,4},{4,0},{1,5},{5,1},{2,6},{6,2},{3,7},{7,3},{8,12},{12,8},{9,1... | collective-permute-start | bytes 1572872 | tf_op jit(solution)/shard_map/ppermute | solution.py:18
  104.7 34.3 %collective-permute-start.27 = (bf16[256,1024]{1,0:T(8,128)(2,1)}, bf16[256,1024]{1,0:T(8,128)(2,1)}, u32[]{:S(2)}, u32[]{:S(2)}) collective-permute-start(bf16[256,1024]{1,0:T(8,128)(2,1)} %broadcast_select_fusion.7), channel_id=1, source_target_pairs={{0,8},{8,0},{1,9},{9,1},{2,10},{10,2},{3,11},{11,3},{4,12},{12,4},... | collective-permute-start | bytes 1572872 | tf_op jit(solution)/shard_map/ppermute | solution.py:18
  104.8 49.4 %collective-permute-start.30 = (bf16[512,1024]{1,0:T(8,128)(2,1)}, bf16[512,1024]{1,0:T(8,128)(2,1)}, u32[]{:S(2)}, u32[]{:S(2)}) collective-permute-start(bf16[512,1024]{1,0:T(8,128)(2,1)} %pad_maximum_fusion.17), channel_id=1, source_target_pairs={{0,16},{16,0},{1,17},{17,1},{2,18},{18,2},{3,19},{19,3},{4,20},{20... | collective-permute-start | bytes 3145736 | tf_op jit(solution)/shard_map/ppermute | solution.py:18
  107.8 34.0 %collective-permute-start.28 = (bf16[512,1024]{1,0:T(8,128)(2,1)}, bf16[512,1024]{1,0:T(8,128)(2,1)}, u32[]{:S(2)}, u32[]{:S(2)}) collective-permute-start(bf16[512,1024]{1,0:T(8,128)(2,1)} %pad_maximum_fusion.17), channel_id=1, source_target_pairs={{0,4},{4,0},{1,5},{5,1},{2,6},{6,2},{3,7},{7,3},{8,12},{12,8},{9,1... | collective-permute-start | bytes 3145736 | tf_op jit(solution)/shard_map/ppermute | solution.py:18
  109.3 41.7 %collective-permute-start.29 = (bf16[256,1024]{1,0:T(8,128)(2,1)}, bf16[256,1024]{1,0:T(8,128)(2,1)}, u32[]{:S(2)}, u32[]{:S(2)}) collective-permute-start(bf16[256,1024]{1,0:T(8,128)(2,1)} %broadcast_select_fusion.6), channel_id=1, source_target_pairs={{0,8},{8,0},{1,9},{9,1},{2,10},{10,2},{3,11},{11,3},{4,12},{12,4},... | collective-permute-start | bytes 1572872 | tf_op jit(solution)/shard_map/ppermute | solution.py:18
  155.2 40.0 %collective-permute-start.35 = (bf16[512,1024]{1,0:T(8,128)(2,1)S(1)}, bf16[512,1024]{1,0:T(8,128)(2,1)S(1)}, u32[]{:S(2)}, u32[]{:S(2)}) collective-permute-start(bf16[512,1024]{1,0:T(8,128)(2,1)S(1)} %pad_maximum_fusion.19), channel_id=1, source_target_pairs={{0,4},{4,0},{1,5},{5,1},{2,6},{6,2},{3,7},{7,3},{8,12},{12,8},{9,1... | collective-permute-start | bytes 3145736 | tf_op jit(solution)/shard_map/ppermute | solution.py:18
  156.8 48.1 %collective-permute-start.36 = (bf16[512,1024]{1,0:T(8,128)(2,1)S(1)}, bf16[512,1024]{1,0:T(8,128)(2,1)S(1)}, u32[]{:S(2)}, u32[]{:S(2)}) collective-permute-start(bf16[512,1024]{1,0:T(8,128)(2,1)S(1)} %pad_maximum_fusion.19), channel_id=1, source_target_pairs={{0,16},{16,0},{1,17},{17,1},{2,18},{18,2},{3,19},{19,3},{4,20},{20... | collective-permute-start | bytes 3145736 | tf_op jit(solution)/shard_map/ppermute | solution.py:18
  157.1 47.8 %collective-permute-start.37 = (bf16[512,1024]{1,0:T(8,128)(2,1)}, bf16[512,1024]{1,0:T(8,128)(2,1)S(1)}, u32[]{:S(2)}, u32[]{:S(2)}) collective-permute-start(bf16[512,1024]{1,0:T(8,128)(2,1)} %collective-permute-done.30), channel_id=1, source_target_pairs={{0,4},{4,0},{1,5},{5,1},{2,6},{6,2},{3,7},{7,3},{8,12},{12,8},{9,1... | collective-permute-start | bytes 3145736 | tf_op jit(solution)/shard_map/ppermute | solution.py:18
  160.0 30.6 %collective-permute-start.33 = (bf16[256,1024]{1,0:T(8,128)(2,1)S(1)}, bf16[256,1024]{1,0:T(8,128)(2,1)S(1)}, u32[]{:S(2)}, u32[]{:S(2)}) collective-permute-start(bf16[256,1024]{1,0:T(8,128)(2,1)S(1)} %slice.2323), channel_id=1, source_target_pairs={{0,8},{8,0},{1,9},{9,1},{2,10},{10,2},{3,11},{11,3},{4,12},{12,4},... | collective-permute-start | bytes 1572872 | tf_op jit(solution)/shard_map/ppermute | solution.py:18
  162.9 28.0 %collective-permute-start.34 = (bf16[256,1024]{1,0:T(8,128)(2,1)S(1)}, bf16[256,1024]{1,0:T(8,128)(2,1)S(1)}, u32[]{:S(2)}, u32[]{:S(2)}) collective-permute-start(bf16[256,1024]{1,0:T(8,128)(2,1)S(1)} %pad_maximum_fusion.40), channel_id=1, source_target_pairs={{0,1},{1,0},{2,3},{3,2},{4,5},{5,4},{6,7},{7,6},{8,9},{9,8},{10,11... | collective-permute-start | bytes 1572872 | tf_op jit(solution)/shard_map/ppermute | solution.py:18
  204.9 58.6 %collective-permute-start.44 = (bf16[512,1024]{1,0:T(8,128)(2,1)S(1)}, bf16[512,1024]{1,0:T(8,128)(2,1)S(1)}, u32[]{:S(2)}, u32[]{:S(2)}) collective-permute-start(bf16[512,1024]{1,0:T(8,128)(2,1)S(1)} %collective-permute-done.36), channel_id=1, source_target_pairs={{0,4},{4,0},{1,5},{5,1},{2,6},{6,2},{3,7},{7,3},{8,12},{12,8},{9,1... | collective-permute-start | bytes 3145736 | tf_op jit(solution)/shard_map/ppermute | solution.py:18
  205.4 58.1 %collective-permute-start.45 = (bf16[512,1024]{1,0:T(8,128)(2,1)S(1)}, bf16[512,1024]{1,0:T(8,128)(2,1)S(1)}, u32[]{:S(2)}, u32[]{:S(2)}) collective-permute-start(bf16[512,1024]{1,0:T(8,128)(2,1)S(1)} %pad_maximum_fusion.20), channel_id=1, source_target_pairs={{0,16},{16,0},{1,17},{17,1},{2,18},{18,2},{3,19},{19,3},{4,20},{20... | collective-permute-start | bytes 3145736 | tf_op jit(solution)/shard_map/ppermute | solution.py:18
  212.9 20.8 %collective-permute-start.41 = (bf16[128,1024]{1,0:T(8,128)(2,1)S(1)}, bf16[128,1024]{1,0:T(8,128)(2,1)S(1)}, u32[]{:S(2)}, u32[]{:S(2)}) collective-permute-start(bf16[128,1024]{1,0:T(8,128)(2,1)S(1)} %get-tuple-element.660), channel_id=1, source_target_pairs={{0,8},{8,0},{1,9},{9,1},{2,10},{10,2},{3,11},{11,3},{4,12},{12,4},... | collective-permute-start | bytes 786440 | tf_op jit(solution)/shard_map/ppermute | solution.py:18
  233.7 29.9 %collective-permute-start.42 = (bf16[256,1024]{1,0:T(8,128)(2,1)S(1)}, bf16[256,1024]{1,0:T(8,128)(2,1)S(1)}, u32[]{:S(2)}, u32[]{:S(2)}) collective-permute-start(bf16[256,1024]{1,0:T(8,128)(2,1)S(1)} %pad_maximum_fusion.41), channel_id=1, source_target_pairs={{0,8},{8,0},{1,9},{9,1},{2,10},{10,2},{3,11},{11,3},{4,12},{12,4},... | collective-permute-start | bytes 1572872 | tf_op jit(solution)/shard_map/ppermute | solution.py:18
  236.2 27.3 %collective-permute-start.43 = (bf16[256,1024]{1,0:T(8,128)(2,1)S(1)}, bf16[256,1024]{1,0:T(8,128)(2,1)S(1)}, u32[]{:S(2)}, u32[]{:S(2)}) collective-permute-start(bf16[256,1024]{1,0:T(8,128)(2,1)S(1)} %pad_maximum_fusion.42), channel_id=1, source_target_pairs={{0,1},{1,0},{2,3},{3,2},{4,5},{5,4},{6,7},{7,6},{8,9},{9,8},{10,11... | collective-permute-start | bytes 1572872 | tf_op jit(solution)/shard_map/ppermute | solution.py:18
  237.8 25.9 %collective-permute-start.46 = (bf16[512,1024]{1,0:T(8,128)(2,1)S(1)}, bf16[512,1024]{1,0:T(8,128)(2,1)S(1)}, u32[]{:S(2)}, u32[]{:S(2)}) collective-permute-start(bf16[512,1024]{1,0:T(8,128)(2,1)S(1)} %pad_maximum_fusion.20), channel_id=1, source_target_pairs={{0,4},{4,0},{1,5},{5,1},{2,6},{6,2},{3,7},{7,3},{8,12},{12,8},{9,1... | collective-permute-start | bytes 3145736 | tf_op jit(solution)/shard_map/ppermute | solution.py:18
  265.9 25.1 %collective-permute-start.49 = (bf16[512,1024]{1,0:T(8,128)(2,1)S(1)}, bf16[512,1024]{1,0:T(8,128)(2,1)S(1)}, u32[]{:S(2)}, u32[]{:S(2)}) collective-permute-start(bf16[512,1024]{1,0:T(8,128)(2,1)S(1)} %collective-permute-done.45), channel_id=1, source_target_pairs={{0,4},{4,0},{1,5},{5,1},{2,6},{6,2},{3,7},{7,3},{8,12},{12,8},{9,1... | collective-permute-start | bytes 3145736 | tf_op jit(solution)/shard_map/ppermute | solution.py:18
  364.6 26.1 %collective-permute-start.63 = (bf16[512,1024]{1,0:T(8,128)(2,1)S(1)}, bf16[512,1024]{1,0:T(8,128)(2,1)S(1)}, u32[]{:S(2)}, u32[]{:S(2)}) collective-permute-start(bf16[512,1024]{1,0:T(8,128)(2,1)S(1)} %convolution_convert_fusion.5), channel_id=1, source_target_pairs={{0,4},{4,0},{1,5},{5,1},{2,6},{6,2},{3,7},{7,3},{8,12},{12,8},{9,1... | collective-permute-start | bytes 3145736 | tf_op jit(solution)/shard_map/ppermute | solution.py:18
  366.2 57.8 %collective-permute-start.67 = (bf16[512,1024]{1,0:T(8,128)(2,1)}, bf16[512,1024]{1,0:T(8,128)(2,1)}, u32[]{:S(2)}, u32[]{:S(2)}) collective-permute-start(bf16[512,1024]{1,0:T(8,128)(2,1)} %convolution_convert_fusion.4), channel_id=1, source_target_pairs={{0,4},{4,0},{1,5},{5,1},{2,6},{6,2},{3,7},{7,3},{8,12},{12,8},{9,1... | collective-permute-start | bytes 3145736 | tf_op jit(solution)/shard_map/ppermute | solution.py:18
  393.2 62.0 %collective-permute-start.70 = (bf16[512,1024]{1,0:T(8,128)(2,1)}, bf16[512,1024]{1,0:T(8,128)(2,1)}, u32[]{:S(2)}, u32[]{:S(2)}) collective-permute-start(bf16[512,1024]{1,0:T(8,128)(2,1)} %convolution_convert_fusion.3), channel_id=1, source_target_pairs={{0,4},{4,0},{1,5},{5,1},{2,6},{6,2},{3,7},{7,3},{8,12},{12,8},{9,1... | collective-permute-start | bytes 3145736 | tf_op jit(solution)/shard_map/ppermute | solution.py:18
  394.8 60.4 %collective-permute-start.71 = (bf16[512,1024]{1,0:T(8,128)(2,1)}, bf16[512,1024]{1,0:T(8,128)(2,1)}, u32[]{:S(2)}, u32[]{:S(2)}) collective-permute-start(bf16[512,1024]{1,0:T(8,128)(2,1)} %add_convert_fusion.6), channel_id=1, source_target_pairs={{0,16},{16,0},{1,17},{17,1},{2,18},{18,2},{3,19},{19,3},{4,20},{20... | collective-permute-start | bytes 3145736 | tf_op jit(solution)/shard_map/ppermute | solution.py:18
  420.7 34.0 %collective-permute-start.68 = (bf16[256,1024]{1,0:T(8,128)(2,1)S(1)}, bf16[256,1024]{1,0:T(8,128)(2,1)S(1)}, u32[]{:S(2)}, u32[]{:S(2)}) collective-permute-start(bf16[256,1024]{1,0:T(8,128)(2,1)S(1)} %slice.2321), channel_id=1, source_target_pairs={{0,8},{8,0},{1,9},{9,1},{2,10},{10,2},{3,11},{11,3},{4,12},{12,4},... | collective-permute-start | bytes 1572872 | tf_op jit(solution)/shard_map/ppermute | solution.py:18
  424.0 31.0 %collective-permute-start.69 = (bf16[256,1024]{1,0:T(8,128)(2,1)S(1)}, bf16[256,1024]{1,0:T(8,128)(2,1)S(1)}, u32[]{:S(2)}, u32[]{:S(2)}) collective-permute-start(bf16[256,1024]{1,0:T(8,128)(2,1)S(1)} %pad_maximum_fusion.46), channel_id=1, source_target_pairs={{0,1},{1,0},{2,3},{3,2},{4,5},{5,4},{6,7},{7,6},{8,9},{9,8},{10,11... | collective-permute-start | bytes 1572872 | tf_op jit(solution)/shard_map/ppermute | solution.py:18
  425.5 72.3 %collective-permute-start.76 = (bf16[512,1024]{1,0:T(8,128)(2,1)S(1)}, bf16[512,1024]{1,0:T(8,128)(2,1)S(1)}, u32[]{:S(2)}, u32[]{:S(2)}) collective-permute-start(bf16[512,1024]{1,0:T(8,128)(2,1)S(1)} %copy-done.122), channel_id=1, source_target_pairs={{0,4},{4,0},{1,5},{5,1},{2,6},{6,2},{3,7},{7,3},{8,12},{12,8},{9,1... | collective-permute-start | bytes 3145736 | tf_op jit(solution)/shard_map/ppermute | solution.py:18
  463.6 59.8 %collective-permute-start.79 = (bf16[512,1024]{1,0:T(8,128)(2,1)S(1)}, bf16[512,1024]{1,0:T(8,128)(2,1)S(1)}, u32[]{:S(2)}, u32[]{:S(2)}) collective-permute-start(bf16[512,1024]{1,0:T(8,128)(2,1)S(1)} %copy-done.121), channel_id=1, source_target_pairs={{0,4},{4,0},{1,5},{5,1},{2,6},{6,2},{3,7},{7,3},{8,12},{12,8},{9,1... | collective-permute-start | bytes 3145736 | tf_op jit(solution)/shard_map/ppermute | solution.py:18
  464.2 59.3 %collective-permute-start.80 = (bf16[512,1024]{1,0:T(8,128)(2,1)S(1)}, bf16[512,1024]{1,0:T(8,128)(2,1)S(1)}, u32[]{:S(2)}, u32[]{:S(2)}) collective-permute-start(bf16[512,1024]{1,0:T(8,128)(2,1)S(1)} %add_convert_fusion.3), channel_id=1, source_target_pairs={{0,16},{16,0},{1,17},{17,1},{2,18},{18,2},{3,19},{19,3},{4,20},{20... | collective-permute-start | bytes 3145736 | tf_op jit(solution)/shard_map/ppermute | solution.py:18
  472.5 22.1 %collective-permute-start.75 = (bf16[128,1024]{1,0:T(8,128)(2,1)S(1)}, bf16[128,1024]{1,0:T(8,128)(2,1)S(1)}, u32[]{:S(2)}, u32[]{:S(2)}) collective-permute-start(bf16[128,1024]{1,0:T(8,128)(2,1)S(1)} %get-tuple-element.804), channel_id=1, source_target_pairs={{0,8},{8,0},{1,9},{9,1},{2,10},{10,2},{3,11},{11,3},{4,12},{12,4},... | collective-permute-start | bytes 786440 | tf_op jit(solution)/shard_map/ppermute | solution.py:18
  494.7 28.7 %collective-permute-start.77 = (bf16[256,1024]{1,0:T(8,128)(2,1)S(1)}, bf16[256,1024]{1,0:T(8,128)(2,1)S(1)}, u32[]{:S(2)}, u32[]{:S(2)}) collective-permute-start(bf16[256,1024]{1,0:T(8,128)(2,1)S(1)} %pad_maximum_fusion.47), channel_id=1, source_target_pairs={{0,8},{8,0},{1,9},{9,1},{2,10},{10,2},{3,11},{11,3},{4,12},{12,4},... | collective-permute-start | bytes 1572872 | tf_op jit(solution)/shard_map/ppermute | solution.py:18
  497.2 26.2 %collective-permute-start.78 = (bf16[256,1024]{1,0:T(8,128)(2,1)S(1)}, bf16[256,1024]{1,0:T(8,128)(2,1)S(1)}, u32[]{:S(2)}, u32[]{:S(2)}) collective-permute-start(bf16[256,1024]{1,0:T(8,128)(2,1)S(1)} %pad_maximum_fusion.48), channel_id=1, source_target_pairs={{0,1},{1,0},{2,3},{3,2},{4,5},{5,4},{6,7},{7,6},{8,9},{9,8},{10,11... | collective-permute-start | bytes 1572872 | tf_op jit(solution)/shard_map/ppermute | solution.py:18
  528.4 31.3 %collective-permute-start.83 = (bf16[512,1024]{1,0:T(8,128)(2,1)}, bf16[512,1024]{1,0:T(8,128)(2,1)}, u32[]{:S(2)}, u32[]{:S(2)}) collective-permute-start(bf16[512,1024]{1,0:T(8,128)(2,1)} %convolution_convert_fusion), channel_id=1, source_target_pairs={{0,4},{4,0},{1,5},{5,1},{2,6},{6,2},{3,7},{7,3},{8,12},{12,8},{9,1... | collective-permute-start | bytes 3145736 | tf_op jit(solution)/shard_map/ppermute | solution.py:18
  529.9 52.6 %collective-permute-start.87 = (bf16[256,1024]{1,0:T(8,128)(2,1)}, bf16[256,1024]{1,0:T(8,128)(2,1)}, u32[]{:S(2)}, u32[]{:S(2)}) collective-permute-start(bf16[256,1024]{1,0:T(8,128)(2,1)} %select_convert_fusion.5), channel_id=1, source_target_pairs={{0,8},{8,0},{1,9},{9,1},{2,10},{10,2},{3,11},{11,3},{4,12},{12,4},... | collective-permute-start | bytes 1572872 | tf_op jit(solution)/shard_map/ppermute | solution.py:18
  530.0 48.5 %collective-permute-start.85 = (bf16[512,1024]{1,0:T(8,128)(2,1)}, bf16[512,1024]{1,0:T(8,128)(2,1)}, u32[]{:S(2)}, u32[]{:S(2)}) collective-permute-start(bf16[512,1024]{1,0:T(8,128)(2,1)} %add_convert_fusion.2), channel_id=1, source_target_pairs={{0,16},{16,0},{1,17},{17,1},{2,18},{18,2},{3,19},{19,3},{4,20},{20... | collective-permute-start | bytes 3145736 | tf_op jit(solution)/shard_map/ppermute | solution.py:18
  532.9 71.7 %collective-permute-start.92 = (bf16[256,1024]{1,0:T(8,128)(2,1)}, bf16[256,1024]{1,0:T(8,128)(2,1)}, u32[]{:S(2)}, u32[]{:S(2)}) collective-permute-start(bf16[256,1024]{1,0:T(8,128)(2,1)} %select_convert_fusion.4), channel_id=1, source_target_pairs={{0,8},{8,0},{1,9},{9,1},{2,10},{10,2},{3,11},{11,3},{4,12},{12,4},... | collective-permute-start | bytes 1572872 | tf_op jit(solution)/shard_map/ppermute | solution.py:18
  593.4 26.5 %collective-permute-start.96 = (bf16[512,512]{0,1:T(8,128)(2,1)S(1)}, bf16[512,512]{0,1:T(8,128)(2,1)S(1)}, u32[]{:S(2)}, u32[]{:S(2)}) collective-permute-start(bf16[512,512]{0,1:T(8,128)(2,1)S(1)} %fusion.28), channel_id=1, source_target_pairs={{0,16},{16,0},{1,17},{17,1},{2,18},{18,2},{3,19},{19,3},{4,20},{20... | collective-permute-start | bytes 1572872 | tf_op jit(solution)/shard_map/ppermute | solution.py:18
  595.4 41.2 %collective-permute-start.101 = (bf16[256,1024]{1,0:T(8,128)(2,1)S(1)}, bf16[256,1024]{1,0:T(8,128)(2,1)S(1)}, u32[]{:S(2)}, u32[]{:S(2)}) collective-permute-start(bf16[256,1024]{1,0:T(8,128)(2,1)S(1)} %select_convert_fusion.2), channel_id=1, source_target_pairs={{0,8},{8,0},{1,9},{9,1},{2,10},{10,2},{3,11},{11,3},{4,12},{12,4},... | collective-permute-start | bytes 1572872 | tf_op jit(solution)/shard_map/ppermute | solution.py:18
  613.1 23.6 %collective-permute-start.100 = (f32[4,512]{1,0:T(4,128)S(1)}, f32[4,512]{1,0:T(4,128)S(1)}, u32[]{:S(2)}, u32[]{:S(2)}) collective-permute-start(f32[4,512]{1,0:T(4,128)S(1)} %slice.1252), channel_id=1, source_target_pairs={{0,16},{16,0},{1,17},{17,1},{2,18},{18,2},{3,19},{19,3},{4,20},{20... | collective-permute-start | bytes 24584 | tf_op jit(solution)/shard_map/ppermute | solution.py:18
  621.6 32.3 %collective-permute-start.104 = (bf16[512,512]{0,1:T(8,128)(2,1)S(1)}, bf16[512,512]{0,1:T(8,128)(2,1)S(1)}, u32[]{:S(2)}, u32[]{:S(2)}) collective-permute-start(bf16[512,512]{0,1:T(8,128)(2,1)S(1)} %pad_maximum_fusion.52), channel_id=1, source_target_pairs={{0,4},{4,0},{1,5},{5,1},{2,6},{6,2},{3,7},{7,3},{8,12},{12,8},{9,1... | collective-permute-start | bytes 1572872 | tf_op jit(solution)/shard_map/ppermute | solution.py:18
  631.1 23.2 %collective-permute-start.105 = (bf16[512,512]{0,1:T(8,128)(2,1)S(1)}, bf16[512,512]{0,1:T(8,128)(2,1)S(1)}, u32[]{:S(2)}, u32[]{:S(2)}) collective-permute-start(bf16[512,512]{0,1:T(8,128)(2,1)S(1)} %pad_maximum_fusion.53), channel_id=1, source_target_pairs={{0,4},{4,0},{1,5},{5,1},{2,6},{6,2},{3,7},{7,3},{8,12},{12,8},{9,1... | collective-permute-start | bytes 1572872 | tf_op jit(solution)/shard_map/ppermute | solution.py:18
  633.8 24.2 %collective-permute-start.106 = (bf16[512,512]{0,1:T(8,128)(2,1)S(1)}, bf16[512,512]{0,1:T(8,128)(2,1)S(1)}, u32[]{:S(2)}, u32[]{:S(2)}) collective-permute-start(bf16[512,512]{0,1:T(8,128)(2,1)S(1)} %fusion.29), channel_id=1, source_target_pairs={{0,16},{16,0},{1,17},{17,1},{2,18},{18,2},{3,19},{19,3},{4,20},{20... | collective-permute-start | bytes 1572872 | tf_op jit(solution)/shard_map/ppermute | solution.py:18
  (254 other events, 2650.5 us)

commit v11 on v10

--- a/solution.py
+++ b/solution.py
@@ -312,6 +312,10 @@
         gate_w.end_line()
         gains = gain_steps.finish()
         qk.end_x(1)
+        vo.end_high()
+        vo.end_x(0)
+        vo.start_x(1)
+        gate_w.start_high()
 
         attn_scale = gains[2]
         ffn_scale = gains[3]
@@ -335,10 +339,6 @@
         query, key_proj = projected[:, :head_width], projected[:, head_width:]
 
         def squares_between():
-            vo.end_high()
-            vo.end_x(0)
-            vo.start_x(1)
-            gate_w.start_high()
             up_w.start_line()
 
         squares = pair_sum(

time: 684 us -> 690 us (level)
  waiting for transfers between devices: 301 us -> 310 us
    ppermute x116, waiting for transfers between devices: 301 us -> 310 us  [swap(): return lax.ppermute(value, axis, FLIP)]
    unnamed x421 -> x425, local copies, waits for them, and re-layouts: 26.2 us -> 26.9 us
  transfers between devices with their start and end apart: 116 -> 116, of which waited for: 50 -> 48; matrix products, arithmetic and copies ran while one was open for 31% -> 31% of each run, Pallas kernels for 0% -> 0%
where the time goes in v11:
time: 690 us; the launch traced here: 683 us
  waiting for transfers between devices  310 us (45%)
  matrix products  127 us (18%)
  starting transfers between devices  114 us (17%)
  other arithmetic  68.4 us (10%)
  local copies, waits for them, and re-layouts  58.1 us (8%)
    ppermute x116, waiting for transfers between devices, swap(): return lax.ppermute(value, axis, FLIP)  310 us
    ppermute x116, starting transfers between devices, swap(): return lax.ppermute(value, axis, FLIP)  114 us
    dot_general x28, matrix products, dot_tn(): return jnp.einsum('sr,sc->rc', a, b, preferred_element_type=F32)  45.4 us
    dot_general x24, matrix products, dot_nt(): return jnp.einsum('sc,rc->sr', a, b, preferred_element_type=F32)  35.8 us
    dot_general x12, matrix products, dot(): return jnp.dot(a, b, preferred_element_type=F32)  32.4 us
    unnamed x425, local copies, waits for them, and re-layouts  26.9 us
  transfers between devices with their start and end apart: 116, of which 48 were waited for; matrix products, arithmetic and copies ran while one was open for 31% of the time, Pallas kernels for 0%

profile of v11, /device:TPU:0, one launch (start us, length us, event | category | flops | bytes accessed | tf_op | source)
XLA Modules:
  0.0 682.9 jit_solution(7325712832649018026)
XLA Ops:
  6.0 3.1 collective-permute-start
  22.6 4.4 collective-permute-done.3
  30.1 2.8 collective-permute-start.10
  41.6 6.0 collective-permute-done.9
  52.5 8.0 %collective-permute-done.12 = bf16[512,512]{0,1:T(8,128)(2,1)S(1)} collective-permute-done((bf16[512,512]{0,1:T(8,128)(2,1)S(1)}, bf16[512,512]{0,1:T(8,128)(2,1)S(1)}, u32[]{:S(2)}, u32[]{:S(2)}) %collective-permute-start.12) | collective-permute-done | bytes 524320 | tf_op jit(solution)/shard_map/ppermute | solution.py:18
  60.4 3.1 collective-permute-done.13
  78.7 12.7 %collective-permute-done.18 = bf16[256,1024]{1,0:T(8,128)(2,1)S(1)} collective-permute-done((bf16[256,1024]{1,0:T(8,128)(2,1)}, bf16[256,1024]{1,0:T(8,128)(2,1)S(1)}, u32[]{:S(2)}, u32[]{:S(2)}) %collective-permute-start.18) | collective-permute-done | bytes 524320 | tf_op jit(solution)/shard_map/ppermute | solution.py:18
  91.4 2.8 pad_maximum_fusion
  105.2 3.1 collective-permute-start.30
  123.0 2.8 fusion.130
  129.2 3.4 fusion.213
  132.6 2.9 fusion.4
  139.4 4.0 collective-permute-done.27
  144.9 15.0 %collective-permute-done.29 = bf16[256,1024]{1,0:T(8,128)(2,1)} collective-permute-done((bf16[256,1024]{1,0:T(8,128)(2,1)}, bf16[256,1024]{1,0:T(8,128)(2,1)}, u32[]{:S(2)}, u32[]{:S(2)}) %collective-permute-start.29) | collective-permute-done | bytes 524320 | tf_op jit(solution)/shard_map/ppermute | solution.py:18
  170.3 25.9 %collective-permute-done.33 = bf16[256,1024]{1,0:T(8,128)(2,1)S(1)} collective-permute-done((bf16[256,1024]{1,0:T(8,128)(2,1)S(1)}, bf16[256,1024]{1,0:T(8,128)(2,1)S(1)}, u32[]{:S(2)}, u32[]{:S(2)}) %collective-permute-start.33) | collective-permute-done | bytes 524320 | tf_op jit(solution)/shard_map/ppermute | solution.py:18
  200.8 8.8 %collective-permute-done.36 = bf16[512,1024]{1,0:T(8,128)(2,1)S(1)} collective-permute-done((bf16[512,1024]{1,0:T(8,128)(2,1)S(1)}, bf16[512,1024]{1,0:T(8,128)(2,1)S(1)}, u32[]{:S(2)}, u32[]{:S(2)}) %collective-permute-start.36) | collective-permute-done | bytes 1048608 | tf_op jit(solution)/shard_map/ppermute | solution.py:18
  211.2 4.0 collective-permute-done.39
  217.5 6.7 collective-permute-done.40
  224.2 15.1 %collective-permute-done.41 = bf16[128,1024]{1,0:T(8,128)(2,1)S(1)} collective-permute-done((bf16[128,1024]{1,0:T(8,128)(2,1)S(1)}, bf16[128,1024]{1,0:T(8,128)(2,1)S(1)}, u32[]{:S(2)}, u32[]{:S(2)}) %collective-permute-start.41) | collective-permute-done | bytes 262176 | tf_op jit(solution)/shard_map/ppermute | solution.py:18
  244.0 25.4 %collective-permute-done.42 = bf16[256,1024]{1,0:T(8,128)(2,1)S(1)} collective-permute-done((bf16[256,1024]{1,0:T(8,128)(2,1)S(1)}, bf16[256,1024]{1,0:T(8,128)(2,1)S(1)}, u32[]{:S(2)}, u32[]{:S(2)}) %collective-permute-start.42) | collective-permute-done | bytes 524320 | tf_op jit(solution)/shard_map/ppermute | solution.py:18
  278.8 3.6 fusion.190
  282.4 5.4 multiply_convert_fusion.2
  287.8 9.2 %collective-permute-done.49 = bf16[512,1024]{1,0:T(8,128)(2,1)S(1)} collective-permute-done((bf16[512,1024]{1,0:T(8,128)(2,1)S(1)}, bf16[512,1024]{1,0:T(8,128)(2,1)S(1)}, u32[]{:S(2)}, u32[]{:S(2)}) %collective-permute-start.49) | collective-permute-done | bytes 1048608 | tf_op jit(solution)/shard_map/ppermute | solution.py:18
  305.8 12.5 %collective-permute-done.52 = bf16[256,1024]{1,0:T(8,128)(2,1)S(1)} collective-permute-done((bf16[256,1024]{1,0:T(8,128)(2,1)S(1)}, bf16[256,1024]{1,0:T(8,128)(2,1)S(1)}, u32[]{:S(2)}, u32[]{:S(2)}) %collective-permute-start.52) | collective-permute-done | bytes 524320 | tf_op jit(solution)/shard_map/ppermute | solution.py:18
  322.2 4.2 collective-permute-done.54
  331.6 4.6 collective-permute-done.56
  340.0 7.7 %collective-permute-done.58 = bf16[256,1024]{1,0:T(8,128)(2,1)S(1)} collective-permute-done((bf16[256,1024]{1,0:T(8,128)(2,1)S(1)}, bf16[256,1024]{1,0:T(8,128)(2,1)S(1)}, u32[]{:S(2)}, u32[]{:S(2)}) %collective-permute-start.58) | collective-permute-done | bytes 524320 | tf_op jit(solution)/shard_map/ppermute | solution.py:18
  357.0 3.0 constant_dynamic-update-slice_fusion.60
  360.0 3.5 convolution_convert_fusion.4
  367.7 2.9 fusion.20
  372.6 3.9 fusion.223
  376.6 5.6 multiply_convert_fusion
  391.3 2.7 fusion.38
  401.4 4.2 fusion.60
  411.7 4.0 add_convert_fusion.5
  416.3 3.0 fusion.58
  420.7 2.7 fusion.64
  431.9 28.3 %collective-permute-done.68 = bf16[256,1024]{1,0:T(8,128)(2,1)S(1)} collective-permute-done((bf16[256,1024]{1,0:T(8,128)(2,1)S(1)}, bf16[256,1024]{1,0:T(8,128)(2,1)S(1)}, u32[]{:S(2)}, u32[]{:S(2)}) %collective-permute-start.68) | collective-permute-done | bytes 524320 | tf_op jit(solution)/shard_map/ppermute | solution.py:18
  470.1 2.8 collective-permute-start.80
  477.2 5.7 collective-permute-done.74
  483.0 17.3 %collective-permute-done.75 = bf16[128,1024]{1,0:T(8,128)(2,1)S(1)} collective-permute-done((bf16[128,1024]{1,0:T(8,128)(2,1)S(1)}, bf16[128,1024]{1,0:T(8,128)(2,1)S(1)}, u32[]{:S(2)}, u32[]{:S(2)}) %collective-permute-start.75) | collective-permute-done | bytes 262176 | tf_op jit(solution)/shard_map/ppermute | solution.py:18
  503.6 25.7 %collective-permute-done.77 = bf16[256,1024]{1,0:T(8,128)(2,1)S(1)} collective-permute-done((bf16[256,1024]{1,0:T(8,128)(2,1)S(1)}, bf16[256,1024]{1,0:T(8,128)(2,1)S(1)}, u32[]{:S(2)}, u32[]{:S(2)}) %collective-permute-start.77) | collective-permute-done | bytes 524320 | tf_op jit(solution)/shard_map/ppermute | solution.py:18
  546.5 3.1 fusion.5
  628.0 8.4 %collective-permute-done.98 = bf16[256,1024]{1,0:T(8,128)(2,1)S(1)} collective-permute-done((bf16[256,1024]{1,0:T(8,128)(2,1)S(1)}, bf16[256,1024]{1,0:T(8,128)(2,1)S(1)}, u32[]{:S(2)}, u32[]{:S(2)}) %collective-permute-start.98) | collective-permute-done | bytes 524320 | tf_op jit(solution)/shard_map/ppermute | solution.py:18
  643.0 4.7 collective-permute-done.102
  648.0 8.1 %collective-permute-done.103 = bf16[128,1024]{1,0:T(8,128)(2,1)S(1)} collective-permute-done((bf16[128,1024]{1,0:T(8,128)(2,1)S(1)}, bf16[128,1024]{1,0:T(8,128)(2,1)S(1)}, u32[]{:S(2)}, u32[]{:S(2)}) %collective-permute-start.103) | collective-permute-done | bytes 262176 | tf_op jit(solution)/shard_map/ppermute | solution.py:18
  658.9 4.7 collective-permute-done.106
  668.8 4.5 collective-permute-done.109
  (964 shorter events, 321.3 us)
Async XLA Ops:
  10.0 19.2 %collective-permute-start.5 = (bf16[128,1024]{1,0:T(8,128)(2,1)}, bf16[128,1024]{1,0:T(8,128)(2,1)}, u32[]{:S(2)}, u32[]{:S(2)}) collective-permute-start(bf16[128,1024]{1,0:T(8,128)(2,1)} %pad_maximum_fusion.58), channel_id=1, source_target_pairs={{0,1},{1,0},{2,3},{3,2},{4,5},{5,4},{6,7},{7,6},{8,9},{9,8},{10,11... | collective-permute-start | bytes 786440 | tf_op jit(solution)/shard_map/ppermute | solution.py:18
  17.9 21.5 %collective-permute-start.8 = (bf16[128,6144]{1,0:T(8,128)(2,1)S(1)}, bf16[128,6144]{1,0:T(8,128)(2,1)S(1)}, u32[]{:S(2)}, u32[]{:S(2)}) collective-permute-start(bf16[128,6144]{1,0:T(8,128)(2,1)S(1)} %copy-done.111), channel_id=1, source_target_pairs={{0,2},{2,0},{1,3},{3,1},{4,6},{6,4},{5,7},{7,5},{8,10},{10,8},{9,1... | collective-permute-start | bytes 4718600 | tf_op jit(solution)/shard_map/ppermute | solution.py:18
  30.1 20.6 %collective-permute-start.10 = (f32[4,512]{1,0:T(4,128)S(1)}, f32[4,512]{1,0:T(4,128)S(1)}, u32[]{:S(2)}, u32[]{:S(2)}) collective-permute-start(f32[4,512]{1,0:T(4,128)S(1)} %pad_maximum_fusion.76), channel_id=1, source_target_pairs={{0,16},{16,0},{1,17},{17,1},{2,18},{18,2},{3,19},{19,3},{4,20},{20... | collective-permute-start | bytes 24584 | tf_op jit(solution)/shard_map/ppermute | solution.py:18
  32.9 18.4 %collective-permute-start.11 = (bf16[512,512]{0,1:T(8,128)(2,1)S(1)}, bf16[512,512]{0,1:T(8,128)(2,1)S(1)}, u32[]{:S(2)}, u32[]{:S(2)}) collective-permute-start(bf16[512,512]{0,1:T(8,128)(2,1)S(1)} %pad_maximum_fusion.36), channel_id=1, source_target_pairs={{0,4},{4,0},{1,5},{5,1},{2,6},{6,2},{3,7},{7,3},{8,12},{12,8},{9,1... | collective-permute-start | bytes 1572872 | tf_op jit(solution)/shard_map/ppermute | solution.py:18
  36.8 23.6 %collective-permute-start.12 = (bf16[512,512]{0,1:T(8,128)(2,1)S(1)}, bf16[512,512]{0,1:T(8,128)(2,1)S(1)}, u32[]{:S(2)}, u32[]{:S(2)}) collective-permute-start(bf16[512,512]{0,1:T(8,128)(2,1)S(1)} %pad_maximum_fusion.36), channel_id=1, source_target_pairs={{0,16},{16,0},{1,17},{17,1},{2,18},{18,2},{3,19},{19,3},{4,20},{20... | collective-permute-start | bytes 1572872 | tf_op jit(solution)/shard_map/ppermute | solution.py:18
  39.8 23.7 %collective-permute-start.13 = (bf16[256,1024]{1,0:T(8,128)(2,1)S(1)}, bf16[256,1024]{1,0:T(8,128)(2,1)S(1)}, u32[]{:S(2)}, u32[]{:S(2)}) collective-permute-start(bf16[256,1024]{1,0:T(8,128)(2,1)S(1)} %pad_maximum_fusion.37), channel_id=1, source_target_pairs={{0,8},{8,0},{1,9},{9,1},{2,10},{10,2},{3,11},{11,3},{4,12},{12,4},... | collective-permute-start | bytes 1572872 | tf_op jit(solution)/shard_map/ppermute | solution.py:18
  67.6 23.8 %collective-permute-start.18 = (bf16[256,1024]{1,0:T(8,128)(2,1)}, bf16[256,1024]{1,0:T(8,128)(2,1)S(1)}, u32[]{:S(2)}, u32[]{:S(2)}) collective-permute-start(bf16[256,1024]{1,0:T(8,128)(2,1)} %broadcast_select_fusion.11), channel_id=1, source_target_pairs={{0,8},{8,0},{1,9},{9,1},{2,10},{10,2},{3,11},{11,3},{4,12},{12,4},... | collective-permute-start | bytes 1572872 | tf_op jit(solution)/shard_map/ppermute | solution.py:18
  69.2 22.2 %collective-permute-start.20 = (bf16[512,512]{0,1:T(8,128)(2,1)}, bf16[512,512]{0,1:T(8,128)(2,1)S(1)}, u32[]{:S(2)}, u32[]{:S(2)}) collective-permute-start(bf16[512,512]{0,1:T(8,128)(2,1)} %copy-done.142), channel_id=1, source_target_pairs={{0,4},{4,0},{1,5},{5,1},{2,6},{6,2},{3,7},{7,3},{8,12},{12,8},{9,1... | collective-permute-start | bytes 1572872 | tf_op jit(solution)/shard_map/ppermute | solution.py:18
  70.8 25.7 %collective-permute-start.21 = (bf16[512,512]{0,1:T(8,128)(2,1)}, bf16[512,512]{0,1:T(8,128)(2,1)S(1)}, u32[]{:S(2)}, u32[]{:S(2)}) collective-permute-start(bf16[512,512]{0,1:T(8,128)(2,1)} %pad_maximum_fusion.39), channel_id=1, source_target_pairs={{0,16},{16,0},{1,17},{17,1},{2,18},{18,2},{3,19},{19,3},{4,20},{20... | collective-permute-start | bytes 1572872 | tf_op jit(solution)/shard_map/ppermute | solution.py:18
  77.2 26.0 %collective-permute-start.22 = (bf16[512,512]{0,1:T(8,128)(2,1)S(1)}, bf16[512,512]{0,1:T(8,128)(2,1)S(1)}, u32[]{:S(2)}, u32[]{:S(2)}) collective-permute-start(bf16[512,512]{0,1:T(8,128)(2,1)S(1)} %copy-done.136), channel_id=1, source_target_pairs={{0,4},{4,0},{1,5},{5,1},{2,6},{6,2},{3,7},{7,3},{8,12},{12,8},{9,1... | collective-permute-start | bytes 1572872 | tf_op jit(solution)/shard_map/ppermute | solution.py:18
  105.2 54.7 %collective-permute-start.30 = (bf16[512,1024]{1,0:T(8,128)(2,1)}, bf16[512,1024]{1,0:T(8,128)(2,1)}, u32[]{:S(2)}, u32[]{:S(2)}) collective-permute-start(bf16[512,1024]{1,0:T(8,128)(2,1)} %pad_maximum_fusion.16), channel_id=1, source_target_pairs={{0,16},{16,0},{1,17},{17,1},{2,18},{18,2},{3,19},{19,3},{4,20},{20... | collective-permute-start | bytes 3145736 | tf_op jit(solution)/shard_map/ppermute | solution.py:18
  112.8 30.6 %collective-permute-start.27 = (bf16[256,1024]{1,0:T(8,128)(2,1)}, bf16[256,1024]{1,0:T(8,128)(2,1)}, u32[]{:S(2)}, u32[]{:S(2)}) collective-permute-start(bf16[256,1024]{1,0:T(8,128)(2,1)} %broadcast_select_fusion.7), channel_id=1, source_target_pairs={{0,8},{8,0},{1,9},{9,1},{2,10},{10,2},{3,11},{11,3},{4,12},{12,4},... | collective-permute-start | bytes 1572872 | tf_op jit(solution)/shard_map/ppermute | solution.py:18
  113.8 31.1 %collective-permute-start.28 = (bf16[512,1024]{1,0:T(8,128)(2,1)}, bf16[512,1024]{1,0:T(8,128)(2,1)}, u32[]{:S(2)}, u32[]{:S(2)}) collective-permute-start(bf16[512,1024]{1,0:T(8,128)(2,1)} %pad_maximum_fusion.16), channel_id=1, source_target_pairs={{0,4},{4,0},{1,5},{5,1},{2,6},{6,2},{3,7},{7,3},{8,12},{12,8},{9,1... | collective-permute-start | bytes 3145736 | tf_op jit(solution)/shard_map/ppermute | solution.py:18
  115.1 44.9 %collective-permute-start.29 = (bf16[256,1024]{1,0:T(8,128)(2,1)}, bf16[256,1024]{1,0:T(8,128)(2,1)}, u32[]{:S(2)}, u32[]{:S(2)}) collective-permute-start(bf16[256,1024]{1,0:T(8,128)(2,1)} %broadcast_select_fusion.6), channel_id=1, source_target_pairs={{0,8},{8,0},{1,9},{9,1},{2,10},{10,2},{3,11},{11,3},{4,12},{12,4},... | collective-permute-start | bytes 1572872 | tf_op jit(solution)/shard_map/ppermute | solution.py:18
  161.0 39.8 %collective-permute-start.35 = (bf16[512,1024]{1,0:T(8,128)(2,1)S(1)}, bf16[512,1024]{1,0:T(8,128)(2,1)S(1)}, u32[]{:S(2)}, u32[]{:S(2)}) collective-permute-start(bf16[512,1024]{1,0:T(8,128)(2,1)S(1)} %pad_maximum_fusion.19), channel_id=1, source_target_pairs={{0,4},{4,0},{1,5},{5,1},{2,6},{6,2},{3,7},{7,3},{8,12},{12,8},{9,1... | collective-permute-start | bytes 3145736 | tf_op jit(solution)/shard_map/ppermute | solution.py:18
  162.3 47.3 %collective-permute-start.36 = (bf16[512,1024]{1,0:T(8,128)(2,1)S(1)}, bf16[512,1024]{1,0:T(8,128)(2,1)S(1)}, u32[]{:S(2)}, u32[]{:S(2)}) collective-permute-start(bf16[512,1024]{1,0:T(8,128)(2,1)S(1)} %pad_maximum_fusion.19), channel_id=1, source_target_pairs={{0,16},{16,0},{1,17},{17,1},{2,18},{18,2},{3,19},{19,3},{4,20},{20... | collective-permute-start | bytes 3145736 | tf_op jit(solution)/shard_map/ppermute | solution.py:18
  162.3 47.3 %collective-permute-start.37 = (bf16[512,1024]{1,0:T(8,128)(2,1)}, bf16[512,1024]{1,0:T(8,128)(2,1)S(1)}, u32[]{:S(2)}, u32[]{:S(2)}) collective-permute-start(bf16[512,1024]{1,0:T(8,128)(2,1)} %collective-permute-done.30), channel_id=1, source_target_pairs={{0,4},{4,0},{1,5},{5,1},{2,6},{6,2},{3,7},{7,3},{8,12},{12,8},{9,1... | collective-permute-start | bytes 3145736 | tf_op jit(solution)/shard_map/ppermute | solution.py:18
  166.0 30.2 %collective-permute-start.33 = (bf16[256,1024]{1,0:T(8,128)(2,1)S(1)}, bf16[256,1024]{1,0:T(8,128)(2,1)S(1)}, u32[]{:S(2)}, u32[]{:S(2)}) collective-permute-start(bf16[256,1024]{1,0:T(8,128)(2,1)S(1)} %slice.2323), channel_id=1, source_target_pairs={{0,8},{8,0},{1,9},{9,1},{2,10},{10,2},{3,11},{11,3},{4,12},{12,4},... | collective-permute-start | bytes 1572872 | tf_op jit(solution)/shard_map/ppermute | solution.py:18
  168.6 27.8 %collective-permute-start.34 = (bf16[256,1024]{1,0:T(8,128)(2,1)S(1)}, bf16[256,1024]{1,0:T(8,128)(2,1)S(1)}, u32[]{:S(2)}, u32[]{:S(2)}) collective-permute-start(bf16[256,1024]{1,0:T(8,128)(2,1)S(1)} %pad_maximum_fusion.40), channel_id=1, source_target_pairs={{0,1},{1,0},{2,3},{3,2},{4,5},{5,4},{6,7},{7,6},{8,9},{9,8},{10,11... | collective-permute-start | bytes 1572872 | tf_op jit(solution)/shard_map/ppermute | solution.py:18
  209.5 59.9 %collective-permute-start.44 = (bf16[512,1024]{1,0:T(8,128)(2,1)S(1)}, bf16[512,1024]{1,0:T(8,128)(2,1)S(1)}, u32[]{:S(2)}, u32[]{:S(2)}) collective-permute-start(bf16[512,1024]{1,0:T(8,128)(2,1)S(1)} %collective-permute-done.36), channel_id=1, source_target_pairs={{0,4},{4,0},{1,5},{5,1},{2,6},{6,2},{3,7},{7,3},{8,12},{12,8},{9,1... | collective-permute-start | bytes 3145736 | tf_op jit(solution)/shard_map/ppermute | solution.py:18
  211.1 58.3 %collective-permute-start.45 = (bf16[512,1024]{1,0:T(8,128)(2,1)S(1)}, bf16[512,1024]{1,0:T(8,128)(2,1)S(1)}, u32[]{:S(2)}, u32[]{:S(2)}) collective-permute-start(bf16[512,1024]{1,0:T(8,128)(2,1)S(1)} %pad_maximum_fusion.20), channel_id=1, source_target_pairs={{0,16},{16,0},{1,17},{17,1},{2,18},{18,2},{3,19},{19,3},{4,20},{20... | collective-permute-start | bytes 3145736 | tf_op jit(solution)/shard_map/ppermute | solution.py:18
  217.5 21.8 %collective-permute-start.41 = (bf16[128,1024]{1,0:T(8,128)(2,1)S(1)}, bf16[128,1024]{1,0:T(8,128)(2,1)S(1)}, u32[]{:S(2)}, u32[]{:S(2)}) collective-permute-start(bf16[128,1024]{1,0:T(8,128)(2,1)S(1)} %get-tuple-element.660), channel_id=1, source_target_pairs={{0,8},{8,0},{1,9},{9,1},{2,10},{10,2},{3,11},{11,3},{4,12},{12,4},... | collective-permute-start | bytes 786440 | tf_op jit(solution)/shard_map/ppermute | solution.py:18
  239.4 30.1 %collective-permute-start.42 = (bf16[256,1024]{1,0:T(8,128)(2,1)S(1)}, bf16[256,1024]{1,0:T(8,128)(2,1)S(1)}, u32[]{:S(2)}, u32[]{:S(2)}) collective-permute-start(bf16[256,1024]{1,0:T(8,128)(2,1)S(1)} %pad_maximum_fusion.41), channel_id=1, source_target_pairs={{0,8},{8,0},{1,9},{9,1},{2,10},{10,2},{3,11},{11,3},{4,12},{12,4},... | collective-permute-start | bytes 1572872 | tf_op jit(solution)/shard_map/ppermute | solution.py:18
  241.9 27.5 %collective-permute-start.43 = (bf16[256,1024]{1,0:T(8,128)(2,1)S(1)}, bf16[256,1024]{1,0:T(8,128)(2,1)S(1)}, u32[]{:S(2)}, u32[]{:S(2)}) collective-permute-start(bf16[256,1024]{1,0:T(8,128)(2,1)S(1)} %pad_maximum_fusion.42), channel_id=1, source_target_pairs={{0,1},{1,0},{2,3},{3,2},{4,5},{5,4},{6,7},{7,6},{8,9},{9,8},{10,11... | collective-permute-start | bytes 1572872 | tf_op jit(solution)/shard_map/ppermute | solution.py:18
  243.5 26.2 %collective-permute-start.46 = (bf16[512,1024]{1,0:T(8,128)(2,1)S(1)}, bf16[512,1024]{1,0:T(8,128)(2,1)S(1)}, u32[]{:S(2)}, u32[]{:S(2)}) collective-permute-start(bf16[512,1024]{1,0:T(8,128)(2,1)S(1)} %pad_maximum_fusion.20), channel_id=1, source_target_pairs={{0,4},{4,0},{1,5},{5,1},{2,6},{6,2},{3,7},{7,3},{8,12},{12,8},{9,1... | collective-permute-start | bytes 3145736 | tf_op jit(solution)/shard_map/ppermute | solution.py:18
  271.9 25.1 %collective-permute-start.49 = (bf16[512,1024]{1,0:T(8,128)(2,1)S(1)}, bf16[512,1024]{1,0:T(8,128)(2,1)S(1)}, u32[]{:S(2)}, u32[]{:S(2)}) collective-permute-start(bf16[512,1024]{1,0:T(8,128)(2,1)S(1)} %collective-permute-done.45), channel_id=1, source_target_pairs={{0,4},{4,0},{1,5},{5,1},{2,6},{6,2},{3,7},{7,3},{8,12},{12,8},{9,1... | collective-permute-start | bytes 3145736 | tf_op jit(solution)/shard_map/ppermute | solution.py:18
  370.5 26.1 %collective-permute-start.63 = (bf16[512,1024]{1,0:T(8,128)(2,1)S(1)}, bf16[512,1024]{1,0:T(8,128)(2,1)S(1)}, u32[]{:S(2)}, u32[]{:S(2)}) collective-permute-start(bf16[512,1024]{1,0:T(8,128)(2,1)S(1)} %convolution_convert_fusion.5), channel_id=1, source_target_pairs={{0,4},{4,0},{1,5},{5,1},{2,6},{6,2},{3,7},{7,3},{8,12},{12,8},{9,1... | collective-permute-start | bytes 3145736 | tf_op jit(solution)/shard_map/ppermute | solution.py:18
  371.7 57.0 %collective-permute-start.67 = (bf16[512,1024]{1,0:T(8,128)(2,1)}, bf16[512,1024]{1,0:T(8,128)(2,1)}, u32[]{:S(2)}, u32[]{:S(2)}) collective-permute-start(bf16[512,1024]{1,0:T(8,128)(2,1)} %convolution_convert_fusion.4), channel_id=1, source_target_pairs={{0,4},{4,0},{1,5},{5,1},{2,6},{6,2},{3,7},{7,3},{8,12},{12,8},{9,1... | collective-permute-start | bytes 3145736 | tf_op jit(solution)/shard_map/ppermute | solution.py:18
  399.2 61.5 %collective-permute-start.70 = (bf16[512,1024]{1,0:T(8,128)(2,1)}, bf16[512,1024]{1,0:T(8,128)(2,1)}, u32[]{:S(2)}, u32[]{:S(2)}) collective-permute-start(bf16[512,1024]{1,0:T(8,128)(2,1)} %convolution_convert_fusion.3), channel_id=1, source_target_pairs={{0,4},{4,0},{1,5},{5,1},{2,6},{6,2},{3,7},{7,3},{8,12},{12,8},{9,1... | collective-permute-start | bytes 3145736 | tf_op jit(solution)/shard_map/ppermute | solution.py:18
  400.3 60.4 %collective-permute-start.71 = (bf16[512,1024]{1,0:T(8,128)(2,1)}, bf16[512,1024]{1,0:T(8,128)(2,1)}, u32[]{:S(2)}, u32[]{:S(2)}) collective-permute-start(bf16[512,1024]{1,0:T(8,128)(2,1)} %add_convert_fusion.6), channel_id=1, source_target_pairs={{0,16},{16,0},{1,17},{17,1},{2,18},{18,2},{3,19},{19,3},{4,20},{20... | collective-permute-start | bytes 3145736 | tf_op jit(solution)/shard_map/ppermute | solution.py:18
  425.4 34.8 %collective-permute-start.68 = (bf16[256,1024]{1,0:T(8,128)(2,1)S(1)}, bf16[256,1024]{1,0:T(8,128)(2,1)S(1)}, u32[]{:S(2)}, u32[]{:S(2)}) collective-permute-start(bf16[256,1024]{1,0:T(8,128)(2,1)S(1)} %slice.2321), channel_id=1, source_target_pairs={{0,8},{8,0},{1,9},{9,1},{2,10},{10,2},{3,11},{11,3},{4,12},{12,4},... | collective-permute-start | bytes 1572872 | tf_op jit(solution)/shard_map/ppermute | solution.py:18
  428.7 31.8 %collective-permute-start.69 = (bf16[256,1024]{1,0:T(8,128)(2,1)S(1)}, bf16[256,1024]{1,0:T(8,128)(2,1)S(1)}, u32[]{:S(2)}, u32[]{:S(2)}) collective-permute-start(bf16[256,1024]{1,0:T(8,128)(2,1)S(1)} %pad_maximum_fusion.46), channel_id=1, source_target_pairs={{0,1},{1,0},{2,3},{3,2},{4,5},{5,4},{6,7},{7,6},{8,9},{9,8},{10,11... | collective-permute-start | bytes 1572872 | tf_op jit(solution)/shard_map/ppermute | solution.py:18
  430.3 73.3 %collective-permute-start.76 = (bf16[512,1024]{1,0:T(8,128)(2,1)S(1)}, bf16[512,1024]{1,0:T(8,128)(2,1)S(1)}, u32[]{:S(2)}, u32[]{:S(2)}) collective-permute-start(bf16[512,1024]{1,0:T(8,128)(2,1)S(1)} %copy-done.124), channel_id=1, source_target_pairs={{0,4},{4,0},{1,5},{5,1},{2,6},{6,2},{3,7},{7,3},{8,12},{12,8},{9,1... | collective-permute-start | bytes 3145736 | tf_op jit(solution)/shard_map/ppermute | solution.py:18
  469.1 60.2 %collective-permute-start.79 = (bf16[512,1024]{1,0:T(8,128)(2,1)S(1)}, bf16[512,1024]{1,0:T(8,128)(2,1)S(1)}, u32[]{:S(2)}, u32[]{:S(2)}) collective-permute-start(bf16[512,1024]{1,0:T(8,128)(2,1)S(1)} %copy-done.123), channel_id=1, source_target_pairs={{0,4},{4,0},{1,5},{5,1},{2,6},{6,2},{3,7},{7,3},{8,12},{12,8},{9,1... | collective-permute-start | bytes 3145736 | tf_op jit(solution)/shard_map/ppermute | solution.py:18
  470.1 59.3 %collective-permute-start.80 = (bf16[512,1024]{1,0:T(8,128)(2,1)S(1)}, bf16[512,1024]{1,0:T(8,128)(2,1)S(1)}, u32[]{:S(2)}, u32[]{:S(2)}) collective-permute-start(bf16[512,1024]{1,0:T(8,128)(2,1)S(1)} %add_convert_fusion.3), channel_id=1, source_target_pairs={{0,16},{16,0},{1,17},{17,1},{2,18},{18,2},{3,19},{19,3},{4,20},{20... | collective-permute-start | bytes 3145736 | tf_op jit(solution)/shard_map/ppermute | solution.py:18
  477.1 23.2 %collective-permute-start.75 = (bf16[128,1024]{1,0:T(8,128)(2,1)S(1)}, bf16[128,1024]{1,0:T(8,128)(2,1)S(1)}, u32[]{:S(2)}, u32[]{:S(2)}) collective-permute-start(bf16[128,1024]{1,0:T(8,128)(2,1)S(1)} %get-tuple-element.804), channel_id=1, source_target_pairs={{0,8},{8,0},{1,9},{9,1},{2,10},{10,2},{3,11},{11,3},{4,12},{12,4},... | collective-permute-start | bytes 786440 | tf_op jit(solution)/shard_map/ppermute | solution.py:18
  500.4 28.9 %collective-permute-start.77 = (bf16[256,1024]{1,0:T(8,128)(2,1)S(1)}, bf16[256,1024]{1,0:T(8,128)(2,1)S(1)}, u32[]{:S(2)}, u32[]{:S(2)}) collective-permute-start(bf16[256,1024]{1,0:T(8,128)(2,1)S(1)} %pad_maximum_fusion.47), channel_id=1, source_target_pairs={{0,8},{8,0},{1,9},{9,1},{2,10},{10,2},{3,11},{11,3},{4,12},{12,4},... | collective-permute-start | bytes 1572872 | tf_op jit(solution)/shard_map/ppermute | solution.py:18
  502.9 26.3 %collective-permute-start.78 = (bf16[256,1024]{1,0:T(8,128)(2,1)S(1)}, bf16[256,1024]{1,0:T(8,128)(2,1)S(1)}, u32[]{:S(2)}, u32[]{:S(2)}) collective-permute-start(bf16[256,1024]{1,0:T(8,128)(2,1)S(1)} %pad_maximum_fusion.48), channel_id=1, source_target_pairs={{0,1},{1,0},{2,3},{3,2},{4,5},{5,4},{6,7},{7,6},{8,9},{9,8},{10,11... | collective-permute-start | bytes 1572872 | tf_op jit(solution)/shard_map/ppermute | solution.py:18
  534.3 30.0 %collective-permute-start.83 = (bf16[512,1024]{1,0:T(8,128)(2,1)}, bf16[512,1024]{1,0:T(8,128)(2,1)}, u32[]{:S(2)}, u32[]{:S(2)}) collective-permute-start(bf16[512,1024]{1,0:T(8,128)(2,1)} %convolution_convert_fusion), channel_id=1, source_target_pairs={{0,4},{4,0},{1,5},{5,1},{2,6},{6,2},{3,7},{7,3},{8,12},{12,8},{9,1... | collective-permute-start | bytes 3145736 | tf_op jit(solution)/shard_map/ppermute | solution.py:18
  535.4 52.6 %collective-permute-start.87 = (bf16[256,1024]{1,0:T(8,128)(2,1)}, bf16[256,1024]{1,0:T(8,128)(2,1)}, u32[]{:S(2)}, u32[]{:S(2)}) collective-permute-start(bf16[256,1024]{1,0:T(8,128)(2,1)} %select_convert_fusion.5), channel_id=1, source_target_pairs={{0,8},{8,0},{1,9},{9,1},{2,10},{10,2},{3,11},{11,3},{4,12},{12,4},... | collective-permute-start | bytes 1572872 | tf_op jit(solution)/shard_map/ppermute | solution.py:18
  535.4 48.5 %collective-permute-start.85 = (bf16[512,1024]{1,0:T(8,128)(2,1)}, bf16[512,1024]{1,0:T(8,128)(2,1)}, u32[]{:S(2)}, u32[]{:S(2)}) collective-permute-start(bf16[512,1024]{1,0:T(8,128)(2,1)} %add_convert_fusion.2), channel_id=1, source_target_pairs={{0,16},{16,0},{1,17},{17,1},{2,18},{18,2},{3,19},{19,3},{4,20},{20... | collective-permute-start | bytes 3145736 | tf_op jit(solution)/shard_map/ppermute | solution.py:18
  537.6 72.8 %collective-permute-start.92 = (bf16[256,1024]{1,0:T(8,128)(2,1)}, bf16[256,1024]{1,0:T(8,128)(2,1)}, u32[]{:S(2)}, u32[]{:S(2)}) collective-permute-start(bf16[256,1024]{1,0:T(8,128)(2,1)} %select_convert_fusion.4), channel_id=1, source_target_pairs={{0,8},{8,0},{1,9},{9,1},{2,10},{10,2},{3,11},{11,3},{4,12},{12,4},... | collective-permute-start | bytes 1572872 | tf_op jit(solution)/shard_map/ppermute | solution.py:18
  598.7 26.5 %collective-permute-start.96 = (bf16[512,512]{0,1:T(8,128)(2,1)S(1)}, bf16[512,512]{0,1:T(8,128)(2,1)S(1)}, u32[]{:S(2)}, u32[]{:S(2)}) collective-permute-start(bf16[512,512]{0,1:T(8,128)(2,1)S(1)} %fusion.28), channel_id=1, source_target_pairs={{0,16},{16,0},{1,17},{17,1},{2,18},{18,2},{3,19},{19,3},{4,20},{20... | collective-permute-start | bytes 1572872 | tf_op jit(solution)/shard_map/ppermute | solution.py:18
  600.8 40.5 %collective-permute-start.101 = (bf16[256,1024]{1,0:T(8,128)(2,1)S(1)}, bf16[256,1024]{1,0:T(8,128)(2,1)S(1)}, u32[]{:S(2)}, u32[]{:S(2)}) collective-permute-start(bf16[256,1024]{1,0:T(8,128)(2,1)S(1)} %select_convert_fusion.2), channel_id=1, source_target_pairs={{0,8},{8,0},{1,9},{9,1},{2,10},{10,2},{3,11},{11,3},{4,12},{12,4},... | collective-permute-start | bytes 1572872 | tf_op jit(solution)/shard_map/ppermute | solution.py:18
  618.0 23.2 %collective-permute-start.100 = (f32[4,512]{1,0:T(4,128)S(1)}, f32[4,512]{1,0:T(4,128)S(1)}, u32[]{:S(2)}, u32[]{:S(2)}) collective-permute-start(f32[4,512]{1,0:T(4,128)S(1)} %slice.1252), channel_id=1, source_target_pairs={{0,16},{16,0},{1,17},{17,1},{2,18},{18,2},{3,19},{19,3},{4,20},{20... | collective-permute-start | bytes 24584 | tf_op jit(solution)/shard_map/ppermute | solution.py:18
  627.3 31.3 %collective-permute-start.104 = (bf16[512,512]{0,1:T(8,128)(2,1)S(1)}, bf16[512,512]{0,1:T(8,128)(2,1)S(1)}, u32[]{:S(2)}, u32[]{:S(2)}) collective-permute-start(bf16[512,512]{0,1:T(8,128)(2,1)S(1)} %pad_maximum_fusion.52), channel_id=1, source_target_pairs={{0,4},{4,0},{1,5},{5,1},{2,6},{6,2},{3,7},{7,3},{8,12},{12,8},{9,1... | collective-permute-start | bytes 1572872 | tf_op jit(solution)/shard_map/ppermute | solution.py:18
  636.4 22.5 %collective-permute-start.105 = (bf16[512,512]{0,1:T(8,128)(2,1)S(1)}, bf16[512,512]{0,1:T(8,128)(2,1)S(1)}, u32[]{:S(2)}, u32[]{:S(2)}) collective-permute-start(bf16[512,512]{0,1:T(8,128)(2,1)S(1)} %pad_maximum_fusion.53), channel_id=1, source_target_pairs={{0,4},{4,0},{1,5},{5,1},{2,6},{6,2},{3,7},{7,3},{8,12},{12,8},{9,1... | collective-permute-start | bytes 1572872 | tf_op jit(solution)/shard_map/ppermute | solution.py:18
  639.5 24.1 %collective-permute-start.106 = (bf16[512,512]{0,1:T(8,128)(2,1)S(1)}, bf16[512,512]{0,1:T(8,128)(2,1)S(1)}, u32[]{:S(2)}, u32[]{:S(2)}) collective-permute-start(bf16[512,512]{0,1:T(8,128)(2,1)S(1)} %fusion.29), channel_id=1, source_target_pairs={{0,16},{16,0},{1,17},{17,1},{2,18},{18,2},{3,19},{19,3},{4,20},{20... | collective-permute-start | bytes 1572872 | tf_op jit(solution)/shard_map/ppermute | solution.py:18
  (256 other events, 2640.3 us)
